TPU v7x, 32 devices: a whole 2x2x4 slice. The times are simulated.
32 devices in a mesh: width: 2 (over y), dp: 16 (over z, x, core).
Axes of the slice: x: 2, y: 2, z: 4, core: 2. Of those that a mesh axis runs over, the one named last changes fastest.
Arguments:
- tokens: bfloat16 [8192, 2048], P(('width', 'dp')), may hold values from -6 to 6
- cotangent: bfloat16 [8192, 2048], P(('width', 'dp')), may hold values from -6 to 6
- lengths: int32 [2, 8], P('width'), may hold values from 1 to 1024, 4096 in all within a row
- levels: int32 [2], P('width'), may hold values from 0 to 1, each once
- step_count: int32 [1], replicated, may hold values from 1 to 5
- weight_in: float32 [2048, 8512], P('dp'), may hold values from -0.125 to 0.125
- moment_in: float32 [2048, 8512], P('dp'), may hold values from -181.01933 to 181.01933
- second_in: float32 [2048, 8512], P('dp'), may hold values from 2048 to 8192
- weight_out: float32 [4096, 2048], P('dp'), may hold values from -0.09375 to 0.09375
- moment_out: float32 [4096, 2048], P('dp'), may hold values from -362.03867 to 362.03867
- second_out: float32 [4096, 2048], P('dp'), may hold values from 8192 to 32768
- small_params: float32 [28096], replicated, may hold values from -9 to 2
- moment_small: float32 [28096], replicated, may hold values from -1024 to 1024
- second_small: float32 [28096], replicated, may hold values from 4096 to 262144
Outputs:
- block_out: bfloat16 [8192, 2048], P(('width', 'dp'))
- grad_tokens: bfloat16 [8192, 2048], P(('width', 'dp'))
- new_weight_in: float32 [2048, 8512], P('dp')
- new_moment_in: float32 [2048, 8512], P('dp')
- new_second_in: float32 [2048, 8512], P('dp')
- low_weight_in: bfloat16 [2048, 8512], P('dp')
- new_weight_out: float32 [4096, 2048], P('dp')
- new_moment_out: float32 [4096, 2048], P('dp')
- new_second_out: float32 [4096, 2048], P('dp')
- low_weight_out: bfloat16 [4096, 2048], P('dp')
- new_small: float32 [28096], replicated
- new_moment_small: float32 [28096], replicated
- new_second_small: float32 [28096], replicated
Inputs may be any that keep to these rules, and one draw needn't show every extreme that they name: Each row of lengths sums to 4096, and its longest sequence has exactly 1024 tokens. `levels`: each level 0 to 1 is held by exactly one width group.
All inputs are finite; a program needn't handle non-finite values.
Results may differ from a plain program's by a relative error of at most 0.0095.
Values may be sent and summed in bfloat16 or wider, within the bound.
No kernel may reach another device: no remote copies, remote signals or barrier semaphores. Data moves between devices by JAX's collectives and lax.ppermute only.
A program may use at most 448 MiB of HBM per device.

v0:
```python
from functools import partial

import jax
import jax.numpy as jnp
from jax import lax
from jax.sharding import PartitionSpec as P

D = 2048
E = 4096
H = 64
P_SIZE = 64
N = 128
KCONV = 4
STRETCH = 256
K = 4352


NORM_EPS = 1e-05
ADAM_EPS = 1e-08
BETA_ONE = 0.5
BETA_TWO = 0.5
MATRIX_RATE = 0.02
MATRIX_DECAY = 0.1
PRECISE = lax.Precision.HIGHEST


def shifted(value, axis, steps):
    count = lax.axis_size(axis)
    initial, last = (max(0, -steps), min(count, count - steps))
    return lax.ppermute(value, axis, [(source, source + steps) for source in range(initial, last)])


def carried_in(x, axis, combine, identity):
    peers, here = (lax.axis_size(axis), lax.axis_index(axis))
    everything = jax.tree.map(
        lambda part, kind: lax.all_gather(part.astype(kind), axis), x, (jnp.bfloat16, jnp.bfloat16)
    )
    start = jax.tree.map(
        lambda part, zero: jnp.broadcast_to(jnp.asarray(zero, part.dtype), part.shape), x, identity
    )

    def lap(k, before):
        reached = k < here
        new = combine(
            before, jax.tree.map(lambda part, own: part[k].astype(own.dtype), everything, x)
        )
        return jax.tree.map(lambda a, b: jnp.where(reached, a, b), new, before)

    return lax.fori_loop(0, peers, lap, start)


def carried_in_2(x, axis, join, neutral):
    count = lax.axis_size(axis)
    place = lax.axis_index(axis)
    ahead = count - 1 - place
    gathered = jax.tree.map(
        lambda a, kind: lax.all_gather(a.astype(kind), axis),
        x,
        jax.tree.map(lambda a: jnp.bfloat16 if a.dtype == jnp.float32 else a.dtype, x),
    )
    state = jax.tree.map(lambda a, e: jnp.zeros_like(a) + jnp.asarray(e, a.dtype), x, neutral)

    def one(lap, state):
        source = count - 1 - lap
        return join(
            state,
            jax.tree.map(
                lambda a, own: lax.dynamic_index_in_dim(a, source, 0, False).astype(own.dtype),
                gathered,
                x,
            ),
        )

    return lax.fori_loop(0, ahead, one, state)


def small_table():
    rate_table = jnp.concatenate(
        [
            jnp.full((D,), 0.3, jnp.float32),
            jnp.full((E,), 0.3, jnp.float32),
            jnp.full((KCONV * K,), 0.2, jnp.float32),
            jnp.full((K,), 0.2, jnp.float32),
            jnp.full((H,), 0.3, jnp.float32),
            jnp.full((H,), 1.0, jnp.float32),
            jnp.full((H,), 0.3, jnp.float32),
        ]
    )
    decay_table = jnp.concatenate(
        [
            jnp.zeros((D + E,), jnp.float32),
            jnp.full((KCONV * K,), 0.1, jnp.float32),
            jnp.zeros((K + 3 * H,), jnp.float32),
        ]
    )
    return (rate_table, decay_table)


def unpack(small_params):
    offset = D + E
    conv_w = small_params[offset : offset + KCONV * K].reshape(KCONV, K)
    offset = offset + KCONV * K
    conv_b = small_params[offset : offset + K]
    offset = offset + K
    a_log = small_params[offset : offset + H]
    dt_bias = small_params[offset + H : offset + 2 * H]
    d_skip = small_params[offset + 2 * H : offset + 3 * H]
    return (small_params[:D], small_params[D : D + E], conv_w, conv_b, a_log, dt_bias, d_skip)


def positions(lengths_row, start, row_count):
    seq_ends = jnp.cumsum(lengths_row)
    place_at = start + jnp.arange(row_count, dtype=jnp.int32)
    before = jnp.sum(
        jnp.where(seq_ends[None, :] <= place_at[:, None], lengths_row[None, :], 0), axis=1
    )
    return place_at - before


def pre_norm(inputs_f, small_params):
    g_in = small_params[:D]
    return (
        inputs_f * lax.rsqrt(jnp.mean(inputs_f * inputs_f, axis=1, keepdims=True) + NORM_EPS) * g_in
    )


def front_part(projected, prior_rows, small_params, seq_place, live_units):
    g_in, g_out, conv_w, conv_b, a_log, dt_bias, d_skip = unpack(small_params)
    row_count = projected.shape[0]
    conv_input = jnp.concatenate([prior_rows, projected[:, E : E + K]], axis=0)
    conv_sum = conv_b + jnp.zeros((row_count, K), jnp.float32)
    for tap_index in range(KCONV):
        valid = (seq_place >= KCONV - 1 - tap_index).astype(jnp.float32)
        conv_sum = (
            conv_sum
            + conv_w[tap_index] * conv_input[tap_index : tap_index + row_count] * valid[:, None]
        )
    activated = jax.nn.silu(conv_sum)
    unit_mask = (jnp.arange(E, dtype=jnp.int32) < live_units).astype(jnp.float32)
    inner_x = activated[:, :E] * unit_mask
    b_values = activated[:, E : E + N]
    c_values = activated[:, E + N :]
    gate_raw = projected[:, :E]
    step_size = jax.nn.softplus(projected[:, E + K :] + dt_bias)
    log_decay = step_size * -jnp.exp(a_log)
    return (gate_raw, inner_x, step_size, log_decay, b_values, c_values)


def stretch_step(carried, pieces):
    values_x, step_size, log_decay, b_values, c_values, seq_place = pieces
    index_row = jnp.arange(STRETCH, dtype=jnp.int32)
    cumulate = jnp.cumsum(log_decay, axis=0)
    visible = (index_row[None, :] <= index_row[:, None]) & (
        seq_place[:, None] >= index_row[:, None] - index_row[None, :]
    )
    gap_log = jnp.where(visible[:, :, None], cumulate[:, None, :] - cumulate[None, :, :], 0.0)
    gram = jnp.einsum("in,jn->ij", c_values, b_values, precision=PRECISE)
    mixing = jnp.where(visible[:, :, None], jnp.exp(gap_log), 0.0) * gram[:, :, None]
    scaled_x = values_x * step_size[:, :, None]
    within = jnp.einsum("ijh,jhp->ihp", mixing, scaled_x, precision=PRECISE)
    carrying = jnp.where((seq_place >= index_row + 1)[:, None], jnp.exp(cumulate), 0.0)
    across = jnp.einsum("in,hpn->ihp", c_values, carried, precision=PRECISE) * carrying[:, :, None]
    tail_ok = seq_place[STRETCH - 1] >= STRETCH - 1 - index_row
    tail_weight = jnp.where(
        tail_ok[:, None],
        jnp.exp(jnp.where(tail_ok[:, None], cumulate[STRETCH - 1][None, :] - cumulate, 0.0)),
        0.0,
    )
    fresh_state = jnp.einsum(
        "jhp,jn->hpn", scaled_x * tail_weight[:, :, None], b_values, precision=PRECISE
    )
    updated = carried * carrying[STRETCH - 1][:, None, None] + fresh_state
    return (updated, within + across)


def local_ssd(inner_x, step_size, log_decay, b_values, c_values, seq_place):
    row_count = inner_x.shape[0]
    blocks = row_count // STRETCH
    pieces = (
        inner_x.reshape(blocks, STRETCH, H, P_SIZE),
        step_size.reshape(blocks, STRETCH, H),
        log_decay.reshape(blocks, STRETCH, H),
        b_values.reshape(blocks, STRETCH, N),
        c_values.reshape(blocks, STRETCH, N),
        seq_place.reshape(blocks, STRETCH),
    )
    final, outputs = lax.scan(stretch_step, jnp.zeros((H, P_SIZE, N), jnp.float32), pieces)
    through = seq_place[row_count - 1] >= row_count
    device_decay = jnp.where(through, jnp.exp(jnp.sum(log_decay, axis=0)), 0.0)
    return (outputs.reshape(row_count, E), device_decay, final)


def inject(state_in, log_decay, c_values, seq_place):
    row_count = log_decay.shape[0]
    cumulate = jnp.cumsum(log_decay, axis=0)
    keeping = (seq_place >= jnp.arange(row_count, dtype=jnp.int32) + 1).astype(jnp.float32)
    factor = jnp.exp(cumulate) * keeping[:, None]
    carried = jnp.einsum("tn,hpn->thp", c_values, state_in, precision=PRECISE) * factor[:, :, None]
    return carried.reshape(row_count, E)


def back_end(y_local, y_carried, inner_x, gate_raw, small_params, live_units):
    d_skip = unpack(small_params)[6]
    row_count = inner_x.shape[0]
    mixed = (
        y_local
        + y_carried
        + (inner_x.reshape(row_count, H, P_SIZE) * d_skip[:, None]).reshape(row_count, E)
    )
    gated = mixed * jax.nn.silu(gate_raw)
    g_out = small_params[D : D + E]
    return (
        gated
        * lax.rsqrt(
            jnp.sum(gated * gated, axis=1, keepdims=True) / live_units.astype(jnp.float32)
            + NORM_EPS
        )
        * g_out
    )


def joined(earlier, later):
    return (earlier[0] * later[0], later[0][:, None, None] * earlier[1] + later[1])


def adamw_step(weight, moment, second, grad, rate, decay, step_float):
    first_new = BETA_ONE * moment + (1.0 - BETA_ONE) * grad
    second_new = BETA_TWO * second + (1.0 - BETA_TWO) * grad * grad
    first_hat = first_new / (1.0 - jnp.power(BETA_ONE, step_float))
    second_hat = second_new / (1.0 - jnp.power(BETA_TWO, step_float))
    return (
        weight - rate * (first_hat / (jnp.sqrt(second_hat) + ADAM_EPS) + decay * weight),
        first_new,
        second_new,
    )


def column_update(weight, moment, second, grad_piece, group_slot, step_float):
    columns = grad_piece.shape[1]
    start = group_slot * columns
    return adamw_step(
        lax.dynamic_slice_in_dim(weight, start, columns, 1),
        lax.dynamic_slice_in_dim(moment, start, columns, 1),
        lax.dynamic_slice_in_dim(second, start, columns, 1),
        grad_piece,
        MATRIX_RATE,
        MATRIX_DECAY,
        step_float,
    )


def per_device(
    tokens,
    cotangent,
    lengths,
    levels,
    step_count,
    weight_in,
    moment_in,
    second_in,
    weight_out,
    moment_out,
    second_out,
    small_params,
    moment_small,
    second_small,
):
    full_in, full_out = (
        lax.all_gather(weight_in.astype(jnp.bfloat16), "dp", axis=0, tiled=True),
        lax.all_gather(weight_out.astype(jnp.bfloat16), "dp", axis=0, tiled=True),
    )
    row_count = tokens.shape[0]
    live_units = jnp.right_shift(jnp.int32(E), lax.axis_size("width") - 1 - levels[0])
    seq_place = positions(lengths[0], lax.axis_index("dp") * row_count, row_count)
    inputs_f = tokens.astype(jnp.float32)
    normed, norm_back = jax.vjp(pre_norm, inputs_f, small_params)
    normed_low = normed.astype(jnp.bfloat16)
    project_low = jnp.dot(normed_low, full_in, preferred_element_type=jnp.float32).astype(
        jnp.bfloat16
    )
    prior_rows = shifted(project_low[row_count - (KCONV - 1) :, E : E + K], "dp", 1)
    front_fn = partial(front_part, seq_place=seq_place, live_units=live_units)
    front_out, front_back = jax.vjp(
        front_fn, project_low.astype(jnp.float32), prior_rows.astype(jnp.float32), small_params
    )
    gate_raw, inner_x, step_size, log_decay, b_values, c_values = front_out
    ssd_fn = partial(local_ssd, seq_place=seq_place)
    ssd_out, ssd_back = jax.vjp(ssd_fn, inner_x, step_size, log_decay, b_values, c_values)
    y_local, device_decay, device_state = ssd_out
    identity = (jnp.ones((H,), jnp.float32), jnp.zeros((H, P_SIZE, N), jnp.float32))
    state_in = carried_in((device_decay, device_state), "dp", joined, identity)[1]
    inject_fn = partial(inject, seq_place=seq_place)
    y_carried, inject_back = jax.vjp(inject_fn, state_in, log_decay, c_values)
    end_fn = partial(back_end, live_units=live_units)
    normed_out, end_back = jax.vjp(end_fn, y_local, y_carried, inner_x, gate_raw, small_params)
    out_low = normed_out.astype(jnp.bfloat16)
    block_out = (inputs_f + jnp.dot(out_low, full_out, preferred_element_type=jnp.float32)).astype(
        jnp.bfloat16
    )
    grad_weight_out = lax.dot_general(
        out_low, cotangent, (((0,), (0,)), ((), ())), preferred_element_type=jnp.float32
    )
    grad_out_low = lax.dot_general(
        cotangent, full_out, (((1,), (1,)), ((), ())), preferred_element_type=jnp.float32
    )
    grad_local, grad_carried, grad_x_end, grad_gate, grad_small_end = end_back(grad_out_low)
    grad_state_in, grad_decay_a, grad_c_a = inject_back(grad_carried)
    grad_after = carried_in_2((device_decay, grad_state_in), "dp", joined, identity)[1]
    grad_device_decay = jnp.sum(grad_after * state_in, axis=(1, 2))
    grad_x_ssd, grad_step, grad_decay_b, grad_b, grad_c_b = ssd_back(
        (grad_local, grad_device_decay, grad_after)
    )
    grad_projected, grad_prior, grad_small_front = front_back(
        (
            grad_gate,
            grad_x_end + grad_x_ssd,
            grad_step,
            grad_decay_a + grad_decay_b,
            grad_b,
            grad_c_a + grad_c_b,
        )
    )
    returned_rows = shifted(grad_prior.astype(jnp.bfloat16), "dp", -1).astype(grad_prior.dtype)
    grad_projected = grad_projected.at[row_count - (KCONV - 1) :, E : E + K].add(returned_rows)
    grad_project_low = grad_projected.astype(jnp.bfloat16)
    grad_weight_in = lax.dot_general(
        normed_low, grad_project_low, (((0,), (0,)), ((), ())), preferred_element_type=jnp.float32
    )
    grad_normed = lax.dot_general(
        grad_project_low, full_in, (((1,), (1,)), ((), ())), preferred_element_type=jnp.float32
    )
    grad_inputs, grad_small_norm = norm_back(grad_normed)
    grad_tokens = (cotangent.astype(jnp.float32) + grad_inputs).astype(jnp.bfloat16)
    step_float = step_count[0].astype(jnp.float32)
    total_small = lax.psum(grad_small_end + grad_small_front + grad_small_norm, ("width", "dp"))
    rate_table, decay_table = small_table()
    new_small, mom_small, sec_small = adamw_step(
        small_params, moment_small, second_small, total_small, rate_table, decay_table, step_float
    )
    group_slot = lax.axis_index("width")
    part_in, part_out = (
        lax.psum_scatter(grad_weight_in, "dp", scatter_dimension=0, tiled=True),
        lax.psum_scatter(grad_weight_out, "dp", scatter_dimension=0, tiled=True),
    )
    part_in, part_out = (
        lax.psum_scatter(part_in, "width", scatter_dimension=1, tiled=True),
        lax.psum_scatter(part_out, "width", scatter_dimension=1, tiled=True),
    )
    piece_in = column_update(weight_in, moment_in, second_in, part_in, group_slot, step_float)
    piece_out = column_update(weight_out, moment_out, second_out, part_out, group_slot, step_float)
    new_in, mom_in, sec_in, new_out, mom_out, sec_out = (
        lax.all_gather(piece_in[0], "width", axis=1, tiled=True),
        lax.all_gather(piece_in[1], "width", axis=1, tiled=True),
        lax.all_gather(piece_in[2], "width", axis=1, tiled=True),
        lax.all_gather(piece_out[0], "width", axis=1, tiled=True),
        lax.all_gather(piece_out[1], "width", axis=1, tiled=True),
        lax.all_gather(piece_out[2], "width", axis=1, tiled=True),
    )
    return (
        block_out,
        grad_tokens,
        new_in,
        mom_in,
        sec_in,
        new_in.astype(jnp.bfloat16),
        new_out,
        mom_out,
        sec_out,
        new_out.astype(jnp.bfloat16),
        new_small,
        mom_small,
        sec_small,
    )


def solution(mesh):
    return jax.shard_map(
        per_device,
        mesh=mesh,
        in_specs=(
            P(("width", "dp"), None),
            P(("width", "dp"), None),
            P("width", None),
            P("width"),
            P(),
            P("dp", None),
            P("dp", None),
            P("dp", None),
            P("dp", None),
            P("dp", None),
            P("dp", None),
            P(),
            P(),
            P(),
        ),
        out_specs=(
            P(("width", "dp"), None),
            P(("width", "dp"), None),
            P("dp", None),
            P("dp", None),
            P("dp", None),
            P("dp", None),
            P("dp", None),
            P("dp", None),
            P("dp", None),
            P("dp", None),
            P(),
            P(),
            P(),
        ),
        check_vma=False,
    )
```

profile of v0, /device:TPU:0, one launch (start us, length us, event | category | flops | bytes accessed | tf_op | source)
XLA Modules:
  0.0 2187.4 jit_solution(13441290092037121017)
XLA Ops:
  7.3 3.5 convert_element_type.165
  14.0 182.8 %all-gather.14.cloned.1.call-done = bf16[2048,8512]{0,1:T(8,128)(2,1)} async-done(((bf16[128,8512]{0,1:T(8,128)(2,1)}), bf16[2048,8512]{0,1:T(8,128)(2,1)}) %all-gather.14.cloned.1.call-update) | async-done | bytes 34865168 | tf_op jit(solution)/shard_map/all_gather | solution.py:269
  196.8 17.8 fusion.148
  223.8 4.1 slice.177
  228.5 12.9 fusion.27
  245.0 4.4 add_convert_fusion
  254.4 32.2 %all-reduce.23 = bf16[1024]{0:T(1024)(128)(2,1)S(1)} all-reduce(bf16[1024]{0:T(1024)(128)(2,1)S(1)} %dynamic-update-slice.2), channel_id=2, replica_groups=mesh['width'=2,'dp'=16] {'dp'}, use_global_device_ids=true, to_apply=%add.23 | all-reduce | flops 1024 | bytes 4096
  288.0 5.9 fusion.89
  293.9 81.8 %all-gather.30.cloned.1.call-done = bf16[1024,64,128]{2,1,0:T(8,128)(2,1)} async-done(((bf16[64,64,128]{2,1,0:T(8,128)(2,1)}), bf16[1024,64,128]{2,1,0:T(8,128)(2,1)}) %all-gather.30.cloned.1.call-update) | async-done | bytes 16777232 | tf_op jit(solution)/shard_map/all_gather | solution.py:36
  375.7 29.2 %while.22 = (s32[]{:T(128)}, f32[64,64,128]{2,1,0:T(8,128)S(1)}, s32[]{:T(128)}, bf16[16,64]{1,0:T(8,128)(2,1)S(1)}, bf16[16,64,64,128]{3,2,1,0:T(8,128)(2,1)}, /*index=5*/s32[]{:T(128)}, s32[]{:T(128)}) while((s32[]{:T(128)}, f32[64,64,128]{2,1,0:T(8,128)S(1)}, s32[]{:T(128)}, bf16[16,64]{1,0:T(8,128)(2,1)S(1)}, ...), condition=%wide.region_7.8_spmd.clone, body=%wide.region_6.7_spmd.clone.sunk | while | flops 2621508 | bytes 5243633 | solution.py:49
  404.9 4.6 fusion.99
  409.6 21.4 fusion.31
  431.0 7.3 multiply_reduce_fusion.11
  438.4 65.1 %all-gather.16.cloned.1.call-done = bf16[4096,2048]{1,0:T(8,128)(2,1)} async-done(((bf16[256,2048]{1,0:T(8,128)(2,1)}), bf16[4096,2048]{1,0:T(8,128)(2,1)}) %all-gather.16.cloned.1.call-update) | async-done | bytes 16777232 | tf_op jit(solution)/shard_map/all_gather | solution.py:270
  503.5 13.7 multiply_reduce_fusion.5
  517.3 8.2 multiply_reduce_fusion.4
  527.5 5.3 fusion.77
  532.9 16.2 fusion.134
  549.2 7.2 multiply_reduce_fusion.8
  560.0 6.3 fusion.83
  566.3 26.5 %fusion.12 = (f32[256,64]{0,1:T(8,128)}, f32[256,64]{0,1:T(8,128)}, f32[256,256]{1,0:T(8,128)S(1)}) fusion(f32[256,256]{1,0:T(8,128)S(1)} %copy-done.30, f32[256,64]{0,1:T(8,128)S(1)} %copy-done.43, pred[256,256]{1,0:T(8,128)(4,1)S(1)} %copy-done.54, f32[64,64,256]{2,1,0:T(8,128)S(1)} %bitcast.207, f32[256,64,64]{0,2,1:T(8,128)} %bitcast.212, ...), kind=kOutput, calls=%fused_computation.18 | convolution fusion | flops 3268313088 | bytes 9240576 | tf_op jit(solution)/shard_map/transpose(jvp())/while/body/eval_jaxpr/ijh,jhp->ihp/dot_general | solution.py:160
  592.9 65.2 %all-gather.32.cloned.1.call-done = bf16[1024,64,128]{2,1,0:T(8,128)(2,1)} async-done(((bf16[64,64,128]{2,1,0:T(8,128)(2,1)}), bf16[1024,64,128]{2,1,0:T(8,128)(2,1)}) %all-gather.32.cloned.1.call-update) | async-done | bytes 16777232 | tf_op jit(solution)/shard_map/all_gather | solution.py:57
  658.3 39.0 %while.21 = (s32[]{:T(128)}, f32[64,64,128]{2,1,0:T(8,128)S(1)}, s32[]{:T(128)}, bf16[16,64]{1,0:T(8,128)(2,1)}, bf16[16,64,64,128]{3,2,1,0:T(8,128)(2,1)}, /*index=5*/s32[]{:T(128)}, s32[]{:T(128)}, s32[]{:T(128)}, s32[]{:T(128)}) while((s32[]{:T(128)}, f32[64,64,128]{2,1,0:T(8,128)S(1)}, s32[]{:T(128)}, bf16[16,64]{1,0:T(8,128)(2,1)}, ...), condition=%wide.region_11.12_spmd, body=%wide.region_10.11_spmd.sunk | while | flops 1572934 | bytes 5243675 | solution.py:74
  697.4 4.7 fusion.95
  702.1 17.5 multiply_reduce_fusion.7
  722.6 4.0 fusion.80
  731.6 21.2 fusion.135
  752.8 7.9 multiply_multiply_fusion.3
  760.7 7.0 pad_add_fusion.1
  780.7 10.7 pad_add_fusion
  796.3 13.9 scatter-add.4
  810.1 28.8 %fusion.50 = f32[2048,8512]{0,1:T(8,128)} fusion(f32[256,8512]{0,1:T(8,128)} %scatter-add.4, bf16[256,2048]{1,0:T(8,128)(2,1)S(1)} %copy-done.11, f32[2048]{0:T(1024)S(1)} %copy-done.45, f32[256]{0:T(256)S(1)} %copy-done.61), kind=kOutput, calls=%fused_computation.103 | convolution fusion | flops 8929755136 | bytes 79504384 | tf_op jit(solution)/shard_map/dot_general | solution.py:326
  839.1 153.9 %reduce-scatter.9.cloned.1.call-done = f32[256,2048]{1,0:T(8,128)} async-done(((f32[4096,2048]{1,0:T(8,128)}), f32[256,2048]{1,0:T(8,128)}) %reduce-scatter.9.cloned.1.call-update) | async-done | bytes 2097168 | tf_op jit(solution)/shard_map/reduce_scatter | solution.py:343
  993.1 665.1 %reduce-scatter.5.cloned.1.call-done = f32[128,8512]{0,1:T(8,128)} async-done(((f32[2048,8512]{0,1:T(8,128)}), f32[128,8512]{0,1:T(8,128)}) %reduce-scatter.5.cloned.1.call-update) | async-done | bytes 4358160 | tf_op jit(solution)/shard_map/reduce_scatter | solution.py:342
  1659.4 19.1 fusion.57
  1679.6 12.0 reduce-scatter.11.cloned.1.call-done
  1691.6 4.5 multiply_subtract_fusion.1
  1697.5 52.5 %reduce-scatter.7.cloned.1.call-done = f32[128,4256]{0,1:T(8,128)} async-done(((f32[128,8512]{0,1:T(8,128)}), f32[128,4256]{0,1:T(8,128)}) %reduce-scatter.7.cloned.1.call-update) | async-done | bytes 2179088 | tf_op jit(solution)/shard_map/reduce_scatter | solution.py:346
  1750.0 7.5 multiply_subtract_fusion
  1758.7 12.7 fusion.46
  1773.2 103.7 %all-reduce.26.cloned.1.call-done = f32[28096]{0:T(1024)} async-done(((f32[28096]{0:T(1024)}), f32[28096]{0:T(1024)}) %all-reduce.26.cloned.1.call-update) | async-done | bytes 112400 | tf_op jit(solution)/shard_map/psum | solution.py:335
  1878.7 34.0 %all-gather.24.cloned.1.call-done = f32[256,2048]{1,0:T(8,128)} async-done(((f32[256,1024]{1,0:T(8,128)}), f32[256,2048]{1,0:T(8,128)}) %all-gather.24.cloned.1.call-update) | async-done | bytes 2097168 | tf_op jit(solution)/shard_map/all_gather | solution.py:355
  1915.4 32.6 %all-gather.28.cloned.1.call-done = f32[256,2048]{1,0:T(8,128)} async-done(((f32[256,1024]{1,0:T(8,128)}), f32[256,2048]{1,0:T(8,128)}) %all-gather.28.cloned.1.call-update) | async-done | bytes 2097168 | tf_op jit(solution)/shard_map/all_gather | solution.py:357
  1948.0 35.1 %all-gather.26.cloned.1.call-done = f32[256,2048]{1,0:T(8,128)} async-done(((f32[256,1024]{1,0:T(8,128)}), f32[256,2048]{1,0:T(8,128)}) %all-gather.26.cloned.1.call-update) | async-done | bytes 2097168 | tf_op jit(solution)/shard_map/all_gather | solution.py:356
  1983.1 60.7 %all-gather.18.cloned.1.call-done = f32[128,8512]{0,1:T(8,128)} async-done(((f32[128,4256]{0,1:T(8,128)}), f32[128,8512]{0,1:T(8,128)}) %all-gather.18.cloned.1.call-update) | async-done | bytes 4358160 | tf_op jit(solution)/shard_map/all_gather | solution.py:352
  2047.2 57.2 %all-gather.22.cloned.1.call-done = f32[128,8512]{0,1:T(8,128)} async-done(((f32[128,4256]{0,1:T(8,128)}), f32[128,8512]{0,1:T(8,128)}) %all-gather.22.cloned.1.call-update) | async-done | bytes 4358160 | tf_op jit(solution)/shard_map/all_gather | solution.py:354
  2104.5 60.6 %all-gather.20.cloned.1.call-done = f32[128,8512]{0,1:T(8,128)} async-done(((f32[128,4256]{0,1:T(8,128)}), f32[128,8512]{0,1:T(8,128)}) %all-gather.20.cloned.1.call-update) | async-done | bytes 4358160 | tf_op jit(solution)/shard_map/all_gather | solution.py:353
  2165.1 4.1 copy.193
  (369 shorter events, 143.6 us)
Async XLA Ops:
  7.2 189.6 %all-gather.14.cloned.1.call-start = ((), (), s32[]{:S(2)}) async-start(), calls=%async_computation.4 | async-start | bytes 37044224 | tf_op jit(solution)/shard_map/all_gather | solution.py:269
  10.7 364.9 %all-gather.30.cloned.1.call-start = ((), (), s32[]{:S(2)}) async-start(), calls=%async_computation.17 | async-start | bytes 17825792 | tf_op jit(solution)/shard_map/all_gather | solution.py:36
  12.3 202.3 %copy-start.44 = (f32[2048]{0:T(1024)}, f32[2048]{0:T(1024)S(1)}, u32[]{:S(2)}) copy-start(f32[2048]{0:T(1024)S(1)} %slice.147) | copy-start | bytes 24580
  13.3 201.3 %copy-start.60 = (f32[256]{0:T(256)}, f32[256]{0:T(256)S(1)}, u32[]{:S(2)}) copy-start(f32[256]{0:T(256)S(1)} %fusion.124) | copy-start | bytes 3076
  13.3 210.2 %copy-start.71 = (f32[256]{0:T(256)}, f32[256]{0:T(256)S(1)}, u32[]{:S(2)}) copy-start(f32[256]{0:T(256)S(1)} %get-tuple-element.593) | copy-start | bytes 3076
  13.3 210.2 %copy-start.79 = (pred[256]{0:T(512)(128)(4,1)}, pred[256]{0:T(512)(128)(4,1)S(1)}, u32[]{:S(2)}) copy-start(pred[256]{0:T(512)(128)(4,1)S(1)} %get-tuple-element.628) | copy-start | bytes 772
  13.4 210.2 %copy-start.82 = (pred[256]{0:T(512)(128)(4,1)}, pred[256]{0:T(512)(128)(4,1)S(1)}, u32[]{:S(2)}) copy-start(pred[256]{0:T(512)(128)(4,1)S(1)} %get-tuple-element.594) | copy-start | bytes 772
  13.9 214.6 %copy-start.63 = (f32[256]{0:T(256)}, f32[256]{0:T(256)S(1)}, u32[]{:S(2)}) copy-start(f32[256]{0:T(256)S(1)} %get-tuple-element.620) | copy-start | bytes 3076
  13.9 214.6 %copy-start.65 = (f32[256]{0:T(256)}, f32[256]{0:T(256)S(1)}, u32[]{:S(2)}) copy-start(f32[256]{0:T(256)S(1)} %get-tuple-element.621) | copy-start | bytes 3076
  13.9 214.6 %copy-start.67 = (f32[256]{0:T(256)}, f32[256]{0:T(256)S(1)}, u32[]{:S(2)}) copy-start(f32[256]{0:T(256)S(1)} %get-tuple-element.622) | copy-start | bytes 3076
  13.9 214.6 %copy-start.69 = (f32[256]{0:T(256)}, f32[256]{0:T(256)S(1)}, u32[]{:S(2)}) copy-start(f32[256]{0:T(256)S(1)} %get-tuple-element.623) | copy-start | bytes 3076
  13.9 200.7 %copy-start.81 = (f32[64]{0:T(128)}, f32[64]{0:T(128)S(1)}, u32[]{:S(2)}) copy-start(f32[64]{0:T(128)S(1)} %get-tuple-element.609) | copy-start | bytes 772
  14.0 239.4 %copy-start.75 = (f32[64]{0:T(128)}, f32[64]{0:T(128)S(1)}, u32[]{:S(2)}) copy-start(f32[64]{0:T(128)S(1)} %get-tuple-element.611) | copy-start | bytes 772
  14.0 214.5 %copy-start.34 = (f32[4352]{0:T(1024)}, f32[4352]{0:T(1024)S(1)}, u32[]{:S(2)}) copy-start(f32[4352]{0:T(1024)S(1)} %get-tuple-element.613) | copy-start | bytes 52228
  14.0 214.5 %copy-start.36 = (f32[4352]{0:T(1024)}, f32[4352]{0:T(1024)S(1)}, u32[]{:S(2)}) copy-start(f32[4352]{0:T(1024)S(1)} %get-tuple-element.614) | copy-start | bytes 52228
  14.0 214.5 %copy-start.38 = (f32[4352]{0:T(1024)}, f32[4352]{0:T(1024)S(1)}, u32[]{:S(2)}) copy-start(f32[4352]{0:T(1024)S(1)} %get-tuple-element.615) | copy-start | bytes 52228
  14.0 214.5 %copy-start.40 = (f32[4352]{0:T(1024)}, f32[4352]{0:T(1024)S(1)}, u32[]{:S(2)}) copy-start(f32[4352]{0:T(1024)S(1)} %get-tuple-element.616) | copy-start | bytes 52228
  219.1 190.5 %copy-start.42 = (f32[256,64]{0,1:T(8,128)}, f32[256,64]{0,1:T(8,128)S(1)}, u32[]{:S(2)}) copy-start(f32[256,64]{0,1:T(8,128)S(1)} %bitcast_bitcast_fusion) | copy-start | bytes 196612
  221.3 6.6 collective-permute-start
  249.4 254.1 %all-gather.16.cloned.1.call-start = ((), (), s32[]{:S(2)}) async-start(), calls=%async_computation.5 | async-start | bytes 17825792 | tf_op jit(solution)/shard_map/all_gather | solution.py:270
  250.6 407.5 %all-gather.32.cloned.1.call-start = ((), (), s32[]{:S(2)}) async-start(), calls=%async_computation.18 | async-start | bytes 17825792 | tf_op jit(solution)/shard_map/all_gather | solution.py:57
  251.2 281.7 %copy-start.26 = (f32[4096]{0:T(1024)}, f32[4096]{0:T(1024)S(1)}, u32[]{:S(2)}) copy-start(f32[4096]{0:T(1024)S(1)} %slice.170) | copy-start | bytes 49156
  251.4 265.9 %copy-start.32 = (f32[4096]{0:T(1024)}, f32[4096]{0:T(1024)S(1)}, u32[]{:S(2)}) copy-start(f32[4096]{0:T(1024)S(1)} %mul.768) | copy-start | bytes 49156
  253.4 156.2 %copy-start.53 = (pred[256,256]{1,0:T(8,128)(4,1)}, pred[256,256]{1,0:T(8,128)(4,1)S(1)}, u32[]{:S(2)}) copy-start(pred[256,256]{1,0:T(8,128)(4,1)S(1)} %fusion.94) | copy-start | bytes 196612
  288.0 121.6 %copy-start.29 = (f32[256,256]{1,0:T(8,128)}, f32[256,256]{1,0:T(8,128)S(1)}, u32[]{:S(2)}) copy-start(f32[256,256]{1,0:T(8,128)S(1)} %fusion.106) | copy-start | bytes 786436
  404.9 155.1 %copy-start = (f32[64,64,128]{2,1,0:T(8,128)}, f32[64,64,128]{2,1,0:T(8,128)S(1)}, u32[]{:S(2)}) copy-start(f32[64,64,128]{2,1,0:T(8,128)S(1)} %get-tuple-element.516) | copy-start | bytes 6291460
  404.9 26.1 %slice-start = ((s8[4456448]{0:T(1024)(128)(4,1)}), s8[4194304]{0:T(1024)(128)(4,1)S(1)}, s32[]{:S(2)}) async-start(s8[4456448]{0:T(1024)(128)(4,1)} %bitcast.209), calls=%async_computation.19 | async-start | bytes 8388608
  431.0 72.5 %copy-start.20 = (bf16[256,2048]{1,0:T(8,128)(2,1)S(1)}, bf16[256,2048]{1,0:T(8,128)(2,1)}, u32[]{:S(2)}) copy-start(bf16[256,2048]{1,0:T(8,128)(2,1)} %param.21) | copy-start | bytes 3145732
  438.4 94.5 %copy-start.55 = (f32[256]{0:T(256)}, f32[256]{0:T(256)S(1)}, u32[]{:S(2)}) copy-start(f32[256]{0:T(256)S(1)} %fusion.133) | copy-start | bytes 3076
  532.9 460.1 %reduce-scatter.9.cloned.1.call-start = ((), (), s32[]{:S(2)}) async-start(), calls=%async_computation.11 | async-start | bytes 35651584 | tf_op jit(solution)/shard_map/reduce_scatter | solution.py:343
  549.2 1109.0 %reduce-scatter.5.cloned.1.call-start = ((), (), s32[]{:S(2)}) async-start(), calls=%async_computation.6 | async-start | bytes 74088448 | tf_op jit(solution)/shard_map/reduce_scatter | solution.py:342
  777.4 14.0 collective-permute-start.1
  838.9 820.0 %copy-start.52 = (f32[4096]{0:T(1024)S(1)}, f32[4096]{0:T(1024)}, u32[]{:S(2)}) copy-start(f32[4096]{0:T(1024)} %get-tuple-element.580) | copy-start | bytes 49156
  839.0 820.2 %copy-start.51 = (f32[4352]{0:T(1024)S(1)}, f32[4352]{0:T(1024)}, u32[]{:S(2)}) copy-start(f32[4352]{0:T(1024)} %get-tuple-element.545) | copy-start | bytes 52228
  839.0 820.2 %copy-start.50 = (f32[4352]{0:T(1024)S(1)}, f32[4352]{0:T(1024)}, u32[]{:S(2)}) copy-start(f32[4352]{0:T(1024)} %get-tuple-element.546) | copy-start | bytes 52228
  839.0 820.2 %copy-start.49 = (f32[4352]{0:T(1024)S(1)}, f32[4352]{0:T(1024)}, u32[]{:S(2)}) copy-start(f32[4352]{0:T(1024)} %get-tuple-element.547) | copy-start | bytes 52228
  839.0 820.3 %copy-start.48 = (f32[4352]{0:T(1024)S(1)}, f32[4352]{0:T(1024)}, u32[]{:S(2)}) copy-start(f32[4352]{0:T(1024)} %get-tuple-element.548) | copy-start | bytes 52228
  839.0 820.4 %copy-start.25 = (f32[28096]{0:T(1024)S(1)}, f32[28096]{0:T(1024)}, u32[]{:S(2)}) copy-start(f32[28096]{0:T(1024)} %param.31) | copy-start | bytes 337156
  839.0 852.6 %reduce-scatter.11.cloned.1.call-start = ((), (), s32[]{:S(2)}) async-start(), calls=%async_computation.12 | async-start | bytes 3145728 | tf_op jit(solution)/shard_map/reduce_scatter | solution.py:347
  993.0 757.0 %reduce-scatter.7.cloned.1.call-start = ((), (), s32[]{:S(2)}) async-start(), calls=%async_computation.7 | async-start | bytes 6537216 | tf_op jit(solution)/shard_map/reduce_scatter | solution.py:346
  1658.2 218.6 %all-reduce.26.cloned.1.call-start = ((), (), s32[]{:S(2)}) async-start(), calls=%async_computation.16 | async-start | bytes 229376 | tf_op jit(solution)/shard_map/psum | solution.py:335
  1679.3 233.4 %all-gather.24.cloned.1.call-start = ((), (), s32[]{:S(2)}) async-start(), calls=%async_computation.13 | async-start | bytes 3145728 | tf_op jit(solution)/shard_map/all_gather | solution.py:355
  1696.1 251.9 %all-gather.28.cloned.1.call-start = ((), (), s32[]{:S(2)}) async-start(), calls=%async_computation.15 | async-start | bytes 3145728 | tf_op jit(solution)/shard_map/all_gather | solution.py:357
  1696.8 286.3 %all-gather.26.cloned.1.call-start = ((), (), s32[]{:S(2)}) async-start(), calls=%async_computation.14 | async-start | bytes 3145728 | tf_op jit(solution)/shard_map/all_gather | solution.py:356
  1697.4 346.4 %all-gather.18.cloned.1.call-start = ((), (), s32[]{:S(2)}) async-start(), calls=%async_computation.8 | async-start | bytes 6537216 | tf_op jit(solution)/shard_map/all_gather | solution.py:352
  1757.5 346.9 %all-gather.22.cloned.1.call-start = ((), (), s32[]{:S(2)}) async-start(), calls=%async_computation.10 | async-start | bytes 6537216 | tf_op jit(solution)/shard_map/all_gather | solution.py:354
  1758.1 406.9 %all-gather.20.cloned.1.call-start = ((), (), s32[]{:S(2)}) async-start(), calls=%async_computation.9 | async-start | bytes 6537216 | tf_op jit(solution)/shard_map/all_gather | solution.py:353
  1771.5 105.4 %copy-start.46 = (f32[28096]{0:T(1024)S(1)}, f32[28096]{0:T(1024)}, u32[]{:S(2)}) copy-start(f32[28096]{0:T(1024)} %param.33) | copy-start | bytes 337156
  (60 other events, 501.0 us)
Sparse Core Ops, SparseCore 0:
  10.9 185.9 all-gather.13
  249.5 126.1 all-gather.29
  378.4 125.0 all-gather.15
  533.0 125.0 all-gather.31
  662.2 330.7 reduce-scatter.8
  997.1 661.0 reduce-scatter.4
  1660.5 31.0 reduce-scatter.10
  1693.9 56.0 reduce-scatter.6
  1756.2 120.6 all-reduce.25
  1878.8 33.8 all-gather.23
  1914.8 33.1 all-gather.27
  1950.0 33.1 all-gather.25
  1985.2 58.5 all-gather.17
  2045.8 58.5 all-gather.21
  2106.4 58.5 all-gather.19
where the time goes:
time: 2200 us; the launch traced here: 2190 us
  waiting for transfers between devices  1660 us (75%)
  matrix products  215 us (10%)
  other arithmetic  195 us (9%)
  local copies, waits for them, and re-layouts  55.7 us (3%)
  blocking collectives  32.2 us (1%)
    reduce_scatter x1, waiting for transfers between devices, per_device(): lax.psum_scatter(grad_weight_in, 'dp', scatter_dimension=0, tiled=True)  665 us
    all_gather x1, waiting for transfers between devices, per_device(): lax.all_gather(weight_in.astype(jnp.bfloat16), 'dp', axis=0, tiled=True)  183 us
    reduce_scatter x1, waiting for transfers between devices, per_device(): lax.psum_scatter(grad_weight_out, 'dp', scatter_dimension=0, tiled=True)  154 us
    psum x1, waiting for transfers between devices, per_device(): lax.psum(grad_small_end + grad_small_front + grad_small_norm, ('width', '...  104 us
    all_gather x1, waiting for transfers between devices, carried_in(): lax.all_gather(part.astype(kind), axis)  81.8 us
    dot_general x3, matrix products, stretch_step(): within = jnp.einsum('ijh,jhp->ihp', mixing, scaled_x, precision=PRECISE)  65.4 us
    all_gather x1, waiting for transfers between devices, carried_in_2(): lax.all_gather(a.astype(kind), axis)  65.2 us
    all_gather x1, waiting for transfers between devices, per_device(): lax.all_gather(weight_out.astype(jnp.bfloat16), 'dp', axis=0, tiled=True)  65.1 us
  transfers between devices with their start and end apart: 17, of which 15 were waited for; matrix products, arithmetic and copies ran while one was open for 17% of the time, Pallas kernels for 0%

commit v1 on v0

v1 whole, which is shorter than its diff:
```python
from functools import partial

import jax
import jax.numpy as jnp
from jax import lax
from jax.experimental import pallas as pl
from jax.experimental.pallas import tpu as pltpu
from jax.sharding import PartitionSpec as P

D = 2048
E = 4096
H = 64
P_SIZE = 64
N = 128
KCONV = 4
STRETCH = 256
K = 4352

NORM_EPS = 1e-05
ADAM_EPS = 1e-08
BETA_ONE = 0.5
BETA_TWO = 0.5
MATRIX_RATE = 0.02
MATRIX_DECAY = 0.1
PRECISE = lax.Precision.HIGHEST
BF = jnp.bfloat16
F32 = jnp.float32
LOW = -1e30
SHARED = 2 * N + H


def small_table():
    rate_table = jnp.concatenate(
        [
            jnp.full((D,), 0.3, F32),
            jnp.full((E,), 0.3, F32),
            jnp.full((KCONV * K,), 0.2, F32),
            jnp.full((K,), 0.2, F32),
            jnp.full((H,), 0.3, F32),
            jnp.full((H,), 1.0, F32),
            jnp.full((H,), 0.3, F32),
        ]
    )
    decay_table = jnp.concatenate(
        [
            jnp.zeros((D + E,), F32),
            jnp.full((KCONV * K,), 0.1, F32),
            jnp.zeros((K + 3 * H,), F32),
        ]
    )
    return (rate_table, decay_table)


def unpack(small_params):
    offset = D + E
    conv_w = small_params[offset : offset + KCONV * K].reshape(KCONV, K)
    offset = offset + KCONV * K
    conv_b = small_params[offset : offset + K]
    offset = offset + K
    a_log = small_params[offset : offset + H]
    dt_bias = small_params[offset + H : offset + 2 * H]
    d_skip = small_params[offset + 2 * H : offset + 3 * H]
    return (small_params[:D], small_params[D : D + E], conv_w, conv_b, a_log, dt_bias, d_skip)


def row_places(lengths_row, row_count):
    seq_ends = jnp.cumsum(lengths_row)
    at = jnp.arange(row_count, dtype=jnp.int32)
    passed = seq_ends[None, :] <= at[:, None]
    begin = jnp.max(jnp.where(passed, seq_ends[None, :], 0), axis=1)
    finish = jnp.min(jnp.where(passed, row_count, seq_ends[None, :]), axis=1)
    return (at - begin, finish - 1 - at)


def adamw_step(weight, moment, second, grad, rate, decay, step_float):
    first_new = BETA_ONE * moment + (1.0 - BETA_ONE) * grad
    second_new = BETA_TWO * second + (1.0 - BETA_TWO) * grad * grad
    first_hat = first_new / (1.0 - jnp.power(BETA_ONE, step_float))
    second_hat = second_new / (1.0 - jnp.power(BETA_TWO, step_float))
    return (
        weight - rate * (first_hat / (jnp.sqrt(second_hat) + ADAM_EPS) + decay * weight),
        first_new,
        second_new,
    )


def sigmoid(v):
    return 1.0 / (1.0 + jnp.exp(-v))


def dot(a, b, dims):
    return lax.dot_general(
        a.astype(BF), b.astype(BF), (dims, ((), ())), preferred_element_type=F32
    )


def spread(columns, heads):
    return jnp.concatenate(
        [
            jnp.broadcast_to(columns[:, h : h + 1], (columns.shape[0], P_SIZE))
            for h in range(heads)
        ],
        axis=1,
    )


def head_sums(values, heads):
    lane = lax.broadcasted_iota(jnp.int32, (values.shape[0], 128), 1)
    total = jnp.zeros((values.shape[0], 128), F32)
    for h in range(heads):
        part = jnp.sum(values[:, h * P_SIZE : (h + 1) * P_SIZE], axis=1, keepdims=True)
        total = jnp.where(lane == h, part, total)
    return total


def convolve(buffer, weights, bias, place):
    total = bias + jnp.zeros((STRETCH, buffer.shape[1]), F32)
    for tap in range(KCONV):
        back = KCONV - 1 - tap
        rows = buffer[8 - back : 8 - back + STRETCH, :]
        if back:
            rows = jnp.where(place >= back, rows, 0.0)
        total = total + weights[tap : tap + 1, :] * rows
    return total


def block_terms(place, remain, dt_in, pdt):
    row = lax.broadcasted_iota(jnp.int32, (STRETCH, STRETCH), 0)
    col = lax.broadcasted_iota(jnp.int32, (STRETCH, STRETCH), 1)
    at = lax.broadcasted_iota(jnp.int32, (STRETCH, 1), 0)
    visible = (col <= row) & (col >= at - place)
    biased = dt_in + pdt[0:1, :]
    step = jnp.maximum(biased, 0.0) + jnp.log1p(jnp.exp(-jnp.abs(biased)))
    log_decay = step * pdt[1:2, :]
    lower = jnp.where(col <= row, 1.0, 0.0).astype(F32)
    cum = lax.dot_general(
        lower, log_decay, (((1,), (0,)), ((), ())), precision=PRECISE, preferred_element_type=F32
    )
    cum_t = jnp.transpose(cum)
    carrying = jnp.where(place >= at + 1, jnp.exp(cum), 0.0)
    tail_ok = remain >= STRETCH - 1 - at
    tail = jnp.exp(jnp.where(tail_ok, cum[STRETCH - 1 : STRETCH, :] - cum, LOW))
    return visible, biased, step, log_decay, cum, cum_t, carrying, tail


def forward_kernel(
    heads,
    gate_ref,
    x_ref,
    bc_ref,
    dt_ref,
    place_ref,
    remain_ref,
    px_ref,
    pbc_ref,
    pdt_ref,
    zin_ref,
    mixed_ref,
    square_ref,
    states_ref,
    state,
    xbuf,
    bcbuf,
):
    @pl.when(pl.program_id(0) == 0)
    def _():
        state[...] = jnp.zeros_like(state)
        xbuf[0:8, :] = jnp.zeros((8, xbuf.shape[1]), F32)
        bcbuf[0:8, :] = jnp.zeros((8, bcbuf.shape[1]), F32)

    place = place_ref[...]
    remain = remain_ref[...]
    xbuf[8 : 8 + STRETCH, :] = x_ref[...].astype(F32)
    bcbuf[8 : 8 + STRETCH, :] = bc_ref[...].astype(F32)
    conv_x = convolve(xbuf, px_ref[0:4, :], px_ref[4:5, :], place)
    conv_bc = convolve(bcbuf, pbc_ref[0:4, :], pbc_ref[4:5, :], place)
    xbuf[0:8, :] = xbuf[STRETCH : STRETCH + 8, :]
    bcbuf[0:8, :] = bcbuf[STRETCH : STRETCH + 8, :]
    x = conv_x * sigmoid(conv_x) * px_ref[7:8, :]
    act_bc = conv_bc * sigmoid(conv_bc)
    b_low = act_bc[:, :N].astype(BF)
    c_low = act_bc[:, N:].astype(BF)
    visible, _, step, _, cum, cum_t, carrying, tail = block_terms(
        place, remain, dt_ref[...].astype(F32), pdt_ref[...]
    )
    scaled = x * spread(step, heads)
    scaled_low = scaled.astype(BF)
    gram = dot(c_low, b_low, ((1,), (1,)))
    old = state[...]
    states_ref[0] = old
    across = dot(c_low, old, ((1,), (1,))) * spread(carrying, heads)
    parts = []
    for h in range(heads):
        decay = jnp.exp(jnp.where(visible, cum[:, h : h + 1] - cum_t[h : h + 1, :], LOW))
        parts.append(
            dot(gram * decay, scaled_low[:, h * P_SIZE : (h + 1) * P_SIZE], ((1,), (0,)))
        )
    mixed = jnp.concatenate(parts, axis=1) + across + px_ref[5:6, :] * x
    fresh = dot(scaled * spread(tail, heads), b_low, ((0,), (0,)))
    for h in range(heads):
        rows = slice(h * P_SIZE, (h + 1) * P_SIZE)
        state[rows, :] = (
            old[rows, :] * carrying[STRETCH - 1 : STRETCH, h : h + 1] + fresh[rows, :]
        )
    gate = gate_ref[...].astype(F32)
    gated = mixed * (gate * sigmoid(gate))
    mixed_ref[...] = mixed
    zin_ref[...] = (gated * px_ref[6:7, :]).astype(BF)
    square_ref[...] = jnp.sum(gated * gated, axis=1, keepdims=True)


def backward_kernel(
    heads,
    gate_ref,
    x_ref,
    bc_ref,
    dt_ref,
    xprev_ref,
    bcprev_ref,
    place_ref,
    remain_ref,
    mixed_ref,
    gout_ref,
    scale_ref,
    pull_ref,
    states_ref,
    px_ref,
    pbc_ref,
    pdt_ref,
    gp_ref,
    low_ref,
    gx_ref,
    gbc_ref,
    gdt_ref,
    gstate,
    xbuf,
    bcbuf,
    gxbuf,
    gbcbuf,
):
    width = x_ref.shape[1]

    @pl.when(pl.program_id(0) == 0)
    def _():
        gstate[...] = jnp.zeros_like(gstate)
        gxbuf[STRETCH : STRETCH + 8, :] = jnp.zeros((8, width), F32)
        gbcbuf[STRETCH : STRETCH + 8, :] = jnp.zeros((8, 2 * N), F32)
        gx_ref[...] = jnp.zeros_like(gx_ref)
        gbc_ref[...] = jnp.zeros_like(gbc_ref)
        gdt_ref[...] = jnp.zeros_like(gdt_ref)

    place = place_ref[...]
    remain = remain_ref[...]
    xbuf[0:8, :] = xprev_ref[8:16, :].astype(F32)
    bcbuf[0:8, :] = bcprev_ref[8:16, :].astype(F32)
    xbuf[8 : 8 + STRETCH, :] = x_ref[...].astype(F32)
    bcbuf[8 : 8 + STRETCH, :] = bc_ref[...].astype(F32)
    conv_x = convolve(xbuf, px_ref[0:4, :], px_ref[4:5, :], place)
    conv_bc = convolve(bcbuf, pbc_ref[0:4, :], pbc_ref[4:5, :], place)
    sig_x = sigmoid(conv_x)
    sig_bc = sigmoid(conv_bc)
    x = conv_x * sig_x * px_ref[7:8, :]
    act_bc = conv_bc * sig_bc
    b_low = act_bc[:, :N].astype(BF)
    c_low = act_bc[:, N:].astype(BF)
    visible, biased, step, log_decay, cum, cum_t, carrying, tail = block_terms(
        place, remain, dt_ref[...].astype(F32), pdt_ref[...]
    )

    gate = gate_ref[...].astype(F32)
    sig = sigmoid(gate)
    silu = gate * sig
    mixed = mixed_ref[...]
    gated = mixed * silu
    g_out = px_ref[6:7, :]
    scale = scale_ref[...]
    upstream = gout_ref[...]
    low_ref[...] = (gated * scale * g_out).astype(BF)
    g_gated = scale * g_out * upstream - gated * pull_ref[...]
    g_mixed = g_gated * silu
    gp_ref[:, 0:width] = (g_gated * mixed * (sig * (1.0 + gate * (1.0 - sig)))).astype(BF)

    step_wide = spread(step, heads)
    carry_wide = spread(carrying, heads)
    tail_wide = spread(tail, heads)
    scaled = x * step_wide
    scaled_low = scaled.astype(BF)
    g_low = g_mixed.astype(BF)
    old = states_ref[0]
    g_new = gstate[...]
    old_low = old.astype(BF)
    g_new_low = g_new.astype(BF)
    gram = dot(c_low, b_low, ((1,), (1,)))
    across = dot(c_low, old_low, ((1,), (1,)))
    returned = dot(b_low, g_new_low, ((1,), (1,))) * tail_wide
    g_carried = g_mixed * carry_wide
    g_carried_low = g_carried.astype(BF)
    tailed_low = (scaled * tail_wide).astype(BF)

    g_gram = jnp.zeros((STRETCH, STRETCH), F32)
    lane = lax.broadcasted_iota(jnp.int32, (STRETCH, 128), 1)
    row_sum = jnp.zeros((STRETCH, 128), F32)
    col_rows = []
    parts = []
    for h in range(heads):
        cols = slice(h * P_SIZE, (h + 1) * P_SIZE)
        decay = jnp.exp(jnp.where(visible, cum[:, h : h + 1] - cum_t[h : h + 1, :], LOW))
        mixing = gram * decay
        g_mixing = dot(g_low[:, cols], scaled_low[:, cols], ((1,), (1,)))
        parts.append(dot(mixing, g_low[:, cols], ((0,), (0,))))
        g_gram = g_gram + g_mixing * decay
        both = g_mixing * mixing
        row_sum = jnp.where(lane == h, jnp.sum(both, axis=1, keepdims=True), row_sum)
        col_rows.append(jnp.sum(both, axis=0, keepdims=True))
    col_rows.append(jnp.zeros((128 - heads, STRETCH), F32))
    col_sum = jnp.transpose(jnp.concatenate(col_rows, axis=0))
    g_scaled = jnp.concatenate(parts, axis=1) + returned
    into = head_sums(g_carried * across, heads)
    outof = head_sums(scaled * returned, heads)
    state_dot = jnp.zeros((1, 128), F32)
    lane_one = lax.broadcasted_iota(jnp.int32, (1, 128), 1)
    product = g_new * old
    for h in range(heads):
        total = jnp.sum(
            jnp.sum(product[h * P_SIZE : (h + 1) * P_SIZE, :], axis=0, keepdims=True),
            axis=1,
            keepdims=True,
        )
        state_dot = jnp.where(lane_one == h, total, state_dot)
    g_c = dot(g_gram, b_low, ((1,), (0,))) + dot(g_carried_low, old_low, ((1,), (0,)))
    g_b = dot(g_gram, c_low, ((0,), (0,))) + dot(tailed_low, g_new_low, ((1,), (0,)))
    g_fresh = dot(g_carried_low, c_low, ((0,), (0,)))
    for h in range(heads):
        rows = slice(h * P_SIZE, (h + 1) * P_SIZE)
        gstate[rows, :] = (
            g_new[rows, :] * carrying[STRETCH - 1 : STRETCH, h : h + 1] + g_fresh[rows, :]
        )
    row = lax.broadcasted_iota(jnp.int32, (STRETCH, STRETCH), 0)
    col = lax.broadcasted_iota(jnp.int32, (STRETCH, STRETCH), 1)
    upper = jnp.where(col >= row, 1.0, 0.0).astype(F32)
    g_cum = row_sum - col_sum + into - outof
    g_decay = lax.dot_general(
        upper, g_cum, (((1,), (0,)), ((), ())), precision=PRECISE, preferred_element_type=F32
    ) + (
        jnp.sum(outof, axis=0, keepdims=True)
        + carrying[STRETCH - 1 : STRETCH, :] * state_dot
    )
    g_step = head_sums(x * g_scaled, heads) + g_decay * pdt_ref[1:2, :]
    g_dt = g_step * sigmoid(biased)
    gdt_ref[0:1, :] += jnp.sum(g_dt, axis=0, keepdims=True)
    gdt_ref[1:2, :] += jnp.sum(g_decay * log_decay, axis=0, keepdims=True)
    g_x = px_ref[5:6, :] * g_mixed + step_wide * g_scaled
    g_conv_x = g_x * px_ref[7:8, :] * (sig_x * (1.0 + conv_x * (1.0 - sig_x)))
    g_act = jnp.concatenate([g_b, g_c], axis=1)
    g_conv_bc = g_act * (sig_bc * (1.0 + conv_bc * (1.0 - sig_bc)))
    gx_ref[4:5, :] += jnp.sum(g_conv_x, axis=0, keepdims=True)
    gx_ref[5:6, :] += jnp.sum(g_mixed * x, axis=0, keepdims=True)
    gx_ref[6:7, :] += jnp.sum(upstream * gated * scale, axis=0, keepdims=True)
    gbc_ref[4:5, :] += jnp.sum(g_conv_bc, axis=0, keepdims=True)
    gxbuf[0:STRETCH, :] = g_conv_x
    gbcbuf[0:STRETCH, :] = g_conv_bc
    g_in_x = jnp.zeros((STRETCH, width), F32)
    g_in_bc = jnp.zeros((STRETCH, 2 * N), F32)
    for tap in range(KCONV):
        back = KCONV - 1 - tap
        rows_x = xbuf[8 - back : 8 - back + STRETCH, :]
        rows_bc = bcbuf[8 - back : 8 - back + STRETCH, :]
        later_x = gxbuf[back : back + STRETCH, :]
        later_bc = gbcbuf[back : back + STRETCH, :]
        if back:
            rows_x = jnp.where(place >= back, rows_x, 0.0)
            rows_bc = jnp.where(place >= back, rows_bc, 0.0)
            later_x = jnp.where(remain >= back, later_x, 0.0)
            later_bc = jnp.where(remain >= back, later_bc, 0.0)
        gx_ref[tap : tap + 1, :] += jnp.sum(g_conv_x * rows_x, axis=0, keepdims=True)
        gbc_ref[tap : tap + 1, :] += jnp.sum(g_conv_bc * rows_bc, axis=0, keepdims=True)
        g_in_x = g_in_x + px_ref[tap : tap + 1, :] * later_x
        g_in_bc = g_in_bc + pbc_ref[tap : tap + 1, :] * later_bc
    gxbuf[STRETCH : STRETCH + 8, :] = gxbuf[0:8, :]
    gbcbuf[STRETCH : STRETCH + 8, :] = gbcbuf[0:8, :]
    gp_ref[:, width : 2 * width] = g_in_x.astype(BF)
    gp_ref[:, 2 * width : 2 * width + 2 * N] = g_in_bc.astype(BF)
    gp_ref[:, 2 * width + 2 * N : 2 * width + 2 * N + 128] = g_dt.astype(BF)


def run_forward(projected, place, remain, px, pbc, pdt):
    total = projected.shape[0]
    width = px.shape[1]
    heads = width // P_SIZE
    blocks = total // STRETCH
    row_spec = lambda w, c: pl.BlockSpec((STRETCH, w), lambda i: (i, c))
    whole = lambda a: pl.BlockSpec(a.shape, lambda i: (0, 0))
    return pl.pallas_call(
        partial(forward_kernel, heads),
        grid=(blocks,),
        in_specs=[
            row_spec(width, 0),
            row_spec(width, 1),
            row_spec(2 * N, width // N),
            row_spec(128, (2 * width + 2 * N) // 128),
            row_spec(1, 0),
            row_spec(1, 0),
            whole(px),
            whole(pbc),
            whole(pdt),
        ],
        out_specs=[
            row_spec(width, 0),
            row_spec(width, 0),
            row_spec(1, 0),
            pl.BlockSpec((1, width, N), lambda i: (i, 0, 0)),
        ],
        out_shape=[
            jax.ShapeDtypeStruct((total, width), BF),
            jax.ShapeDtypeStruct((total, width), F32),
            jax.ShapeDtypeStruct((total, 1), F32),
            jax.ShapeDtypeStruct((blocks, width, N), F32),
        ],
        scratch_shapes=[
            pltpu.VMEM((width, N), F32),
            pltpu.VMEM((STRETCH + 8, width), F32),
            pltpu.VMEM((STRETCH + 8, 2 * N), F32),
        ],
        cost_estimate=pl.CostEstimate(
            flops=total * 256 * 1000, bytes_accessed=total * 5000, transcendentals=total * 1500
        ),
        name="scan_forward",
    )(projected, projected, projected, projected, place, remain, px, pbc, pdt)


def run_backward(projected, place, remain, mixed, g_out_low, scale, pull, states, px, pbc, pdt):
    total = projected.shape[0]
    width = px.shape[1]
    heads = width // P_SIZE
    blocks = total // STRETCH
    columns = projected.shape[1]
    rev = lambda i: blocks - 1 - i
    row_spec = lambda w, c: pl.BlockSpec((STRETCH, w), lambda i: (rev(i), c))
    prev_spec = lambda w, c: pl.BlockSpec(
        (16, w), lambda i: (jnp.maximum(rev(i) * (STRETCH // 16) - 1, 0), c)
    )
    whole = lambda a: pl.BlockSpec(a.shape, lambda i: (0, 0))
    fixed = lambda w: pl.BlockSpec((8, w), lambda i: (0, 0))
    return pl.pallas_call(
        partial(backward_kernel, heads),
        grid=(blocks,),
        in_specs=[
            row_spec(width, 0),
            row_spec(width, 1),
            row_spec(2 * N, width // N),
            row_spec(128, (2 * width + 2 * N) // 128),
            prev_spec(width, 1),
            prev_spec(2 * N, width // N),
            row_spec(1, 0),
            row_spec(1, 0),
            row_spec(width, 0),
            row_spec(width, 0),
            row_spec(1, 0),
            row_spec(1, 0),
            pl.BlockSpec((1, width, N), lambda i: (rev(i), 0, 0)),
            whole(px),
            whole(pbc),
            whole(pdt),
        ],
        out_specs=[
            row_spec(columns, 0),
            row_spec(width, 0),
            fixed(width),
            fixed(2 * N),
            fixed(128),
        ],
        out_shape=[
            jax.ShapeDtypeStruct((total, columns), BF),
            jax.ShapeDtypeStruct((total, width), BF),
            jax.ShapeDtypeStruct((8, width), F32),
            jax.ShapeDtypeStruct((8, 2 * N), F32),
            jax.ShapeDtypeStruct((8, 128), F32),
        ],
        scratch_shapes=[
            pltpu.VMEM((width, N), F32),
            pltpu.VMEM((STRETCH + 8, width), F32),
            pltpu.VMEM((STRETCH + 8, 2 * N), F32),
            pltpu.VMEM((STRETCH + 8, width), F32),
            pltpu.VMEM((STRETCH + 8, 2 * N), F32),
        ],
        cost_estimate=pl.CostEstimate(
            flops=total * 256 * 3000, bytes_accessed=total * 8000, transcendentals=total * 2000
        ),
        name="scan_backward",
    )(
        projected,
        projected,
        projected,
        projected,
        projected,
        projected,
        place,
        remain,
        mixed,
        g_out_low,
        scale,
        pull,
        states,
        px,
        pbc,
        pdt,
    )


def pad_to(values, width, axis):
    missing = width - values.shape[axis]
    if missing == 0:
        return values
    pads = [(0, 0)] * values.ndim
    pads[axis] = (0, missing)
    return jnp.pad(values, pads)


def width_sum(values):
    if lax.axis_size("width") == 2:
        return values.astype(F32) + lax.ppermute(values, "width", [(0, 1), (1, 0)]).astype(F32)
    return jnp.sum(lax.all_gather(values, "width").astype(F32), axis=0)


def per_device(
    tokens,
    cotangent,
    lengths,
    levels,
    step_count,
    weight_in,
    moment_in,
    second_in,
    weight_out,
    moment_out,
    second_out,
    small_params,
    moment_small,
    second_small,
):
    dp = lax.axis_size("dp")
    here = lax.axis_index("dp")
    rows = tokens.shape[0]
    total = rows * dp
    units = E // dp
    own_heads = H // dp
    wide = max(units, 128)
    shard = weight_in.shape[0]

    inputs_f = tokens.astype(F32)
    root = lax.rsqrt(jnp.mean(inputs_f * inputs_f, axis=1, keepdims=True) + NORM_EPS)
    g_in, g_out, conv_w, conv_b, a_log, dt_bias, d_skip = unpack(small_params)
    normed_low = (inputs_f * root * g_in).astype(BF)
    normed_all = lax.all_gather(normed_low, "dp", axis=0, tiled=True)

    weight_low = weight_in.astype(BF)
    pairs = jnp.concatenate(
        [
            weight_low[:, :E].reshape(shard, dp, units),
            weight_low[:, E : 2 * E].reshape(shard, dp, units),
        ],
        axis=2,
    ).transpose(1, 0, 2)
    own_cols = lax.all_to_all(pairs, "dp", 0, 0).reshape(D, 2 * units)
    shared = lax.all_gather(weight_low[:, 2 * E :], "dp", axis=0, tiled=True)
    own_dt = lax.dynamic_slice_in_dim(shared, 2 * N + here * own_heads, own_heads, 1)
    weight_own = jnp.concatenate(
        [
            pad_to(own_cols[:, :units], wide, 1),
            pad_to(own_cols[:, units:], wide, 1),
            shared[:, : 2 * N],
            pad_to(own_dt, 128, 1),
        ],
        axis=1,
    )
    out_weight_low = pad_to(weight_out.astype(BF), wide, 0)

    live_units = jnp.right_shift(jnp.int32(E), lax.axis_size("width") - 1 - levels[0])
    live = live_units.astype(F32)
    place, remain = row_places(lengths[0], total)
    place = place[:, None]
    remain = remain[:, None]
    own = lambda v: lax.dynamic_slice_in_dim(v, here * units, units, v.ndim - 1)
    own_h = lambda v: lax.dynamic_slice_in_dim(v, here * own_heads, own_heads, 0)
    unit_mask = (here * units + jnp.arange(units, dtype=jnp.int32) < live_units).astype(F32)
    px = pad_to(
        jnp.concatenate(
            [
                own(conv_w[:, :E]),
                own(conv_b[:E])[None],
                jnp.repeat(own_h(d_skip), P_SIZE)[None],
                own(g_out)[None],
                unit_mask[None],
            ],
            axis=0,
        ),
        wide,
        1,
    )
    pbc = pad_to(jnp.concatenate([conv_w[:, E:], conv_b[None, E:]], axis=0), 8, 0)
    pdt = pad_to(
        pad_to(jnp.stack([own_h(dt_bias), -jnp.exp(own_h(a_log))]), 128, 1), 8, 0
    )

    projected = jnp.dot(normed_all, weight_own, preferred_element_type=F32).astype(BF)
    zin, mixed, square, states = run_forward(projected, place, remain, px, pbc, pdt)

    partial_out = jnp.dot(zin, out_weight_low, preferred_element_type=F32).astype(BF)
    summed_out = lax.psum_scatter(partial_out, "dp", scatter_dimension=0, tiled=True)

    cotangent_all = lax.all_gather(cotangent, "dp", axis=0, tiled=True)
    g_out_low = lax.dot_general(
        cotangent_all, out_weight_low, (((1,), (1,)), ((), ())), preferred_element_type=F32
    )
    pull_part = jnp.sum(g_out_low * zin.astype(F32), axis=1)
    both = jnp.sum(lax.all_gather(jnp.stack([square[:, 0], pull_part]), "dp"), axis=0)
    scale = lax.rsqrt(both[0] / live + NORM_EPS)
    pull = scale * scale * scale / live * both[1]

    block_out = (
        inputs_f
        + summed_out.astype(F32)
        * lax.dynamic_slice_in_dim(scale, here * rows, rows, 0)[:, None]
    ).astype(BF)

    g_projected, out_low, gx, gbc, gdt = run_backward(
        projected,
        place,
        remain,
        mixed,
        g_out_low,
        scale[:, None],
        pull[:, None],
        states,
        px,
        pbc,
        pdt,
    )

    partial_normed = lax.dot_general(
        g_projected, weight_own, (((1,), (1,)), ((), ())), preferred_element_type=F32
    ).astype(BF)
    g_normed = lax.psum_scatter(partial_normed, "dp", scatter_dimension=0, tiled=True).astype(F32)
    g_weight = lax.dot_general(
        normed_all, g_projected, (((0,), (0,)), ((), ())), preferred_element_type=F32
    ).astype(BF)
    g_weight_out = lax.dot_general(
        out_low, cotangent_all, (((0,), (0,)), ((), ())), preferred_element_type=F32
    )[:units].astype(BF)

    g_pairs = jnp.concatenate(
        [g_weight[:, :units], g_weight[:, wide : wide + units]], axis=1
    ).reshape(dp, shard, 2 * units)
    g_pairs = lax.all_to_all(g_pairs, "dp", 0, 0).transpose(1, 0, 2)
    g_shared = lax.dynamic_update_slice_in_dim(
        pad_to(g_weight[:, 2 * wide : 2 * wide + 2 * N], SHARED, 1),
        g_weight[:, 2 * wide + 2 * N : 2 * wide + 2 * N + own_heads],
        2 * N + here * own_heads,
        1,
    )
    g_shared = lax.psum_scatter(g_shared, "dp", scatter_dimension=0, tiled=True)
    g_rows = jnp.concatenate(
        [
            g_pairs[:, :, :units].reshape(shard, E),
            g_pairs[:, :, units:].reshape(shard, E),
            g_shared,
        ],
        axis=1,
    )
    total_in = width_sum(g_rows)
    total_out = width_sum(g_weight_out)

    ratio = root * g_in
    lean = jnp.sum(g_in * g_normed * inputs_f, axis=1, keepdims=True)
    g_inputs = ratio * g_normed - inputs_f * (root * root * root / D * lean)
    grad_tokens = (cotangent.astype(F32) + g_inputs).astype(BF)
    g_g_in = jnp.sum(g_normed * inputs_f * root, axis=0)

    packed = jnp.concatenate(
        [
            g_g_in,
            gbc[:5].reshape(-1),
            gx[:5, :units].reshape(-1),
            gx[6, :units],
            jnp.sum(gx[5, :units].reshape(own_heads, P_SIZE), axis=1),
            gdt[1, :own_heads],
            gdt[0, :own_heads],
        ]
    )
    everyone = lax.all_gather(packed, "dp")
    everyone = jnp.sum(lax.all_gather(everyone, "width"), axis=0)
    cut = D + 10 * N
    common = jnp.sum(everyone[:, :cut], axis=0)
    bc_part = common[D:].reshape(5, 2 * N)
    mine = everyone[:, cut:]
    x_part = mine[:, : 5 * units].reshape(dp, 5, units).transpose(1, 0, 2).reshape(5, E)
    heads_part = mine[:, 6 * units :].reshape(dp, 3, own_heads).transpose(1, 0, 2).reshape(3, H)
    conv_part = jnp.concatenate([x_part, bc_part], axis=1)
    total_small = jnp.concatenate(
        [
            common[:D],
            mine[:, 5 * units : 6 * units].reshape(E),
            conv_part.reshape(-1),
            heads_part[1],
            heads_part[2],
            heads_part[0],
        ]
    )
    step_float = step_count[0].astype(F32)
    rate_table, decay_table = small_table()
    new_small, mom_small, sec_small = adamw_step(
        small_params, moment_small, second_small, total_small, rate_table, decay_table, step_float
    )
    new_in, mom_in, sec_in = adamw_step(
        weight_in, moment_in, second_in, total_in, MATRIX_RATE, MATRIX_DECAY, step_float
    )
    new_out, mom_out, sec_out = adamw_step(
        weight_out, moment_out, second_out, total_out, MATRIX_RATE, MATRIX_DECAY, step_float
    )
    return (
        block_out,
        grad_tokens,
        new_in,
        mom_in,
        sec_in,
        new_in.astype(BF),
        new_out,
        mom_out,
        sec_out,
        new_out.astype(BF),
        new_small,
        mom_small,
        sec_small,
    )


def solution(mesh):
    return jax.shard_map(
        per_device,
        mesh=mesh,
        in_specs=(
            P(("width", "dp"), None),
            P(("width", "dp"), None),
            P("width", None),
            P("width"),
            P(),
            P("dp", None),
            P("dp", None),
            P("dp", None),
            P("dp", None),
            P("dp", None),
            P("dp", None),
            P(),
            P(),
            P(),
        ),
        out_specs=(
            P(("width", "dp"), None),
            P(("width", "dp"), None),
            P("dp", None),
            P("dp", None),
            P("dp", None),
            P("dp", None),
            P("dp", None),
            P("dp", None),
            P("dp", None),
            P("dp", None),
            P(),
            P(),
            P(),
        ),
        check_vma=False,
    )
```

time: 2200 us -> 1030 us (0.47)
  waiting for transfers between devices: 1660 us -> 642 us
  other arithmetic: 195 us -> 62.3 us
  Pallas kernels: 0 us -> 125 us
  matrix products: 215 us -> 97.6 us
    reduce_scatter x4 -> x2, waiting for transfers between devices: 884 us -> 227 us  [the longest x1 179 us: per_device(): lax.psum_scatter(partial_out, 'dp', scatter_dimension=0, tiled=True)]
    all_gather x10 -> x3, waiting for transfers between devices: 675 us -> 224 us  [the longest x1 125 us: per_device(): normed_all = lax.all_gather(normed_low, 'dp', axis=0, tiled=True)]
    pallas_call x0 -> x2, Pallas kernels: none -> 125 us  [the longest x1 80.7 us: run_backward(): pl.pallas_call(partial(backward_kernel, heads), grid=(blocks,), in_specs=...]
    dot_general x20 -> x6, matrix products: 215 us -> 97.6 us  [the longest x1 23.1 us: per_device(): lax.dot_general(g_projected, weight_own, (((1,), (1,)), ((), ())), prefer...]
    unnamed x15 -> x9, waiting for transfers between devices: 2.44 us -> 113 us
    psum x1 -> x0, waiting for transfers between devices: 104 us -> none  [per_device(): lax.psum(grad_small_end + grad_small_front + grad_small_norm, ('width', '...]
    ppermute x2, waiting for transfers between devices: 0.01 us -> 59.4 us  [width_sum(): lax.ppermute(values, 'width', [(0, 1), (1, 0)]).astype(F32)]
    reduce_sum x11 -> x6, other arithmetic: 47 us -> 2.6 us  [the longest x1 1.97 us: per_device(): g_g_in = jnp.sum(g_normed * inputs_f * root, axis=0)]
  transfers between devices with their start and end apart: 17 -> 11, of which waited for: 15 -> 9; matrix products, arithmetic and copies ran while one was open for 17% -> 13% of each run, Pallas kernels for 0% -> 4%
where the time goes in v1:
time: 1030 us; the launch traced here: 1020 us
  waiting for transfers between devices  642 us (62%)
  Pallas kernels  125 us (12%)
  matrix products  97.6 us (9%)
  other arithmetic  62.3 us (6%)
  local copies, waits for them, and re-layouts  34.8 us (3%)
  blocking collectives  29.7 us (3%)
  between operations  16.9 us (2%)
  starting transfers between devices  13.6 us (1%)
    reduce_scatter x1, waiting for transfers between devices, per_device(): lax.psum_scatter(partial_out, 'dp', scatter_dimension=0, tiled=True)  179 us
    all_gather x1, waiting for transfers between devices, per_device(): normed_all = lax.all_gather(normed_low, 'dp', axis=0, tiled=True)  125 us
    unnamed x9, waiting for transfers between devices  113 us
    pallas_call x1, Pallas kernels, run_backward(): pl.pallas_call(partial(backward_kernel, heads), grid=(blocks,), in_specs=...  80.7 us
    ppermute x2, waiting for transfers between devices, width_sum(): lax.ppermute(values, 'width', [(0, 1), (1, 0)]).astype(F32)  59.4 us
    all_gather x1, waiting for transfers between devices, per_device(): cotangent_all = lax.all_gather(cotangent, 'dp', axis=0, tiled=True)  58 us
    reduce_scatter x1, waiting for transfers between devices, per_device(): lax.psum_scatter(partial_normed, 'dp', scatter_dimension=0, tiled=True)  47.9 us
    pallas_call x1, Pallas kernels, run_forward(): pl.pallas_call(partial(forward_kernel, heads), grid=(blocks,), in_specs=[...  44.3 us
  transfers between devices with their start and end apart: 11, of which 9 were waited for; matrix products, arithmetic and copies ran while one was open for 13% of the time, Pallas kernels for 4%

profile of v1, /device:TPU:0, one launch (start us, length us, event | category | flops | bytes accessed | tf_op | source)
XLA Modules:
  0.0 1021.8 jit_solution(3651190386912462893)
XLA Ops:
  7.2 3.6 copy.105
  13.0 1.3 fusion.9
  15.6 1.5 maximum_bitcast_fusion
  17.1 7.5 all-to-all-start
  26.9 2.0 copy.108
  30.8 3.9 iota_subtract_fusion
  34.7 41.2 %all-gather.10.cloned.1.call-done = bf16[2048,320]{1,0:T(8,128)(2,1)} async-done(((bf16[128,320]{1,0:T(8,128)(2,1)}), bf16[2048,320]{1,0:T(8,128)(2,1)}) %all-gather.10.cloned.1.call-update) | async-done | bytes 1310736 | tf_op jit(solution)/shard_map/all_gather | solution.py:565
  75.9 1.3 slice.170
  77.2 1.3 constant_dynamic-slice_fusion.2
  78.5 124.8 %all-gather.8.cloned.1.call-done = bf16[4096,2048]{1,0:T(8,128)(2,1)} async-done(((bf16[256,2048]{1,0:T(8,128)(2,1)}), bf16[4096,2048]{1,0:T(8,128)(2,1)}) %all-gather.8.cloned.1.call-update) | async-done | bytes 16777232 | tf_op jit(solution)/shard_map/all_gather | solution.py:554
  203.3 22.7 %convolution_convert_fusion.2.gate_ref.x_ref.bc_ref.dt_ref.xprev_ref.bcprev_ref = bf16[4096,896]{1,0:T(8,128)(2,1)} fusion(bf16[4096,2048]{1,0:T(8,128)(2,1)} %all-gather.8.cloned.1.call-done, bf16[2048,4]{1,0:T(8,128)(2,1)S(1)} %constant_dynamic-slice_fusion.2, bf16[2048,256]{1,0:T(8,128)(2,1)S(1)} %slice.170, bf16[2048,512]{1,0:T(8,128)(2,1)} %bitcast.1), kind=kOutput, calls=%fused_computation.4 | convolution fusion | flops 15050735616 | bytes 27279360 | tf_op jit(solution)/shard_map/dot_general | solution.py:605
  226.0 44.3 %scan_forward.1 = (bf16[4096,256]{1,0:T(8,128)(2,1)}, f32[4096,256]{1,0:T(8,128)}, f32[4096,1]{1,0:T(8,128)}, f32[16,256,128]{2,1,0:T(8,128)}) custom-call(bf16[4096,896]{1,0:T(8,128)(2,1)} %convolution_convert_fusion.2.gate_ref.x_ref.bc_ref.dt_ref.xprev_ref.bcprev_ref, ...), custom_call_target="tpu_custom_call" | custom-call | flops 1048576000 | bytes 20480000 | tf_op jit(solution)/shard_map/scan_forward/pallas_call | solution.py:393
  270.3 2.2 reduce.1
  272.5 58.0 %all-gather.12.cloned.1.call-done = bf16[4096,2048]{1,0:T(8,128)(2,1)} async-done(((bf16[256,2048]{1,0:T(8,128)(2,1)}), bf16[4096,2048]{1,0:T(8,128)(2,1)}) %all-gather.12.cloned.1.call-update) | async-done | bytes 16777232 | tf_op jit(solution)/shard_map/all_gather | solution.py:611
  330.6 13.3 %multiply_reduce_fusion = (f32[4096]{0:T(1024)S(1)}, f32[4096,256]{1,0:T(8,128)}) fusion(bf16[4096,256]{1,0:T(8,128)(2,1)} %get-tuple-element.22, bf16[4096,2048]{1,0:T(8,128)(2,1)} %all-gather.12.cloned.1.call-done, f32[256,2048]{1,0:T(8,128)S(1)} %copy-done.3), kind=kOutput, calls=%fused_computation.16 | convolution fusion | flops 4298633216 | bytes 25182208 | tf_op jit(solution)/shard_map/dot_general | solution.py:612
  343.9 19.9 %all-gather.3 = f32[16,2,4096]{2,1,0:T(2,128)S(1)} all-gather(f32[1,2,4096]{2,1,0:T(2,128)S(1)} %maximum_bitcast_fusion.1), channel_id=2, replica_groups=mesh['width'=2,'dp'=16] {'dp'}, dimensions={0}, use_global_device_ids=true | all-gather | bytes 557056 | tf_op jit(solution)/shard_map/all_gather | solution.py:616
  364.0 2.0 copy.111
  366.7 2.0 copy.113
  368.6 3.8 divide_multiply_fusion.pull_ref
  372.4 80.7 %scan_backward.1 = (bf16[4096,896]{1,0:T(8,128)(2,1)}, bf16[4096,256]{1,0:T(8,128)(2,1)}, f32[8,256]{1,0:T(8,128)}, f32[8,256]{1,0:T(8,128)}, f32[8,128]{1,0:T(8,128)}) custom-call(bf16[4096,896]{1,0:T(8,128)(2,1)} %convolution_convert_fusion.2.gate_ref.x_ref.bc_ref.dt_ref.xprev_ref.bcprev_ref, ...), custom_call_target="tpu_custom_call" | custom-call | flops 3145728000 | bytes 32768000 | tf_op jit(solution)/shard_map/scan_backward/pallas_call | solution.py:444
  453.1 20.4 %convolution_convert_fusion.3 = bf16[2048,896]{0,1:T(8,128)(2,1)S(1)} fusion(bf16[4096,2048]{1,0:T(8,128)(2,1)} %all-gather.8.cloned.1.call-done, bf16[4096,896]{1,0:T(8,128)(2,1)} %get-tuple-element.26), kind=kOutput, calls=%fused_computation.18 | convolution fusion | flops 15034220544 | bytes 27787264 | tf_op jit(solution)/shard_map/dot_general | solution.py:644
  473.8 1.6 copy-done.9
  475.4 1.6 copy.122
  477.1 23.1 %convolution_convert_fusion = bf16[4096,2048]{1,0:T(8,128)(2,1)} fusion(bf16[4096,896]{1,0:T(8,128)(2,1)} %get-tuple-element.26, bf16[2048,4]{1,0:T(8,128)(2,1)S(1)} %copy-done.12, bf16[2048,256]{1,0:T(8,128)(2,1)S(1)} %slice.170, bf16[2048,512]{1,0:T(8,128)(2,1)} %bitcast.1), kind=kOutput, calls=%fused_computation | convolution fusion | flops 15055454208 | bytes 27279360 | tf_op jit(solution)/shard_map/dot_general | solution.py:640
  500.2 1.5 copy-done.4
  501.7 9.8 convolution_convert_fusion.1
  511.6 3.5 copy_bitcast_fusion
  515.0 3.7 all-to-all-start.1
  518.8 24.4 %reduce-scatter.10.cloned.1.call-done = bf16[128,320]{1,0:T(8,128)(2,1)} async-done(((bf16[2048,320]{1,0:T(8,128)(2,1)}), bf16[128,320]{1,0:T(8,128)(2,1)}) %reduce-scatter.10.cloned.1.call-update) | async-done | bytes 81936
  543.2 1.0 copy.123
  544.2 18.8 %all-to-all-done.1 = bf16[16,128,512]{1,2,0:T(8,128)(2,1)S(1)} async-done(((bf16[16,128,512]{1,2,0:T(8,128)(2,1)}), bf16[16,128,512]{1,2,0:T(8,128)(2,1)S(1)}, u32[]{:S(2)}, u32[]{:S(2)}) %all-to-all-start.1) | async-done | bytes 2097184 | tf_op jit(solution)/shard_map/all_to_all | solution.py:654
  562.9 1.3 copy-done.5
  564.3 2.0 fusion.37
  566.3 13.1 %pad_maximum_fusion = bf16[128,8512]{0,1:T(8,128)(2,1)} fusion(bf16[128,320]{0,1:T(8,128)(2,1)S(1)} %copy.123, bf16[128,4096]{0,1:T(8,128)(2,1)S(1)} %bitcast.68, bf16[128,4096]{0,1:T(8,128)(2,1)S(1)} %bitcast.66), kind=kLoop, calls=%fused_computation.24 | loop fusion | flops 6537216 | bytes 4358144 | tf_op jit(solution)/shard_map/concatenate | solution.py:662
  579.4 1.5 collective-permute-start
  580.9 8.4 convolution_convert_fusion.4
  592.1 0.8 slice_bitcast_fusion.3
  592.8 59.4 %collective-permute-done.1 = bf16[256,2048]{1,0:T(8,128)(2,1)} collective-permute-done((bf16[256,2048]{1,0:T(8,128)(2,1)S(1)}, bf16[256,2048]{1,0:T(8,128)(2,1)}, u32[]{:S(2)}, u32[]{:S(2)}) %collective-permute-start.1) | collective-permute-done | bytes 1048608 | tf_op jit(solution)/shard_map/ppermute | solution.py:521
  652.2 7.7 fusion.31
  659.9 20.8 %fusion.33 = (bf16[128,8512]{0,1:T(8,128)(2,1)}, f32[128,8512]{0,1:T(8,128)}, f32[128,8512]{0,1:T(8,128)}, f32[128,8512]{0,1:T(8,128)}) fusion(f32[128,8512]{0,1:T(8,128)} %param.19, f32[]{:T(128)} %bitcast.20, bf16[128,8512]{0,1:T(8,128)(2,1)} %collective-permute-done, bf16[128,320]{0,1:T(8,128)(2,1)S(1)} %copy.123, bf16[128,4096]{0,1:T(8,128)(2,1)S(1)} %bitcast.69, ...), kind=kLoop, calls=%fused_computation.90 | loop fusion | flops 25059328 | bytes 32686084 | tf_op jit(solution)/shard_map/convert_element_type | solution.py:726
  680.7 47.9 %reduce-scatter.8.cloned.1.call-done = bf16[256,2048]{1,0:T(8,128)(2,1)} async-done(((bf16[4096,2048]{1,0:T(8,128)(2,1)}), bf16[256,2048]{1,0:T(8,128)(2,1)}) %reduce-scatter.8.cloned.1.call-update) | async-done | bytes 1048592 | tf_op jit(solution)/shard_map/reduce_scatter | solution.py:643
  728.7 2.0 fusion.13
  732.0 178.8 %reduce-scatter.6.cloned.1.call-done = bf16[256,2048]{1,0:T(8,128)(2,1)} async-done(((bf16[4096,2048]{1,0:T(8,128)(2,1)}), bf16[256,2048]{1,0:T(8,128)(2,1)}) %reduce-scatter.6.cloned.1.call-update) | async-done | bytes 1048592 | tf_op jit(solution)/shard_map/reduce_scatter | solution.py:609
  910.7 3.5 fusion.6
  914.3 87.7 %all-reduce.8.cloned.1.call-done = f32[78016]{0:T(1024)} async-done(((f32[78016]{0:T(1024)}), f32[78016]{0:T(1024)}) %all-reduce.8.cloned.1.call-update) | async-done | bytes 312080
  1002.0 1.2 reshape.246
  1003.2 9.8 all-gather.2
  1014.0 0.8 multiply_subtract_fusion.2
  (144 shorter events, 11.8 us)
Async XLA Ops:
  7.2 4.4 copy-start.13
  7.2 4.4 copy-start.1
  7.2 68.7 %all-gather.10.cloned.1.call-start = ((), (), s32[]{:S(2)}) async-start(), calls=%async_computation.6 | async-start | bytes 1671168 | tf_op jit(solution)/shard_map/all_gather | solution.py:565
  11.5 191.8 %all-gather.8.cloned.1.call-start = ((), (), s32[]{:S(2)}) async-start(), calls=%async_computation.5 | async-start | bytes 17825792 | tf_op jit(solution)/shard_map/all_gather | solution.py:554
  11.6 0.9 copy-start.15
  11.9 0.6 copy-start.24
  12.4 0.6 copy-start.21
  14.3 316.2 %all-gather.12.cloned.1.call-start = ((), (), s32[]{:S(2)}) async-start(), calls=%async_computation.8 | async-start | bytes 17825792 | tf_op jit(solution)/shard_map/all_gather | solution.py:611
  17.1 7.6 slice-start
  17.1 8.8 copy-start.27
  17.1 61.3 %all-to-all-start = ((bf16[16,128,512]{2,1,0:T(8,128)(2,1)}), bf16[16,128,512]{2,1,0:T(8,128)(2,1)}, u32[]{:S(2)}, u32[]{:S(2)}) async-start(bf16[16,128,512]{2,1,0:T(8,128)(2,1)} %maximum_bitcast_fusion), calls=%async_computation | async-start | bytes 4194304 | tf_op jit(solution)/shard_map/all_to_all | solution.py:564
  24.7 518.5 %reduce-scatter.10.cloned.1.call-start = ((), (), s32[]{:S(2)}) async-start(), calls=%async_computation.11 | async-start | bytes 1671168
  26.1 4.1 slice-start.1
  78.4 147.5 %copy-start.11 = (bf16[2048,4]{1,0:T(8,128)(2,1)}, bf16[2048,4]{1,0:T(8,128)(2,1)S(1)}, u32[]{:S(2)}) copy-start(bf16[2048,4]{1,0:T(8,128)(2,1)S(1)} %constant_dynamic-slice_fusion.2) | copy-start | bytes 49156
  226.0 104.6 %copy-start.3 = (f32[256,2048]{1,0:T(8,128)S(1)}, f32[256,2048]{1,0:T(8,128)}, u32[]{:S(2)}) copy-start(f32[256,2048]{1,0:T(8,128)} %param.22) | copy-start | bytes 6291460
  366.6 5.8 copy-start
  473.6 1.8 copy-start.9
  475.4 1.6 copy-start.12
  477.0 251.7 %reduce-scatter.8.cloned.1.call-start = ((), (), s32[]{:S(2)}) async-start(), calls=%async_computation.9 | async-start | bytes 17825792 | tf_op jit(solution)/shard_map/reduce_scatter | solution.py:643
  500.1 1.6 copy-start.4
  500.2 410.6 %reduce-scatter.6.cloned.1.call-start = ((), (), s32[]{:S(2)}) async-start(), calls=%async_computation.7 | async-start | bytes 17825792 | tf_op jit(solution)/shard_map/reduce_scatter | solution.py:609
  515.0 47.9 %all-to-all-start.1 = ((bf16[16,128,512]{1,2,0:T(8,128)(2,1)}), bf16[16,128,512]{1,2,0:T(8,128)(2,1)S(1)}, u32[]{:S(2)}, u32[]{:S(2)}) async-start(bf16[16,128,512]{1,2,0:T(8,128)(2,1)} %copy_bitcast_fusion), calls=%async_computation.3 | async-start | bytes 4194304 | tf_op jit(solution)/shard_map/all_to_all | solution.py:654
  518.7 483.2 %all-reduce.8.cloned.1.call-start = ((), (), s32[]{:S(2)}) async-start(), calls=%async_computation.10 | async-start | bytes 630784
  562.9 1.3 copy-start.5
  566.3 14.6 %copy-start.8 = (bf16[4096,256]{1,0:T(8,128)(2,1)S(1)}, bf16[4096,256]{1,0:T(8,128)(2,1)}, u32[]{:S(2)}) copy-start(bf16[4096,256]{1,0:T(8,128)(2,1)} %get-tuple-element.27) | copy-start | bytes 6291460
  579.4 80.5 %collective-permute-start = (bf16[128,8512]{0,1:T(8,128)(2,1)}, bf16[128,8512]{0,1:T(8,128)(2,1)}, u32[]{:S(2)}, u32[]{:S(2)}) collective-permute-start(bf16[128,8512]{0,1:T(8,128)(2,1)} %pad_maximum_fusion), channel_id=1, source_target_pairs={{0,16},{16,0},{1,17},{17,1},{2,18},{18,2},{3,19},{19,3},{4,20},{20... | collective-permute-start | bytes 6537224 | tf_op jit(solution)/shard_map/ppermute | solution.py:521
  580.9 9.6 copy-start.28
  580.9 10.9 %copy-start.26 = (f32[8,256]{1,0:T(8,128)S(1)}, f32[8,256]{1,0:T(8,128)}, u32[]{:S(2)}) copy-start(f32[8,256]{1,0:T(8,128)} %get-tuple-element.28) | copy-start | bytes 24580
  580.9 10.9 %copy-start.23 = (f32[8,256]{1,0:T(8,128)S(1)}, f32[8,256]{1,0:T(8,128)}, u32[]{:S(2)}) copy-start(f32[8,256]{1,0:T(8,128)} %get-tuple-element.29) | copy-start | bytes 24580
  589.3 63.0 %collective-permute-start.1 = (bf16[256,2048]{1,0:T(8,128)(2,1)S(1)}, bf16[256,2048]{1,0:T(8,128)(2,1)}, u32[]{:S(2)}, u32[]{:S(2)}) collective-permute-start(bf16[256,2048]{1,0:T(8,128)(2,1)S(1)} %convolution_convert_fusion.4), channel_id=1, source_target_pairs={{0,16},{16,0},{1,17},{17,1},{2,18},{18,2},{3,19},{19,3},{4,20},{20... | collective-permute-start | bytes 3145736 | tf_op jit(solution)/shard_map/ppermute | solution.py:521
  659.9 68.8 %copy-start.2 = (bf16[256,2048]{1,0:T(8,128)(2,1)S(1)}, bf16[256,2048]{1,0:T(8,128)(2,1)}, u32[]{:S(2)}) copy-start(bf16[256,2048]{1,0:T(8,128)(2,1)} %param.14) | copy-start | bytes 3145732
  659.9 68.8 %copy-start.16 = (f32[2048]{0:T(1024)S(1)}, f32[2048]{0:T(1024)}, u32[]{:S(2)}) copy-start(f32[2048]{0:T(1024)} %copy-done.15) | copy-start | bytes 24580
  659.9 68.8 %copy-start.22 = (f32[256]{0:T(256)S(1)}, f32[256]{0:T(256)}, u32[]{:S(2)}) copy-start(f32[256]{0:T(256)} %copy-done.21) | copy-start | bytes 3076
  680.7 50.5 %copy-start.25 = (f32[256]{0:T(256)S(1)}, f32[256]{0:T(256)}, u32[]{:S(2)}) copy-start(f32[256]{0:T(256)} %copy-done.24) | copy-start | bytes 3076
  680.7 230.0 %copy-start.7 = (bf16[256,2048]{1,0:T(8,128)(2,1)S(1)}, bf16[256,2048]{1,0:T(8,128)(2,1)}, u32[]{:S(2)}) copy-start(bf16[256,2048]{1,0:T(8,128)(2,1)} %param.15) | copy-start | bytes 3145732
  728.7 182.1 %copy-start.6 = (bf16[256,2048]{1,0:T(8,128)(2,1)S(1)}, bf16[256,2048]{1,0:T(8,128)(2,1)}, u32[]{:S(2)}) copy-start(bf16[256,2048]{1,0:T(8,128)(2,1)} %reduce-scatter.8.cloned.1.call-done) | copy-start | bytes 3145732
  731.2 0.7 copy-start.10
  914.3 99.7 %copy-start.14 = (f32[28096]{0:T(1024)S(1)}, f32[28096]{0:T(1024)}, u32[]{:S(2)}) copy-start(f32[28096]{0:T(1024)} %param.25) | copy-start | bytes 337156
  914.3 99.7 %copy-start.17 = (f32[28096]{0:T(1024)S(1)}, f32[28096]{0:T(1024)}, u32[]{:S(2)}) copy-start(f32[28096]{0:T(1024)} %param.27) | copy-start | bytes 337156
  914.3 99.7 %copy-start.18 = (f32[28096]{0:T(1024)S(1)}, f32[28096]{0:T(1024)}, u32[]{:S(2)}) copy-start(f32[28096]{0:T(1024)} %param.26) | copy-start | bytes 337156
  914.3 99.7 %copy-start.19 = (f32[28096]{0:T(1024)S(1)}, f32[28096]{0:T(1024)}, u32[]{:S(2)}) copy-start(f32[28096]{0:T(1024)} %constant.67.clone.1) | copy-start | bytes 337156
  914.3 99.7 %copy-start.20 = (f32[28096]{0:T(1024)S(1)}, f32[28096]{0:T(1024)}, u32[]{:S(2)}) copy-start(f32[28096]{0:T(1024)} %constant.68.clone.1) | copy-start | bytes 337156
Sparse Core Ops, SparseCore 0:
  11.6 64.2 all-gather.9
  78.6 124.6 all-gather.7
  205.5 125.0 all-gather.11
  477.1 66.0 reduce-scatter.9
  547.7 180.9 reduce-scatter.7
  733.2 177.4 reduce-scatter.5
  914.5 87.4 all-reduce.7

commit v2 on v1

--- a/solution.py
+++ b/solution.py
@@ -27,6 +27,7 @@
 F32 = jnp.float32
 LOW = -1e30
 SHARED = 2 * N + H
+SPLITS = 1
 
 
 def small_table():
@@ -227,27 +228,23 @@
     px_ref,
     pbc_ref,
     pdt_ref,
-    gp_ref,
-    low_ref,
-    gx_ref,
-    gbc_ref,
-    gdt_ref,
-    gstate,
-    xbuf,
-    bcbuf,
-    gxbuf,
-    gbcbuf,
+    gstate_in,
+    gx_in,
+    gbc_in,
+    gdt_in,
+    *rest,
 ):
+    gp_ref, low_ref, gstate, gx_ref, gbc_ref, gdt_ref, xbuf, bcbuf, gxbuf, gbcbuf = rest[-10:]
     width = x_ref.shape[1]
 
     @pl.when(pl.program_id(0) == 0)
     def _():
-        gstate[...] = jnp.zeros_like(gstate)
-        gxbuf[STRETCH : STRETCH + 8, :] = jnp.zeros((8, width), F32)
-        gbcbuf[STRETCH : STRETCH + 8, :] = jnp.zeros((8, 2 * N), F32)
-        gx_ref[...] = jnp.zeros_like(gx_ref)
-        gbc_ref[...] = jnp.zeros_like(gbc_ref)
-        gdt_ref[...] = jnp.zeros_like(gdt_ref)
+        gstate[...] = gstate_in[...]
+        gxbuf[STRETCH : STRETCH + 8, :] = gx_in[8:16, :]
+        gbcbuf[STRETCH : STRETCH + 8, :] = gbc_in[8:16, :]
+        gx_ref[...] = gx_in[...]
+        gbc_ref[...] = gbc_in[...]
+        gdt_ref[...] = gdt_in[...]
 
     place = place_ref[...]
     remain = remain_ref[...]
@@ -376,8 +373,10 @@
         gbc_ref[tap : tap + 1, :] += jnp.sum(g_conv_bc * rows_bc, axis=0, keepdims=True)
         g_in_x = g_in_x + px_ref[tap : tap + 1, :] * later_x
         g_in_bc = g_in_bc + pbc_ref[tap : tap + 1, :] * later_bc
-    gxbuf[STRETCH : STRETCH + 8, :] = gxbuf[0:8, :]
-    gbcbuf[STRETCH : STRETCH + 8, :] = gbcbuf[0:8, :]
+    gxbuf[STRETCH : STRETCH + 8, :] = g_conv_x[0:8, :]
+    gbcbuf[STRETCH : STRETCH + 8, :] = g_conv_bc[0:8, :]
+    gx_ref[8:16, :] = g_conv_x[0:8, :]
+    gbc_ref[8:16, :] = g_conv_bc[0:8, :]
     gp_ref[:, width : 2 * width] = g_in_x.astype(BF)
     gp_ref[:, 2 * width : 2 * width + 2 * N] = g_in_bc.astype(BF)
     gp_ref[:, 2 * width + 2 * N : 2 * width + 2 * N + 128] = g_dt.astype(BF)
@@ -428,22 +427,30 @@
     )(projected, projected, projected, projected, place, remain, px, pbc, pdt)
 
 
-def run_backward(projected, place, remain, mixed, g_out_low, scale, pull, states, px, pbc, pdt):
+def run_backward(carried, first, count, projected, rows_in, states, px, pbc, pdt):
     total = projected.shape[0]
     width = px.shape[1]
     heads = width // P_SIZE
-    blocks = total // STRETCH
     columns = projected.shape[1]
-    rev = lambda i: blocks - 1 - i
+    rev = lambda i: first + count - 1 - i
     row_spec = lambda w, c: pl.BlockSpec((STRETCH, w), lambda i: (rev(i), c))
     prev_spec = lambda w, c: pl.BlockSpec(
         (16, w), lambda i: (jnp.maximum(rev(i) * (STRETCH // 16) - 1, 0), c)
     )
     whole = lambda a: pl.BlockSpec(a.shape, lambda i: (0, 0))
-    fixed = lambda w: pl.BlockSpec((8, w), lambda i: (0, 0))
-    return pl.pallas_call(
+    fixed = lambda r, w: pl.BlockSpec((r, w), lambda i: (0, 0))
+    place, remain, mixed, g_out_low, scale, pull = rows_in
+    gstate, gx, gbc, gdt = carried[:4]
+    filled = tuple(carried[4:])
+    operands = (
+        (projected,) * 6
+        + (place, remain, mixed, g_out_low, scale, pull, states, px, pbc, pdt)
+        + (gstate, gx, gbc, gdt)
+        + filled
+    )
+    results = pl.pallas_call(
         partial(backward_kernel, heads),
-        grid=(blocks,),
+        grid=(count,),
         in_specs=[
             row_spec(width, 0),
             row_spec(width, 1),
@@ -461,50 +468,177 @@
             whole(px),
             whole(pbc),
             whole(pdt),
-        ],
+            whole(gstate),
+            whole(gx),
+            whole(gbc),
+            whole(gdt),
+        ]
+        + [pl.BlockSpec(memory_space=pl.ANY)] * len(filled),
         out_specs=[
             row_spec(columns, 0),
             row_spec(width, 0),
-            fixed(width),
-            fixed(2 * N),
-            fixed(128),
+            fixed(width, N),
+            fixed(16, width),
+            fixed(16, 2 * N),
+            fixed(8, 128),
         ],
         out_shape=[
             jax.ShapeDtypeStruct((total, columns), BF),
             jax.ShapeDtypeStruct((total, width), BF),
-            jax.ShapeDtypeStruct((8, width), F32),
-            jax.ShapeDtypeStruct((8, 2 * N), F32),
+            jax.ShapeDtypeStruct((width, N), F32),
+            jax.ShapeDtypeStruct((16, width), F32),
+            jax.ShapeDtypeStruct((16, 2 * N), F32),
             jax.ShapeDtypeStruct((8, 128), F32),
         ],
         scratch_shapes=[
-            pltpu.VMEM((width, N), F32),
             pltpu.VMEM((STRETCH + 8, width), F32),
             pltpu.VMEM((STRETCH + 8, 2 * N), F32),
             pltpu.VMEM((STRETCH + 8, width), F32),
             pltpu.VMEM((STRETCH + 8, 2 * N), F32),
         ],
+        input_output_aliases={20: 0, 21: 1} if filled else {},
         cost_estimate=pl.CostEstimate(
-            flops=total * 256 * 3000, bytes_accessed=total * 8000, transcendentals=total * 2000
+            flops=count * STRETCH * 256 * 3000,
+            bytes_accessed=count * STRETCH * 8000,
+            transcendentals=count * STRETCH * 2000,
         ),
         name="scan_backward",
-    )(
-        projected,
-        projected,
-        projected,
-        projected,
-        projected,
-        projected,
-        place,
-        remain,
-        mixed,
-        g_out_low,
-        scale,
-        pull,
-        states,
-        px,
-        pbc,
-        pdt,
-    )
+    )(*operands)
+    return tuple(results[2:]) + tuple(results[:2])
+
+
+def after(value, *others):
+    return lax.optimization_barrier((value, others))[0]
+
+
+def ring_chips():
+    return [(z * 2 + x) for x, z in [(0, 0), (0, 1), (0, 2), (0, 3), (1, 3), (1, 2), (1, 1), (1, 0)]]
+
+
+def hop(values, steps):
+    chips = ring_chips()
+    count = len(chips)
+    pairs = [
+        (2 * chips[p] + core, 2 * chips[(p + steps) % count] + core)
+        for p in range(count)
+        for core in (0, 1)
+    ]
+    return lax.ppermute(values, "dp", pairs)
+
+
+def swap(values):
+    return lax.ppermute(values, "dp", [(i, i ^ 1) for i in range(lax.axis_size("dp"))])
+
+
+def ring_place():
+    here = lax.axis_index("dp")
+    core = here % 2
+    chip = here // 2
+    spot = jnp.where(chip % 2 == 0, chip // 2, 7 - chip // 2)
+    return core, spot
+
+
+def ring_chip(spot):
+    spot = spot % 8
+    return jnp.where(spot < 4, spot * 2, (7 - spot) * 2 + 1)
+
+
+def gather_rows(values, pieces=2):
+    if lax.axis_size("dp") != 16:
+        return lax.all_gather(values, "dp", axis=0, tiled=True)
+    rows = values.shape[0]
+    core, spot = ring_place()
+    chip = ring_chip(spot)
+    out = jnp.zeros((16 * rows,) + values.shape[1:], values.dtype)
+
+    def put(out, part, device, offset):
+        return lax.dynamic_update_slice_in_dim(out, part, device * rows + offset, 0)
+
+    out = put(out, values, 2 * chip + core, 0)
+    out = put(out, swap(values), 2 * chip + 1 - core, 0)
+    size = rows // pieces
+    ahead = [values[i * size : (i + 1) * size] for i in range(pieces)]
+    behind = list(ahead)
+    for step in range(1, 5):
+        for i in range(pieces):
+            for way, held in ((1, ahead), (-1, behind)):
+                part, offset = held[i], i * size
+                if step == 4:
+                    half = size // 2
+                    part = part[:half] if way == 1 else part[half:]
+                    offset = offset + (0 if way == 1 else half)
+                part = hop(part, way)
+                held[i] = part
+                source = ring_chip(spot - way * step)
+                out = put(out, part, 2 * source + core, offset)
+                out = put(out, swap(part), 2 * source + 1 - core, offset)
+    return out
+
+
+def scatter_product(left, right, first, second):
+    total = left.shape[0]
+    if lax.axis_size("dp") != 16:
+        full = jnp.dot(left, right, preferred_element_type=F32).astype(BF)
+        return lax.psum_scatter(full, "dp", scatter_dimension=0, tiled=True).astype(F32)
+    core, spot = ring_place()
+    half = right.shape[1] // 2
+    mine = after(lax.dynamic_slice_in_dim(right, core * half, half, 1), first)
+    theirs = swap(lax.dynamic_slice_in_dim(right, (1 - core) * half, half, 1))
+    product = jnp.dot(left, mine, preferred_element_type=F32) + jnp.dot(
+        swap(left), theirs, preferred_element_type=F32
+    )
+    rows = total // 8
+    product = product.reshape(8, rows, half)
+    done = ring_sum(
+        lambda steps: lax.dynamic_index_in_dim(product, ring_chip(spot + steps), 0, False),
+        rows,
+        second,
+    )
+    own = rows // 2
+    kept = lax.dynamic_slice_in_dim(done, core * own, own, 0)
+    got = swap(lax.dynamic_slice_in_dim(done, (1 - core) * own, own, 0))
+    first = core == 0
+    return jnp.concatenate(
+        [jnp.where(first, kept, got), jnp.where(first, got, kept)], axis=1
+    )
+
+
+def scatter_rows(values):
+    if lax.axis_size("dp") != 16:
+        return lax.psum_scatter(values, "dp", scatter_dimension=0, tiled=True).astype(F32)
+    core, spot = ring_place()
+    rows = values.shape[0] // 16
+    split = values.reshape(8, 2, rows, values.shape[1])
+    pick = lambda c: lax.dynamic_index_in_dim(split, c, 1, False)
+    both = pick(core).astype(F32) + swap(pick(1 - core)).astype(F32)
+    return ring_sum(
+        lambda steps: lax.dynamic_index_in_dim(both, ring_chip(spot + steps), 0, False), rows
+    )
+
+
+def ring_sum(part, rows, second=None):
+    mid = rows // 2
+    far = part(4).astype(BF)
+    up = hop(far[:mid], 1).astype(F32)
+    down = hop(far[mid:], -1).astype(F32)
+    near = part(3)
+    up = jnp.concatenate([near[:mid] + up, near[mid:]], axis=0)
+    near = part(-3)
+    down = jnp.concatenate([near[:mid], near[mid:] + down], axis=0)
+    if second is not None:
+        up, down, _ = lax.optimization_barrier((up, down, second))
+    for step in (2, 1):
+        up = part(step) + hop(up.astype(BF), 1).astype(F32)
+        down = part(-step) + hop(down.astype(BF), -1).astype(F32)
+    return part(0) + hop(up.astype(BF), 1).astype(F32) + hop(down.astype(BF), -1).astype(F32)
+
+
+def tree_sum(values):
+    if lax.axis_size("dp") != 16 or lax.axis_size("width") != 2:
+        return lax.psum(values, ("width", "dp"))
+    for bit in (1, 2, 4, 8):
+        values = values + lax.ppermute(values, "dp", [(i, i ^ bit) for i in range(16)])
+    return values + lax.ppermute(values, "width", [(0, 1), (1, 0)])
 
 
 def pad_to(values, width, axis):
@@ -562,7 +696,7 @@
         axis=2,
     ).transpose(1, 0, 2)
     own_cols = lax.all_to_all(pairs, "dp", 0, 0).reshape(D, 2 * units)
-    shared = lax.all_gather(weight_low[:, 2 * E :], "dp", axis=0, tiled=True)
+    shared = gather_rows(weight_low[:, 2 * E :], 1)
     own_dt = lax.dynamic_slice_in_dim(shared, 2 * N + here * own_heads, own_heads, 1)
     weight_own = jnp.concatenate(
         [
@@ -608,7 +742,8 @@
     partial_out = jnp.dot(zin, out_weight_low, preferred_element_type=F32).astype(BF)
     summed_out = lax.psum_scatter(partial_out, "dp", scatter_dimension=0, tiled=True)
 
-    cotangent_all = lax.all_gather(cotangent, "dp", axis=0, tiled=True)
+    later = after(cotangent, normed_all, weight_own)
+    cotangent_all = lax.all_gather(later, "dp", axis=0, tiled=True)
     g_out_low = lax.dot_general(
         cotangent_all, out_weight_low, (((1,), (1,)), ((), ())), preferred_element_type=F32
     )
@@ -623,52 +758,50 @@
         * lax.dynamic_slice_in_dim(scale, here * rows, rows, 0)[:, None]
     ).astype(BF)
 
-    g_projected, out_low, gx, gbc, gdt = run_backward(
-        projected,
-        place,
-        remain,
-        mixed,
-        g_out_low,
-        scale[:, None],
-        pull[:, None],
-        states,
-        px,
-        pbc,
-        pdt,
-    )
-
-    partial_normed = lax.dot_general(
-        g_projected, weight_own, (((1,), (1,)), ((), ())), preferred_element_type=F32
-    ).astype(BF)
-    g_normed = lax.psum_scatter(partial_normed, "dp", scatter_dimension=0, tiled=True).astype(F32)
+    rows_in = (place, remain, mixed, g_out_low, scale[:, None], pull[:, None])
+    carried = (
+        jnp.zeros((wide, N), F32),
+        jnp.zeros((16, wide), F32),
+        jnp.zeros((16, 2 * N), F32),
+        jnp.zeros((8, 128), F32),
+    )
+    span = total // STRETCH // SPLITS
+    for turn in reversed(range(SPLITS)):
+        carried = run_backward(
+            carried, turn * span, span, projected, rows_in, states, px, pbc, pdt
+        )
+    _, gx, gbc, gdt, g_projected, out_low = carried
+
     g_weight = lax.dot_general(
         normed_all, g_projected, (((0,), (0,)), ((), ())), preferred_element_type=F32
     ).astype(BF)
     g_weight_out = lax.dot_general(
         out_low, cotangent_all, (((0,), (0,)), ((), ())), preferred_element_type=F32
     )[:units].astype(BF)
-
-    g_pairs = jnp.concatenate(
-        [g_weight[:, :units], g_weight[:, wide : wide + units]], axis=1
-    ).reshape(dp, shard, 2 * units)
-    g_pairs = lax.all_to_all(g_pairs, "dp", 0, 0).transpose(1, 0, 2)
+    total_out = width_sum(g_weight_out)
+
+    g_pairs = lax.all_to_all(
+        jnp.concatenate(
+            [g_weight[:, :units], g_weight[:, wide : wide + units]], axis=1
+        ).reshape(dp, shard, 2 * units),
+        "dp",
+        0,
+        0,
+    )
+    g_normed = scatter_product(g_projected, weight_own.T, g_weight, g_pairs)
+    sum_pairs = width_sum(g_pairs).transpose(1, 0, 2)
+    totals = [
+        sum_pairs[:, :, :units].reshape(shard, E),
+        sum_pairs[:, :, units:].reshape(shard, E),
+    ]
     g_shared = lax.dynamic_update_slice_in_dim(
         pad_to(g_weight[:, 2 * wide : 2 * wide + 2 * N], SHARED, 1),
         g_weight[:, 2 * wide + 2 * N : 2 * wide + 2 * N + own_heads],
         2 * N + here * own_heads,
         1,
     )
-    g_shared = lax.psum_scatter(g_shared, "dp", scatter_dimension=0, tiled=True)
-    g_rows = jnp.concatenate(
-        [
-            g_pairs[:, :, :units].reshape(shard, E),
-            g_pairs[:, :, units:].reshape(shard, E),
-            g_shared,
-        ],
-        axis=1,
-    )
-    total_in = width_sum(g_rows)
-    total_out = width_sum(g_weight_out)
+    totals.append(width_sum(scatter_rows(g_shared).astype(BF)))
+    total_in = jnp.concatenate(totals, axis=1)
 
     ratio = root * g_in
     lean = jnp.sum(g_in * g_normed * inputs_f, axis=1, keepdims=True)
@@ -676,36 +809,23 @@
     grad_tokens = (cotangent.astype(F32) + g_inputs).astype(BF)
     g_g_in = jnp.sum(g_normed * inputs_f * root, axis=0)
 
-    packed = jnp.concatenate(
+    def placed(part, size):
+        spots = jnp.zeros(part.shape[:-1] + (size,), F32)
+        return lax.dynamic_update_slice_in_dim(
+            spots, part, here * part.shape[-1], part.ndim - 1
+        )
+
+    conv_part = jnp.concatenate([placed(gx[:5, :units], E), gbc[:5]], axis=1)
+    early = jnp.concatenate(
         [
-            g_g_in,
-            gbc[:5].reshape(-1),
-            gx[:5, :units].reshape(-1),
-            gx[6, :units],
-            jnp.sum(gx[5, :units].reshape(own_heads, P_SIZE), axis=1),
-            gdt[1, :own_heads],
-            gdt[0, :own_heads],
+            placed(gx[6, :units], E),
+            conv_part.reshape(-1),
+            placed(gdt[1, :own_heads], H),
+            placed(gdt[0, :own_heads], H),
+            placed(jnp.sum(gx[5, :units].reshape(own_heads, P_SIZE), axis=1), H),
         ]
     )
-    everyone = lax.all_gather(packed, "dp")
-    everyone = jnp.sum(lax.all_gather(everyone, "width"), axis=0)
-    cut = D + 10 * N
-    common = jnp.sum(everyone[:, :cut], axis=0)
-    bc_part = common[D:].reshape(5, 2 * N)
-    mine = everyone[:, cut:]
-    x_part = mine[:, : 5 * units].reshape(dp, 5, units).transpose(1, 0, 2).reshape(5, E)
-    heads_part = mine[:, 6 * units :].reshape(dp, 3, own_heads).transpose(1, 0, 2).reshape(3, H)
-    conv_part = jnp.concatenate([x_part, bc_part], axis=1)
-    total_small = jnp.concatenate(
-        [
-            common[:D],
-            mine[:, 5 * units : 6 * units].reshape(E),
-            conv_part.reshape(-1),
-            heads_part[1],
-            heads_part[2],
-            heads_part[0],
-        ]
-    )
+    total_small = jnp.concatenate([tree_sum(g_g_in), tree_sum(early)])
     step_float = step_count[0].astype(F32)
     rate_table, decay_table = small_table()
     new_small, mom_small, sec_small = adamw_step(

time: 1030 us -> 768 us (0.75)
  waiting for transfers between devices: 642 us -> 289 us
  starting transfers between devices: 13.6 us -> 81.3 us
  local copies, waits for them, and re-layouts: 34.8 us -> 55.3 us
    ppermute x0 -> x47, waiting for transfers between devices: none -> 188 us  [the longest x24 145 us: hop(): return lax.ppermute(values, 'dp', pairs)]
    reduce_scatter x1, waiting for transfers between devices: 179 us -> 0.01 us  [per_device(): lax.psum_scatter(partial_out, 'dp', scatter_dimension=0, tiled=True)]
    unnamed x9 -> x3, waiting for transfers between devices: 113 us -> 0.05 us
    all_gather x1, waiting for transfers between devices: 125 us -> 33.5 us  [per_device(): normed_all = lax.all_gather(normed_low, 'dp', axis=0, tiled=True)]
    ppermute x0 -> x47, starting transfers between devices: none -> 65.2 us  [the longest x24 55.9 us: hop(): return lax.ppermute(values, 'dp', pairs)]
    all_gather x2 -> x1, waiting for transfers between devices: 99.2 us -> 40.7 us  [per_device(): cotangent_all = lax.all_gather(later, 'dp', axis=0, tiled=True)]
    reduce_scatter x1 -> x0, waiting for transfers between devices: 47.9 us -> none  [per_device(): lax.psum_scatter(partial_normed, 'dp', scatter_dimension=0, tiled=True)]
    ppermute x2 -> x3, waiting for transfers between devices: 59.4 us -> 26.9 us  [width_sum(): lax.ppermute(values, 'width', [(0, 1), (1, 0)]).astype(F32)]
  transfers between devices with their start and end apart: 11 -> 55, of which waited for: 9 -> 21; matrix products, arithmetic and copies ran while one was open for 13% -> 29% of each run, Pallas kernels for 4% -> 16%
where the time goes in v2:
time: 768 us; the launch traced here: 763 us
  waiting for transfers between devices  289 us (38%)
  Pallas kernels  125 us (16%)
  matrix products  107 us (14%)
  starting transfers between devices  81.3 us (11%)
  other arithmetic  69.2 us (9%)
  local copies, waits for them, and re-layouts  55.3 us (7%)
  blocking collectives  19.5 us (3%)
  between operations  16.3 us (2%)
    ppermute x24, waiting for transfers between devices, hop(): return lax.ppermute(values, 'dp', pairs)  145 us
    pallas_call x1, Pallas kernels, run_backward(): pl.pallas_call(partial(backward_kernel, heads), grid=(count,), in_specs=[...  81.1 us
    ppermute x24, starting transfers between devices, hop(): return lax.ppermute(values, 'dp', pairs)  55.9 us
    pallas_call x1, Pallas kernels, run_forward(): pl.pallas_call(partial(forward_kernel, heads), grid=(blocks,), in_specs=[...  43.8 us
    all_gather x1, waiting for transfers between devices, per_device(): cotangent_all = lax.all_gather(later, 'dp', axis=0, tiled=True)  40.7 us
    all_gather x1, waiting for transfers between devices, per_device(): normed_all = lax.all_gather(normed_low, 'dp', axis=0, tiled=True)  33.5 us
    ppermute x8, waiting for transfers between devices, tree_sum(): lax.ppermute(values, 'dp', [(i, i ^ bit) for i in range(16)])  28.6 us
    ppermute x3, waiting for transfers between devices, width_sum(): lax.ppermute(values, 'width', [(0, 1), (1, 0)]).astype(F32)  26.9 us
  transfers between devices with their start and end apart: 55, of which 21 were waited for; matrix products, arithmetic and copies ran while one was open for 29% of the time, Pallas kernels for 16%

profile of v2, /device:TPU:0, one launch (start us, length us, event | category | flops | bytes accessed | tf_op | source)
XLA Modules:
  0.0 762.5 jit_solution(7414241230745665321)
XLA Ops:
  10.5 2.5 fusion.6
  13.1 3.5 copy.97
  18.6 7.4 all-to-all-start
  29.5 65.4 %collective-permute-done.1 = bf16[128,320]{1,0:T(8,128)(2,1)S(1)} collective-permute-done((bf16[128,320]{1,0:T(8,128)(2,1)S(1)}, bf16[128,320]{1,0:T(8,128)(2,1)S(1)}, u32[]{:S(2)}, u32[]{:S(2)}) %collective-permute-start.1) | collective-permute-done | bytes 81952 | tf_op jit(solution)/shard_map/ppermute | solution.py:526
  94.9 12.7 %collective-permute-start.5 = (bf16[128,320]{1,0:T(8,128)(2,1)S(1)}, bf16[128,320]{1,0:T(8,128)(2,1)S(1)}, u32[]{:S(2)}, u32[]{:S(2)}) collective-permute-start(bf16[128,320]{1,0:T(8,128)(2,1)S(1)} %collective-permute-done.1), channel_id=1, source_target_pairs={{0,4},{1,5},{4,8},{5,9},{8,12},{9,13},{12,14},{13,15},{14,10},{15,... | collective-permute-start | bytes 245768 | tf_op jit(solution)/shard_map/ppermute | solution.py:526
  109.2 3.6 collective-permute-done.5
  112.7 7.8 %collective-permute-start.9 = (bf16[128,320]{1,0:T(8,128)(2,1)S(1)}, bf16[128,320]{1,0:T(8,128)(2,1)S(1)}, u32[]{:S(2)}, u32[]{:S(2)}) collective-permute-start(bf16[128,320]{1,0:T(8,128)(2,1)S(1)} %collective-permute-done.5), channel_id=1, source_target_pairs={{0,4},{1,5},{4,8},{5,9},{8,12},{9,13},{12,14},{13,15},{14,10},{15,... | collective-permute-start | bytes 245768 | tf_op jit(solution)/shard_map/ppermute | solution.py:526
  123.9 2.3 collective-permute-done.9
  126.2 2.3 collective-permute-start.13
  128.4 3.3 collective-permute-done.11
  135.1 4.3 collective-permute-done.15
  146.4 3.5 fusion.2
  149.9 33.5 %all-gather.5.cloned.1.call-done = bf16[4096,2048]{1,0:T(8,128)(2,1)} async-done(((bf16[256,2048]{1,0:T(8,128)(2,1)}), bf16[4096,2048]{1,0:T(8,128)(2,1)}) %all-gather.5.cloned.1.call-update) | async-done | bytes 16777232 | tf_op jit(solution)/shard_map/all_gather | solution.py:688
  189.8 3.9 iota_subtract_fusion
  193.7 23.5 %convolution_convert_fusion.1.gate_ref.x_ref.bc_ref.dt_ref.xprev_ref.bcprev_ref = bf16[4096,896]{1,0:T(8,128)(2,1)} fusion(bf16[4096,2048]{1,0:T(8,128)(2,1)} %all-gather.5.cloned.1.call-done, bf16[2048,4]{1,0:T(8,128)(2,1)S(1)} %copy-done.8, bf16[2048,256]{1,0:T(8,128)(2,1)S(1)} %slice.224, bf16[2048,512]{1,0:T(8,128)(2,1)} %bitcast.1), kind=kOutput, calls=%fused_computation.4 | convolution fusion | flops 15050735616 | bytes 27279360 | tf_op jit(solution)/shard_map/dot_general | solution.py:739
  217.3 43.8 %scan_forward.1 = (bf16[4096,256]{1,0:T(8,128)(2,1)}, f32[4096,256]{1,0:T(8,128)}, f32[4096,1]{1,0:T(8,128)}, f32[16,256,128]{2,1,0:T(8,128)}) custom-call(bf16[4096,896]{1,0:T(8,128)(2,1)} %convolution_convert_fusion.1.gate_ref.x_ref.bc_ref.dt_ref.xprev_ref.bcprev_ref, ...), custom_call_target="tpu_custom_call" | custom-call | flops 1048576000 | bytes 20480000 | tf_op jit(solution)/shard_map/scan_forward/pallas_call | solution.py:392
  261.0 2.3 reduce.1
  263.4 10.1 %convolution_convert_fusion = bf16[4096,2048]{1,0:T(8,128)(2,1)} fusion(bf16[4096,256]{1,0:T(8,128)(2,1)} %get-tuple-element.26, f32[256,2048]{1,0:T(8,128)S(1)} %copy-done.2), kind=kOutput, calls=%fused_computation | convolution fusion | flops 4303880192 | bytes 20971520 | tf_op jit(solution)/shard_map/dot_general | solution.py:742
  273.5 40.7 %all-gather.7.cloned.1.call-done = bf16[4096,2048]{1,0:T(8,128)(2,1)} async-done(((bf16[256,2048]{1,0:T(8,128)(2,1)}), bf16[4096,2048]{1,0:T(8,128)(2,1)}) %all-gather.7.cloned.1.call-update) | async-done | bytes 16777232 | tf_op jit(solution)/shard_map/all_gather | solution.py:746
  314.2 13.6 %multiply_reduce_fusion = (f32[4096]{0:T(1024)S(1)}, f32[4096,256]{1,0:T(8,128)}) fusion(bf16[4096,256]{1,0:T(8,128)(2,1)} %get-tuple-element.26, bf16[4096,2048]{1,0:T(8,128)(2,1)} %all-gather.7.cloned.1.call-done, f32[256,2048]{1,0:T(8,128)S(1)} %copy-done.2), kind=kOutput, calls=%fused_computation.17 | convolution fusion | flops 4298633216 | bytes 25182208 | tf_op jit(solution)/shard_map/dot_general | solution.py:747
  327.8 19.5 %all-gather.1 = f32[16,2,4096]{2,1,0:T(2,128)S(1)} all-gather(f32[1,2,4096]{2,1,0:T(2,128)S(1)} %maximum_bitcast_fusion.1), channel_id=2, replica_groups=mesh['width'=2,'dp'=16] {'dp'}, dimensions={0}, use_global_device_ids=true | all-gather | bytes 557056 | tf_op jit(solution)/shard_map/all_gather | solution.py:751
  352.2 4.5 divide_multiply_fusion.pull_ref
  358.7 81.1 %scan_backward.1 = (bf16[4096,896]{1,0:T(8,128)(2,1)}, bf16[4096,256]{1,0:T(8,128)(2,1)}, f32[256,128]{1,0:T(8,128)}, f32[16,256]{1,0:T(8,128)}, f32[16,256]{1,0:T(8,128)}, /*index=5*/f32[8,128]{1,0:T(8,128)}) custom-call(bf16[4096,896]{1,0:T(8,128)(2,1)} %convolution_convert_fusion.1.gate_ref.x_ref.bc_ref.dt_ref.xprev_ref.bcprev_ref, ...), custom_call_target="tpu_custom_call" | custom-call | flops 3145728000 | bytes 32768000 | tf_op jit(solution)/shard_map/scan_backward/pallas_call | solution.py:451
  440.2 3.7 dynamic-slice_bitcast_fusion
  445.0 18.2 %convolution_convert_fusion.2 = bf16[2048,896]{0,1:T(8,128)(2,1)S(1)} fusion(bf16[4096,2048]{1,0:T(8,128)(2,1)} %all-gather.5.cloned.1.call-done, bf16[4096,896]{1,0:T(8,128)(2,1)S(1)} %copy-done.25), kind=kOutput, calls=%fused_computation.19 | convolution fusion | flops 15034220544 | bytes 27787264 | tf_op jit(solution)/shard_map/dot_general | solution.py:775
  467.0 4.8 all-to-all-start.1
  471.8 14.6 %fusion.53 = f32[4096,1024]{1,0:T(8,128)} fusion(bf16[4096,896]{1,0:T(8,128)(2,1)} %get-tuple-element.31, bf16[896,1024]{0,1:T(8,128)(2,1)S(1)} %get-tuple-element.32), kind=kOutput, calls=%fused_computation.165 | convolution fusion | flops 7516192768 | bytes 25952256 | tf_op jit(solution)/shard_map/dot_general | solution.py:587
  486.3 18.3 %convolution_add_fusion = f32[4096,1024]{1,0:T(8,128)} fusion(f32[4096,1024]{1,0:T(8,128)} %fusion.53, bf16[4096,896]{1,0:T(8,128)(2,1)} %collective-permute-done.17, bf16[896,1024]{0,1:T(8,128)(2,1)} %collective-permute-done.18), kind=kOutput, calls=%fused_computation.1 | convolution fusion | flops 7520387072 | bytes 42729472 | tf_op jit(solution)/shard_map/dot_general | solution.py:587
  510.4 25.3 %collective-permute-done.19 = bf16[256,1024]{1,0:T(8,128)(2,1)S(1)} collective-permute-done((bf16[256,1024]{1,0:T(8,128)(2,1)S(1)}, bf16[256,1024]{1,0:T(8,128)(2,1)S(1)}, u32[]{:S(2)}, u32[]{:S(2)}) %collective-permute-start.19) | collective-permute-done | bytes 524320 | tf_op jit(solution)/shard_map/ppermute | solution.py:526
  541.6 12.9 %collective-permute-start.21 = (bf16[512,1024]{1,0:T(8,128)(2,1)}, bf16[512,1024]{1,0:T(8,128)(2,1)}, u32[]{:S(2)}, u32[]{:S(2)}) collective-permute-start(bf16[512,1024]{1,0:T(8,128)(2,1)} %pad_maximum_fusion.1), channel_id=1, source_target_pairs={{0,4},{1,5},{4,8},{5,9},{8,12},{9,13},{12,14},{13,15},{14,10},{15,... | collective-permute-start | bytes 3145736 | tf_op jit(solution)/shard_map/ppermute | solution.py:526
  556.7 2.7 constant_dynamic-slice_fusion.1
  561.1 16.3 %collective-permute-done.21 = bf16[512,1024]{1,0:T(8,128)(2,1)} collective-permute-done((bf16[512,1024]{1,0:T(8,128)(2,1)}, bf16[512,1024]{1,0:T(8,128)(2,1)}, u32[]{:S(2)}, u32[]{:S(2)}) %collective-permute-start.21) | collective-permute-done | bytes 1048608 | tf_op jit(solution)/shard_map/ppermute | solution.py:526
  577.5 3.2 fusion.16
  580.7 2.5 collective-permute-start.22
  585.5 22.9 %collective-permute-done.46 = f32[26048]{0:T(1024)S(1)} collective-permute-done((f32[26048]{0:T(1024)S(1)}, f32[26048]{0:T(1024)S(1)}, u32[]{:S(2)}, u32[]{:S(2)}) %collective-permute-start.46) | collective-permute-done | bytes 104224 | tf_op jit(solution)/shard_map/ppermute | solution.py:640
  610.9 3.6 fusion.17
  625.2 15.4 %collective-permute-done.35 = bf16[128,320]{0,1:T(8,128)(2,1)} collective-permute-done((bf16[128,320]{0,1:T(8,128)(2,1)}, bf16[128,320]{0,1:T(8,128)(2,1)}, u32[]{:S(2)}, u32[]{:S(2)}) %collective-permute-start.35) | collective-permute-done | bytes 81952 | tf_op jit(solution)/shard_map/ppermute | solution.py:526
  642.2 5.5 collective-permute-start.23
  647.7 3.2 fusion.15
  650.9 8.3 %convolution_convert_fusion.3 = bf16[256,2048]{1,0:T(8,128)(2,1)S(1)} fusion(bf16[4096,256]{1,0:T(8,128)(2,1)S(1)} %copy-done.5, bf16[4096,2048]{1,0:T(8,128)(2,1)} %all-gather.7.cloned.1.call-done), kind=kOutput, calls=%fused_computation.22 | convolution fusion | flops 4295491584 | bytes 19922944 | tf_op jit(solution)/shard_map/dot_general | solution.py:778
  666.0 14.8 %collective-permute-done.49 = f32[26048]{0:T(1024)S(1)} collective-permute-done((f32[26048]{0:T(1024)S(1)}, f32[26048]{0:T(1024)S(1)}, u32[]{:S(2)}, u32[]{:S(2)}) %collective-permute-start.49) | collective-permute-done | bytes 104224 | tf_op jit(solution)/shard_map/ppermute | solution.py:641
  681.4 4.1 collective-permute-done.37
  687.6 2.8 fusion.18
  692.2 5.6 fusion.43
  699.7 26.9 %collective-permute-done.28 = bf16[16,128,512]{1,2,0:T(8,128)(2,1)S(1)} collective-permute-done((bf16[16,128,512]{1,2,0:T(8,128)(2,1)}, bf16[16,128,512]{1,2,0:T(8,128)(2,1)S(1)}, u32[]{:S(2)}, u32[]{:S(2)}) %collective-permute-start.28) | collective-permute-done | bytes 2097184 | tf_op jit(solution)/shard_map/ppermute | solution.py:655
  734.0 10.9 %fusion.45 = (bf16[128,8512]{0,1:T(8,128)(2,1)}, f32[128,8512]{0,1:T(8,128)}, f32[128,8512]{0,1:T(8,128)}, f32[128,8512]{0,1:T(8,128)}) fusion(f32[128,8512]{0,1:T(8,128)S(1)} %bitcast.150, f32[]{:T(128)} %bitcast.47, f32[128,320]{0,1:T(8,128)S(1)} %convert_add_fusion.3, f32[128,4096]{0,1:T(8,128)} %bitcast.159, f32[128,4096]{0,1:T(8,128)S(1)} %bitcast.158, ...), kind=kLoop, calls=%fused_computation.159 | loop fusion | flops 18522112 | bytes 32686084 | tf_op jit(solution)/shard_map/convert_element_type | solution.py:846
  746.7 2.9 collective-permute-done.43
  751.1 3.9 fusion.11
  (273 shorter events, 97.8 us)
Async XLA Ops:
  7.2 176.2 %all-gather.5.cloned.1.call-start = ((), (), s32[]{:S(2)}) async-start(), calls=%async_computation.3 | async-start | bytes 17825792 | tf_op jit(solution)/shard_map/all_gather | solution.py:688
  18.6 127.8 %all-to-all-start = ((bf16[16,128,512]{2,1,0:T(8,128)(2,1)}), bf16[16,128,512]{2,1,0:T(8,128)(2,1)}, u32[]{:S(2)}, u32[]{:S(2)}) async-start(bf16[16,128,512]{2,1,0:T(8,128)(2,1)} %maximum_bitcast_fusion), calls=%async_computation | async-start | bytes 4194304 | tf_op jit(solution)/shard_map/all_to_all | solution.py:698
  26.0 288.2 %all-gather.7.cloned.1.call-start = ((), (), s32[]{:S(2)}) async-start(), calls=%async_computation.5 | async-start | bytes 17825792 | tf_op jit(solution)/shard_map/all_gather | solution.py:746
  27.5 67.4 %collective-permute-start.1 = (bf16[128,320]{1,0:T(8,128)(2,1)S(1)}, bf16[128,320]{1,0:T(8,128)(2,1)S(1)}, u32[]{:S(2)}, u32[]{:S(2)}) collective-permute-start(bf16[128,320]{1,0:T(8,128)(2,1)S(1)} %get-tuple-element.70), channel_id=1, source_target_pairs={{0,4},{1,5},{4,8},{5,9},{8,12},{9,13},{12,14},{13,15},{14,10},{15,... | collective-permute-start | bytes 245768 | tf_op jit(solution)/shard_map/ppermute | solution.py:526
  29.3 78.3 %collective-permute-start.3 = (bf16[128,320]{1,0:T(8,128)(2,1)S(1)}, bf16[128,320]{1,0:T(8,128)(2,1)S(1)}, u32[]{:S(2)}, u32[]{:S(2)}) collective-permute-start(bf16[128,320]{1,0:T(8,128)(2,1)S(1)} %get-tuple-element.70), channel_id=1, source_target_pairs={{0,2},{1,3},{4,0},{5,1},{8,4},{9,5},{12,8},{13,9},{14,12},{15,13},... | collective-permute-start | bytes 245768 | tf_op jit(solution)/shard_map/ppermute | solution.py:526
  29.5 78.4 %collective-permute-start = (bf16[128,320]{1,0:T(8,128)(2,1)S(1)}, bf16[128,320]{1,0:T(8,128)(2,1)S(1)}, u32[]{:S(2)}, u32[]{:S(2)}) collective-permute-start(bf16[128,320]{1,0:T(8,128)(2,1)S(1)} %get-tuple-element.70), channel_id=1, source_target_pairs={{0,1},{1,0},{2,3},{3,2},{4,5},{5,4},{6,7},{7,6},{8,9},{9,8},{10,11... | collective-permute-start | bytes 245768 | tf_op jit(solution)/shard_map/ppermute | solution.py:530
  94.9 26.4 %collective-permute-start.2 = (bf16[128,320]{1,0:T(8,128)(2,1)S(1)}, bf16[128,320]{1,0:T(8,128)(2,1)S(1)}, u32[]{:S(2)}, u32[]{:S(2)}) collective-permute-start(bf16[128,320]{1,0:T(8,128)(2,1)S(1)} %collective-permute-done.1), channel_id=1, source_target_pairs={{0,1},{1,0},{2,3},{3,2},{4,5},{5,4},{6,7},{7,6},{8,9},{9,8},{10,11... | collective-permute-start | bytes 245768 | tf_op jit(solution)/shard_map/ppermute | solution.py:530
  94.9 17.8 %collective-permute-start.5 = (bf16[128,320]{1,0:T(8,128)(2,1)S(1)}, bf16[128,320]{1,0:T(8,128)(2,1)S(1)}, u32[]{:S(2)}, u32[]{:S(2)}) collective-permute-start(bf16[128,320]{1,0:T(8,128)(2,1)S(1)} %collective-permute-done.1), channel_id=1, source_target_pairs={{0,4},{1,5},{4,8},{5,9},{8,12},{9,13},{12,14},{13,15},{14,10},{15,... | collective-permute-start | bytes 245768 | tf_op jit(solution)/shard_map/ppermute | solution.py:526
  107.6 15.0 %collective-permute-start.4 = (bf16[128,320]{1,0:T(8,128)(2,1)S(1)}, bf16[128,320]{1,0:T(8,128)(2,1)S(1)}, u32[]{:S(2)}, u32[]{:S(2)}) collective-permute-start(bf16[128,320]{1,0:T(8,128)(2,1)S(1)} %collective-permute-done.3), channel_id=1, source_target_pairs={{0,1},{1,0},{2,3},{3,2},{4,5},{5,4},{6,7},{7,6},{8,9},{9,8},{10,11... | collective-permute-start | bytes 245768 | tf_op jit(solution)/shard_map/ppermute | solution.py:530
  107.9 13.2 %collective-permute-start.7 = (bf16[128,320]{1,0:T(8,128)(2,1)S(1)}, bf16[128,320]{1,0:T(8,128)(2,1)S(1)}, u32[]{:S(2)}, u32[]{:S(2)}) collective-permute-start(bf16[128,320]{1,0:T(8,128)(2,1)S(1)} %collective-permute-done.3), channel_id=1, source_target_pairs={{0,2},{1,3},{4,0},{5,1},{8,4},{9,5},{12,8},{13,9},{14,12},{15,13},... | collective-permute-start | bytes 245768 | tf_op jit(solution)/shard_map/ppermute | solution.py:526
  112.7 19.1 %collective-permute-start.6 = (bf16[128,320]{1,0:T(8,128)(2,1)S(1)}, bf16[128,320]{1,0:T(8,128)(2,1)S(1)}, u32[]{:S(2)}, u32[]{:S(2)}) collective-permute-start(bf16[128,320]{1,0:T(8,128)(2,1)S(1)} %collective-permute-done.5), channel_id=1, source_target_pairs={{0,1},{1,0},{2,3},{3,2},{4,5},{5,4},{6,7},{7,6},{8,9},{9,8},{10,11... | collective-permute-start | bytes 245768 | tf_op jit(solution)/shard_map/ppermute | solution.py:530
  112.7 13.5 %collective-permute-start.9 = (bf16[128,320]{1,0:T(8,128)(2,1)S(1)}, bf16[128,320]{1,0:T(8,128)(2,1)S(1)}, u32[]{:S(2)}, u32[]{:S(2)}) collective-permute-start(bf16[128,320]{1,0:T(8,128)(2,1)S(1)} %collective-permute-done.5), channel_id=1, source_target_pairs={{0,4},{1,5},{4,8},{5,9},{8,12},{9,13},{12,14},{13,15},{14,10},{15,... | collective-permute-start | bytes 245768 | tf_op jit(solution)/shard_map/ppermute | solution.py:526
  121.0 12.6 %collective-permute-start.8 = (bf16[128,320]{1,0:T(8,128)(2,1)S(1)}, bf16[128,320]{1,0:T(8,128)(2,1)S(1)}, u32[]{:S(2)}, u32[]{:S(2)}) collective-permute-start(bf16[128,320]{1,0:T(8,128)(2,1)S(1)} %collective-permute-done.7), channel_id=1, source_target_pairs={{0,1},{1,0},{2,3},{3,2},{4,5},{5,4},{6,7},{7,6},{8,9},{9,8},{10,11... | collective-permute-start | bytes 245768 | tf_op jit(solution)/shard_map/ppermute | solution.py:530
  121.3 10.5 %collective-permute-start.11 = (bf16[128,320]{1,0:T(8,128)(2,1)S(1)}, bf16[128,320]{1,0:T(8,128)(2,1)S(1)}, u32[]{:S(2)}, u32[]{:S(2)}) collective-permute-start(bf16[128,320]{1,0:T(8,128)(2,1)S(1)} %collective-permute-done.7), channel_id=1, source_target_pairs={{0,2},{1,3},{4,0},{5,1},{8,4},{9,5},{12,8},{13,9},{14,12},{15,13},... | collective-permute-start | bytes 245768 | tf_op jit(solution)/shard_map/ppermute | solution.py:526
  126.2 8.8 %collective-permute-start.13 = (bf16[64,320]{1,0:T(8,128)(2,1)S(1)}, bf16[64,320]{1,0:T(8,128)(2,1)S(1)}, u32[]{:S(2)}, u32[]{:S(2)}) collective-permute-start(bf16[64,320]{1,0:T(8,128)(2,1)S(1)} %slice.222), channel_id=1, source_target_pairs={{0,4},{1,5},{4,8},{5,9},{8,12},{9,13},{12,14},{13,15},{14,10},{15,... | collective-permute-start | bytes 122888 | tf_op jit(solution)/shard_map/ppermute | solution.py:526
  131.8 7.6 collective-permute-start.15
  131.8 7.6 collective-permute-start.10
  131.9 8.8 %collective-permute-start.12 = (bf16[128,320]{1,0:T(8,128)(2,1)S(1)}, bf16[128,320]{1,0:T(8,128)(2,1)S(1)}, u32[]{:S(2)}, u32[]{:S(2)}) collective-permute-start(bf16[128,320]{1,0:T(8,128)(2,1)S(1)} %collective-permute-done.11), channel_id=1, source_target_pairs={{0,1},{1,0},{2,3},{3,2},{4,5},{5,4},{6,7},{7,6},{8,9},{9,8},{10,11... | collective-permute-start | bytes 245768 | tf_op jit(solution)/shard_map/ppermute | solution.py:530
  135.0 7.0 collective-permute-start.14
  183.4 567.6 %reduce-scatter.2.cloned.1.call-start = ((), (), s32[]{:S(2)}) async-start(), calls=%async_computation.4 | async-start | bytes 17825792 | tf_op jit(solution)/shard_map/reduce_scatter | solution.py:743
  439.8 46.6 %collective-permute-start.17 = (bf16[4096,896]{1,0:T(8,128)(2,1)}, bf16[4096,896]{1,0:T(8,128)(2,1)}, u32[]{:S(2)}, u32[]{:S(2)}) collective-permute-start(bf16[4096,896]{1,0:T(8,128)(2,1)} %get-tuple-element.31), channel_id=1, source_target_pairs={{0,1},{1,0},{2,3},{3,2},{4,5},{5,4},{6,7},{7,6},{8,9},{9,8},{10,11... | collective-permute-start | bytes 22020104 | tf_op jit(solution)/shard_map/ppermute | solution.py:530
  443.9 42.4 %collective-permute-start.18 = (bf16[896,1024]{0,1:T(8,128)(2,1)}, bf16[896,1024]{0,1:T(8,128)(2,1)}, u32[]{:S(2)}, u32[]{:S(2)}) collective-permute-start(bf16[896,1024]{0,1:T(8,128)(2,1)} %get-tuple-element.64), channel_id=1, source_target_pairs={{0,1},{1,0},{2,3},{3,2},{4,5},{5,4},{6,7},{7,6},{8,9},{9,8},{10,11... | collective-permute-start | bytes 5505032 | tf_op jit(solution)/shard_map/ppermute | solution.py:530
  467.0 74.7 %all-to-all-start.1 = ((bf16[16,128,512]{1,2,0:T(8,128)(2,1)}), bf16[16,128,512]{1,2,0:T(8,128)(2,1)}, u32[]{:S(2)}, u32[]{:S(2)}) async-start(bf16[16,128,512]{1,2,0:T(8,128)(2,1)} %copy_bitcast_fusion), calls=%async_computation.2 | async-start | bytes 4194304 | tf_op jit(solution)/shard_map/all_to_all | solution.py:783
  506.5 29.2 %collective-permute-start.19 = (bf16[256,1024]{1,0:T(8,128)(2,1)S(1)}, bf16[256,1024]{1,0:T(8,128)(2,1)S(1)}, u32[]{:S(2)}, u32[]{:S(2)}) collective-permute-start(bf16[256,1024]{1,0:T(8,128)(2,1)S(1)} %get-tuple-element.83), channel_id=1, source_target_pairs={{0,4},{1,5},{4,8},{5,9},{8,12},{9,13},{12,14},{13,15},{14,10},{15,... | collective-permute-start | bytes 1572872 | tf_op jit(solution)/shard_map/ppermute | solution.py:526
  508.4 29.2 %collective-permute-start.20 = (bf16[256,1024]{1,0:T(8,128)(2,1)S(1)}, bf16[256,1024]{1,0:T(8,128)(2,1)S(1)}, u32[]{:S(2)}, u32[]{:S(2)}) collective-permute-start(bf16[256,1024]{1,0:T(8,128)(2,1)S(1)} %get-tuple-element.82), channel_id=1, source_target_pairs={{0,2},{1,3},{4,0},{5,1},{8,4},{9,5},{12,8},{13,9},{14,12},{15,13},... | collective-permute-start | bytes 1572872 | tf_op jit(solution)/shard_map/ppermute | solution.py:526
  541.6 35.9 %collective-permute-start.21 = (bf16[512,1024]{1,0:T(8,128)(2,1)}, bf16[512,1024]{1,0:T(8,128)(2,1)}, u32[]{:S(2)}, u32[]{:S(2)}) collective-permute-start(bf16[512,1024]{1,0:T(8,128)(2,1)} %pad_maximum_fusion.1), channel_id=1, source_target_pairs={{0,4},{1,5},{4,8},{5,9},{8,12},{9,13},{12,14},{13,15},{14,10},{15,... | collective-permute-start | bytes 3145736 | tf_op jit(solution)/shard_map/ppermute | solution.py:526
  559.6 48.8 %collective-permute-start.29 = (bf16[8,128,320]{1,2,0:T(8,128)(2,1)S(1)}, bf16[8,128,320]{1,2,0:T(8,128)(2,1)S(1)}, u32[]{:S(2)}, u32[]{:S(2)}) collective-permute-start(bf16[8,128,320]{1,2,0:T(8,128)(2,1)S(1)} %bitcast.162), channel_id=1, source_target_pairs={{0,1},{1,0},{2,3},{3,2},{4,5},{5,4},{6,7},{7,6},{8,9},{9,8},{10,11... | collective-permute-start | bytes 1966088 | tf_op jit(solution)/shard_map/ppermute | solution.py:530
  561.1 49.8 %collective-permute-start.24 = (bf16[512,1024]{1,0:T(8,128)(2,1)}, bf16[512,1024]{1,0:T(8,128)(2,1)}, u32[]{:S(2)}, u32[]{:S(2)}) collective-permute-start(bf16[512,1024]{1,0:T(8,128)(2,1)} %pad_maximum_fusion.2), channel_id=1, source_target_pairs={{0,2},{1,3},{4,0},{5,1},{8,4},{9,5},{12,8},{13,9},{14,12},{15,13},... | collective-permute-start | bytes 3145736 | tf_op jit(solution)/shard_map/ppermute | solution.py:526
  580.7 30.2 %collective-permute-start.22 = (bf16[512,1024]{1,0:T(8,128)(2,1)}, bf16[512,1024]{1,0:T(8,128)(2,1)}, u32[]{:S(2)}, u32[]{:S(2)}) collective-permute-start(bf16[512,1024]{1,0:T(8,128)(2,1)} %fusion.16), channel_id=1, source_target_pairs={{0,4},{1,5},{4,8},{5,9},{8,12},{9,13},{12,14},{13,15},{14,10},{15,... | collective-permute-start | bytes 3145736 | tf_op jit(solution)/shard_map/ppermute | solution.py:526
  585.4 23.0 %collective-permute-start.46 = (f32[26048]{0:T(1024)S(1)}, f32[26048]{0:T(1024)S(1)}, u32[]{:S(2)}, u32[]{:S(2)}) collective-permute-start(f32[26048]{0:T(1024)S(1)} %add.650), channel_id=1, source_target_pairs={{0,2},{1,3},{2,0},{3,1},{4,6},{5,7},{6,4},{7,5},{8,10},{9,11},{10,... | collective-permute-start | bytes 312584 | tf_op jit(solution)/shard_map/ppermute | solution.py:640
  608.4 13.7 %collective-permute-start.47 = (f32[26048]{0:T(1024)S(1)}, f32[26048]{0:T(1024)}, u32[]{:S(2)}, u32[]{:S(2)}) collective-permute-start(f32[26048]{0:T(1024)S(1)} %add.651), channel_id=1, source_target_pairs={{0,4},{1,5},{2,6},{3,7},{4,0},{5,1},{6,2},{7,3},{8,12},{9,13},{10,... | collective-permute-start | bytes 312584 | tf_op jit(solution)/shard_map/ppermute | solution.py:640
  608.9 5.8 collective-permute-start.30
  614.5 33.1 %collective-permute-start.25 = (bf16[512,1024]{1,0:T(8,128)(2,1)S(1)}, bf16[512,1024]{1,0:T(8,128)(2,1)}, u32[]{:S(2)}, u32[]{:S(2)}) collective-permute-start(bf16[512,1024]{1,0:T(8,128)(2,1)S(1)} %get-tuple-element.57), channel_id=1, source_target_pairs={{0,2},{1,3},{4,0},{5,1},{8,4},{9,5},{12,8},{13,9},{14,12},{15,13},... | collective-permute-start | bytes 3145736 | tf_op jit(solution)/shard_map/ppermute | solution.py:526
  617.7 22.8 %collective-permute-start.35 = (bf16[128,320]{0,1:T(8,128)(2,1)}, bf16[128,320]{0,1:T(8,128)(2,1)}, u32[]{:S(2)}, u32[]{:S(2)}) collective-permute-start(bf16[128,320]{0,1:T(8,128)(2,1)} %pad_maximum_fusion.7), channel_id=1, source_target_pairs={{0,2},{1,3},{4,0},{5,1},{8,4},{9,5},{12,8},{13,9},{14,12},{15,13},... | collective-permute-start | bytes 245768 | tf_op jit(solution)/shard_map/ppermute | solution.py:526
  620.7 19.8 %collective-permute-start.32 = (bf16[128,320]{0,1:T(8,128)(2,1)}, bf16[128,320]{0,1:T(8,128)(2,1)}, u32[]{:S(2)}, u32[]{:S(2)}) collective-permute-start(bf16[128,320]{0,1:T(8,128)(2,1)} %fusion.30), channel_id=1, source_target_pairs={{0,4},{1,5},{4,8},{5,9},{8,12},{9,13},{12,14},{13,15},{14,10},{15,... | collective-permute-start | bytes 245768 | tf_op jit(solution)/shard_map/ppermute | solution.py:526
  623.7 37.9 %collective-permute-start.48 = (f32[26048]{0:T(1024)}, f32[26048]{0:T(1024)S(1)}, u32[]{:S(2)}, u32[]{:S(2)}) collective-permute-start(f32[26048]{0:T(1024)} %add.652), channel_id=1, source_target_pairs={{0,8},{1,9},{2,10},{3,11},{4,12},{5,13},{6,14},{7,15},{8,0},{9,1},... | collective-permute-start | bytes 312584 | tf_op jit(solution)/shard_map/ppermute | solution.py:640
  642.2 20.9 %collective-permute-start.36 = (bf16[128,320]{0,1:T(8,128)(2,1)}, bf16[128,320]{0,1:T(8,128)(2,1)}, u32[]{:S(2)}, u32[]{:S(2)}) collective-permute-start(bf16[128,320]{0,1:T(8,128)(2,1)} %get-tuple-element.73), channel_id=1, source_target_pairs={{0,2},{1,3},{4,0},{5,1},{8,4},{9,5},{12,8},{13,9},{14,12},{15,13},... | collective-permute-start | bytes 245768 | tf_op jit(solution)/shard_map/ppermute | solution.py:526
  642.2 45.4 %collective-permute-start.23 = (bf16[512,1024]{1,0:T(8,128)(2,1)S(1)}, bf16[512,1024]{1,0:T(8,128)(2,1)}, u32[]{:S(2)}, u32[]{:S(2)}) collective-permute-start(bf16[512,1024]{1,0:T(8,128)(2,1)S(1)} %get-tuple-element.56), channel_id=1, source_target_pairs={{0,4},{1,5},{4,8},{5,9},{8,12},{9,13},{12,14},{13,15},{14,10},{15,... | collective-permute-start | bytes 3145736 | tf_op jit(solution)/shard_map/ppermute | solution.py:526
  650.9 36.7 %collective-permute-start.26 = (bf16[512,1024]{1,0:T(8,128)(2,1)}, bf16[512,1024]{1,0:T(8,128)(2,1)}, u32[]{:S(2)}, u32[]{:S(2)}) collective-permute-start(bf16[512,1024]{1,0:T(8,128)(2,1)} %fusion.15), channel_id=1, source_target_pairs={{0,2},{1,3},{4,0},{5,1},{8,4},{9,5},{12,8},{13,9},{14,12},{15,13},... | collective-permute-start | bytes 3145736 | tf_op jit(solution)/shard_map/ppermute | solution.py:526
  659.3 31.4 %collective-permute-start.39 = (bf16[256,2048]{1,0:T(8,128)(2,1)S(1)}, bf16[256,2048]{1,0:T(8,128)(2,1)}, u32[]{:S(2)}, u32[]{:S(2)}) collective-permute-start(bf16[256,2048]{1,0:T(8,128)(2,1)S(1)} %convolution_convert_fusion.3), channel_id=1, source_target_pairs={{0,16},{16,0},{1,17},{17,1},{2,18},{18,2},{3,19},{19,3},{4,20},{20... | collective-permute-start | bytes 3145736 | tf_op jit(solution)/shard_map/ppermute | solution.py:655
  662.4 18.4 %collective-permute-start.49 = (f32[26048]{0:T(1024)S(1)}, f32[26048]{0:T(1024)S(1)}, u32[]{:S(2)}, u32[]{:S(2)}) collective-permute-start(f32[26048]{0:T(1024)S(1)} %add.653), channel_id=1, source_target_pairs={{0,16},{16,0},{1,17},{17,1},{2,18},{18,2},{3,19},{19,3},{4,20},{20... | collective-permute-start | bytes 312584 | tf_op jit(solution)/shard_map/ppermute | solution.py:641
  663.0 18.3 %collective-permute-start.33 = (bf16[128,320]{0,1:T(8,128)(2,1)}, bf16[128,320]{0,1:T(8,128)(2,1)S(1)}, u32[]{:S(2)}, u32[]{:S(2)}) collective-permute-start(bf16[128,320]{0,1:T(8,128)(2,1)} %get-tuple-element.72), channel_id=1, source_target_pairs={{0,4},{1,5},{4,8},{5,9},{8,12},{9,13},{12,14},{13,15},{14,10},{15,... | collective-permute-start | bytes 245768 | tf_op jit(solution)/shard_map/ppermute | solution.py:526
  685.5 12.3 %collective-permute-start.38 = (bf16[128,320]{0,1:T(8,128)(2,1)S(1)}, bf16[128,320]{0,1:T(8,128)(2,1)S(1)}, u32[]{:S(2)}, u32[]{:S(2)}) collective-permute-start(bf16[128,320]{0,1:T(8,128)(2,1)S(1)} %fusion.33), channel_id=1, source_target_pairs={{0,16},{16,0},{1,17},{17,1},{2,18},{18,2},{3,19},{19,3},{4,20},{20... | collective-permute-start | bytes 245768 | tf_op jit(solution)/shard_map/ppermute | solution.py:655
  687.1 39.5 %collective-permute-start.28 = (bf16[16,128,512]{1,2,0:T(8,128)(2,1)}, bf16[16,128,512]{1,2,0:T(8,128)(2,1)S(1)}, u32[]{:S(2)}, u32[]{:S(2)}) collective-permute-start(bf16[16,128,512]{1,2,0:T(8,128)(2,1)} %all-to-all-done.1), channel_id=1, source_target_pairs={{0,16},{16,0},{1,17},{17,1},{2,18},{18,2},{3,19},{19,3},{4,20},{20... | collective-permute-start | bytes 6291464 | tf_op jit(solution)/shard_map/ppermute | solution.py:655
  690.6 7.2 collective-permute-start.27
  699.6 29.1 %collective-permute-start.40 = (f32[2048]{0:T(1024)S(1)}, f32[2048]{0:T(1024)S(1)}, u32[]{:S(2)}, u32[]{:S(2)}) collective-permute-start(f32[2048]{0:T(1024)S(1)} %get-tuple-element.39), channel_id=1, source_target_pairs={{0,1},{1,0},{2,3},{3,2},{4,5},{5,4},{6,7},{7,6},{8,9},{9,8},{10,11... | collective-permute-start | bytes 24584 | tf_op jit(solution)/shard_map/ppermute | solution.py:640
  732.5 12.4 %collective-permute-start.42 = (f32[2048]{0:T(1024)S(1)}, f32[2048]{0:T(1024)S(1)}, u32[]{:S(2)}, u32[]{:S(2)}) collective-permute-start(f32[2048]{0:T(1024)S(1)} %add.646), channel_id=1, source_target_pairs={{0,4},{1,5},{2,6},{3,7},{4,0},{5,1},{6,2},{7,3},{8,12},{9,13},{10,... | collective-permute-start | bytes 24584 | tf_op jit(solution)/shard_map/ppermute | solution.py:640
  749.5 5.4 collective-permute-start.44
  (38 other events, 243.0 us)
Sparse Core Ops, SparseCore 0:
  13.2 170.1 all-gather.4
  185.6 128.5 all-gather.6
  318.3 208.1 reduce-scatter.1

commit v3 on v2

--- a/solution.py
+++ b/solution.py
@@ -4,6 +4,7 @@
 import jax.numpy as jnp
 from jax import lax
 from jax.experimental import pallas as pl
+from jax.experimental.layout import Layout, with_layout_constraint
 from jax.experimental.pallas import tpu as pltpu
 from jax.sharding import PartitionSpec as P
 
@@ -27,7 +28,8 @@
 F32 = jnp.float32
 LOW = -1e30
 SHARED = 2 * N + H
-SPLITS = 1
+BACK_PARTS = 1
+FRONT_PARTS = 1
 
 
 def small_table():
@@ -150,33 +152,30 @@
     x_ref,
     bc_ref,
     dt_ref,
+    xprev_ref,
+    bcprev_ref,
     place_ref,
     remain_ref,
     px_ref,
     pbc_ref,
     pdt_ref,
-    zin_ref,
-    mixed_ref,
-    square_ref,
-    states_ref,
-    state,
-    xbuf,
-    bcbuf,
+    state_in,
+    *rest,
 ):
+    zin_ref, mixed_ref, square_ref, states_ref, state, xbuf, bcbuf = rest[-7:]
+
     @pl.when(pl.program_id(0) == 0)
     def _():
-        state[...] = jnp.zeros_like(state)
-        xbuf[0:8, :] = jnp.zeros((8, xbuf.shape[1]), F32)
-        bcbuf[0:8, :] = jnp.zeros((8, bcbuf.shape[1]), F32)
-
+        state[...] = state_in[...]
+
+    xbuf[0:8, :] = xprev_ref[8:16, :].astype(F32)
+    bcbuf[0:8, :] = bcprev_ref[8:16, :].astype(F32)
     place = place_ref[...]
     remain = remain_ref[...]
     xbuf[8 : 8 + STRETCH, :] = x_ref[...].astype(F32)
     bcbuf[8 : 8 + STRETCH, :] = bc_ref[...].astype(F32)
     conv_x = convolve(xbuf, px_ref[0:4, :], px_ref[4:5, :], place)
     conv_bc = convolve(bcbuf, pbc_ref[0:4, :], pbc_ref[4:5, :], place)
-    xbuf[0:8, :] = xbuf[STRETCH : STRETCH + 8, :]
-    bcbuf[0:8, :] = bcbuf[STRETCH : STRETCH + 8, :]
     x = conv_x * sigmoid(conv_x) * px_ref[7:8, :]
     act_bc = conv_bc * sigmoid(conv_bc)
     b_low = act_bc[:, :N].astype(BF)
@@ -382,49 +381,62 @@
     gp_ref[:, 2 * width + 2 * N : 2 * width + 2 * N + 128] = g_dt.astype(BF)
 
 
-def run_forward(projected, place, remain, px, pbc, pdt):
+def run_forward(carried, first, count, projected, place, remain, px, pbc, pdt):
     total = projected.shape[0]
     width = px.shape[1]
     heads = width // P_SIZE
-    blocks = total // STRETCH
-    row_spec = lambda w, c: pl.BlockSpec((STRETCH, w), lambda i: (i, c))
+    row_spec = lambda w, c: pl.BlockSpec((STRETCH, w), lambda i: (first + i, c))
+    prev_spec = lambda w, c: pl.BlockSpec(
+        (16, w), lambda i: (jnp.maximum((first + i) * (STRETCH // 16) - 1, 0), c)
+    )
     whole = lambda a: pl.BlockSpec(a.shape, lambda i: (0, 0))
-    return pl.pallas_call(
+    state = carried[0]
+    filled = tuple(carried[1:])
+    results = pl.pallas_call(
         partial(forward_kernel, heads),
-        grid=(blocks,),
+        grid=(count,),
         in_specs=[
             row_spec(width, 0),
             row_spec(width, 1),
             row_spec(2 * N, width // N),
             row_spec(128, (2 * width + 2 * N) // 128),
+            prev_spec(width, 1),
+            prev_spec(2 * N, width // N),
             row_spec(1, 0),
             row_spec(1, 0),
             whole(px),
             whole(pbc),
             whole(pdt),
-        ],
+            whole(state),
+        ]
+        + [pl.BlockSpec(memory_space=pl.ANY)] * len(filled),
         out_specs=[
             row_spec(width, 0),
             row_spec(width, 0),
             row_spec(1, 0),
-            pl.BlockSpec((1, width, N), lambda i: (i, 0, 0)),
+            pl.BlockSpec((1, width, N), lambda i: (first + i, 0, 0)),
+            whole(state),
         ],
         out_shape=[
             jax.ShapeDtypeStruct((total, width), BF),
             jax.ShapeDtypeStruct((total, width), F32),
             jax.ShapeDtypeStruct((total, 1), F32),
-            jax.ShapeDtypeStruct((blocks, width, N), F32),
+            jax.ShapeDtypeStruct((total // STRETCH, width, N), F32),
+            jax.ShapeDtypeStruct((width, N), F32),
         ],
         scratch_shapes=[
-            pltpu.VMEM((width, N), F32),
             pltpu.VMEM((STRETCH + 8, width), F32),
             pltpu.VMEM((STRETCH + 8, 2 * N), F32),
         ],
+        input_output_aliases={12: 0, 13: 1, 14: 2, 15: 3} if filled else {},
         cost_estimate=pl.CostEstimate(
-            flops=total * 256 * 1000, bytes_accessed=total * 5000, transcendentals=total * 1500
+            flops=count * STRETCH * 256 * 20000,
+            bytes_accessed=count * STRETCH * 5000,
+            transcendentals=count * STRETCH * 1500,
         ),
         name="scan_forward",
-    )(projected, projected, projected, projected, place, remain, px, pbc, pdt)
+    )(*((projected,) * 6 + (place, remain, px, pbc, pdt, state) + filled))
+    return (results[4],) + tuple(results[:4])
 
 
 def run_backward(carried, first, count, projected, rows_in, states, px, pbc, pdt):
@@ -498,7 +510,7 @@
         ],
         input_output_aliases={20: 0, 21: 1} if filled else {},
         cost_estimate=pl.CostEstimate(
-            flops=count * STRETCH * 256 * 3000,
+            flops=count * STRETCH * 256 * 40000,
             bytes_accessed=count * STRETCH * 8000,
             transcendentals=count * STRETCH * 2000,
         ),
@@ -509,6 +521,15 @@
 
 def after(value, *others):
     return lax.optimization_barrier((value, others))[0]
+
+
+def by_row(values):
+    return with_layout_constraint(values, Layout(major_to_minor=(0, 1)))
+
+
+def cuts(count, parts):
+    edges = [count * i // parts for i in range(parts + 1)]
+    return list(zip(edges[:-1], edges[1:]))
 
 
 def ring_chips():
@@ -543,94 +564,157 @@
     return jnp.where(spot < 4, spot * 2, (7 - spot) * 2 + 1)
 
 
-def gather_rows(values, pieces=2):
+class RingSum:
+    def __init__(self, chunk, rows):
+        self.chunk = chunk
+        self.mid = rows // 2
+        self.step = 4
+        self.last = self.sent = ()
+        self.ready = (chunk(4, ()),)
+
+    def settle(self, others):
+        self.last, self.ready, _ = lax.optimization_barrier((self.last, self.ready, others))
+
+    def advance(self, *others):
+        self.settle(others)
+        mid = self.mid
+        if self.step == 4:
+            up, down = self.ready[0][:mid], self.ready[0][mid:]
+        else:
+            up, down = (value.astype(F32) for value in self.last)
+            first, second = self.ready
+            if self.step == 3:
+                up = jnp.concatenate([first[:mid] + up, first[mid:]], axis=0)
+                down = jnp.concatenate([second[:mid], second[mid:] + down], axis=0)
+            else:
+                up, down = first + up, second + down
+        self.sent = lax.optimization_barrier((up.astype(BF), down.astype(BF)))
+        up, down = self.sent
+        self.last = (by_row(hop(by_row(up), 1)), by_row(hop(by_row(down), -1)))
+        self.step -= 1
+        self.ready = tuple(
+            self.chunk(steps, self.sent)
+            for steps in sorted({self.step, -self.step}, reverse=True)
+        )
+
+    def finish(self, others):
+        self.settle(others)
+        return self.ready[0] + self.last[0].astype(F32) + self.last[1].astype(F32)
+
+
+class Scatter:
+    def __init__(self, left, right, *gate):
+        self.ring = lax.axis_size("dp") == 16
+        self.last = self.sent = ()
+        if not self.ring:
+            full = jnp.dot(left, right, preferred_element_type=F32).astype(BF)
+            self.done = lax.psum_scatter(full, "dp", scatter_dimension=0, tiled=True).astype(F32)
+            return
+        self.core, spot = ring_place()
+        half = right.shape[1] // 2
+        take = lambda c: lax.dynamic_slice_in_dim(right, c * half, half, 1)
+        sides = ((left, take(self.core)), (swap(left), swap(take(1 - self.core))))
+        sides = lax.optimization_barrier((sides, gate))[0]
+        self.rows = rows = left.shape[0] // 8
+
+        def chunk(steps, deps):
+            start = ring_chip(spot + steps) * rows
+            return by_row(
+                sum(
+                    jnp.dot(
+                        lax.dynamic_slice_in_dim(after(side, deps), start, rows, 0),
+                        weight,
+                        preferred_element_type=F32,
+                    )
+                    for side, weight in sides
+                )
+            )
+
+        self.sum = RingSum(chunk, rows)
+
+    def advance(self, *others):
+        if self.ring:
+            self.sum.advance(*others)
+            self.last, self.sent = self.sum.last, self.sum.sent
+
+    def ready(self):
+        return self.sum.ready if self.ring else ()
+
+    def finish(self, *others):
+        if not self.ring:
+            return self.done
+        done = self.sum.finish(others)
+        own = self.rows // 2
+        kept = lax.dynamic_slice_in_dim(done, self.core * own, own, 0)
+        got = swap(lax.dynamic_slice_in_dim(done, (1 - self.core) * own, own, 0))
+        first = self.core == 0
+        return jnp.concatenate(
+            [jnp.where(first, kept, got), jnp.where(first, got, kept)], axis=1
+        )
+
+
+def other_width(values):
+    return lax.ppermute(values, "width", [(0, 1), (1, 0)])
+
+
+def in_order(mine, other):
+    first = lax.axis_index("width") == 0
+    return jnp.where(first, mine, other), jnp.where(first, other, mine)
+
+
+def same_core():
+    return [[2 * chip + core for chip in range(8)] for core in (0, 1)]
+
+
+def gather_blocks(block):
     if lax.axis_size("dp") != 16:
-        return lax.all_gather(values, "dp", axis=0, tiled=True)
-    rows = values.shape[0]
-    core, spot = ring_place()
-    chip = ring_chip(spot)
-    out = jnp.zeros((16 * rows,) + values.shape[1:], values.dtype)
-
-    def put(out, part, device, offset):
-        return lax.dynamic_update_slice_in_dim(out, part, device * rows + offset, 0)
-
-    out = put(out, values, 2 * chip + core, 0)
-    out = put(out, swap(values), 2 * chip + 1 - core, 0)
-    size = rows // pieces
-    ahead = [values[i * size : (i + 1) * size] for i in range(pieces)]
-    behind = list(ahead)
-    for step in range(1, 5):
-        for i in range(pieces):
-            for way, held in ((1, ahead), (-1, behind)):
-                part, offset = held[i], i * size
-                if step == 4:
-                    half = size // 2
-                    part = part[:half] if way == 1 else part[half:]
-                    offset = offset + (0 if way == 1 else half)
-                part = hop(part, way)
-                held[i] = part
-                source = ring_chip(spot - way * step)
-                out = put(out, part, 2 * source + core, offset)
-                out = put(out, swap(part), 2 * source + 1 - core, offset)
-    return out
-
-
-def scatter_product(left, right, first, second):
-    total = left.shape[0]
-    if lax.axis_size("dp") != 16:
-        full = jnp.dot(left, right, preferred_element_type=F32).astype(BF)
-        return lax.psum_scatter(full, "dp", scatter_dimension=0, tiled=True).astype(F32)
-    core, spot = ring_place()
-    half = right.shape[1] // 2
-    mine = after(lax.dynamic_slice_in_dim(right, core * half, half, 1), first)
-    theirs = swap(lax.dynamic_slice_in_dim(right, (1 - core) * half, half, 1))
-    product = jnp.dot(left, mine, preferred_element_type=F32) + jnp.dot(
-        swap(left), theirs, preferred_element_type=F32
-    )
-    rows = total // 8
-    product = product.reshape(8, rows, half)
-    done = ring_sum(
-        lambda steps: lax.dynamic_index_in_dim(product, ring_chip(spot + steps), 0, False),
-        rows,
-        second,
-    )
-    own = rows // 2
-    kept = lax.dynamic_slice_in_dim(done, core * own, own, 0)
-    got = swap(lax.dynamic_slice_in_dim(done, (1 - core) * own, own, 0))
-    first = core == 0
-    return jnp.concatenate(
-        [jnp.where(first, kept, got), jnp.where(first, got, kept)], axis=1
-    )
-
-
-def scatter_rows(values):
-    if lax.axis_size("dp") != 16:
-        return lax.psum_scatter(values, "dp", scatter_dimension=0, tiled=True).astype(F32)
-    core, spot = ring_place()
-    rows = values.shape[0] // 16
-    split = values.reshape(8, 2, rows, values.shape[1])
-    pick = lambda c: lax.dynamic_index_in_dim(split, c, 1, False)
-    both = pick(core).astype(F32) + swap(pick(1 - core)).astype(F32)
-    return ring_sum(
-        lambda steps: lax.dynamic_index_in_dim(both, ring_chip(spot + steps), 0, False), rows
-    )
-
-
-def ring_sum(part, rows, second=None):
-    mid = rows // 2
-    far = part(4).astype(BF)
-    up = hop(far[:mid], 1).astype(F32)
-    down = hop(far[mid:], -1).astype(F32)
-    near = part(3)
-    up = jnp.concatenate([near[:mid] + up, near[mid:]], axis=0)
-    near = part(-3)
-    down = jnp.concatenate([near[:mid], near[mid:] + down], axis=0)
-    if second is not None:
-        up, down, _ = lax.optimization_barrier((up, down, second))
-    for step in (2, 1):
-        up = part(step) + hop(up.astype(BF), 1).astype(F32)
-        down = part(-step) + hop(down.astype(BF), -1).astype(F32)
-    return part(0) + hop(up.astype(BF), 1).astype(F32) + hop(down.astype(BF), -1).astype(F32)
+        return lax.all_gather(block, "dp")
+    copies = jnp.broadcast_to(block[None], (8,) + block.shape)
+    mine = lax.all_to_all(copies, "dp", 0, 0, axis_index_groups=same_core())
+    theirs = swap(mine)
+    first = lax.axis_index("dp") % 2 == 0
+    pair = jnp.stack([jnp.where(first, mine, theirs), jnp.where(first, theirs, mine)], axis=1)
+    return pair.reshape((16,) + block.shape)
+
+
+def adamw_kernel(count, base_ref, weight_ref, moment_ref, second_ref, *refs):
+    new_ref, first_ref, squares_ref, low_ref = refs[-4:]
+    shape = weight_ref.shape
+    grad = sum(ref[...].astype(F32).reshape(shape) for ref in refs[:count])
+    base = base_ref[0, 0]
+    weight = weight_ref[...]
+    first = BETA_ONE * moment_ref[...] + (1.0 - BETA_ONE) * grad
+    squares = BETA_TWO * second_ref[...] + (1.0 - BETA_TWO) * grad * grad
+    new = weight - MATRIX_RATE * (
+        (first / base) / (jnp.sqrt(squares / base) + ADAM_EPS) + MATRIX_DECAY * weight
+    )
+    new_ref[...] = new
+    first_ref[...] = first
+    squares_ref[...] = squares
+    low_ref[...] = new.astype(BF)
+
+
+def adamw_rows(base, weight, moment, second, grads, first, size, count, grad_spec, filled):
+    columns = weight.shape[1]
+    spec = pl.BlockSpec((size, columns), lambda i: (first // size + i, 0))
+    used = 4 + len(grads)
+    return pl.pallas_call(
+        partial(adamw_kernel, len(grads)),
+        grid=(count,),
+        in_specs=[pl.BlockSpec(memory_space=pltpu.SMEM), spec, spec, spec]
+        + [grad_spec] * len(grads)
+        + [pl.BlockSpec(memory_space=pl.ANY)] * len(filled),
+        out_specs=[spec] * 4,
+        out_shape=[jax.ShapeDtypeStruct(weight.shape, F32)] * 3
+        + [jax.ShapeDtypeStruct(weight.shape, BF)],
+        input_output_aliases={used + i: i for i in range(len(filled))},
+        cost_estimate=pl.CostEstimate(
+            flops=count * columns * size * 10000,
+            bytes_accessed=count * columns * size * 30,
+            transcendentals=count * columns * size,
+        ),
+        name="adamw",
+    )(base, weight, moment, second, *grads, *filled)
 
 
 def tree_sum(values):
@@ -685,18 +769,14 @@
     root = lax.rsqrt(jnp.mean(inputs_f * inputs_f, axis=1, keepdims=True) + NORM_EPS)
     g_in, g_out, conv_w, conv_b, a_log, dt_bias, d_skip = unpack(small_params)
     normed_low = (inputs_f * root * g_in).astype(BF)
+    weight_low = weight_in.T.astype(BF)
     normed_all = lax.all_gather(normed_low, "dp", axis=0, tiled=True)
-
-    weight_low = weight_in.astype(BF)
     pairs = jnp.concatenate(
-        [
-            weight_low[:, :E].reshape(shard, dp, units),
-            weight_low[:, E : 2 * E].reshape(shard, dp, units),
-        ],
-        axis=2,
-    ).transpose(1, 0, 2)
-    own_cols = lax.all_to_all(pairs, "dp", 0, 0).reshape(D, 2 * units)
-    shared = gather_rows(weight_low[:, 2 * E :], 1)
+        [weight_low[:E].reshape(dp, units, shard), weight_low[E : 2 * E].reshape(dp, units, shard)],
+        axis=1,
+    )
+    own_cols = lax.all_to_all(pairs, "dp", 0, 0).transpose(1, 0, 2).reshape(2 * units, D).T
+    shared = gather_blocks(weight_low[2 * E :]).transpose(1, 0, 2).reshape(SHARED, D).T
     own_dt = lax.dynamic_slice_in_dim(shared, 2 * N + here * own_heads, own_heads, 1)
     weight_own = jnp.concatenate(
         [
@@ -707,7 +787,7 @@
         ],
         axis=1,
     )
-    out_weight_low = pad_to(weight_out.astype(BF), wide, 0)
+    out_weight_low = by_row(pad_to(weight_out.astype(BF), wide, 0))
 
     live_units = jnp.right_shift(jnp.int32(E), lax.axis_size("width") - 1 - levels[0])
     live = live_units.astype(F32)
@@ -736,14 +816,18 @@
         pad_to(jnp.stack([own_h(dt_bias), -jnp.exp(own_h(a_log))]), 128, 1), 8, 0
     )
 
+    cotangent_all = lax.all_gather(
+        after(cotangent, normed_all, weight_own), "dp", axis=0, tiled=True
+    )
     projected = jnp.dot(normed_all, weight_own, preferred_element_type=F32).astype(BF)
-    zin, mixed, square, states = run_forward(projected, place, remain, px, pbc, pdt)
-
+    carried = (jnp.zeros((wide, N), F32),)
+    for begin, end in cuts(total // STRETCH, FRONT_PARTS):
+        carried = run_forward(
+            carried, begin, end - begin, projected, place, remain, px, pbc, pdt
+        )
+    _, zin, mixed, square, states = carried
     partial_out = jnp.dot(zin, out_weight_low, preferred_element_type=F32).astype(BF)
     summed_out = lax.psum_scatter(partial_out, "dp", scatter_dimension=0, tiled=True)
-
-    later = after(cotangent, normed_all, weight_own)
-    cotangent_all = lax.all_gather(later, "dp", axis=0, tiled=True)
     g_out_low = lax.dot_general(
         cotangent_all, out_weight_low, (((1,), (1,)), ((), ())), preferred_element_type=F32
     )
@@ -751,12 +835,6 @@
     both = jnp.sum(lax.all_gather(jnp.stack([square[:, 0], pull_part]), "dp"), axis=0)
     scale = lax.rsqrt(both[0] / live + NORM_EPS)
     pull = scale * scale * scale / live * both[1]
-
-    block_out = (
-        inputs_f
-        + summed_out.astype(F32)
-        * lax.dynamic_slice_in_dim(scale, here * rows, rows, 0)[:, None]
-    ).astype(BF)
 
     rows_in = (place, remain, mixed, g_out_low, scale[:, None], pull[:, None])
     carried = (
@@ -765,43 +843,137 @@
         jnp.zeros((16, 2 * N), F32),
         jnp.zeros((8, 128), F32),
     )
-    span = total // STRETCH // SPLITS
-    for turn in reversed(range(SPLITS)):
+    for begin, end in reversed(cuts(total // STRETCH, BACK_PARTS)):
         carried = run_backward(
-            carried, turn * span, span, projected, rows_in, states, px, pbc, pdt
+            carried, begin, end - begin, projected, rows_in, states, px, pbc, pdt
         )
     _, gx, gbc, gdt, g_projected, out_low = carried
+    block_out = (
+        inputs_f
+        + summed_out.astype(F32)
+        * lax.dynamic_slice_in_dim(scale, here * rows, rows, 0)[:, None]
+    ).astype(BF)
 
     g_weight = lax.dot_general(
-        normed_all, g_projected, (((0,), (0,)), ((), ())), preferred_element_type=F32
+        g_projected, normed_all, (((0,), (0,)), ((), ())), preferred_element_type=F32
     ).astype(BF)
+    g_heads = g_weight[2 * wide + 2 * N : 2 * wide + 2 * N + own_heads]
+    g_shared = jnp.concatenate(
+        [
+            g_weight[2 * wide : 2 * wide + 2 * N],
+            lax.dynamic_update_slice_in_dim(
+                jnp.zeros((H, D), BF), g_heads, here * own_heads, 0
+            ),
+        ],
+        axis=0,
+    )
+    g_both = jnp.stack([g_weight[:units], g_weight[wide : wide + units]])
+    paired = lax.axis_size("width") == 2
+
+    def to_owners(values):
+        return lax.all_to_all(
+            values.reshape(-1, dp, shard).transpose(1, 0, 2), "dp", 0, 0
+        )
+
+    def half(slot):
+        return jnp.concatenate(
+            [
+                lax.dynamic_index_in_dim(g_both, slot, 0, False),
+                lax.dynamic_slice_in_dim(g_shared, slot * (SHARED // 2), SHARED // 2, 0),
+            ],
+            axis=0,
+        )
+
+    inward = Scatter(g_projected, weight_own.T, g_weight)
+    if paired:
+        slot = lax.axis_index("width")
+        g_kept = half(slot)
+        g_got = other_width(half(1 - slot))
+    inward.advance()
     g_weight_out = lax.dot_general(
-        out_low, cotangent_all, (((0,), (0,)), ((), ())), preferred_element_type=F32
+        after(out_low, inward.sent),
+        cotangent_all,
+        (((0,), (0,)), ((), ())),
+        preferred_element_type=F32,
     )[:units].astype(BF)
-    total_out = width_sum(g_weight_out)
-
-    g_pairs = lax.all_to_all(
-        jnp.concatenate(
-            [g_weight[:, :units], g_weight[:, wide : wide + units]], axis=1
-        ).reshape(dp, shard, 2 * units),
-        "dp",
-        0,
-        0,
-    )
-    g_normed = scatter_product(g_projected, weight_own.T, g_weight, g_pairs)
-    sum_pairs = width_sum(g_pairs).transpose(1, 0, 2)
-    totals = [
-        sum_pairs[:, :, :units].reshape(shard, E),
-        sum_pairs[:, :, units:].reshape(shard, E),
-    ]
-    g_shared = lax.dynamic_update_slice_in_dim(
-        pad_to(g_weight[:, 2 * wide : 2 * wide + 2 * N], SHARED, 1),
-        g_weight[:, 2 * wide + 2 * N : 2 * wide + 2 * N + own_heads],
-        2 * N + here * own_heads,
-        1,
-    )
-    totals.append(width_sum(scatter_rows(g_shared).astype(BF)))
-    total_in = jnp.concatenate(totals, axis=1)
+    inward.advance(g_weight_out)
+    if paired:
+        g_kept, g_got, _ = lax.optimization_barrier((g_kept, g_got, inward.sent))
+        g_half = to_owners((g_kept.astype(F32) + g_got.astype(F32)).astype(BF))
+        total_out = other_width(after(g_weight_out, inward.sent))
+        inward.advance()
+        inward.advance(total_out)
+        total_out = g_weight_out.astype(F32) + total_out.astype(F32)
+        g_half = after(g_half, inward.sent)
+        g_shared = jnp.sum(g_half[:, units:].astype(F32), axis=0).astype(BF)
+        g_half = g_half[:, :units]
+        g_peer = other_width(g_half)
+        g_apart = other_width(g_shared)
+    else:
+        inward.advance()
+        inward.advance()
+        total_out = width_sum(g_weight_out)
+        g_pairs = width_sum(to_owners(g_both.reshape(-1, D)))
+        g_gate, g_x = g_pairs[:, :units], g_pairs[:, units:]
+        g_apart = lax.psum_scatter(
+            g_shared.reshape(SHARED, dp, shard).transpose(1, 0, 2), "dp", scatter_dimension=0
+        )
+        g_apart = width_sum(g_apart)
+    simple = paired and units % 128 == 0 and shard == 128
+    step_float = step_count[0].astype(F32)
+    new_out, mom_out, sec_out = adamw_step(
+        weight_out,
+        moment_out,
+        second_out,
+        after(total_out, inward.sent),
+        MATRIX_RATE,
+        MATRIX_DECAY,
+        step_float,
+    )
+    if paired:
+        g_normed = inward.finish(new_out, g_peer, g_apart)
+        g_gate, g_x = in_order(g_half, g_peer)
+        g_pairs = jnp.concatenate([g_gate, g_x], axis=0)
+        g_apart = jnp.concatenate(in_order(g_shared, g_apart), axis=0)
+    else:
+        g_normed = inward.finish(new_out)
+    if simple:
+        base = (1.0 - jnp.power(BETA_ONE, step_float)).reshape(1, 1)
+        own = (weight_in.T, moment_in.T, second_in.T)
+        moved = adamw_rows(
+            base,
+            *own,
+            (g_pairs,),
+            0,
+            4 * units,
+            dp // 2,
+            pl.BlockSpec((4, units, shard), lambda i: (i, 0, 0)),
+            (),
+        )
+        results = adamw_rows(
+            base,
+            *own,
+            (g_apart,),
+            2 * E,
+            H,
+            SHARED // H,
+            pl.BlockSpec((H, shard), lambda i: (i, 0)),
+            tuple(moved),
+        )
+        new_in, mom_in, sec_in, low_in = (result.T for result in results)
+    else:
+        total_in = jnp.concatenate(
+            [
+                g_gate.transpose(2, 0, 1).reshape(shard, E),
+                g_x.transpose(2, 0, 1).reshape(shard, E),
+                g_apart.T,
+            ],
+            axis=1,
+        ).astype(F32)
+        new_in, mom_in, sec_in = adamw_step(
+            weight_in, moment_in, second_in, total_in, MATRIX_RATE, MATRIX_DECAY, step_float
+        )
+        low_in = new_in.astype(BF)
 
     ratio = root * g_in
     lean = jnp.sum(g_in * g_normed * inputs_f, axis=1, keepdims=True)
@@ -825,17 +997,10 @@
             placed(jnp.sum(gx[5, :units].reshape(own_heads, P_SIZE), axis=1), H),
         ]
     )
-    total_small = jnp.concatenate([tree_sum(g_g_in), tree_sum(early)])
-    step_float = step_count[0].astype(F32)
+    total_small = tree_sum(jnp.concatenate([g_g_in, early]))
     rate_table, decay_table = small_table()
     new_small, mom_small, sec_small = adamw_step(
         small_params, moment_small, second_small, total_small, rate_table, decay_table, step_float
-    )
-    new_in, mom_in, sec_in = adamw_step(
-        weight_in, moment_in, second_in, total_in, MATRIX_RATE, MATRIX_DECAY, step_float
-    )
-    new_out, mom_out, sec_out = adamw_step(
-        weight_out, moment_out, second_out, total_out, MATRIX_RATE, MATRIX_DECAY, step_float
     )
     return (
         block_out,
@@ -843,7 +1008,7 @@
         new_in,
         mom_in,
         sec_in,
-        new_in.astype(BF),
+        low_in,
         new_out,
         mom_out,
         sec_out,

time: 768 us -> 688 us (0.90)
  waiting for transfers between devices: 289 us -> 241 us
  starting transfers between devices: 81.3 us -> 47.5 us
  local copies, waits for them, and re-layouts: 55.3 us -> 36.8 us
  Pallas kernels: 125 us -> 143 us
  matrix products: 107 us -> 116 us
    ppermute x24 -> x8, waiting for transfers between devices: 145 us -> 49.5 us  [hop(): return lax.ppermute(values, 'dp', pairs)]
    all_to_all x2 -> x3, waiting for transfers between devices: 0.01 us -> 73.1 us  [the longest x1 43.7 us: per_device(): lax.all_to_all(pairs, 'dp', 0, 0).transpose(1, 0, 2).reshape(2 * units, D)]
    ppermute x24 -> x8, starting transfers between devices: 55.9 us -> 17.4 us  [hop(): return lax.ppermute(values, 'dp', pairs)]
    all_gather x1, waiting for transfers between devices: 33.5 us -> 71.4 us  [per_device(): normed_all = lax.all_gather(normed_low, 'dp', axis=0, tiled=True)]
    ppermute x3 -> x4, waiting for transfers between devices: 26.9 us -> 0.75 us  [other_width(): return lax.ppermute(values, 'width', [(0, 1), (1, 0)])]
    ppermute x8 -> x4, waiting for transfers between devices: 28.6 us -> 9.14 us  [tree_sum(): lax.ppermute(values, 'dp', [(i, i ^ bit) for i in range(16)])]
    pallas_call x1 -> x3, Pallas kernels: 43.8 us -> 61.4 us  [the longest x1 44.5 us: run_forward(): pl.pallas_call(partial(forward_kernel, heads), grid=(count,), in_specs=[r...]
    convert_element_type x8 -> x5, other arithmetic: 24.2 us -> 8.32 us  [the longest x4 5.91 us: advance(): self.sent = lax.optimization_barrier((up.astype(BF), down.astype(BF)))]
  transfers between devices with their start and end apart: 55 -> 27, of which waited for: 21 -> 16; matrix products, arithmetic and copies ran while one was open for 29% -> 30% of each run, Pallas kernels for 16% -> 21%
where the time goes in v3:
time: 688 us; the launch traced here: 683 us
  waiting for transfers between devices  241 us (35%)
  Pallas kernels  143 us (21%)
  matrix products  116 us (17%)
  other arithmetic  63.9 us (9%)
  starting transfers between devices  47.5 us (7%)
  local copies, waits for them, and re-layouts  36.8 us (5%)
  blocking collectives  19.5 us (3%)
  between operations  16.3 us (2%)
    pallas_call x1, Pallas kernels, run_backward(): pl.pallas_call(partial(backward_kernel, heads), grid=(count,), in_specs=[...  81.1 us
    all_gather x1, waiting for transfers between devices, per_device(): normed_all = lax.all_gather(normed_low, 'dp', axis=0, tiled=True)  71.4 us
    ppermute x8, waiting for transfers between devices, hop(): return lax.ppermute(values, 'dp', pairs)  49.5 us
    dot_general x16, matrix products, chunk(): jnp.dot(lax.dynamic_slice_in_dim(after(side, deps), start, rows, 0), weig...  47.2 us
    pallas_call x1, Pallas kernels, run_forward(): pl.pallas_call(partial(forward_kernel, heads), grid=(count,), in_specs=[r...  44.5 us
    all_to_all x1, waiting for transfers between devices, per_device(): lax.all_to_all(pairs, 'dp', 0, 0).transpose(1, 0, 2).reshape(2 * units, D)  43.7 us
    all_gather x1, waiting for transfers between devices, per_device(): lax.all_gather(after(cotangent, normed_all, weight_own), 'dp', axis=0, ti...  35.5 us
    all_to_all x1, waiting for transfers between devices, gather_blocks(): mine = lax.all_to_all(copies, 'dp', 0, 0, axis_index_groups=same_core())  29.4 us
  transfers between devices with their start and end apart: 27, of which 16 were waited for; matrix products, arithmetic and copies ran while one was open for 30% of the time, Pallas kernels for 21%

profile of v3, /device:TPU:0, one launch (start us, length us, event | category | flops | bytes accessed | tf_op | source)
XLA Modules:
  0.0 683.5 jit_solution(6915002481718950586)
XLA Ops:
  10.6 2.5 fusion.5
  16.5 7.3 %all-to-all-start.1 = ((bf16[8,320,128]{2,1,0:T(8,128)(2,1)}), bf16[8,320,128]{2,1,0:T(8,128)(2,1)}, u32[]{:S(2)}, u32[]{:S(2)}) async-start(bf16[8,320,128]{2,1,0:T(8,128)(2,1)} %broadcast_in_dim.38), calls=%async_computation.1 | async-start | bytes 1310720 | tf_op jit(solution)/shard_map/all_to_all | solution.py:673
  28.4 29.4 %all-to-all-done.1 = bf16[8,320,128]{2,1,0:T(8,128)(2,1)} async-done(((bf16[8,320,128]{2,1,0:T(8,128)(2,1)}), bf16[8,320,128]{2,1,0:T(8,128)(2,1)}, u32[]{:S(2)}, u32[]{:S(2)}) %all-to-all-start.1) | async-done | bytes 655392 | tf_op jit(solution)/shard_map/all_to_all | solution.py:673
  57.8 5.5 all-to-all-start
  72.1 43.7 %all-to-all-done = bf16[16,512,128]{1,2,0:T(8,128)(2,1)S(1)} async-done(((bf16[16,512,128]{1,2,0:T(8,128)(2,1)}), bf16[16,512,128]{1,2,0:T(8,128)(2,1)S(1)}, u32[]{:S(2)}, u32[]{:S(2)}) %all-to-all-start) | async-done | bytes 2097184 | tf_op jit(solution)/shard_map/all_to_all | solution.py:778
  115.8 3.0 fusion.1
  118.8 71.4 %all-gather.5.cloned.1.call-done = bf16[4096,2048]{1,0:T(8,128)(2,1)} async-done(((bf16[256,2048]{1,0:T(8,128)(2,1)}), bf16[4096,2048]{1,0:T(8,128)(2,1)}) %all-gather.5.cloned.1.call-update) | async-done | bytes 16777232 | tf_op jit(solution)/shard_map/all_gather | solution.py:773
  197.8 5.1 iota_subtract_fusion
  202.9 22.1 %convolution_convert_fusion.1.gate_ref.x_ref.bc_ref.dt_ref.xprev_ref.bcprev_ref = bf16[4096,896]{1,0:T(8,128)(2,1)} fusion(bf16[4096,2048]{1,0:T(8,128)(2,1)} %all-gather.5.cloned.1.call-done, bf16[2048,4]{1,0:T(8,128)(2,1)S(1)} %copy-done.9, bf16[2048,256]{1,0:T(8,128)(2,1)S(1)} %slice.149, bf16[2048,512]{1,0:T(8,128)(2,1)S(1)} %bitcast.102), kind=kOutput, calls=%fused_computation.3 | convolution fusion | flops 15050735616 | bytes 27279360 | tf_op jit(solution)/shard_map/dot_general | solution.py:822
  225.6 44.5 %scan_forward.1 = (bf16[4096,256]{1,0:T(8,128)(2,1)}, f32[4096,256]{1,0:T(8,128)}, f32[4096,1]{1,0:T(8,128)}, f32[16,256,128]{2,1,0:T(8,128)}, f32[256,128]{1,0:T(8,128)}) custom-call(bf16[4096,896]{1,0:T(8,128)(2,1)} %convolution_convert_fusion.1.gate_ref.x_ref.bc_ref.dt_ref.xprev_ref.bcprev_ref, ...), custom_call_target="tpu_custom_call" | custom-call | flops 20971520000 | bytes 20480000 | tf_op jit(solution)/shard_map/scan_forward/pallas_call | solution.py:395
  272.5 10.1 %convolution_convert_fusion = bf16[4096,2048]{1,0:T(8,128)(2,1)} fusion(bf16[4096,256]{1,0:T(8,128)(2,1)} %get-tuple-element.72, f32[256,2048]{1,0:T(8,128)S(1)} %copy-done.5), kind=kOutput, calls=%fused_computation | convolution fusion | flops 4303880192 | bytes 20971520 | tf_op jit(solution)/shard_map/dot_general | solution.py:829
  282.6 35.5 %all-gather.7.cloned.1.call-done = bf16[4096,2048]{1,0:T(8,128)(2,1)} async-done(((bf16[256,2048]{1,0:T(8,128)(2,1)}), bf16[4096,2048]{1,0:T(8,128)(2,1)}) %all-gather.7.cloned.1.call-update) | async-done | bytes 16777232 | tf_op jit(solution)/shard_map/all_gather | solution.py:819
  318.2 13.6 %multiply_reduce_fusion = (f32[4096]{0:T(1024)S(1)}, f32[4096,256]{1,0:T(8,128)}) fusion(bf16[4096,256]{1,0:T(8,128)(2,1)} %get-tuple-element.72, bf16[4096,2048]{1,0:T(8,128)(2,1)} %all-gather.7.cloned.1.call-done, f32[256,2048]{1,0:T(8,128)S(1)} %copy-done.5), kind=kOutput, calls=%fused_computation.10 | convolution fusion | flops 4298633216 | bytes 25182208 | tf_op jit(solution)/shard_map/dot_general | solution.py:831
  331.8 19.5 %all-gather.1 = f32[16,2,4096]{2,1,0:T(2,128)S(1)} all-gather(f32[1,2,4096]{2,1,0:T(2,128)S(1)} %maximum_bitcast_fusion), channel_id=2, replica_groups=mesh['width'=2,'dp'=16] {'dp'}, dimensions={0}, use_global_device_ids=true | all-gather | bytes 557056 | tf_op jit(solution)/shard_map/all_gather | solution.py:835
  356.2 4.6 divide_multiply_fusion.pull_ref
  362.0 81.1 %scan_backward.1 = (bf16[4096,896]{1,0:T(8,128)(2,1)}, bf16[4096,256]{1,0:T(8,128)(2,1)}, f32[256,128]{1,0:T(8,128)}, f32[16,256]{1,0:T(8,128)}, f32[16,256]{1,0:T(8,128)}, /*index=5*/f32[8,128]{1,0:T(8,128)}) custom-call(bf16[4096,896]{1,0:T(8,128)(2,1)} %convolution_convert_fusion.1.gate_ref.x_ref.bc_ref.dt_ref.xprev_ref.bcprev_ref, ...), custom_call_target="tpu_custom_call" | custom-call | flops 41943040000 | bytes 32768000 | tf_op jit(solution)/shard_map/scan_backward/pallas_call | solution.py:463
  444.2 3.7 dynamic-slice_bitcast_fusion
  449.3 18.2 %convolution_convert_fusion.2 = bf16[896,2048]{1,0:T(8,128)(2,1)S(1)} fusion(bf16[4096,896]{1,0:T(8,128)(2,1)S(1)} %copy-done.29, bf16[4096,2048]{1,0:T(8,128)(2,1)} %all-gather.5.cloned.1.call-done), kind=kOutput, calls=%fused_computation.12 | convolution fusion | flops 15034220544 | bytes 27787264 | tf_op jit(solution)/shard_map/dot_general | solution.py:857
  474.9 3.2 fusion.39
  478.2 2.6 convolution_add_fusion.7
  483.1 4.5 fusion.33
  487.7 4.5 convolution_convert_fusion.3
  492.2 3.2 convolution_add_fusion.5
  495.4 3.1 fusion.36
  501.0 3.4 collective-permute-done.3
  504.4 3.5 collective-permute-done.4
  512.4 3.1 bitcast_bitcast_fusion
  515.5 4.7 all-to-all-start.2
  521.7 3.1 fusion.27
  524.8 3.2 fusion.30
  530.5 2.5 convolution_add_fusion.4
  533.0 4.8 collective-permute-done.5
  537.8 6.1 collective-permute-done.6
  547.1 3.1 collective-permute-start.7
  550.4 3.1 fusion.21
  553.5 2.5 convolution_add_fusion.1
  556.0 3.1 fusion.24
  563.2 21.6 %collective-permute-done.7 = bf16[512,1024]{1,0:T(8,128)(2,1)S(1)} collective-permute-done((bf16[512,1024]{1,0:T(8,128)(2,1)S(1)}, bf16[512,1024]{1,0:T(8,128)(2,1)S(1)}, u32[]{:S(2)}, u32[]{:S(2)}) %collective-permute-start.7) | collective-permute-done | bytes 1048608 | tf_op jit(solution)/shard_map/ppermute | solution.py:547
  589.6 9.8 %collective-permute-start.10 = (bf16[512,1024]{1,0:T(8,128)(2,1)}, bf16[512,1024]{1,0:T(8,128)(2,1)S(1)}, u32[]{:S(2)}, u32[]{:S(2)}) collective-permute-start(bf16[512,1024]{1,0:T(8,128)(2,1)} %add_convert_fusion.2), channel_id=1, source_target_pairs={{0,4},{1,5},{4,8},{5,9},{8,12},{9,13},{12,14},{13,15},{14,10},{15,... | collective-permute-start | bytes 3145736 | tf_op jit(solution)/shard_map/ppermute | solution.py:547
  601.0 7.2 %fusion.70 = (bf16[256,2048]{1,0:T(8,128)(2,1)}, f32[256,2048]{1,0:T(8,128)}, f32[256,2048]{1,0:T(8,128)}, f32[256,2048]{1,0:T(8,128)}) fusion(f32[256,2048]{1,0:T(8,128)S(1)} %copy-done.6, f32[]{:T(128)} %bitcast.30, f32[256,2048]{1,0:T(8,128)} %convert_add_fusion.2, f32[256,2048]{1,0:T(8,128)} %param.24, f32[256,2048]{1,0:T(8,128)} %param.23), kind=kLoop, calls=%fused_computation.166 | loop fusion | flops 7864320 | bytes 15728644 | tf_op jit(solution)/shard_map/convert_element_type | solution.py:1015
  608.2 3.2 fusion.18
  615.4 6.0 collective-permute-done.10
  624.3 3.5 convert_add_fusion.1
  642.0 2.6 collective-permute-done.17
  646.4 13.5 %adamw.2 = (f32[8512,128]{1,0:T(8,128)}, f32[8512,128]{1,0:T(8,128)}, f32[8512,128]{1,0:T(8,128)}, bf16[8512,128]{1,0:T(8,128)(2,1)}) custom-call(f32[1,1]{1,0:T(1,128)} %bitcast.36.base_ref, f32[8512,128]{1,0:T(8,128)} %bitcast.99, f32[8512,128]{1,0:T(8,128)} %bitcast.106, f32[8512,128]{1,0:T(8,128)} %bitcast.108, ...), custom_call_target="tpu_custom_call" | custom-call | flops 10485760000 | bytes 31457280 | tf_op jit(solution)/shard_map/adamw/pallas_call | solution.py:701
  660.0 3.4 adamw.3
  663.9 6.6 collective-permute-done.19
  672.0 3.9 fusion.10
  (220 shorter events, 98.3 us)
Async XLA Ops:
  7.2 183.0 %all-gather.5.cloned.1.call-start = ((), (), s32[]{:S(2)}) async-start(), calls=%async_computation.4 | async-start | bytes 17825792 | tf_op jit(solution)/shard_map/all_gather | solution.py:773
  16.5 41.3 %all-to-all-start.1 = ((bf16[8,320,128]{2,1,0:T(8,128)(2,1)}), bf16[8,320,128]{2,1,0:T(8,128)(2,1)}, u32[]{:S(2)}, u32[]{:S(2)}) async-start(bf16[8,320,128]{2,1,0:T(8,128)(2,1)} %broadcast_in_dim.38), calls=%async_computation.1 | async-start | bytes 1310720 | tf_op jit(solution)/shard_map/all_to_all | solution.py:673
  57.8 58.0 %all-to-all-start = ((bf16[16,512,128]{1,2,0:T(8,128)(2,1)}), bf16[16,512,128]{1,2,0:T(8,128)(2,1)S(1)}, u32[]{:S(2)}, u32[]{:S(2)}) async-start(bf16[16,512,128]{1,2,0:T(8,128)(2,1)} %pad_maximum_fusion), calls=%async_computation | async-start | bytes 4194304 | tf_op jit(solution)/shard_map/all_to_all | solution.py:778
  63.3 254.8 %all-gather.7.cloned.1.call-start = ((), (), s32[]{:S(2)}) async-start(), calls=%async_computation.6 | async-start | bytes 17825792 | tf_op jit(solution)/shard_map/all_gather | solution.py:819
  63.4 2.4 collective-permute-start
  115.8 74.6 %slice-start.4 = ((f32[28096]{0:T(1024)}), f32[17408]{0:T(1024)S(1)}, s32[]{:S(2)}) async-start(f32[28096]{0:T(1024)} %param.25), calls=%async_computation.11 | async-start | bytes 139264 | tf_op jit(solution)/shard_map/slice | solution.py:59
  115.8 74.6 %copy-start.14 = (f32[28096]{0:T(1024)S(1)}, f32[28096]{0:T(1024)}, u32[]{:S(2)}) copy-start(f32[28096]{0:T(1024)} %param.25) | copy-start | bytes 337156
  115.8 75.8 %copy-start.30 = (s32[1,8]{1,0:T(1,128)S(1)}, s32[1,8]{1,0:T(1,128)}, u32[]{:S(2)}) copy-start(s32[1,8]{1,0:T(1,128)} %param.16) | copy-start | bytes 100
  190.2 481.8 %reduce-scatter.2.cloned.1.call-start = ((), (), s32[]{:S(2)}) async-start(), calls=%async_computation.5 | async-start | bytes 17825792 | tf_op jit(solution)/shard_map/reduce_scatter | solution.py:830
  192.0 5.3 slice-start.5
  197.8 5.1 copy-start.9
  354.2 6.6 copy-start.7
  443.1 31.8 %collective-permute-start.1 = (bf16[4096,896]{1,0:T(8,128)(2,1)}, bf16[4096,896]{1,0:T(8,128)(2,1)}, u32[]{:S(2)}, u32[]{:S(2)}) collective-permute-start(bf16[4096,896]{1,0:T(8,128)(2,1)} %get-tuple-element.111), channel_id=1, source_target_pairs={{0,1},{1,0},{2,3},{3,2},{4,5},{5,4},{6,7},{7,6},{8,9},{9,8},{10,11... | collective-permute-start | bytes 22020104 | tf_op jit(solution)/shard_map/ppermute | solution.py:551
  444.2 5.1 copy-start.29
  448.0 50.5 %copy-start.10 = (bf16[896,1024]{0,1:T(8,128)(2,1)}, bf16[896,1024]{0,1:T(8,128)(2,1)S(1)}, u32[]{:S(2)}) copy-start(bf16[896,1024]{0,1:T(8,128)(2,1)S(1)} %get-tuple-element.79) | copy-start | bytes 5505028
  448.0 27.0 %collective-permute-start.2 = (bf16[896,1024]{0,1:T(8,128)(2,1)}, bf16[896,1024]{0,1:T(8,128)(2,1)}, u32[]{:S(2)}, u32[]{:S(2)}) collective-permute-start(bf16[896,1024]{0,1:T(8,128)(2,1)} %get-tuple-element.147), channel_id=1, source_target_pairs={{0,1},{1,0},{2,3},{3,2},{4,5},{5,4},{6,7},{7,6},{8,9},{9,8},{10,11... | collective-permute-start | bytes 5505032 | tf_op jit(solution)/shard_map/ppermute | solution.py:551
  471.0 41.4 %collective-permute-start.12 = (bf16[416,2048]{1,0:T(8,128)(2,1)}, bf16[416,2048]{1,0:T(8,128)(2,1)}, u32[]{:S(2)}, u32[]{:S(2)}) collective-permute-start(bf16[416,2048]{1,0:T(8,128)(2,1)} %pad_maximum_fusion.4), channel_id=1, source_target_pairs={{0,16},{16,0},{1,17},{17,1},{2,18},{18,2},{3,19},{19,3},{4,20},{20... | collective-permute-start | bytes 5111816 | tf_op jit(solution)/shard_map/ppermute | solution.py:657
  474.8 12.8 %slice-start = ((s8[16777216]{0:T(1024)(128)(4,1)}), s8[4194304]{0:T(1024)(128)(4,1)S(1)}, s32[]{:S(2)}) async-start(s8[16777216]{0:T(1024)(128)(4,1)} %bitcast.97), calls=%async_computation.7 | async-start | bytes 8388608
  474.9 12.7 %slice-start.1 = ((s8[16777216]{0:T(1024)(128)(4,1)}), s8[4194304]{0:T(1024)(128)(4,1)S(1)}, s32[]{:S(2)}) async-start(s8[16777216]{0:T(1024)(128)(4,1)} %bitcast.97), calls=%async_computation.8 | async-start | bytes 8388608
  478.2 9.5 %slice-start.2 = ((s8[16777216]{0:T(1024)(128)(4,1)}), s8[4194304]{0:T(1024)(128)(4,1)S(1)}, s32[]{:S(2)}) async-start(s8[16777216]{0:T(1024)(128)(4,1)} %bitcast.97), calls=%async_computation.9 | async-start | bytes 8388608
  480.9 23.5 %collective-permute-start.3 = (bf16[256,1024]{1,0:T(8,128)(2,1)S(1)}, bf16[256,1024]{1,0:T(8,128)(2,1)S(1)}, u32[]{:S(2)}, u32[]{:S(2)}) collective-permute-start(bf16[256,1024]{1,0:T(8,128)(2,1)S(1)} %get-tuple-element.82), channel_id=1, source_target_pairs={{0,4},{1,5},{4,8},{5,9},{8,12},{9,13},{12,14},{13,15},{14,10},{15,... | collective-permute-start | bytes 1572872 | tf_op jit(solution)/shard_map/ppermute | solution.py:547
  481.0 26.9 %collective-permute-start.4 = (bf16[256,1024]{1,0:T(8,128)(2,1)S(1)}, bf16[256,1024]{1,0:T(8,128)(2,1)S(1)}, u32[]{:S(2)}, u32[]{:S(2)}) collective-permute-start(bf16[256,1024]{1,0:T(8,128)(2,1)S(1)} %get-tuple-element.83), channel_id=1, source_target_pairs={{0,2},{1,3},{4,0},{5,1},{8,4},{9,5},{12,8},{13,9},{14,12},{15,13},... | collective-permute-start | bytes 1572872 | tf_op jit(solution)/shard_map/ppermute | solution.py:547
  483.1 4.5 slice-start.3
  483.1 4.5 copy-start.8
  510.4 27.4 %collective-permute-start.5 = (bf16[512,1024]{1,0:T(8,128)(2,1)}, bf16[512,1024]{1,0:T(8,128)(2,1)}, u32[]{:S(2)}, u32[]{:S(2)}) collective-permute-start(bf16[512,1024]{1,0:T(8,128)(2,1)} %pad_maximum_fusion.6), channel_id=1, source_target_pairs={{0,4},{1,5},{4,8},{5,9},{8,12},{9,13},{12,14},{13,15},{14,10},{15,... | collective-permute-start | bytes 3145736 | tf_op jit(solution)/shard_map/ppermute | solution.py:547
  512.0 31.9 %collective-permute-start.6 = (bf16[512,1024]{1,0:T(8,128)(2,1)}, bf16[512,1024]{1,0:T(8,128)(2,1)}, u32[]{:S(2)}, u32[]{:S(2)}) collective-permute-start(bf16[512,1024]{1,0:T(8,128)(2,1)} %pad_maximum_fusion.7), channel_id=1, source_target_pairs={{0,2},{1,3},{4,0},{5,1},{8,4},{9,5},{12,8},{13,9},{14,12},{15,13},... | collective-permute-start | bytes 3145736 | tf_op jit(solution)/shard_map/ppermute | solution.py:547
  515.5 83.9 %all-to-all-start.2 = ((bf16[16,416,128]{2,1,0:T(8,128)(2,1)}), bf16[16,416,128]{2,1,0:T(8,128)(2,1)S(1)}, u32[]{:S(2)}, u32[]{:S(2)}) async-start(bf16[16,416,128]{2,1,0:T(8,128)(2,1)} %bitcast_bitcast_fusion), calls=%async_computation.3 | async-start | bytes 3407872 | tf_op jit(solution)/shard_map/all_to_all | solution.py:874
  520.2 41.4 %collective-permute-start.9 = (bf16[256,2048]{1,0:T(8,128)(2,1)S(1)}, bf16[256,2048]{1,0:T(8,128)(2,1)S(1)}, u32[]{:S(2)}, u32[]{:S(2)}) collective-permute-start(bf16[256,2048]{1,0:T(8,128)(2,1)S(1)} %convolution_convert_fusion.3), channel_id=1, source_target_pairs={{0,16},{16,0},{1,17},{17,1},{2,18},{18,2},{3,19},{19,3},{4,20},{20... | collective-permute-start | bytes 3145736 | tf_op jit(solution)/shard_map/ppermute | solution.py:657
  547.1 37.8 %collective-permute-start.7 = (bf16[512,1024]{1,0:T(8,128)(2,1)S(1)}, bf16[512,1024]{1,0:T(8,128)(2,1)S(1)}, u32[]{:S(2)}, u32[]{:S(2)}) collective-permute-start(bf16[512,1024]{1,0:T(8,128)(2,1)S(1)} %add_convert_fusion.4), channel_id=1, source_target_pairs={{0,4},{1,5},{4,8},{5,9},{8,12},{9,13},{12,14},{13,15},{14,10},{15,... | collective-permute-start | bytes 3145736 | tf_op jit(solution)/shard_map/ppermute | solution.py:547
  550.2 36.7 %collective-permute-start.8 = (bf16[512,1024]{1,0:T(8,128)(2,1)S(1)}, bf16[512,1024]{1,0:T(8,128)(2,1)S(1)}, u32[]{:S(2)}, u32[]{:S(2)}) collective-permute-start(bf16[512,1024]{1,0:T(8,128)(2,1)S(1)} %add_convert_fusion.3), channel_id=1, source_target_pairs={{0,2},{1,3},{4,0},{5,1},{8,4},{9,5},{12,8},{13,9},{14,12},{15,13},... | collective-permute-start | bytes 3145736 | tf_op jit(solution)/shard_map/ppermute | solution.py:547
  589.6 31.8 %collective-permute-start.10 = (bf16[512,1024]{1,0:T(8,128)(2,1)}, bf16[512,1024]{1,0:T(8,128)(2,1)S(1)}, u32[]{:S(2)}, u32[]{:S(2)}) collective-permute-start(bf16[512,1024]{1,0:T(8,128)(2,1)} %add_convert_fusion.2), channel_id=1, source_target_pairs={{0,4},{1,5},{4,8},{5,9},{8,12},{9,13},{12,14},{13,15},{14,10},{15,... | collective-permute-start | bytes 3145736 | tf_op jit(solution)/shard_map/ppermute | solution.py:547
  599.4 24.2 %collective-permute-start.11 = (bf16[512,1024]{1,0:T(8,128)(2,1)}, bf16[512,1024]{1,0:T(8,128)(2,1)}, u32[]{:S(2)}, u32[]{:S(2)}) collective-permute-start(bf16[512,1024]{1,0:T(8,128)(2,1)} %add_convert_fusion.1), channel_id=1, source_target_pairs={{0,2},{1,3},{4,0},{5,1},{8,4},{9,5},{12,8},{13,9},{14,12},{15,13},... | collective-permute-start | bytes 3145736 | tf_op jit(solution)/shard_map/ppermute | solution.py:547
  599.5 24.8 %collective-permute-start.13 = (bf16[16,256,128]{2,1,0:T(8,128)(2,1)S(1)}, bf16[16,256,128]{2,1,0:T(8,128)(2,1)S(1)}, u32[]{:S(2)}, u32[]{:S(2)}) collective-permute-start(bf16[16,256,128]{2,1,0:T(8,128)(2,1)S(1)} %slice.138), channel_id=1, source_target_pairs={{0,16},{16,0},{1,17},{17,1},{2,18},{18,2},{3,19},{19,3},{4,20},{20... | collective-permute-start | bytes 3145736 | tf_op jit(solution)/shard_map/ppermute | solution.py:657
  608.2 4.7 copy-start.12
  611.5 12.8 %collective-permute-start.14 = (bf16[160,128]{1,0:T(8,128)(2,1)S(1)}, bf16[160,128]{1,0:T(8,128)(2,1)S(1)}, u32[]{:S(2)}, u32[]{:S(2)}) collective-permute-start(bf16[160,128]{1,0:T(8,128)(2,1)S(1)} %slice_reduce_fusion), channel_id=1, source_target_pairs={{0,16},{16,0},{1,17},{17,1},{2,18},{18,2},{3,19},{19,3},{4,20},{20... | collective-permute-start | bytes 122888 | tf_op jit(solution)/shard_map/ppermute | solution.py:657
  630.1 3.9 collective-permute-start.15
  637.5 1.9 collective-permute-start.16
  639.5 5.1 collective-permute-start.17
  644.6 18.8 %collective-permute-start.18 = (f32[28096]{0:T(1024)S(1)}, f32[28096]{0:T(1024)S(1)}, u32[]{:S(2)}, u32[]{:S(2)}) collective-permute-start(f32[28096]{0:T(1024)S(1)} %add.409), channel_id=1, source_target_pairs={{0,4},{1,5},{2,6},{3,7},{4,0},{5,1},{6,2},{7,3},{8,12},{9,13},{10,... | collective-permute-start | bytes 337160 | tf_op jit(solution)/shard_map/ppermute | solution.py:724
  659.9 4.0 copy-start.26
  659.9 12.0 %copy-start.2 = (f32[256,1024]{1,0:T(8,128)S(1)}, f32[256,1024]{1,0:T(8,128)}, u32[]{:S(2)}) copy-start(f32[256,1024]{1,0:T(8,128)} %copy-done.1) | copy-start | bytes 3145732
  659.9 12.0 %copy-start.4 = (f32[256,1024]{1,0:T(8,128)S(1)}, f32[256,1024]{1,0:T(8,128)}, u32[]{:S(2)}) copy-start(f32[256,1024]{1,0:T(8,128)} %copy-done.3) | copy-start | bytes 3145732
  663.4 7.1 %collective-permute-start.19 = (f32[28096]{0:T(1024)S(1)}, f32[28096]{0:T(1024)S(1)}, u32[]{:S(2)}, u32[]{:S(2)}) collective-permute-start(f32[28096]{0:T(1024)S(1)} %add.410), channel_id=1, source_target_pairs={{0,8},{1,9},{2,10},{3,11},{4,12},{5,13},{6,14},{7,15},{8,0},{9,1},... | collective-permute-start | bytes 337160 | tf_op jit(solution)/shard_map/ppermute | solution.py:724
  670.5 5.3 collective-permute-start.20
  671.9 3.9 copy-start.15
  671.9 3.9 copy-start.19
  671.9 3.9 copy-start.20
  672.0 3.9 copy-start.21
  (16 other events, 34.9 us)
Sparse Core Ops, SparseCore 0:
  13.3 176.8 all-gather.4
  192.3 125.8 all-gather.6
  322.3 185.1 reduce-scatter.1

commit v4 on v3

--- a/solution.py
+++ b/solution.py
@@ -97,23 +97,32 @@
     )
 
 
-def spread(columns, heads):
-    return jnp.concatenate(
-        [
-            jnp.broadcast_to(columns[:, h : h + 1], (columns.shape[0], P_SIZE))
-            for h in range(heads)
-        ],
-        axis=1,
-    )
-
-
-def head_sums(values, heads):
-    lane = lax.broadcasted_iota(jnp.int32, (values.shape[0], 128), 1)
-    total = jnp.zeros((values.shape[0], 128), F32)
-    for h in range(heads):
-        part = jnp.sum(values[:, h * P_SIZE : (h + 1) * P_SIZE], axis=1, keepdims=True)
-        total = jnp.where(lane == h, part, total)
-    return total
+def split(values, count):
+    parts = []
+    for _ in range(count):
+        part = values.astype(BF)
+        values = values - part.astype(F32)
+        parts.append(part)
+    return parts
+
+
+def head_lanes(heads):
+    row = lax.broadcasted_iota(jnp.int32, (128, heads * P_SIZE), 0)
+    lane = lax.broadcasted_iota(jnp.int32, (128, heads * P_SIZE), 1)
+    return jnp.where(lane // P_SIZE == row, 1.0, 0.0).astype(BF)
+
+
+def spread(columns, lanes):
+    return sum(dot(part, lanes, ((1,), (0,))) for part in split(columns, 2))
+
+
+def head_sums(values, lanes):
+    return sum(dot(part, lanes, ((1,), (1,))) for part in split(values, 2))
+
+
+def running(mask, values):
+    mask = jnp.where(mask, 1.0, 0.0).astype(BF)
+    return sum(dot(mask, part, ((1,), (0,))) for part in split(values, 3))
 
 
 def convolve(buffer, weights, bias, place):
@@ -131,19 +140,15 @@
     row = lax.broadcasted_iota(jnp.int32, (STRETCH, STRETCH), 0)
     col = lax.broadcasted_iota(jnp.int32, (STRETCH, STRETCH), 1)
     at = lax.broadcasted_iota(jnp.int32, (STRETCH, 1), 0)
-    visible = (col <= row) & (col >= at - place)
     biased = dt_in + pdt[0:1, :]
     step = jnp.maximum(biased, 0.0) + jnp.log1p(jnp.exp(-jnp.abs(biased)))
     log_decay = step * pdt[1:2, :]
-    lower = jnp.where(col <= row, 1.0, 0.0).astype(F32)
-    cum = lax.dot_general(
-        lower, log_decay, (((1,), (0,)), ((), ())), precision=PRECISE, preferred_element_type=F32
-    )
+    cum = running(col <= row, log_decay)
     cum_t = jnp.transpose(cum)
     carrying = jnp.where(place >= at + 1, jnp.exp(cum), 0.0)
     tail_ok = remain >= STRETCH - 1 - at
     tail = jnp.exp(jnp.where(tail_ok, cum[STRETCH - 1 : STRETCH, :] - cum, LOW))
-    return visible, biased, step, log_decay, cum, cum_t, carrying, tail
+    return row, col, biased, step, log_decay, cum, cum_t, carrying, tail
 
 
 def forward_kernel(
@@ -180,15 +185,17 @@
     act_bc = conv_bc * sigmoid(conv_bc)
     b_low = act_bc[:, :N].astype(BF)
     c_low = act_bc[:, N:].astype(BF)
-    visible, _, step, _, cum, cum_t, carrying, tail = block_terms(
+    row, col, _, step, _, cum, cum_t, carrying, tail = block_terms(
         place, remain, dt_ref[...].astype(F32), pdt_ref[...]
     )
-    scaled = x * spread(step, heads)
+    visible = (col <= row) & (row - col <= place)
+    lanes = head_lanes(heads)
+    scaled = x * spread(step, lanes)
     scaled_low = scaled.astype(BF)
     gram = dot(c_low, b_low, ((1,), (1,)))
     old = state[...]
     states_ref[0] = old
-    across = dot(c_low, old, ((1,), (1,))) * spread(carrying, heads)
+    across = dot(c_low, old, ((1,), (1,))) * spread(carrying, lanes)
     parts = []
     for h in range(heads):
         decay = jnp.exp(jnp.where(visible, cum[:, h : h + 1] - cum_t[h : h + 1, :], LOW))
@@ -196,7 +203,7 @@
             dot(gram * decay, scaled_low[:, h * P_SIZE : (h + 1) * P_SIZE], ((1,), (0,)))
         )
     mixed = jnp.concatenate(parts, axis=1) + across + px_ref[5:6, :] * x
-    fresh = dot(scaled * spread(tail, heads), b_low, ((0,), (0,)))
+    fresh = dot(scaled * spread(tail, lanes), b_low, ((0,), (0,)))
     for h in range(heads):
         rows = slice(h * P_SIZE, (h + 1) * P_SIZE)
         state[rows, :] = (
@@ -259,9 +266,11 @@
     act_bc = conv_bc * sig_bc
     b_low = act_bc[:, :N].astype(BF)
     c_low = act_bc[:, N:].astype(BF)
-    visible, biased, step, log_decay, cum, cum_t, carrying, tail = block_terms(
+    row, col, biased, step, log_decay, cum, cum_t, carrying, tail = block_terms(
         place, remain, dt_ref[...].astype(F32), pdt_ref[...]
     )
+    visible = (col >= row) & (col - row <= remain)
+    lanes = head_lanes(heads)
 
     gate = gate_ref[...].astype(F32)
     sig = sigmoid(gate)
@@ -276,9 +285,9 @@
     g_mixed = g_gated * silu
     gp_ref[:, 0:width] = (g_gated * mixed * (sig * (1.0 + gate * (1.0 - sig)))).astype(BF)
 
-    step_wide = spread(step, heads)
-    carry_wide = spread(carrying, heads)
-    tail_wide = spread(tail, heads)
+    step_wide = spread(step, lanes)
+    carry_wide = spread(carrying, lanes)
+    tail_wide = spread(tail, lanes)
     scaled = x * step_wide
     scaled_low = scaled.astype(BF)
     g_low = g_mixed.astype(BF)
@@ -286,7 +295,7 @@
     g_new = gstate[...]
     old_low = old.astype(BF)
     g_new_low = g_new.astype(BF)
-    gram = dot(c_low, b_low, ((1,), (1,)))
+    gram = dot(b_low, c_low, ((1,), (1,)))
     across = dot(c_low, old_low, ((1,), (1,)))
     returned = dot(b_low, g_new_low, ((1,), (1,))) * tail_wide
     g_carried = g_mixed * carry_wide
@@ -295,24 +304,24 @@
 
     g_gram = jnp.zeros((STRETCH, STRETCH), F32)
     lane = lax.broadcasted_iota(jnp.int32, (STRETCH, 128), 1)
-    row_sum = jnp.zeros((STRETCH, 128), F32)
-    col_rows = []
+    sources = jnp.zeros((STRETCH, 128), F32)
+    target_rows = []
     parts = []
     for h in range(heads):
         cols = slice(h * P_SIZE, (h + 1) * P_SIZE)
-        decay = jnp.exp(jnp.where(visible, cum[:, h : h + 1] - cum_t[h : h + 1, :], LOW))
+        decay = jnp.exp(jnp.where(visible, cum_t[h : h + 1, :] - cum[:, h : h + 1], LOW))
         mixing = gram * decay
-        g_mixing = dot(g_low[:, cols], scaled_low[:, cols], ((1,), (1,)))
-        parts.append(dot(mixing, g_low[:, cols], ((0,), (0,))))
+        g_mixing = dot(scaled_low[:, cols], g_low[:, cols], ((1,), (1,)))
+        parts.append(dot(mixing, g_low[:, cols], ((1,), (0,))))
         g_gram = g_gram + g_mixing * decay
         both = g_mixing * mixing
-        row_sum = jnp.where(lane == h, jnp.sum(both, axis=1, keepdims=True), row_sum)
-        col_rows.append(jnp.sum(both, axis=0, keepdims=True))
-    col_rows.append(jnp.zeros((128 - heads, STRETCH), F32))
-    col_sum = jnp.transpose(jnp.concatenate(col_rows, axis=0))
+        sources = jnp.where(lane == h, jnp.sum(both, axis=1, keepdims=True), sources)
+        target_rows.append(jnp.sum(both, axis=0, keepdims=True))
+    target_rows.append(jnp.zeros((128 - heads, STRETCH), F32))
+    targets = jnp.transpose(jnp.concatenate(target_rows, axis=0))
     g_scaled = jnp.concatenate(parts, axis=1) + returned
-    into = head_sums(g_carried * across, heads)
-    outof = head_sums(scaled * returned, heads)
+    into = head_sums(g_carried * across, lanes)
+    outof = head_sums(scaled * returned, lanes)
     state_dot = jnp.zeros((1, 128), F32)
     lane_one = lax.broadcasted_iota(jnp.int32, (1, 128), 1)
     product = g_new * old
@@ -323,25 +332,20 @@
             keepdims=True,
         )
         state_dot = jnp.where(lane_one == h, total, state_dot)
-    g_c = dot(g_gram, b_low, ((1,), (0,))) + dot(g_carried_low, old_low, ((1,), (0,)))
-    g_b = dot(g_gram, c_low, ((0,), (0,))) + dot(tailed_low, g_new_low, ((1,), (0,)))
+    g_c = dot(g_gram, b_low, ((0,), (0,))) + dot(g_carried_low, old_low, ((1,), (0,)))
+    g_b = dot(g_gram, c_low, ((1,), (0,))) + dot(tailed_low, g_new_low, ((1,), (0,)))
     g_fresh = dot(g_carried_low, c_low, ((0,), (0,)))
     for h in range(heads):
         rows = slice(h * P_SIZE, (h + 1) * P_SIZE)
         gstate[rows, :] = (
             g_new[rows, :] * carrying[STRETCH - 1 : STRETCH, h : h + 1] + g_fresh[rows, :]
         )
-    row = lax.broadcasted_iota(jnp.int32, (STRETCH, STRETCH), 0)
-    col = lax.broadcasted_iota(jnp.int32, (STRETCH, STRETCH), 1)
-    upper = jnp.where(col >= row, 1.0, 0.0).astype(F32)
-    g_cum = row_sum - col_sum + into - outof
-    g_decay = lax.dot_general(
-        upper, g_cum, (((1,), (0,)), ((), ())), precision=PRECISE, preferred_element_type=F32
-    ) + (
+    g_cum = targets - sources + into - outof
+    g_decay = running(col >= row, g_cum) + (
         jnp.sum(outof, axis=0, keepdims=True)
         + carrying[STRETCH - 1 : STRETCH, :] * state_dot
     )
-    g_step = head_sums(x * g_scaled, heads) + g_decay * pdt_ref[1:2, :]
+    g_step = head_sums(x * g_scaled, lanes) + g_decay * pdt_ref[1:2, :]
     g_dt = g_step * sigmoid(biased)
     gdt_ref[0:1, :] += jnp.sum(g_dt, axis=0, keepdims=True)
     gdt_ref[1:2, :] += jnp.sum(g_decay * log_decay, axis=0, keepdims=True)
@@ -677,10 +681,9 @@
     return pair.reshape((16,) + block.shape)
 
 
-def adamw_kernel(count, base_ref, weight_ref, moment_ref, second_ref, *refs):
-    new_ref, first_ref, squares_ref, low_ref = refs[-4:]
-    shape = weight_ref.shape
-    grad = sum(ref[...].astype(F32).reshape(shape) for ref in refs[:count])
+def adamw_kernel(first_ref, base_ref, weight_ref, moment_ref, second_ref, grad_ref, *refs):
+    new_ref, first_moment_ref, squares_ref, low_ref = refs[-4:]
+    grad = grad_ref[...].astype(F32).reshape(weight_ref.shape)
     base = base_ref[0, 0]
     weight = weight_ref[...]
     first = BETA_ONE * moment_ref[...] + (1.0 - BETA_ONE) * grad
@@ -689,39 +692,54 @@
         (first / base) / (jnp.sqrt(squares / base) + ADAM_EPS) + MATRIX_DECAY * weight
     )
     new_ref[...] = new
-    first_ref[...] = first
+    first_moment_ref[...] = first
     squares_ref[...] = squares
     low_ref[...] = new.astype(BF)
 
 
-def adamw_rows(base, weight, moment, second, grads, first, size, count, grad_spec, filled):
+def adamw_rows(base, state, grad, first, size, filled):
+    weight = state[0]
     columns = weight.shape[1]
-    spec = pl.BlockSpec((size, columns), lambda i: (first // size + i, 0))
-    used = 4 + len(grads)
-    return pl.pallas_call(
-        partial(adamw_kernel, len(grads)),
-        grid=(count,),
-        in_specs=[pl.BlockSpec(memory_space=pltpu.SMEM), spec, spec, spec]
-        + [grad_spec] * len(grads)
-        + [pl.BlockSpec(memory_space=pl.ANY)] * len(filled),
-        out_specs=[spec] * 4,
-        out_shape=[jax.ShapeDtypeStruct(weight.shape, F32)] * 3
-        + [jax.ShapeDtypeStruct(weight.shape, BF)],
-        input_output_aliases={used + i: i for i in range(len(filled))},
-        cost_estimate=pl.CostEstimate(
-            flops=count * columns * size * 10000,
-            bytes_accessed=count * columns * size * 30,
-            transcendentals=count * columns * size,
-        ),
-        name="adamw",
-    )(base, weight, moment, second, *grads, *filled)
+    spec = pl.BlockSpec((size, columns), lambda i, at: (at[0] + i, 0))
+    if grad.ndim == 3:
+        units = grad.shape[1]
+        count = grad.shape[0] * units // size
+        grad_spec = pl.BlockSpec((size // units, units, columns), lambda i, at: (i, 0, 0))
+    else:
+        count = grad.shape[0] // size
+        grad_spec = pl.BlockSpec((size, columns), lambda i, at: (i, 0))
+    return tuple(
+        pl.pallas_call(
+            adamw_kernel,
+            grid_spec=pltpu.PrefetchScalarGridSpec(
+                num_scalar_prefetch=1,
+                grid=(count,),
+                in_specs=[pl.BlockSpec(memory_space=pltpu.SMEM), spec, spec, spec, grad_spec]
+                + [pl.BlockSpec(memory_space=pl.ANY)] * len(filled),
+                out_specs=[spec] * 4,
+            ),
+            out_shape=[jax.ShapeDtypeStruct(weight.shape, F32)] * 3
+            + [jax.ShapeDtypeStruct(weight.shape, BF)],
+            input_output_aliases={6 + i: i for i in range(len(filled))},
+            cost_estimate=pl.CostEstimate(
+                flops=count * columns * size * 10000,
+                bytes_accessed=count * columns * size * 30,
+                transcendentals=count * columns * size,
+            ),
+            name="adamw",
+        )(jnp.reshape(first, (1,)).astype(jnp.int32), base, *state, grad, *filled)
+    )
 
 
 def tree_sum(values):
     if lax.axis_size("dp") != 16 or lax.axis_size("width") != 2:
         return lax.psum(values, ("width", "dp"))
-    for bit in (1, 2, 4, 8):
-        values = values + lax.ppermute(values, "dp", [(i, i ^ bit) for i in range(16)])
+    for low, high in ((1, 2), (4, 8)):
+        near, far, across = (
+            lax.ppermute(values, "dp", [(i, i ^ mask) for i in range(16)])
+            for mask in (low, high, low ^ high)
+        )
+        values = (values + near) + (far + across)
     return values + lax.ppermute(values, "width", [(0, 1), (1, 0)])
 
 
@@ -930,38 +948,26 @@
         MATRIX_DECAY,
         step_float,
     )
-    if paired:
-        g_normed = inward.finish(new_out, g_peer, g_apart)
-        g_gate, g_x = in_order(g_half, g_peer)
-        g_pairs = jnp.concatenate([g_gate, g_x], axis=0)
-        g_apart = jnp.concatenate(in_order(g_shared, g_apart), axis=0)
-    else:
-        g_normed = inward.finish(new_out)
     if simple:
         base = (1.0 - jnp.power(BETA_ONE, step_float)).reshape(1, 1)
         own = (weight_in.T, moment_in.T, second_in.T)
-        moved = adamw_rows(
-            base,
-            *own,
-            (g_pairs,),
-            0,
-            4 * units,
-            dp // 2,
-            pl.BlockSpec((4, units, shard), lambda i: (i, 0, 0)),
-            (),
-        )
-        results = adamw_rows(
-            base,
-            *own,
-            (g_apart,),
-            2 * E,
-            H,
-            SHARED // H,
-            pl.BlockSpec((H, shard), lambda i: (i, 0)),
-            tuple(moved),
-        )
-        new_in, mom_in, sec_in, low_in = (result.T for result in results)
+        size = 4 * units
+        blocks = E // size
+        moved = adamw_rows(base, own, after(g_half, inward.sent), slot * blocks, size, ())
+        g_normed = inward.finish(new_out, g_peer, g_apart, moved)
+    elif paired:
+        g_normed = inward.finish(new_out, g_peer, g_apart)
     else:
+        g_normed = inward.finish(new_out)
+    if paired:
+        g_apart = jnp.concatenate(in_order(g_shared, g_apart), axis=0)
+    if simple:
+        moved = adamw_rows(base, own, g_peer, (1 - slot) * blocks, size, moved)
+        moved = adamw_rows(base, own, g_apart, 2 * E // H, H, moved)
+        new_in, mom_in, sec_in, low_in = (result.T for result in moved)
+    else:
+        if paired:
+            g_gate, g_x = in_order(g_half, g_peer)
         total_in = jnp.concatenate(
             [
                 g_gate.transpose(2, 0, 1).reshape(shard, E),

time: 688 us -> 672 us (0.977)
  Pallas kernels: 143 us -> 95.1 us
  waiting for transfers between devices: 241 us -> 276 us
    pallas_call x1, Pallas kernels: 81.1 us -> 51.1 us  [run_backward(): pl.pallas_call(partial(backward_kernel, heads), grid=(count,), in_specs=[...]
    all_gather x1, waiting for transfers between devices: 35.5 us -> 53.4 us  [per_device(): lax.all_gather(after(cotangent, normed_all, weight_own), 'dp', axis=0, ti...]
    pallas_call x1, Pallas kernels: 44.5 us -> 26.8 us  [run_forward(): pl.pallas_call(partial(forward_kernel, heads), grid=(count,), in_specs=[r...]
    ppermute x8, waiting for transfers between devices: 49.5 us -> 59.9 us  [hop(): return lax.ppermute(values, 'dp', pairs)]
    pallas_call x2 -> x3, Pallas kernels: 16.9 us -> 17.3 us  [adamw_rows(): pl.pallas_call(adamw_kernel, grid_spec=pltpu.PrefetchScalarGridSpec(num_s...]
  transfers between devices with their start and end apart: 27 -> 29, of which waited for: 16 -> 16; matrix products, arithmetic and copies ran while one was open for 30% -> 31% of each run, Pallas kernels for 21% -> 14%
where the time goes in v4:
time: 672 us; the launch traced here: 667 us
  waiting for transfers between devices  276 us (41%)
  matrix products  113 us (17%)
  Pallas kernels  95.1 us (14%)
  other arithmetic  62.5 us (9%)
  starting transfers between devices  45.8 us (7%)
  local copies, waits for them, and re-layouts  38 us (6%)
  blocking collectives  19.5 us (3%)
  between operations  16.2 us (2%)
    all_gather x1, waiting for transfers between devices, per_device(): normed_all = lax.all_gather(normed_low, 'dp', axis=0, tiled=True)  71.4 us
    ppermute x8, waiting for transfers between devices, hop(): return lax.ppermute(values, 'dp', pairs)  59.9 us
    all_gather x1, waiting for transfers between devices, per_device(): lax.all_gather(after(cotangent, normed_all, weight_own), 'dp', axis=0, ti...  53.4 us
    pallas_call x1, Pallas kernels, run_backward(): pl.pallas_call(partial(backward_kernel, heads), grid=(count,), in_specs=[...  51.1 us
    dot_general x16, matrix products, chunk(): jnp.dot(lax.dynamic_slice_in_dim(after(side, deps), start, rows, 0), weig...  44.9 us
    all_to_all x1, waiting for transfers between devices, per_device(): lax.all_to_all(pairs, 'dp', 0, 0).transpose(1, 0, 2).reshape(2 * units, D)  43.7 us
    all_to_all x1, waiting for transfers between devices, gather_blocks(): mine = lax.all_to_all(copies, 'dp', 0, 0, axis_index_groups=same_core())  29.4 us
    pallas_call x1, Pallas kernels, run_forward(): pl.pallas_call(partial(forward_kernel, heads), grid=(count,), in_specs=[r...  26.8 us
  transfers between devices with their start and end apart: 29, of which 16 were waited for; matrix products, arithmetic and copies ran while one was open for 31% of the time, Pallas kernels for 14%

profile of v4, /device:TPU:0, one launch (start us, length us, event | category | flops | bytes accessed | tf_op | source)
XLA Modules:
  0.0 666.7 jit_solution(9563055466941323950)
XLA Ops:
  10.6 2.5 fusion.5
  16.5 7.3 %all-to-all-start.1 = ((bf16[8,320,128]{2,1,0:T(8,128)(2,1)}), bf16[8,320,128]{2,1,0:T(8,128)(2,1)}, u32[]{:S(2)}, u32[]{:S(2)}) async-start(bf16[8,320,128]{2,1,0:T(8,128)(2,1)} %broadcast_in_dim.38), calls=%async_computation.1 | async-start | bytes 1310720 | tf_op jit(solution)/shard_map/all_to_all | solution.py:677
  28.4 29.4 %all-to-all-done.1 = bf16[8,320,128]{2,1,0:T(8,128)(2,1)} async-done(((bf16[8,320,128]{2,1,0:T(8,128)(2,1)}), bf16[8,320,128]{2,1,0:T(8,128)(2,1)}, u32[]{:S(2)}, u32[]{:S(2)}) %all-to-all-start.1) | async-done | bytes 655392 | tf_op jit(solution)/shard_map/all_to_all | solution.py:677
  57.8 5.5 all-to-all-start
  72.1 43.7 %all-to-all-done = bf16[16,512,128]{1,2,0:T(8,128)(2,1)S(1)} async-done(((bf16[16,512,128]{1,2,0:T(8,128)(2,1)}), bf16[16,512,128]{1,2,0:T(8,128)(2,1)S(1)}, u32[]{:S(2)}, u32[]{:S(2)}) %all-to-all-start) | async-done | bytes 2097184 | tf_op jit(solution)/shard_map/all_to_all | solution.py:796
  115.8 3.0 fusion.1
  118.8 71.4 %all-gather.5.cloned.1.call-done = bf16[4096,2048]{1,0:T(8,128)(2,1)} async-done(((bf16[256,2048]{1,0:T(8,128)(2,1)}), bf16[4096,2048]{1,0:T(8,128)(2,1)}) %all-gather.5.cloned.1.call-update) | async-done | bytes 16777232 | tf_op jit(solution)/shard_map/all_gather | solution.py:791
  197.9 5.1 iota_subtract_fusion
  202.9 22.0 %convolution_convert_fusion.1.gate_ref.x_ref.bc_ref.dt_ref.xprev_ref.bcprev_ref = bf16[4096,896]{1,0:T(8,128)(2,1)} fusion(bf16[4096,2048]{1,0:T(8,128)(2,1)} %all-gather.5.cloned.1.call-done, bf16[2048,4]{1,0:T(8,128)(2,1)S(1)} %copy-done.3, bf16[2048,256]{1,0:T(8,128)(2,1)S(1)} %slice.149, bf16[2048,512]{1,0:T(8,128)(2,1)S(1)} %bitcast.115), kind=kOutput, calls=%fused_computation.3 | convolution fusion | flops 15050735616 | bytes 27279360 | tf_op jit(solution)/shard_map/dot_general | solution.py:840
  225.6 26.8 %scan_forward.1 = (bf16[4096,256]{1,0:T(8,128)(2,1)}, f32[4096,256]{1,0:T(8,128)}, f32[4096,1]{1,0:T(8,128)}, f32[16,256,128]{2,1,0:T(8,128)}, f32[256,128]{1,0:T(8,128)}) custom-call(bf16[4096,896]{1,0:T(8,128)(2,1)} %convolution_convert_fusion.1.gate_ref.x_ref.bc_ref.dt_ref.xprev_ref.bcprev_ref, ...), custom_call_target="tpu_custom_call" | custom-call | flops 20971520000 | bytes 20480000 | tf_op jit(solution)/shard_map/scan_forward/pallas_call | solution.py:399
  254.8 9.9 %convolution_convert_fusion = bf16[4096,2048]{1,0:T(8,128)(2,1)} fusion(bf16[4096,256]{1,0:T(8,128)(2,1)} %get-tuple-element.77, f32[256,2048]{1,0:T(8,128)S(1)} %copy-done.1), kind=kOutput, calls=%fused_computation | convolution fusion | flops 4303880192 | bytes 20971520 | tf_op jit(solution)/shard_map/dot_general | solution.py:847
  264.8 53.4 %all-gather.7.cloned.1.call-done = bf16[4096,2048]{1,0:T(8,128)(2,1)} async-done(((bf16[256,2048]{1,0:T(8,128)(2,1)}), bf16[4096,2048]{1,0:T(8,128)(2,1)}) %all-gather.7.cloned.1.call-update) | async-done | bytes 16777232 | tf_op jit(solution)/shard_map/all_gather | solution.py:837
  318.2 13.6 %multiply_reduce_fusion = (f32[4096]{0:T(1024)S(1)}, f32[4096,256]{1,0:T(8,128)}) fusion(bf16[4096,256]{1,0:T(8,128)(2,1)} %get-tuple-element.77, bf16[4096,2048]{1,0:T(8,128)(2,1)} %all-gather.7.cloned.1.call-done, f32[256,2048]{1,0:T(8,128)S(1)} %copy-done.1), kind=kOutput, calls=%fused_computation.10 | convolution fusion | flops 4298633216 | bytes 25182208 | tf_op jit(solution)/shard_map/dot_general | solution.py:849
  331.8 19.5 %all-gather.1 = f32[16,2,4096]{2,1,0:T(2,128)S(1)} all-gather(f32[1,2,4096]{2,1,0:T(2,128)S(1)} %maximum_bitcast_fusion), channel_id=2, replica_groups=mesh['width'=2,'dp'=16] {'dp'}, dimensions={0}, use_global_device_ids=true | all-gather | bytes 557056 | tf_op jit(solution)/shard_map/all_gather | solution.py:853
  357.5 4.5 divide_multiply_fusion.pull_ref
  363.3 51.1 %scan_backward.1 = (bf16[4096,896]{1,0:T(8,128)(2,1)}, bf16[4096,256]{1,0:T(8,128)(2,1)}, f32[256,128]{1,0:T(8,128)}, f32[16,256]{1,0:T(8,128)}, f32[16,256]{1,0:T(8,128)}, /*index=5*/f32[8,128]{1,0:T(8,128)}) custom-call(bf16[4096,896]{1,0:T(8,128)(2,1)} %convolution_convert_fusion.1.gate_ref.x_ref.bc_ref.dt_ref.xprev_ref.bcprev_ref, ...), custom_call_target="tpu_custom_call" | custom-call | flops 41943040000 | bytes 32768000 | tf_op jit(solution)/shard_map/scan_backward/pallas_call | solution.py:467
  415.5 4.4 dynamic-slice_bitcast_fusion
  421.1 18.2 %convolution_convert_fusion.2 = bf16[896,2048]{1,0:T(8,128)(2,1)S(1)} fusion(bf16[4096,896]{1,0:T(8,128)(2,1)S(1)} %copy-done.24, bf16[4096,2048]{1,0:T(8,128)(2,1)} %all-gather.5.cloned.1.call-done), kind=kOutput, calls=%fused_computation.12 | convolution fusion | flops 15034220544 | bytes 27787264 | tf_op jit(solution)/shard_map/dot_general | solution.py:875
  446.6 3.2 fusion.39
  449.9 2.6 convolution_add_fusion.7
  455.7 3.2 fusion.33
  459.4 4.5 convolution_convert_fusion.3
  463.9 2.5 convolution_add_fusion.5
  466.4 3.1 fusion.36
  469.5 2.5 convolution_add_fusion.6
  473.3 8.5 %collective-permute-done.4 = bf16[256,1024]{1,0:T(8,128)(2,1)} collective-permute-done((bf16[256,1024]{1,0:T(8,128)(2,1)}, bf16[256,1024]{1,0:T(8,128)(2,1)}, u32[]{:S(2)}, u32[]{:S(2)}) %collective-permute-start.4) | collective-permute-done | bytes 524320 | tf_op jit(solution)/shard_map/ppermute | solution.py:551
  488.4 3.1 bitcast_bitcast_fusion
  491.5 4.4 all-to-all-start.2
  496.0 3.1 fusion.27
  499.1 3.2 fusion.30
  507.3 16.8 %collective-permute-done.5 = bf16[512,1024]{1,0:T(8,128)(2,1)} collective-permute-done((bf16[512,1024]{1,0:T(8,128)(2,1)}, bf16[512,1024]{1,0:T(8,128)(2,1)}, u32[]{:S(2)}, u32[]{:S(2)}) %collective-permute-start.5) | collective-permute-done | bytes 1048608 | tf_op jit(solution)/shard_map/ppermute | solution.py:551
  524.0 7.2 %collective-permute-done.6 = bf16[512,1024]{1,0:T(8,128)(2,1)} collective-permute-done((bf16[512,1024]{1,0:T(8,128)(2,1)}, bf16[512,1024]{1,0:T(8,128)(2,1)}, u32[]{:S(2)}, u32[]{:S(2)}) %collective-permute-start.6) | collective-permute-done | bytes 1048608 | tf_op jit(solution)/shard_map/ppermute | solution.py:551
  534.5 2.5 collective-permute-start.7
  537.2 3.1 fusion.21
  542.8 3.1 fusion.24
  548.7 23.0 %collective-permute-done.7 = bf16[512,1024]{1,0:T(8,128)(2,1)S(1)} collective-permute-done((bf16[512,1024]{1,0:T(8,128)(2,1)S(1)}, bf16[512,1024]{1,0:T(8,128)(2,1)S(1)}, u32[]{:S(2)}, u32[]{:S(2)}) %collective-permute-start.7) | collective-permute-done | bytes 1048608 | tf_op jit(solution)/shard_map/ppermute | solution.py:551
  576.5 8.2 %collective-permute-start.10 = (bf16[512,1024]{1,0:T(8,128)(2,1)}, bf16[512,1024]{1,0:T(8,128)(2,1)}, u32[]{:S(2)}, u32[]{:S(2)}) collective-permute-start(bf16[512,1024]{1,0:T(8,128)(2,1)} %add_convert_fusion.2), channel_id=1, source_target_pairs={{0,4},{1,5},{4,8},{5,9},{8,12},{9,13},{12,14},{13,15},{14,10},{15,... | collective-permute-start | bytes 3145736 | tf_op jit(solution)/shard_map/ppermute | solution.py:551
  584.7 4.2 fusion.70
  591.8 3.1 fusion.18
  594.9 2.5 convolution_add_fusion
  600.2 7.0 %adamw.3 = (f32[8512,128]{1,0:T(8,128)}, f32[8512,128]{1,0:T(8,128)}, f32[8512,128]{1,0:T(8,128)}, bf16[8512,128]{1,0:T(8,128)(2,1)}) custom-call(s32[1]{0:T(128)} %bitcast.36.first_ref, f32[1,1]{1,0:T(1,128)} %bitcast.37.base_ref, f32[8512,128]{1,0:T(8,128)} %bitcast.99, f32[8512,128]{1,0:T(8,128)} %bitcast.104, f32[8512,128]{1,0:T(8,128)} %bitcast.107, ...), custom_call_target="tpu_custom_call" | custom-call | flops 5242880000 | bytes 15728640 | tf_op jit(solution)/shard_map/adamw/pallas_call | solution.py:712
  608.2 7.3 %collective-permute-done.14 = bf16[160,128]{1,0:T(8,128)(2,1)S(1)} collective-permute-done((bf16[160,128]{1,0:T(8,128)(2,1)S(1)}, bf16[160,128]{1,0:T(8,128)(2,1)S(1)}, u32[]{:S(2)}, u32[]{:S(2)}) %collective-permute-start.14) | collective-permute-done | bytes 40992 | tf_op jit(solution)/shard_map/ppermute | solution.py:661
  615.5 3.7 convert_add_fusion.1
  628.6 7.0 %adamw.4 = (f32[8512,128]{1,0:T(8,128)}, f32[8512,128]{1,0:T(8,128)}, f32[8512,128]{1,0:T(8,128)}, bf16[8512,128]{1,0:T(8,128)(2,1)}) custom-call(s32[1]{0:T(128)} %bitcast.40.first_ref, f32[1,1]{1,0:T(1,128)} %bitcast.37.base_ref, f32[8512,128]{1,0:T(8,128)} %bitcast.100, ...), custom_call_target="tpu_custom_call", output_to_operand_aliasing={{0}: (6, {}), {1}: (7, {}), {2}: (8, {}), {3}: (9, {})} | custom-call | flops 5242880000 | bytes 15728640 | tf_op jit(solution)/shard_map/adamw/pallas_call | solution.py:712
  635.7 3.3 adamw.5
  639.9 2.5 collective-permute-start.19
  646.0 8.2 %collective-permute-done.20 = f32[28096]{0:T(1024)S(1)} collective-permute-done((f32[28096]{0:T(1024)S(1)}, f32[28096]{0:T(1024)S(1)}, u32[]{:S(2)}, u32[]{:S(2)}) %collective-permute-start.20) | collective-permute-done | bytes 112416 | tf_op jit(solution)/shard_map/ppermute | solution.py:739
  655.1 3.9 fusion.10
  (211 shorter events, 98.8 us)
Async XLA Ops:
  7.2 183.0 %all-gather.5.cloned.1.call-start = ((), (), s32[]{:S(2)}) async-start(), calls=%async_computation.4 | async-start | bytes 17825792 | tf_op jit(solution)/shard_map/all_gather | solution.py:791
  16.5 41.3 %all-to-all-start.1 = ((bf16[8,320,128]{2,1,0:T(8,128)(2,1)}), bf16[8,320,128]{2,1,0:T(8,128)(2,1)}, u32[]{:S(2)}, u32[]{:S(2)}) async-start(bf16[8,320,128]{2,1,0:T(8,128)(2,1)} %broadcast_in_dim.38), calls=%async_computation.1 | async-start | bytes 1310720 | tf_op jit(solution)/shard_map/all_to_all | solution.py:677
  57.8 58.0 %all-to-all-start = ((bf16[16,512,128]{1,2,0:T(8,128)(2,1)}), bf16[16,512,128]{1,2,0:T(8,128)(2,1)S(1)}, u32[]{:S(2)}, u32[]{:S(2)}) async-start(bf16[16,512,128]{1,2,0:T(8,128)(2,1)} %pad_maximum_fusion), calls=%async_computation | async-start | bytes 4194304 | tf_op jit(solution)/shard_map/all_to_all | solution.py:796
  63.4 254.9 %all-gather.7.cloned.1.call-start = ((), (), s32[]{:S(2)}) async-start(), calls=%async_computation.6 | async-start | bytes 17825792 | tf_op jit(solution)/shard_map/all_gather | solution.py:837
  63.4 2.4 collective-permute-start
  115.8 74.6 %slice-start.4 = ((f32[28096]{0:T(1024)}), f32[17408]{0:T(1024)S(1)}, s32[]{:S(2)}) async-start(f32[28096]{0:T(1024)} %param.25), calls=%async_computation.11 | async-start | bytes 139264 | tf_op jit(solution)/shard_map/slice | solution.py:59
  115.8 74.6 %copy-start.10 = (f32[28096]{0:T(1024)S(1)}, f32[28096]{0:T(1024)}, u32[]{:S(2)}) copy-start(f32[28096]{0:T(1024)} %param.25) | copy-start | bytes 337156
  115.8 75.8 %copy-start.25 = (s32[1,8]{1,0:T(1,128)S(1)}, s32[1,8]{1,0:T(1,128)}, u32[]{:S(2)}) copy-start(s32[1,8]{1,0:T(1,128)} %param.16) | copy-start | bytes 100
  190.2 464.9 %reduce-scatter.2.cloned.1.call-start = ((), (), s32[]{:S(2)}) async-start(), calls=%async_computation.5 | async-start | bytes 17825792 | tf_op jit(solution)/shard_map/reduce_scatter | solution.py:848
  192.0 5.3 slice-start.5
  197.9 5.1 copy-start.3
  414.4 32.3 %collective-permute-start.1 = (bf16[4096,896]{1,0:T(8,128)(2,1)}, bf16[4096,896]{1,0:T(8,128)(2,1)}, u32[]{:S(2)}, u32[]{:S(2)}) collective-permute-start(bf16[4096,896]{1,0:T(8,128)(2,1)} %get-tuple-element.116), channel_id=1, source_target_pairs={{0,1},{1,0},{2,3},{3,2},{4,5},{5,4},{6,7},{7,6},{8,9},{9,8},{10,11... | collective-permute-start | bytes 22020104 | tf_op jit(solution)/shard_map/ppermute | solution.py:555
  415.5 5.6 copy-start.24
  419.9 26.7 %collective-permute-start.2 = (bf16[896,1024]{0,1:T(8,128)(2,1)}, bf16[896,1024]{0,1:T(8,128)(2,1)}, u32[]{:S(2)}, u32[]{:S(2)}) collective-permute-start(bf16[896,1024]{0,1:T(8,128)(2,1)} %get-tuple-element.157), channel_id=1, source_target_pairs={{0,1},{1,0},{2,3},{3,2},{4,5},{5,4},{6,7},{7,6},{8,9},{9,8},{10,11... | collective-permute-start | bytes 5505032 | tf_op jit(solution)/shard_map/ppermute | solution.py:555
  443.6 44.9 %collective-permute-start.12 = (bf16[416,2048]{1,0:T(8,128)(2,1)}, bf16[416,2048]{1,0:T(8,128)(2,1)}, u32[]{:S(2)}, u32[]{:S(2)}) collective-permute-start(bf16[416,2048]{1,0:T(8,128)(2,1)} %pad_maximum_fusion.3), channel_id=1, source_target_pairs={{0,16},{16,0},{1,17},{17,1},{2,18},{18,2},{3,19},{19,3},{4,20},{20... | collective-permute-start | bytes 5111816 | tf_op jit(solution)/shard_map/ppermute | solution.py:661
  445.2 13.7 %slice-start = ((s8[16777216]{0:T(1024)(128)(4,1)}), s8[4194304]{0:T(1024)(128)(4,1)S(1)}, s32[]{:S(2)}) async-start(s8[16777216]{0:T(1024)(128)(4,1)} %bitcast.102), calls=%async_computation.7 | async-start | bytes 8388608
  446.6 12.3 %slice-start.1 = ((s8[16777216]{0:T(1024)(128)(4,1)}), s8[4194304]{0:T(1024)(128)(4,1)S(1)}, s32[]{:S(2)}) async-start(s8[16777216]{0:T(1024)(128)(4,1)} %bitcast.102), calls=%async_computation.8 | async-start | bytes 8388608
  449.9 9.1 %slice-start.2 = ((s8[16777216]{0:T(1024)(128)(4,1)}), s8[4194304]{0:T(1024)(128)(4,1)S(1)}, s32[]{:S(2)}) async-start(s8[16777216]{0:T(1024)(128)(4,1)} %bitcast.102), calls=%async_computation.9 | async-start | bytes 8388608
  453.6 19.7 %collective-permute-start.3 = (bf16[256,1024]{1,0:T(8,128)(2,1)}, bf16[256,1024]{1,0:T(8,128)(2,1)}, u32[]{:S(2)}, u32[]{:S(2)}) collective-permute-start(bf16[256,1024]{1,0:T(8,128)(2,1)} %get-tuple-element.87), channel_id=1, source_target_pairs={{0,4},{1,5},{4,8},{5,9},{8,12},{9,13},{12,14},{13,15},{14,10},{15,... | collective-permute-start | bytes 1572872 | tf_op jit(solution)/shard_map/ppermute | solution.py:551
  453.6 28.2 %collective-permute-start.4 = (bf16[256,1024]{1,0:T(8,128)(2,1)}, bf16[256,1024]{1,0:T(8,128)(2,1)}, u32[]{:S(2)}, u32[]{:S(2)}) collective-permute-start(bf16[256,1024]{1,0:T(8,128)(2,1)} %get-tuple-element.88), channel_id=1, source_target_pairs={{0,2},{1,3},{4,0},{5,1},{8,4},{9,5},{12,8},{13,9},{14,12},{15,13},... | collective-permute-start | bytes 1572872 | tf_op jit(solution)/shard_map/ppermute | solution.py:551
  455.7 3.7 copy-start.2
  486.4 37.6 %collective-permute-start.5 = (bf16[512,1024]{1,0:T(8,128)(2,1)}, bf16[512,1024]{1,0:T(8,128)(2,1)}, u32[]{:S(2)}, u32[]{:S(2)}) collective-permute-start(bf16[512,1024]{1,0:T(8,128)(2,1)} %pad_maximum_fusion.5), channel_id=1, source_target_pairs={{0,4},{1,5},{4,8},{5,9},{8,12},{9,13},{12,14},{13,15},{14,10},{15,... | collective-permute-start | bytes 3145736 | tf_op jit(solution)/shard_map/ppermute | solution.py:551
  486.4 44.8 %collective-permute-start.6 = (bf16[512,1024]{1,0:T(8,128)(2,1)}, bf16[512,1024]{1,0:T(8,128)(2,1)}, u32[]{:S(2)}, u32[]{:S(2)}) collective-permute-start(bf16[512,1024]{1,0:T(8,128)(2,1)} %pad_maximum_fusion.6), channel_id=1, source_target_pairs={{0,2},{1,3},{4,0},{5,1},{8,4},{9,5},{12,8},{13,9},{14,12},{15,13},... | collective-permute-start | bytes 3145736 | tf_op jit(solution)/shard_map/ppermute | solution.py:551
  491.5 97.4 %all-to-all-start.2 = ((bf16[16,416,128]{2,1,0:T(8,128)(2,1)}), bf16[16,416,128]{2,1,0:T(8,128)(2,1)}, u32[]{:S(2)}, u32[]{:S(2)}) async-start(bf16[16,416,128]{2,1,0:T(8,128)(2,1)} %bitcast_bitcast_fusion), calls=%async_computation.3 | async-start | bytes 3407872 | tf_op jit(solution)/shard_map/all_to_all | solution.py:892
  495.9 52.4 %collective-permute-start.9 = (bf16[256,2048]{1,0:T(8,128)(2,1)S(1)}, bf16[256,2048]{1,0:T(8,128)(2,1)S(1)}, u32[]{:S(2)}, u32[]{:S(2)}) collective-permute-start(bf16[256,2048]{1,0:T(8,128)(2,1)S(1)} %convolution_convert_fusion.3), channel_id=1, source_target_pairs={{0,16},{16,0},{1,17},{17,1},{2,18},{18,2},{3,19},{19,3},{4,20},{20... | collective-permute-start | bytes 3145736 | tf_op jit(solution)/shard_map/ppermute | solution.py:661
  534.5 37.2 %collective-permute-start.7 = (bf16[512,1024]{1,0:T(8,128)(2,1)S(1)}, bf16[512,1024]{1,0:T(8,128)(2,1)S(1)}, u32[]{:S(2)}, u32[]{:S(2)}) collective-permute-start(bf16[512,1024]{1,0:T(8,128)(2,1)S(1)} %add_convert_fusion.4), channel_id=1, source_target_pairs={{0,4},{1,5},{4,8},{5,9},{8,12},{9,13},{12,14},{13,15},{14,10},{15,... | collective-permute-start | bytes 3145736 | tf_op jit(solution)/shard_map/ppermute | solution.py:551
  537.0 36.8 %collective-permute-start.8 = (bf16[512,1024]{1,0:T(8,128)(2,1)S(1)}, bf16[512,1024]{1,0:T(8,128)(2,1)S(1)}, u32[]{:S(2)}, u32[]{:S(2)}) collective-permute-start(bf16[512,1024]{1,0:T(8,128)(2,1)S(1)} %add_convert_fusion.3), channel_id=1, source_target_pairs={{0,2},{1,3},{4,0},{5,1},{8,4},{9,5},{12,8},{13,9},{14,12},{15,13},... | collective-permute-start | bytes 3145736 | tf_op jit(solution)/shard_map/ppermute | solution.py:551
  575.2 9.6 %copy-start.4 = (f32[256,2048]{1,0:T(8,128)S(1)}, f32[256,2048]{1,0:T(8,128)}, u32[]{:S(2)}) copy-start(f32[256,2048]{1,0:T(8,128)} %param.24) | copy-start | bytes 6291460
  575.2 9.6 %copy-start.5 = (f32[256,2048]{1,0:T(8,128)S(1)}, f32[256,2048]{1,0:T(8,128)}, u32[]{:S(2)}) copy-start(f32[256,2048]{1,0:T(8,128)} %param.23) | copy-start | bytes 6291460
  576.5 30.7 %collective-permute-start.10 = (bf16[512,1024]{1,0:T(8,128)(2,1)}, bf16[512,1024]{1,0:T(8,128)(2,1)}, u32[]{:S(2)}, u32[]{:S(2)}) collective-permute-start(bf16[512,1024]{1,0:T(8,128)(2,1)} %add_convert_fusion.2), channel_id=1, source_target_pairs={{0,4},{1,5},{4,8},{5,9},{8,12},{9,13},{12,14},{13,15},{14,10},{15,... | collective-permute-start | bytes 3145736 | tf_op jit(solution)/shard_map/ppermute | solution.py:551
  584.7 23.4 %collective-permute-start.11 = (bf16[512,1024]{1,0:T(8,128)(2,1)}, bf16[512,1024]{1,0:T(8,128)(2,1)}, u32[]{:S(2)}, u32[]{:S(2)}) collective-permute-start(bf16[512,1024]{1,0:T(8,128)(2,1)} %add_convert_fusion.1), channel_id=1, source_target_pairs={{0,2},{1,3},{4,0},{5,1},{8,4},{9,5},{12,8},{13,9},{14,12},{15,13},... | collective-permute-start | bytes 3145736 | tf_op jit(solution)/shard_map/ppermute | solution.py:551
  591.3 24.2 %collective-permute-start.13 = (bf16[16,256,128]{2,1,0:T(8,128)(2,1)}, bf16[16,256,128]{2,1,0:T(8,128)(2,1)S(1)}, u32[]{:S(2)}, u32[]{:S(2)}) collective-permute-start(bf16[16,256,128]{2,1,0:T(8,128)(2,1)} %slice.138.grad_ref), channel_id=1, source_target_pairs={{0,16},{16,0},{1,17},{17,1},{2,18},{18,2},{3,19},{19,3},{4,20},{20... | collective-permute-start | bytes 3145736 | tf_op jit(solution)/shard_map/ppermute | solution.py:661
  598.6 16.9 %collective-permute-start.14 = (bf16[160,128]{1,0:T(8,128)(2,1)S(1)}, bf16[160,128]{1,0:T(8,128)(2,1)S(1)}, u32[]{:S(2)}, u32[]{:S(2)}) collective-permute-start(bf16[160,128]{1,0:T(8,128)(2,1)S(1)} %slice_reduce_fusion), channel_id=1, source_target_pairs={{0,16},{16,0},{1,17},{17,1},{2,18},{18,2},{3,19},{19,3},{4,20},{20... | collective-permute-start | bytes 122888 | tf_op jit(solution)/shard_map/ppermute | solution.py:661
  615.5 3.7 copy-start.9
  620.6 3.2 collective-permute-start.15
  626.3 12.7 %collective-permute-start.16 = (f32[28096]{0:T(1024)S(1)}, f32[28096]{0:T(1024)S(1)}, u32[]{:S(2)}, u32[]{:S(2)}) collective-permute-start(f32[28096]{0:T(1024)S(1)} %concatenate.54), channel_id=1, source_target_pairs={{0,1},{1,0},{2,3},{3,2},{4,5},{5,4},{6,7},{7,6},{8,9},{9,8},{10,11... | collective-permute-start | bytes 337160 | tf_op jit(solution)/shard_map/ppermute | solution.py:739
  626.8 12.2 %collective-permute-start.17 = (f32[28096]{0:T(1024)S(1)}, f32[28096]{0:T(1024)S(1)}, u32[]{:S(2)}, u32[]{:S(2)}) collective-permute-start(f32[28096]{0:T(1024)S(1)} %concatenate.54), channel_id=1, source_target_pairs={{0,2},{1,3},{2,0},{3,1},{4,6},{5,7},{6,4},{7,5},{8,10},{9,11},{10,... | collective-permute-start | bytes 337160 | tf_op jit(solution)/shard_map/ppermute | solution.py:739
  628.6 10.4 %collective-permute-start.18 = (f32[28096]{0:T(1024)S(1)}, f32[28096]{0:T(1024)}, u32[]{:S(2)}, u32[]{:S(2)}) collective-permute-start(f32[28096]{0:T(1024)S(1)} %concatenate.54), channel_id=1, source_target_pairs={{0,3},{1,2},{2,1},{3,0},{4,7},{5,6},{6,5},{7,4},{8,11},{9,10},{10,... | collective-permute-start | bytes 337160 | tf_op jit(solution)/shard_map/ppermute | solution.py:739
  635.7 9.4 %copy-start.21 = (f32[256]{0:T(256)S(1)}, f32[256]{0:T(256)}, u32[]{:S(2)}) copy-start(f32[256]{0:T(256)} %copy-done.20) | copy-start | bytes 3076
  639.9 6.1 collective-permute-start.19
  642.5 11.8 %collective-permute-start.20 = (f32[28096]{0:T(1024)S(1)}, f32[28096]{0:T(1024)S(1)}, u32[]{:S(2)}, u32[]{:S(2)}) collective-permute-start(f32[28096]{0:T(1024)S(1)} %add_add_fusion.1), channel_id=1, source_target_pairs={{0,8},{1,9},{2,10},{3,11},{4,12},{5,13},{6,14},{7,15},{8,0},{9,1},... | collective-permute-start | bytes 337160 | tf_op jit(solution)/shard_map/ppermute | solution.py:739
  643.9 10.3 %collective-permute-start.21 = (f32[28096]{0:T(1024)S(1)}, f32[28096]{0:T(1024)S(1)}, u32[]{:S(2)}, u32[]{:S(2)}) collective-permute-start(f32[28096]{0:T(1024)S(1)} %add_add_fusion.1), channel_id=1, source_target_pairs={{0,12},{1,13},{2,14},{3,15},{4,8},{5,9},{6,10},{7,11},{8,4},{9,5},... | collective-permute-start | bytes 337160 | tf_op jit(solution)/shard_map/ppermute | solution.py:739
  654.3 4.9 collective-permute-start.22
  655.0 4.1 copy-start.11
  655.0 4.1 copy-start.14
  655.0 4.1 copy-start.15
  655.1 4.1 copy-start.16
  655.1 4.1 copy-start.17
  (13 other events, 29.1 us)
Sparse Core Ops, SparseCore 0:
  13.3 176.8 all-gather.4
  192.3 125.8 all-gather.6
  322.3 194.0 reduce-scatter.1

commit v5 on v4

--- a/solution.py
+++ b/solution.py
@@ -568,6 +568,110 @@
     return jnp.where(spot < 4, spot * 2, (7 - spot) * 2 + 1)
 
 
+def absorb_kernel(count, by_rows, starts_ref, *refs):
+    pieces = refs[:count]
+    weight_ref = refs[count]
+    kept_ref, product_ref, held = refs[-3:]
+    for j in range(count):
+
+        @pl.when(pl.program_id(0) == j)
+        def _(j=j):
+            held[...] = pieces[j][...]
+
+    values = held[...]
+    kept_ref[...] = values
+    product_ref[...] = lax.dot_general(
+        values,
+        weight_ref[...],
+        (((1,), (1 if by_rows else 0,)), ((), ())),
+        preferred_element_type=F32,
+    ).astype(product_ref.dtype)
+
+
+def absorb(pieces, starts, total, filled, weight, by_rows, kind):
+    size, depth = pieces[0].shape
+    columns = weight.shape[0 if by_rows else 1]
+    count = len(pieces)
+    whole = lambda a: pl.BlockSpec(a.shape, lambda i, at: (0, 0))
+    placed = lambda w: pl.BlockSpec((size, w), lambda i, at: (at[i], 0))
+    return pl.pallas_call(
+        partial(absorb_kernel, count, by_rows),
+        grid_spec=pltpu.PrefetchScalarGridSpec(
+            num_scalar_prefetch=1,
+            grid=(count,),
+            in_specs=[whole(piece) for piece in pieces]
+            + [whole(weight)]
+            + [pl.BlockSpec(memory_space=pl.ANY)] * len(filled),
+            out_specs=[placed(depth), placed(columns)],
+            scratch_shapes=[pltpu.VMEM((size, depth), BF)],
+        ),
+        out_shape=[
+            jax.ShapeDtypeStruct((total, depth), BF),
+            jax.ShapeDtypeStruct((total, columns), kind),
+        ],
+        input_output_aliases={count + 2: 0, count + 3: 1} if filled else {},
+        cost_estimate=pl.CostEstimate(
+            flops=40 * count * size * depth * columns,
+            bytes_accessed=4 * count * size * depth + 2 * depth * columns,
+            transcendentals=0,
+        ),
+        name="absorb_rows",
+    )(starts, *pieces, weight, *filled)
+
+
+class Gather:
+    def __init__(self, values):
+        self.rows = values.shape[0]
+        self.core, self.spot = ring_place()
+        self.last = (values, values)
+        self.arrived = [((values, ring_chip(self.spot), 0),)]
+        self.swapped = []
+        self.sent = self.filled = ()
+
+    def settle(self, *others):
+        self.last, self.filled, _ = lax.optimization_barrier((self.last, self.filled, others))
+        step = len(self.swapped)
+        if step:
+            offset = self.rows // 2 if step == 4 else 0
+            self.arrived.append(
+                (
+                    (self.last[0], ring_chip(self.spot - step), 0),
+                    (self.last[1], ring_chip(self.spot + step), offset),
+                )
+            )
+        self.swapped.append([by_row(swap(by_row(piece))) for piece, _, _ in self.arrived[-1]])
+
+    def advance(self):
+        ahead, behind = self.last
+        if len(self.swapped) == 4:
+            ahead, behind = ahead[: self.rows // 2], behind[self.rows // 2 :]
+        self.sent, self.swapped[-1] = lax.optimization_barrier(
+            ((ahead, behind), self.swapped[-1])
+        )
+        ahead, behind = self.sent
+        self.last = (by_row(hop(by_row(ahead), 1)), by_row(hop(by_row(behind), -1)))
+
+    def take(self, weight, *hops):
+        pieces, starts = [], []
+        for k in hops:
+            for (piece, chip, offset), other in zip(self.arrived[k], self.swapped[k]):
+                for part, core in ((piece, self.core), (other, 1 - self.core)):
+                    pieces.append(part)
+                    starts.append(((2 * chip + core) * self.rows + offset) // piece.shape[0])
+        pieces, _ = lax.optimization_barrier((pieces, self.sent))
+        self.filled = tuple(
+            absorb(
+                pieces,
+                jnp.stack(starts).astype(jnp.int32),
+                16 * self.rows,
+                self.filled,
+                weight,
+                False,
+                BF,
+            )
+        )
+
+
 class RingSum:
     def __init__(self, chunk, rows):
         self.chunk = chunk
@@ -666,19 +770,44 @@
     return jnp.where(first, mine, other), jnp.where(first, other, mine)
 
 
-def same_core():
-    return [[2 * chip + core for chip in range(8)] for core in (0, 1)]
-
-
-def gather_blocks(block):
-    if lax.axis_size("dp") != 16:
-        return lax.all_gather(block, "dp")
-    copies = jnp.broadcast_to(block[None], (8,) + block.shape)
-    mine = lax.all_to_all(copies, "dp", 0, 0, axis_index_groups=same_core())
-    theirs = swap(mine)
-    first = lax.axis_index("dp") % 2 == 0
-    pair = jnp.stack([jnp.where(first, mine, theirs), jnp.where(first, theirs, mine)], axis=1)
-    return pair.reshape((16,) + block.shape)
+def weight_halves(weight_low, units):
+    dp = lax.axis_size("dp")
+    heads = weight_low[: 2 * E].reshape(2, dp, units, weight_low.shape[1])
+    common = weight_low[2 * E :]
+    if lax.axis_size("width") == 2:
+        slot = lax.axis_index("width")
+        heads = lax.dynamic_slice_in_dim(heads, slot, 1, 0)
+        common = lax.dynamic_slice_in_dim(common, slot * (SHARED // 2), SHARED // 2, 0)
+    return jnp.concatenate(
+        [
+            heads.transpose(1, 0, 2, 3).reshape(dp, -1, heads.shape[3]),
+            jnp.broadcast_to(common[None], (dp,) + common.shape),
+        ],
+        axis=1,
+    )
+
+
+def join_weight(mine, units, wide, *gate):
+    own_heads = units // P_SIZE
+    if lax.axis_size("width") == 2:
+        other = after(other_width(mine), gate)
+        first, second = in_order(mine, other)
+        gate_rows, x_rows = first[:units], second[:units]
+        shared = jnp.concatenate([first[units:], second[units:]], axis=0)
+    else:
+        gate_rows, x_rows, shared = mine[:units], mine[units : 2 * units], mine[2 * units :]
+    own_dt = lax.dynamic_slice_in_dim(
+        shared, 2 * N + lax.axis_index("dp") * own_heads, own_heads, 0
+    )
+    return jnp.concatenate(
+        [
+            pad_to(gate_rows, wide, 0),
+            pad_to(x_rows, wide, 0),
+            shared[: 2 * N],
+            pad_to(own_dt, 128, 0),
+        ],
+        axis=0,
+    ).T
 
 
 def adamw_kernel(first_ref, base_ref, weight_ref, moment_ref, second_ref, grad_ref, *refs):
@@ -788,23 +917,15 @@
     g_in, g_out, conv_w, conv_b, a_log, dt_bias, d_skip = unpack(small_params)
     normed_low = (inputs_f * root * g_in).astype(BF)
     weight_low = weight_in.T.astype(BF)
-    normed_all = lax.all_gather(normed_low, "dp", axis=0, tiled=True)
-    pairs = jnp.concatenate(
-        [weight_low[:E].reshape(dp, units, shard), weight_low[E : 2 * E].reshape(dp, units, shard)],
-        axis=1,
-    )
-    own_cols = lax.all_to_all(pairs, "dp", 0, 0).transpose(1, 0, 2).reshape(2 * units, D).T
-    shared = gather_blocks(weight_low[2 * E :]).transpose(1, 0, 2).reshape(SHARED, D).T
-    own_dt = lax.dynamic_slice_in_dim(shared, 2 * N + here * own_heads, own_heads, 1)
-    weight_own = jnp.concatenate(
-        [
-            pad_to(own_cols[:, :units], wide, 1),
-            pad_to(own_cols[:, units:], wide, 1),
-            shared[:, : 2 * N],
-            pad_to(own_dt, 128, 1),
-        ],
-        axis=1,
-    )
+    ring = dp == 16
+    if ring:
+        gather = Gather(by_row(normed_low))
+        gather.settle()
+        gather.advance()
+    else:
+        normed_all = lax.all_gather(normed_low, "dp", axis=0, tiled=True)
+    mine = lax.all_to_all(weight_halves(weight_low, units), "dp", 0, 0)
+    mine = mine.transpose(1, 0, 2).reshape(-1, D)
     out_weight_low = by_row(pad_to(weight_out.astype(BF), wide, 0))
 
     live_units = jnp.right_shift(jnp.int32(E), lax.axis_size("width") - 1 - levels[0])
@@ -834,10 +955,28 @@
         pad_to(jnp.stack([own_h(dt_bias), -jnp.exp(own_h(a_log))]), 128, 1), 8, 0
     )
 
-    cotangent_all = lax.all_gather(
-        after(cotangent, normed_all, weight_own), "dp", axis=0, tiled=True
-    )
-    projected = jnp.dot(normed_all, weight_own, preferred_element_type=F32).astype(BF)
+    if ring:
+        gather.settle(mine, place, remain)
+        gather.advance()
+        mine = after(mine, gather.sent)
+        released = after(cotangent, gather.sent)
+        gather.settle()
+        gather.advance()
+        weight_own = by_row(join_weight(mine, units, wide, gather.sent))
+        gather.take(weight_own, 0, 1)
+        gather.take(weight_own, 2)
+        gather.settle()
+        gather.advance()
+        gather.take(weight_own, 3)
+        gather.settle()
+        gather.sent = ()
+        gather.take(weight_own, 4)
+        normed_all, projected = gather.filled
+    else:
+        weight_own = join_weight(mine, units, wide)
+        released = after(cotangent, normed_all, weight_own)
+        projected = jnp.dot(normed_all, weight_own, preferred_element_type=F32).astype(BF)
+    cotangent_all = lax.all_gather(released, "dp", axis=0, tiled=True)
     carried = (jnp.zeros((wide, N), F32),)
     for begin, end in cuts(total // STRETCH, FRONT_PARTS):
         carried = run_forward(

time: 672 us -> 633 us (0.942)
  waiting for transfers between devices: 276 us -> 202 us
  Pallas kernels: 95.1 us -> 137 us
  matrix products: 113 us -> 96.5 us
  starting transfers between devices: 45.8 us -> 60.7 us
  other arithmetic: 62.5 us -> 52.5 us
    all_gather x2 -> x1, waiting for transfers between devices: 125 us -> 0.02 us  [per_device(): cotangent_all = lax.all_gather(released, 'dp', axis=0, tiled=True)]
    ppermute x8 -> x16, waiting for transfers between devices: 59.9 us -> 142 us  [hop(): return lax.ppermute(values, 'dp', pairs)]
    all_to_all x2 -> x1, waiting for transfers between devices: 73.1 us -> 24.4 us  [per_device(): mine = lax.all_to_all(weight_halves(weight_low, units), 'dp', 0, 0)]
    pallas_call x0 -> x4, Pallas kernels: none -> 41.9 us  [absorb(): pl.pallas_call(partial(absorb_kernel, count, by_rows), grid_spec=pltpu.Pr...]
    dot_general x1 -> x0, matrix products: 22 us -> none  [per_device(): jnp.dot(normed_all, weight_own, preferred_element_type=F32).astype(BF)]
    ppermute x8 -> x16, starting transfers between devices: 15.1 us -> 31.6 us  [hop(): return lax.ppermute(values, 'dp', pairs)]
    ppermute x4 -> x5, waiting for transfers between devices: 7.35 us -> 19.1 us  [other_width(): return lax.ppermute(values, 'width', [(0, 1), (1, 0)])]
  transfers between devices with their start and end apart: 29 -> 44, of which waited for: 16 -> 25; matrix products, arithmetic and copies ran while one was open for 31% -> 29% of each run, Pallas kernels for 14% -> 22%
where the time goes in v5:
time: 633 us; the launch traced here: 624 us
  waiting for transfers between devices  202 us (32%)
  Pallas kernels  137 us (22%)
  matrix products  96.5 us (15%)
  starting transfers between devices  60.7 us (10%)
  other arithmetic  52.5 us (8%)
  local copies, waits for them, and re-layouts  37.2 us (6%)
  blocking collectives  20.6 us (3%)
  between operations  16.9 us (3%)
    ppermute x16, waiting for transfers between devices, hop(): return lax.ppermute(values, 'dp', pairs)  142 us
    pallas_call x1, Pallas kernels, run_backward(): pl.pallas_call(partial(backward_kernel, heads), grid=(count,), in_specs=[...  51.2 us
    dot_general x16, matrix products, chunk(): jnp.dot(lax.dynamic_slice_in_dim(after(side, deps), start, rows, 0), weig...  47.4 us
    pallas_call x4, Pallas kernels, absorb(): pl.pallas_call(partial(absorb_kernel, count, by_rows), grid_spec=pltpu.Pr...  41.9 us
    ppermute x16, starting transfers between devices, hop(): return lax.ppermute(values, 'dp', pairs)  31.6 us
    pallas_call x1, Pallas kernels, run_forward(): pl.pallas_call(partial(forward_kernel, heads), grid=(count,), in_specs=[r...  26.6 us
    all_to_all x1, waiting for transfers between devices, per_device(): mine = lax.all_to_all(weight_halves(weight_low, units), 'dp', 0, 0)  24.4 us
    all_gather x1, blocking collectives, per_device(): lax.all_gather(jnp.stack([square[:, 0], pull_part]), 'dp')  20.6 us
  transfers between devices with their start and end apart: 44, of which 25 were waited for; matrix products, arithmetic and copies ran while one was open for 29% of the time, Pallas kernels for 22%

profile of v5, /device:TPU:0, one launch (start us, length us, event | category | flops | bytes accessed | tf_op | source)
XLA Modules:
  0.0 623.8 jit_solution(9479134818702366241)
XLA Ops:
  11.3 7.5 %all-to-all-start = ((bf16[16,416,128]{2,1,0:T(8,128)(2,1)}), bf16[16,416,128]{2,1,0:T(8,128)(2,1)}, u32[]{:S(2)}, u32[]{:S(2)}) async-start(bf16[16,416,128]{2,1,0:T(8,128)(2,1)} %pad_maximum_fusion.1), calls=%async_computation | async-start | bytes 3407872 | tf_op jit(solution)/shard_map/all_to_all | solution.py:927
  25.0 3.9 iota_subtract_fusion
  28.9 24.4 %all-to-all-done = bf16[16,416,128]{2,1,0:T(8,128)(2,1)} async-done(((bf16[16,416,128]{2,1,0:T(8,128)(2,1)}), bf16[16,416,128]{2,1,0:T(8,128)(2,1)}, u32[]{:S(2)}, u32[]{:S(2)}) %all-to-all-start) | async-done | bytes 1703968 | tf_op jit(solution)/shard_map/all_to_all | solution.py:927
  56.1 13.8 %collective-permute-done.1.refs_2_ = bf16[256,2048]{1,0:T(8,128)(2,1)} collective-permute-done((bf16[256,2048]{1,0:T(8,128)(2,1)S(1)}, bf16[256,2048]{1,0:T(8,128)(2,1)}, u32[]{:S(2)}, u32[]{:S(2)}) %collective-permute-start.1) | collective-permute-done | bytes 1048608 | tf_op jit(solution)/shard_map/ppermute | solution.py:551
  72.4 3.8 collective-permute-done.3.refs_3_
  76.4 10.7 %collective-permute-start.5 = (bf16[256,2048]{1,0:T(8,128)(2,1)}, bf16[256,2048]{1,0:T(8,128)(2,1)}, u32[]{:S(2)}, u32[]{:S(2)}) collective-permute-start(bf16[256,2048]{1,0:T(8,128)(2,1)} %collective-permute-done.1.refs_2_), channel_id=1, source_target_pairs={{0,4},{1,5},{4,8},{5,9},{8,12},{9,13},{12,14},{13,15},{14,10},{15,... | collective-permute-start | bytes 3145736 | tf_op jit(solution)/shard_map/ppermute | solution.py:551
  90.8 19.3 %collective-permute-done.5.refs_0_ = bf16[256,2048]{1,0:T(8,128)(2,1)} collective-permute-done((bf16[256,2048]{1,0:T(8,128)(2,1)}, bf16[256,2048]{1,0:T(8,128)(2,1)}, u32[]{:S(2)}, u32[]{:S(2)}) %collective-permute-start.5) | collective-permute-done | bytes 1048608 | tf_op jit(solution)/shard_map/ppermute | solution.py:551
  116.8 11.8 %collective-permute-done.11 = bf16[416,2048]{1,0:T(8,128)(2,1)} collective-permute-done((bf16[416,2048]{1,0:T(8,128)(2,1)}, bf16[416,2048]{1,0:T(8,128)(2,1)}, u32[]{:S(2)}, u32[]{:S(2)}) %collective-permute-start.11) | collective-permute-done | bytes 1703968 | tf_op jit(solution)/shard_map/ppermute | solution.py:765
  128.6 3.8 copy.87
  139.6 13.8 %absorb_rows.4 = (bf16[4096,2048]{1,0:T(8,128)(2,1)}, bf16[4096,896]{1,0:T(8,128)(2,1)}) custom-call(s32[6]{0:T(128)} %stack.106.starts_ref, bf16[256,2048]{1,0:T(8,128)(2,1)} %copy-done.11, bf16[256,2048]{1,0:T(8,128)(2,1)} %collective-permute-done.refs_1_, bf16[256,2048]{1,0:T(8,128)(2,1)} %collective-permute-done.1.refs_2_, bf16[256,2048]{1,0:T(8,128)(2,1)} %copy-done.27, ...), custom_call_target="tpu_custom_call" | custom-call | flops 112742891520 | bytes 16252928 | tf_op jit(solution)/shard_map/absorb_rows/pallas_call | solution.py:597
  153.3 10.4 %absorb_rows.5 = (bf16[4096,2048]{1,0:T(8,128)(2,1)}, bf16[4096,896]{1,0:T(8,128)(2,1)}) custom-call(s32[4]{0:T(128)} %get-tuple-element.297.starts_ref, bf16[256,2048]{1,0:T(8,128)(2,1)} %collective-permute-done.5.refs_0_, bf16[256,2048]{1,0:T(8,128)(2,1)} %collective-permute-done.7.refs_1_, ...), custom_call_target="tpu_custom_call", output_to_operand_aliasing={{0}: (6, {}), {1}: (7, {})} | custom-call | flops 75161927680 | bytes 12058624 | tf_op jit(solution)/shard_map/absorb_rows/pallas_call | solution.py:597
  163.8 17.5 %collective-permute-done.10.refs_2_ = bf16[256,2048]{1,0:T(8,128)(2,1)} collective-permute-done((bf16[256,2048]{1,0:T(8,128)(2,1)}, bf16[256,2048]{1,0:T(8,128)(2,1)}, u32[]{:S(2)}, u32[]{:S(2)}) %collective-permute-start.10) | collective-permute-done | bytes 1048608 | tf_op jit(solution)/shard_map/ppermute | solution.py:551
  188.2 10.3 %absorb_rows.6 = (bf16[4096,2048]{1,0:T(8,128)(2,1)}, bf16[4096,896]{1,0:T(8,128)(2,1)}) custom-call(s32[4]{0:T(128)} %pad_add_fusion.2.starts_ref, bf16[256,2048]{1,0:T(8,128)(2,1)} %collective-permute-done.9.refs_0_, bf16[256,2048]{1,0:T(8,128)(2,1)} %copy-done.28, ...), custom_call_target="tpu_custom_call", output_to_operand_aliasing={{0}: (6, {}), {1}: (7, {})} | custom-call | flops 75161927680 | bytes 12058624 | tf_op jit(solution)/shard_map/absorb_rows/pallas_call | solution.py:597
  198.5 12.8 %collective-permute-done.14.refs_0_ = bf16[128,2048]{1,0:T(8,128)(2,1)} collective-permute-done((bf16[128,2048]{1,0:T(8,128)(2,1)S(1)}, bf16[128,2048]{1,0:T(8,128)(2,1)}, u32[]{:S(2)}, u32[]{:S(2)}) %collective-permute-start.14) | collective-permute-done | bytes 524320 | tf_op jit(solution)/shard_map/ppermute | solution.py:551
  211.3 13.8 %collective-permute-done.15.refs_2_ = bf16[128,2048]{1,0:T(8,128)(2,1)} collective-permute-done((bf16[128,2048]{1,0:T(8,128)(2,1)S(1)}, bf16[128,2048]{1,0:T(8,128)(2,1)}, u32[]{:S(2)}, u32[]{:S(2)}) %collective-permute-start.15) | collective-permute-done | bytes 524320 | tf_op jit(solution)/shard_map/ppermute | solution.py:551
  228.8 7.3 %absorb_rows.7 = (bf16[4096,2048]{1,0:T(8,128)(2,1)}, bf16[4096,896]{1,0:T(8,128)(2,1)}) custom-call(s32[4]{0:T(128)} %get-tuple-element.296.starts_ref, bf16[128,2048]{1,0:T(8,128)(2,1)} %collective-permute-done.14.refs_0_, bf16[128,2048]{1,0:T(8,128)(2,1)} %copy-done.30, ...), custom_call_target="tpu_custom_call", output_to_operand_aliasing={{0}: (6, {}), {1}: (7, {})} | custom-call | flops 37580963840 | bytes 7864320 | tf_op jit(solution)/shard_map/absorb_rows/pallas_call | solution.py:597
  236.7 26.6 %scan_forward.1 = (bf16[4096,256]{1,0:T(8,128)(2,1)}, f32[4096,256]{1,0:T(8,128)}, f32[4096,1]{1,0:T(8,128)}, f32[16,256,128]{2,1,0:T(8,128)}, f32[256,128]{1,0:T(8,128)}) custom-call(bf16[4096,896]{1,0:T(8,128)(2,1)} %get-tuple-element.189.gate_ref.x_ref.bc_ref.dt_ref.xprev_ref.bcprev_ref, ...), custom_call_target="tpu_custom_call" | custom-call | flops 20971520000 | bytes 20480000 | tf_op jit(solution)/shard_map/scan_forward/pallas_call | solution.py:399
  265.8 9.8 %convolution_convert_fusion = bf16[4096,2048]{1,0:T(8,128)(2,1)} fusion(bf16[4096,256]{1,0:T(8,128)(2,1)} %get-tuple-element.190, f32[256,2048]{1,0:T(8,128)S(1)} %copy-done.2), kind=kOutput, calls=%fused_computation | convolution fusion | flops 4303880192 | bytes 20971520 | tf_op jit(solution)/shard_map/dot_general | solution.py:986
  275.6 14.3 %multiply_reduce_fusion = (f32[4096]{0:T(1024)S(1)}, f32[4096,256]{1,0:T(8,128)}) fusion(bf16[4096,256]{1,0:T(8,128)(2,1)} %get-tuple-element.190, bf16[4096,2048]{1,0:T(8,128)(2,1)} %all-gather.4.cloned.1.call-done, f32[256,2048]{1,0:T(8,128)S(1)} %copy-done.2), kind=kOutput, calls=%fused_computation.9 | convolution fusion | flops 4298633216 | bytes 25182208 | tf_op jit(solution)/shard_map/dot_general | solution.py:988
  289.9 20.6 %all-gather.1 = f32[16,2,4096]{2,1,0:T(2,128)S(1)} all-gather(f32[1,2,4096]{2,1,0:T(2,128)S(1)} %maximum_bitcast_fusion), channel_id=2, replica_groups=mesh['width'=2,'dp'=16] {'dp'}, dimensions={0}, use_global_device_ids=true | all-gather | bytes 557056 | tf_op jit(solution)/shard_map/all_gather | solution.py:992
  316.7 4.5 divide_multiply_fusion.pull_ref
  322.4 51.2 %scan_backward.1 = (bf16[4096,896]{1,0:T(8,128)(2,1)}, bf16[4096,256]{1,0:T(8,128)(2,1)}, f32[256,128]{1,0:T(8,128)}, f32[16,256]{1,0:T(8,128)}, f32[16,256]{1,0:T(8,128)}, /*index=5*/f32[8,128]{1,0:T(8,128)}) custom-call(bf16[4096,896]{1,0:T(8,128)(2,1)} %get-tuple-element.189.gate_ref.x_ref.bc_ref.dt_ref.xprev_ref.bcprev_ref, ...), custom_call_target="tpu_custom_call" | custom-call | flops 41943040000 | bytes 32768000 | tf_op jit(solution)/shard_map/scan_backward/pallas_call | solution.py:467
  374.7 4.2 dynamic-slice_bitcast_fusion
  379.3 20.5 %convolution_convert_fusion.1 = bf16[896,2048]{1,0:T(8,128)(2,1)S(1)} fusion(bf16[4096,896]{1,0:T(8,128)(2,1)} %get-tuple-element.230, bf16[4096,2048]{1,0:T(8,128)(2,1)} %get-tuple-element.196), kind=kOutput, calls=%fused_computation.12 | convolution fusion | flops 15034220544 | bytes 27787264 | tf_op jit(solution)/shard_map/dot_general | solution.py:1014
  405.0 3.3 fusion.41
  408.3 3.0 convolution_add_fusion.7
  414.3 4.6 fusion.35
  419.2 4.5 convolution_convert_fusion.2
  423.7 3.2 convolution_add_fusion.5
  426.9 3.1 fusion.38
  434.9 11.3 %collective-permute-done.21 = bf16[256,1024]{1,0:T(8,128)(2,1)S(1)} collective-permute-done((bf16[256,1024]{1,0:T(8,128)(2,1)S(1)}, bf16[256,1024]{1,0:T(8,128)(2,1)S(1)}, u32[]{:S(2)}, u32[]{:S(2)}) %collective-permute-start.21) | collective-permute-done | bytes 524320 | tf_op jit(solution)/shard_map/ppermute | solution.py:551
  452.5 4.4 all-to-all-start.1
  457.5 3.1 fusion.29
  460.6 3.2 fusion.32
  468.7 13.9 %collective-permute-done.22 = bf16[512,1024]{1,0:T(8,128)(2,1)} collective-permute-done((bf16[512,1024]{1,0:T(8,128)(2,1)}, bf16[512,1024]{1,0:T(8,128)(2,1)}, u32[]{:S(2)}, u32[]{:S(2)}) %collective-permute-start.22) | collective-permute-done | bytes 1048608 | tf_op jit(solution)/shard_map/ppermute | solution.py:551
  482.6 7.4 %collective-permute-done.23 = bf16[512,1024]{1,0:T(8,128)(2,1)} collective-permute-done((bf16[512,1024]{1,0:T(8,128)(2,1)}, bf16[512,1024]{1,0:T(8,128)(2,1)}, u32[]{:S(2)}, u32[]{:S(2)}) %collective-permute-start.23) | collective-permute-done | bytes 1048608 | tf_op jit(solution)/shard_map/ppermute | solution.py:551
  495.5 3.1 fusion.23
  501.0 3.1 fusion.26
  507.0 23.2 %collective-permute-done.24 = bf16[512,1024]{1,0:T(8,128)(2,1)S(1)} collective-permute-done((bf16[512,1024]{1,0:T(8,128)(2,1)S(1)}, bf16[512,1024]{1,0:T(8,128)(2,1)S(1)}, u32[]{:S(2)}, u32[]{:S(2)}) %collective-permute-start.24) | collective-permute-done | bytes 1048608 | tf_op jit(solution)/shard_map/ppermute | solution.py:551
  534.8 8.1 %collective-permute-start.27 = (bf16[512,1024]{1,0:T(8,128)(2,1)}, bf16[512,1024]{1,0:T(8,128)(2,1)}, u32[]{:S(2)}, u32[]{:S(2)}) collective-permute-start(bf16[512,1024]{1,0:T(8,128)(2,1)} %add_convert_fusion.2), channel_id=1, source_target_pairs={{0,4},{1,5},{4,8},{5,9},{8,12},{9,13},{12,14},{13,15},{14,10},{15,... | collective-permute-start | bytes 3145736 | tf_op jit(solution)/shard_map/ppermute | solution.py:551
  542.9 4.2 fusion.72
  549.9 3.1 fusion.20
  558.2 7.0 %adamw.3 = (f32[8512,128]{1,0:T(8,128)}, f32[8512,128]{1,0:T(8,128)}, f32[8512,128]{1,0:T(8,128)}, bf16[8512,128]{1,0:T(8,128)(2,1)}) custom-call(s32[1]{0:T(128)} %bitcast.47.first_ref, f32[1,1]{1,0:T(1,128)} %bitcast.48.base_ref, f32[8512,128]{1,0:T(8,128)} %bitcast.104, f32[8512,128]{1,0:T(8,128)} %bitcast.111, f32[8512,128]{1,0:T(8,128)} %bitcast.114, ...), custom_call_target="tpu_custom_call" | custom-call | flops 5242880000 | bytes 15728640 | tf_op jit(solution)/shard_map/adamw/pallas_call | solution.py:841
  565.9 7.3 %collective-permute-done.31 = bf16[160,128]{1,0:T(8,128)(2,1)S(1)} collective-permute-done((bf16[160,128]{1,0:T(8,128)(2,1)S(1)}, bf16[160,128]{1,0:T(8,128)(2,1)S(1)}, u32[]{:S(2)}, u32[]{:S(2)}) %collective-permute-start.31) | collective-permute-done | bytes 40992 | tf_op jit(solution)/shard_map/ppermute | solution.py:765
  585.2 7.0 %adamw.4 = (f32[8512,128]{1,0:T(8,128)}, f32[8512,128]{1,0:T(8,128)}, f32[8512,128]{1,0:T(8,128)}, bf16[8512,128]{1,0:T(8,128)(2,1)}) custom-call(s32[1]{0:T(128)} %bitcast.51.first_ref, f32[1,1]{1,0:T(1,128)} %bitcast.48.base_ref, f32[8512,128]{1,0:T(8,128)} %bitcast.105, ...), custom_call_target="tpu_custom_call", output_to_operand_aliasing={{0}: (6, {}), {1}: (7, {}), {2}: (8, {}), {3}: (9, {})} | custom-call | flops 5242880000 | bytes 15728640 | tf_op jit(solution)/shard_map/adamw/pallas_call | solution.py:841
  592.2 3.3 adamw.5
  602.6 8.2 %collective-permute-done.37 = f32[28096]{0:T(1024)S(1)} collective-permute-done((f32[28096]{0:T(1024)S(1)}, f32[28096]{0:T(1024)S(1)}, u32[]{:S(2)}, u32[]{:S(2)}) %collective-permute-start.37) | collective-permute-done | bytes 112416 | tf_op jit(solution)/shard_map/ppermute | solution.py:868
  611.6 3.9 fusion.11
  (266 shorter events, 124.0 us)
Async XLA Ops:
  11.3 42.1 %all-to-all-start = ((bf16[16,416,128]{2,1,0:T(8,128)(2,1)}), bf16[16,416,128]{2,1,0:T(8,128)(2,1)}, u32[]{:S(2)}, u32[]{:S(2)}) async-start(bf16[16,416,128]{2,1,0:T(8,128)(2,1)} %pad_maximum_fusion.1), calls=%async_computation | async-start | bytes 3407872 | tf_op jit(solution)/shard_map/all_to_all | solution.py:927
  18.8 256.8 %all-gather.4.cloned.1.call-start = ((), (), s32[]{:S(2)}) async-start(), calls=%async_computation.4 | async-start | bytes 17825792 | tf_op jit(solution)/shard_map/all_gather | solution.py:979
  19.5 3.5 collective-permute-start
  23.0 46.8 %collective-permute-start.1 = (bf16[256,2048]{1,0:T(8,128)(2,1)S(1)}, bf16[256,2048]{1,0:T(8,128)(2,1)}, u32[]{:S(2)}, u32[]{:S(2)}) collective-permute-start(bf16[256,2048]{1,0:T(8,128)(2,1)S(1)} %fusion.6.refs_0_), channel_id=1, source_target_pairs={{0,4},{1,5},{4,8},{5,9},{8,12},{9,13},{12,14},{13,15},{14,10},{15,... | collective-permute-start | bytes 3145736 | tf_op jit(solution)/shard_map/ppermute | solution.py:551
  24.7 47.2 %collective-permute-start.2 = (bf16[256,2048]{1,0:T(8,128)(2,1)S(1)}, bf16[256,2048]{1,0:T(8,128)(2,1)}, u32[]{:S(2)}, u32[]{:S(2)}) collective-permute-start(bf16[256,2048]{1,0:T(8,128)(2,1)S(1)} %fusion.6.refs_0_), channel_id=1, source_target_pairs={{0,2},{1,3},{4,0},{5,1},{8,4},{9,5},{12,8},{13,9},{14,12},{15,13},... | collective-permute-start | bytes 3145736 | tf_op jit(solution)/shard_map/ppermute | solution.py:551
  71.9 4.3 collective-permute-start.3
  71.9 4.5 collective-permute-start.4
  76.2 36.6 %copy-start.27 = (bf16[256,2048]{1,0:T(8,128)(2,1)}, bf16[256,2048]{1,0:T(8,128)(2,1)S(1)}, u32[]{:S(2)}) copy-start(bf16[256,2048]{1,0:T(8,128)(2,1)S(1)} %collective-permute-done.3.refs_3_) | copy-start | bytes 3145732
  76.4 33.7 %collective-permute-start.5 = (bf16[256,2048]{1,0:T(8,128)(2,1)}, bf16[256,2048]{1,0:T(8,128)(2,1)}, u32[]{:S(2)}, u32[]{:S(2)}) collective-permute-start(bf16[256,2048]{1,0:T(8,128)(2,1)} %collective-permute-done.1.refs_2_), channel_id=1, source_target_pairs={{0,4},{1,5},{4,8},{5,9},{8,12},{9,13},{12,14},{13,15},{14,10},{15,... | collective-permute-start | bytes 3145736 | tf_op jit(solution)/shard_map/ppermute | solution.py:551
  87.1 25.2 %collective-permute-start.6 = (bf16[256,2048]{1,0:T(8,128)(2,1)}, bf16[256,2048]{1,0:T(8,128)(2,1)}, u32[]{:S(2)}, u32[]{:S(2)}) collective-permute-start(bf16[256,2048]{1,0:T(8,128)(2,1)} %collective-permute-done.2.refs_4_), channel_id=1, source_target_pairs={{0,2},{1,3},{4,0},{5,1},{8,4},{9,5},{12,8},{13,9},{14,12},{15,13},... | collective-permute-start | bytes 3145736 | tf_op jit(solution)/shard_map/ppermute | solution.py:551
  89.3 39.3 %collective-permute-start.11 = (bf16[416,2048]{1,0:T(8,128)(2,1)}, bf16[416,2048]{1,0:T(8,128)(2,1)}, u32[]{:S(2)}, u32[]{:S(2)}) collective-permute-start(bf16[416,2048]{1,0:T(8,128)(2,1)} %copy.86), channel_id=1, source_target_pairs={{0,16},{16,0},{1,17},{17,1},{2,18},{18,2},{3,19},{19,3},{4,20},{20... | collective-permute-start | bytes 5111816 | tf_op jit(solution)/shard_map/ppermute | solution.py:765
  112.3 3.0 collective-permute-start.7
  112.3 4.5 collective-permute-start.8
  114.1 497.5 %reduce-scatter.2.cloned.1.call-start = ((), (), s32[]{:S(2)}) async-start(), calls=%async_computation.3 | async-start | bytes 17825792 | tf_op jit(solution)/shard_map/reduce_scatter | solution.py:987
  134.6 46.7 %collective-permute-start.10 = (bf16[256,2048]{1,0:T(8,128)(2,1)}, bf16[256,2048]{1,0:T(8,128)(2,1)}, u32[]{:S(2)}, u32[]{:S(2)}) collective-permute-start(bf16[256,2048]{1,0:T(8,128)(2,1)} %collective-permute-done.6.refs_2_), channel_id=1, source_target_pairs={{0,2},{1,3},{4,0},{5,1},{8,4},{9,5},{12,8},{13,9},{14,12},{15,13},... | collective-permute-start | bytes 3145736 | tf_op jit(solution)/shard_map/ppermute | solution.py:551
  136.2 45.1 %collective-permute-start.9 = (bf16[256,2048]{1,0:T(8,128)(2,1)}, bf16[256,2048]{1,0:T(8,128)(2,1)}, u32[]{:S(2)}, u32[]{:S(2)}) collective-permute-start(bf16[256,2048]{1,0:T(8,128)(2,1)} %collective-permute-done.5.refs_0_), channel_id=1, source_target_pairs={{0,4},{1,5},{4,8},{5,9},{8,12},{9,13},{12,14},{13,15},{14,10},{15,... | collective-permute-start | bytes 3145736 | tf_op jit(solution)/shard_map/ppermute | solution.py:551
  153.3 28.5 %slice-start.4 = ((f32[28096]{0:T(1024)}), f32[17408]{0:T(1024)S(1)}, s32[]{:S(2)}) async-start(f32[28096]{0:T(1024)} %param.25), calls=%async_computation.9 | async-start | bytes 139264 | tf_op jit(solution)/shard_map/slice | solution.py:59
  153.3 28.6 %copy-start.13 = (f32[28096]{0:T(1024)S(1)}, f32[28096]{0:T(1024)}, u32[]{:S(2)}) copy-start(f32[28096]{0:T(1024)} %param.25) | copy-start | bytes 337156
  181.3 4.6 collective-permute-start.12
  181.3 4.6 collective-permute-start.13
  185.9 41.1 %slice-start.5 = ((f32[28096]{0:T(1024)}), f32[256]{0:T(256)S(1)}, s32[]{:S(2)}) async-start(f32[28096]{0:T(1024)} %param.25), calls=%async_computation.10 | async-start | bytes 2048 | tf_op jit(solution)/shard_map/slice | solution.py:953
  185.9 25.4 %collective-permute-start.14 = (bf16[128,2048]{1,0:T(8,128)(2,1)S(1)}, bf16[128,2048]{1,0:T(8,128)(2,1)}, u32[]{:S(2)}, u32[]{:S(2)}) collective-permute-start(bf16[128,2048]{1,0:T(8,128)(2,1)S(1)} %slice.132), channel_id=1, source_target_pairs={{0,4},{1,5},{4,8},{5,9},{8,12},{9,13},{12,14},{13,15},{14,10},{15,... | collective-permute-start | bytes 1572872 | tf_op jit(solution)/shard_map/ppermute | solution.py:551
  187.8 37.3 %collective-permute-start.15 = (bf16[128,2048]{1,0:T(8,128)(2,1)S(1)}, bf16[128,2048]{1,0:T(8,128)(2,1)}, u32[]{:S(2)}, u32[]{:S(2)}) collective-permute-start(bf16[128,2048]{1,0:T(8,128)(2,1)S(1)} %slice.133), channel_id=1, source_target_pairs={{0,2},{1,3},{4,0},{5,1},{8,4},{9,5},{12,8},{13,9},{14,12},{15,13},... | collective-permute-start | bytes 1572872 | tf_op jit(solution)/shard_map/ppermute | solution.py:551
  225.1 2.4 collective-permute-start.16
  225.1 2.9 collective-permute-start.17
  373.6 31.4 %collective-permute-start.18 = (bf16[4096,896]{1,0:T(8,128)(2,1)}, bf16[4096,896]{1,0:T(8,128)(2,1)}, u32[]{:S(2)}, u32[]{:S(2)}) collective-permute-start(bf16[4096,896]{1,0:T(8,128)(2,1)} %get-tuple-element.230), channel_id=1, source_target_pairs={{0,1},{1,0},{2,3},{3,2},{4,5},{5,4},{6,7},{7,6},{8,9},{9,8},{10,11... | collective-permute-start | bytes 22020104 | tf_op jit(solution)/shard_map/ppermute | solution.py:555
  378.9 26.0 %collective-permute-start.19 = (bf16[896,1024]{0,1:T(8,128)(2,1)}, bf16[896,1024]{0,1:T(8,128)(2,1)}, u32[]{:S(2)}, u32[]{:S(2)}) collective-permute-start(bf16[896,1024]{0,1:T(8,128)(2,1)} %get-tuple-element.273), channel_id=1, source_target_pairs={{0,1},{1,0},{2,3},{3,2},{4,5},{5,4},{6,7},{7,6},{8,9},{9,8},{10,11... | collective-permute-start | bytes 5505032 | tf_op jit(solution)/shard_map/ppermute | solution.py:555
  403.3 47.5 %collective-permute-start.29 = (bf16[416,2048]{1,0:T(8,128)(2,1)}, bf16[416,2048]{1,0:T(8,128)(2,1)S(1)}, u32[]{:S(2)}, u32[]{:S(2)}) collective-permute-start(bf16[416,2048]{1,0:T(8,128)(2,1)} %pad_maximum_fusion.3), channel_id=1, source_target_pairs={{0,16},{16,0},{1,17},{17,1},{2,18},{18,2},{3,19},{19,3},{4,20},{20... | collective-permute-start | bytes 5111816 | tf_op jit(solution)/shard_map/ppermute | solution.py:765
  412.2 22.8 %collective-permute-start.20 = (bf16[256,1024]{1,0:T(8,128)(2,1)}, bf16[256,1024]{1,0:T(8,128)(2,1)S(1)}, u32[]{:S(2)}, u32[]{:S(2)}) collective-permute-start(bf16[256,1024]{1,0:T(8,128)(2,1)} %get-tuple-element.201), channel_id=1, source_target_pairs={{0,4},{1,5},{4,8},{5,9},{8,12},{9,13},{12,14},{13,15},{14,10},{15,... | collective-permute-start | bytes 1572872 | tf_op jit(solution)/shard_map/ppermute | solution.py:551
  412.2 34.1 %collective-permute-start.21 = (bf16[256,1024]{1,0:T(8,128)(2,1)S(1)}, bf16[256,1024]{1,0:T(8,128)(2,1)S(1)}, u32[]{:S(2)}, u32[]{:S(2)}) collective-permute-start(bf16[256,1024]{1,0:T(8,128)(2,1)S(1)} %get-tuple-element.202), channel_id=1, source_target_pairs={{0,2},{1,3},{4,0},{5,1},{8,4},{9,5},{12,8},{13,9},{14,12},{15,13},... | collective-permute-start | bytes 1572872 | tf_op jit(solution)/shard_map/ppermute | solution.py:551
  448.8 33.8 %collective-permute-start.22 = (bf16[512,1024]{1,0:T(8,128)(2,1)}, bf16[512,1024]{1,0:T(8,128)(2,1)}, u32[]{:S(2)}, u32[]{:S(2)}) collective-permute-start(bf16[512,1024]{1,0:T(8,128)(2,1)} %pad_maximum_fusion.4), channel_id=1, source_target_pairs={{0,4},{1,5},{4,8},{5,9},{8,12},{9,13},{12,14},{13,15},{14,10},{15,... | collective-permute-start | bytes 3145736 | tf_op jit(solution)/shard_map/ppermute | solution.py:551
  448.8 41.2 %collective-permute-start.23 = (bf16[512,1024]{1,0:T(8,128)(2,1)}, bf16[512,1024]{1,0:T(8,128)(2,1)}, u32[]{:S(2)}, u32[]{:S(2)}) collective-permute-start(bf16[512,1024]{1,0:T(8,128)(2,1)} %pad_maximum_fusion.5), channel_id=1, source_target_pairs={{0,2},{1,3},{4,0},{5,1},{8,4},{9,5},{12,8},{13,9},{14,12},{15,13},... | collective-permute-start | bytes 3145736 | tf_op jit(solution)/shard_map/ppermute | solution.py:551
  452.5 94.6 %all-to-all-start.1 = ((bf16[16,416,128]{2,1,0:T(8,128)(2,1)}), bf16[16,416,128]{2,1,0:T(8,128)(2,1)}, u32[]{:S(2)}, u32[]{:S(2)}) async-start(bf16[16,416,128]{2,1,0:T(8,128)(2,1)} %bitcast_bitcast_fusion), calls=%async_computation.2 | async-start | bytes 3407872 | tf_op jit(solution)/shard_map/all_to_all | solution.py:1031
  456.9 49.7 %collective-permute-start.26 = (bf16[256,2048]{1,0:T(8,128)(2,1)S(1)}, bf16[256,2048]{1,0:T(8,128)(2,1)S(1)}, u32[]{:S(2)}, u32[]{:S(2)}) collective-permute-start(bf16[256,2048]{1,0:T(8,128)(2,1)S(1)} %convolution_convert_fusion.2), channel_id=1, source_target_pairs={{0,16},{16,0},{1,17},{17,1},{2,18},{18,2},{3,19},{19,3},{4,20},{20... | collective-permute-start | bytes 3145736 | tf_op jit(solution)/shard_map/ppermute | solution.py:765
  493.2 37.0 %collective-permute-start.24 = (bf16[512,1024]{1,0:T(8,128)(2,1)S(1)}, bf16[512,1024]{1,0:T(8,128)(2,1)S(1)}, u32[]{:S(2)}, u32[]{:S(2)}) collective-permute-start(bf16[512,1024]{1,0:T(8,128)(2,1)S(1)} %add_convert_fusion.4), channel_id=1, source_target_pairs={{0,4},{1,5},{4,8},{5,9},{8,12},{9,13},{12,14},{13,15},{14,10},{15,... | collective-permute-start | bytes 3145736 | tf_op jit(solution)/shard_map/ppermute | solution.py:551
  495.1 37.0 %collective-permute-start.25 = (bf16[512,1024]{1,0:T(8,128)(2,1)S(1)}, bf16[512,1024]{1,0:T(8,128)(2,1)S(1)}, u32[]{:S(2)}, u32[]{:S(2)}) collective-permute-start(bf16[512,1024]{1,0:T(8,128)(2,1)S(1)} %add_convert_fusion.3), channel_id=1, source_target_pairs={{0,2},{1,3},{4,0},{5,1},{8,4},{9,5},{12,8},{13,9},{14,12},{15,13},... | collective-permute-start | bytes 3145736 | tf_op jit(solution)/shard_map/ppermute | solution.py:551
  534.8 30.4 %collective-permute-start.27 = (bf16[512,1024]{1,0:T(8,128)(2,1)}, bf16[512,1024]{1,0:T(8,128)(2,1)}, u32[]{:S(2)}, u32[]{:S(2)}) collective-permute-start(bf16[512,1024]{1,0:T(8,128)(2,1)} %add_convert_fusion.2), channel_id=1, source_target_pairs={{0,4},{1,5},{4,8},{5,9},{8,12},{9,13},{12,14},{13,15},{14,10},{15,... | collective-permute-start | bytes 3145736 | tf_op jit(solution)/shard_map/ppermute | solution.py:551
  542.9 23.1 %collective-permute-start.28 = (bf16[512,1024]{1,0:T(8,128)(2,1)}, bf16[512,1024]{1,0:T(8,128)(2,1)}, u32[]{:S(2)}, u32[]{:S(2)}) collective-permute-start(bf16[512,1024]{1,0:T(8,128)(2,1)} %add_convert_fusion.1), channel_id=1, source_target_pairs={{0,2},{1,3},{4,0},{5,1},{8,4},{9,5},{12,8},{13,9},{14,12},{15,13},... | collective-permute-start | bytes 3145736 | tf_op jit(solution)/shard_map/ppermute | solution.py:551
  549.4 23.9 %collective-permute-start.30 = (bf16[16,256,128]{2,1,0:T(8,128)(2,1)}, bf16[16,256,128]{2,1,0:T(8,128)(2,1)S(1)}, u32[]{:S(2)}, u32[]{:S(2)}) collective-permute-start(bf16[16,256,128]{2,1,0:T(8,128)(2,1)} %slice.155.grad_ref), channel_id=1, source_target_pairs={{0,16},{16,0},{1,17},{17,1},{2,18},{18,2},{3,19},{19,3},{4,20},{20... | collective-permute-start | bytes 3145736 | tf_op jit(solution)/shard_map/ppermute | solution.py:765
  556.7 16.6 %collective-permute-start.31 = (bf16[160,128]{1,0:T(8,128)(2,1)S(1)}, bf16[160,128]{1,0:T(8,128)(2,1)S(1)}, u32[]{:S(2)}, u32[]{:S(2)}) collective-permute-start(bf16[160,128]{1,0:T(8,128)(2,1)S(1)} %slice_reduce_fusion), channel_id=1, source_target_pairs={{0,16},{16,0},{1,17},{17,1},{2,18},{18,2},{3,19},{19,3},{4,20},{20... | collective-permute-start | bytes 122888 | tf_op jit(solution)/shard_map/ppermute | solution.py:765
  577.0 3.2 collective-permute-start.32
  582.8 12.7 %collective-permute-start.33 = (f32[28096]{0:T(1024)S(1)}, f32[28096]{0:T(1024)S(1)}, u32[]{:S(2)}, u32[]{:S(2)}) collective-permute-start(f32[28096]{0:T(1024)S(1)} %concatenate.57), channel_id=1, source_target_pairs={{0,1},{1,0},{2,3},{3,2},{4,5},{5,4},{6,7},{7,6},{8,9},{9,8},{10,11... | collective-permute-start | bytes 337160 | tf_op jit(solution)/shard_map/ppermute | solution.py:868
  583.3 12.2 %collective-permute-start.34 = (f32[28096]{0:T(1024)S(1)}, f32[28096]{0:T(1024)}, u32[]{:S(2)}, u32[]{:S(2)}) collective-permute-start(f32[28096]{0:T(1024)S(1)} %concatenate.57), channel_id=1, source_target_pairs={{0,2},{1,3},{2,0},{3,1},{4,6},{5,7},{6,4},{7,5},{8,10},{9,11},{10,... | collective-permute-start | bytes 337160 | tf_op jit(solution)/shard_map/ppermute | solution.py:868
  585.2 10.4 %collective-permute-start.35 = (f32[28096]{0:T(1024)S(1)}, f32[28096]{0:T(1024)}, u32[]{:S(2)}, u32[]{:S(2)}) collective-permute-start(f32[28096]{0:T(1024)S(1)} %concatenate.57), channel_id=1, source_target_pairs={{0,3},{1,2},{2,1},{3,0},{4,7},{5,6},{6,5},{7,4},{8,11},{9,10},{10,... | collective-permute-start | bytes 337160 | tf_op jit(solution)/shard_map/ppermute | solution.py:868
  596.5 6.1 collective-permute-start.36
  599.1 11.8 %collective-permute-start.37 = (f32[28096]{0:T(1024)S(1)}, f32[28096]{0:T(1024)S(1)}, u32[]{:S(2)}, u32[]{:S(2)}) collective-permute-start(f32[28096]{0:T(1024)S(1)} %add_add_fusion.1), channel_id=1, source_target_pairs={{0,8},{1,9},{2,10},{3,11},{4,12},{5,13},{6,14},{7,15},{8,0},{9,1},... | collective-permute-start | bytes 337160 | tf_op jit(solution)/shard_map/ppermute | solution.py:868
  600.5 10.3 %collective-permute-start.38 = (f32[28096]{0:T(1024)S(1)}, f32[28096]{0:T(1024)S(1)}, u32[]{:S(2)}, u32[]{:S(2)}) collective-permute-start(f32[28096]{0:T(1024)S(1)} %add_add_fusion.1), channel_id=1, source_target_pairs={{0,12},{1,13},{2,14},{3,15},{4,8},{5,9},{6,10},{7,11},{8,4},{9,5},... | collective-permute-start | bytes 337160 | tf_op jit(solution)/shard_map/ppermute | solution.py:868
  610.9 4.9 collective-permute-start.39
  (35 other events, 159.5 us)
Sparse Core Ops, SparseCore 0:
  114.2 155.6 all-gather.3
  275.7 195.4 reduce-scatter.1

commit v6 on v5

--- a/solution.py
+++ b/solution.py
@@ -213,7 +213,8 @@
     gated = mixed * (gate * sigmoid(gate))
     mixed_ref[...] = mixed
     zin_ref[...] = (gated * px_ref[6:7, :]).astype(BF)
-    square_ref[...] = jnp.sum(gated * gated, axis=1, keepdims=True)
+    ones = jnp.ones((8, gated.shape[1]), BF)
+    square_ref[...] = sum(dot(ones, part, ((1,), (1,))) for part in split(gated * gated, 2))
 
 
 def backward_kernel(
@@ -228,8 +229,8 @@
     remain_ref,
     mixed_ref,
     gout_ref,
-    scale_ref,
-    pull_ref,
+    sums_ref,
+    live_ref,
     states_ref,
     px_ref,
     pbc_ref,
@@ -278,10 +279,15 @@
     mixed = mixed_ref[...]
     gated = mixed * silu
     g_out = px_ref[6:7, :]
-    scale = scale_ref[...]
+    sums = jnp.transpose(
+        jnp.concatenate([sums_ref[...], jnp.zeros((120, STRETCH), F32)], axis=0)
+    )
+    live = live_ref[0, 0]
+    scale = lax.rsqrt(sums[:, 0:1] / live + NORM_EPS)
+    pull = scale * scale * scale / live * sums[:, 1:2]
     upstream = gout_ref[...]
     low_ref[...] = (gated * scale * g_out).astype(BF)
-    g_gated = scale * g_out * upstream - gated * pull_ref[...]
+    g_gated = scale * g_out * upstream - gated * pull
     g_mixed = g_gated * silu
     gp_ref[:, 0:width] = (g_gated * mixed * (sig * (1.0 + gate * (1.0 - sig)))).astype(BF)
 
@@ -417,14 +423,14 @@
         out_specs=[
             row_spec(width, 0),
             row_spec(width, 0),
-            row_spec(1, 0),
+            pl.BlockSpec((8, STRETCH), lambda i: (0, first + i)),
             pl.BlockSpec((1, width, N), lambda i: (first + i, 0, 0)),
             whole(state),
         ],
         out_shape=[
             jax.ShapeDtypeStruct((total, width), BF),
             jax.ShapeDtypeStruct((total, width), F32),
-            jax.ShapeDtypeStruct((total, 1), F32),
+            jax.ShapeDtypeStruct((8, total), F32),
             jax.ShapeDtypeStruct((total // STRETCH, width, N), F32),
             jax.ShapeDtypeStruct((width, N), F32),
         ],
@@ -455,12 +461,12 @@
     )
     whole = lambda a: pl.BlockSpec(a.shape, lambda i: (0, 0))
     fixed = lambda r, w: pl.BlockSpec((r, w), lambda i: (0, 0))
-    place, remain, mixed, g_out_low, scale, pull = rows_in
+    place, remain, mixed, g_out_low, sums, live = rows_in
     gstate, gx, gbc, gdt = carried[:4]
     filled = tuple(carried[4:])
     operands = (
         (projected,) * 6
-        + (place, remain, mixed, g_out_low, scale, pull, states, px, pbc, pdt)
+        + (place, remain, mixed, g_out_low, sums, live, states, px, pbc, pdt)
         + (gstate, gx, gbc, gdt)
         + filled
     )
@@ -478,8 +484,8 @@
             row_spec(1, 0),
             row_spec(width, 0),
             row_spec(width, 0),
-            row_spec(1, 0),
-            row_spec(1, 0),
+            pl.BlockSpec((8, STRETCH), lambda i: (0, rev(i))),
+            pl.BlockSpec(memory_space=pltpu.SMEM),
             pl.BlockSpec((1, width, N), lambda i: (rev(i), 0, 0)),
             whole(px),
             whole(pbc),
@@ -710,8 +716,17 @@
         return self.ready[0] + self.last[0].astype(F32) + self.last[1].astype(F32)
 
 
+def column_halves(weight):
+    if lax.axis_size("dp") != 16:
+        return ()
+    core = lax.axis_index("dp") % 2
+    half = weight.shape[1] // 2
+    take = lambda c: lax.dynamic_slice_in_dim(weight, c * half, half, 1)
+    return lax.optimization_barrier((take(core), swap(take(1 - core))))
+
+
 class Scatter:
-    def __init__(self, left, right, *gate):
+    def __init__(self, left, right, halves, *gate):
         self.ring = lax.axis_size("dp") == 16
         self.last = self.sent = ()
         if not self.ring:
@@ -719,9 +734,7 @@
             self.done = lax.psum_scatter(full, "dp", scatter_dimension=0, tiled=True).astype(F32)
             return
         self.core, spot = ring_place()
-        half = right.shape[1] // 2
-        take = lambda c: lax.dynamic_slice_in_dim(right, c * half, half, 1)
-        sides = ((left, take(self.core)), (swap(left), swap(take(1 - self.core))))
+        sides = ((left, halves[0]), (swap(left), halves[1]))
         sides = lax.optimization_barrier((sides, gate))[0]
         self.rows = rows = left.shape[0] // 8
 
@@ -860,16 +873,23 @@
     )
 
 
+def stepwise():
+    return lax.axis_size("dp") == 16 and lax.axis_size("width") == 2
+
+
+def quad_sum(values, low, high):
+    near, far, across = (
+        lax.ppermute(values, "dp", [(i, i ^ mask) for i in range(16)])
+        for mask in (low, high, low ^ high)
+    )
+    return (values + near) + (far + across)
+
+
 def tree_sum(values):
-    if lax.axis_size("dp") != 16 or lax.axis_size("width") != 2:
+    if not stepwise():
         return lax.psum(values, ("width", "dp"))
-    for low, high in ((1, 2), (4, 8)):
-        near, far, across = (
-            lax.ppermute(values, "dp", [(i, i ^ mask) for i in range(16)])
-            for mask in (low, high, low ^ high)
-        )
-        values = (values + near) + (far + across)
-    return values + lax.ppermute(values, "width", [(0, 1), (1, 0)])
+    values = quad_sum(quad_sum(values, 1, 2), 4, 8)
+    return values + other_width(values)
 
 
 def pad_to(values, width, axis):
@@ -989,28 +1009,43 @@
         cotangent_all, out_weight_low, (((1,), (1,)), ((), ())), preferred_element_type=F32
     )
     pull_part = jnp.sum(g_out_low * zin.astype(F32), axis=1)
-    both = jnp.sum(lax.all_gather(jnp.stack([square[:, 0], pull_part]), "dp"), axis=0)
-    scale = lax.rsqrt(both[0] / live + NORM_EPS)
-    pull = scale * scale * scale / live * both[1]
-
-    rows_in = (place, remain, mixed, g_out_low, scale[:, None], pull[:, None])
+    both = jnp.sum(lax.all_gather(jnp.stack([square[0], pull_part]), "dp"), axis=0)
+    rows_in = (place, remain, mixed, g_out_low, pad_to(both, 8, 0), live.reshape(1, 1))
+    scale = lax.rsqrt(lax.dynamic_slice_in_dim(both[0], here * rows, rows, 0) / live + NORM_EPS)
     carried = (
         jnp.zeros((wide, N), F32),
         jnp.zeros((16, wide), F32),
         jnp.zeros((16, 2 * N), F32),
         jnp.zeros((8, 128), F32),
     )
+    halves = column_halves(weight_own.T)
     for begin, end in reversed(cuts(total // STRETCH, BACK_PARTS)):
         carried = run_backward(
-            carried, begin, end - begin, projected, rows_in, states, px, pbc, pdt
+            (after(carried[0], halves),) + carried[1:], begin, end - begin, projected, rows_in, states, px, pbc, pdt
         )
     _, gx, gbc, gdt, g_projected, out_low = carried
     block_out = (
         inputs_f
         + summed_out.astype(F32)
-        * lax.dynamic_slice_in_dim(scale, here * rows, rows, 0)[:, None]
+        * scale[:, None]
     ).astype(BF)
 
+    def placed(part, size):
+        spots = jnp.zeros(part.shape[:-1] + (size,), F32)
+        return lax.dynamic_update_slice_in_dim(
+            spots, part, here * part.shape[-1], part.ndim - 1
+        )
+
+    conv_part = jnp.concatenate([placed(gx[:5, :units], E), gbc[:5]], axis=1)
+    early = jnp.concatenate(
+        [
+            placed(gx[6, :units], E),
+            conv_part.reshape(-1),
+            placed(gdt[1, :own_heads], H),
+            placed(gdt[0, :own_heads], H),
+            placed(jnp.sum(gx[5, :units].reshape(own_heads, P_SIZE), axis=1), H),
+        ]
+    )
     g_weight = lax.dot_general(
         g_projected, normed_all, (((0,), (0,)), ((), ())), preferred_element_type=F32
     ).astype(BF)
@@ -1041,7 +1076,9 @@
             axis=0,
         )
 
-    inward = Scatter(g_projected, weight_own.T, g_weight)
+    if stepwise():
+        early = quad_sum(early, 1, 2)
+    inward = Scatter(g_projected, weight_own.T, halves, g_weight)
     if paired:
         slot = lax.axis_index("width")
         g_kept = half(slot)
@@ -1053,13 +1090,18 @@
         (((0,), (0,)), ((), ())),
         preferred_element_type=F32,
     )[:units].astype(BF)
-    inward.advance(g_weight_out)
+    if stepwise():
+        inward.advance(g_weight_out)
+    else:
+        inward.advance(g_weight_out)
     if paired:
         g_kept, g_got, _ = lax.optimization_barrier((g_kept, g_got, inward.sent))
         g_half = to_owners((g_kept.astype(F32) + g_got.astype(F32)).astype(BF))
         total_out = other_width(after(g_weight_out, inward.sent))
         inward.advance()
         inward.advance(total_out)
+        if stepwise():
+            early = quad_sum(after(early, inward.ready()), 4, 8)
         total_out = g_weight_out.astype(F32) + total_out.astype(F32)
         g_half = after(g_half, inward.sent)
         g_shared = jnp.sum(g_half[:, units:].astype(F32), axis=0).astype(BF)
@@ -1126,23 +1168,12 @@
     grad_tokens = (cotangent.astype(F32) + g_inputs).astype(BF)
     g_g_in = jnp.sum(g_normed * inputs_f * root, axis=0)
 
-    def placed(part, size):
-        spots = jnp.zeros(part.shape[:-1] + (size,), F32)
-        return lax.dynamic_update_slice_in_dim(
-            spots, part, here * part.shape[-1], part.ndim - 1
-        )
-
-    conv_part = jnp.concatenate([placed(gx[:5, :units], E), gbc[:5]], axis=1)
-    early = jnp.concatenate(
-        [
-            placed(gx[6, :units], E),
-            conv_part.reshape(-1),
-            placed(gdt[1, :own_heads], H),
-            placed(gdt[0, :own_heads], H),
-            placed(jnp.sum(gx[5, :units].reshape(own_heads, P_SIZE), axis=1), H),
-        ]
-    )
-    total_small = tree_sum(jnp.concatenate([g_g_in, early]))
+    if stepwise():
+        small = quad_sum(quad_sum(g_g_in, 1, 2), 4, 8)
+        total_small = jnp.concatenate([small, early])
+        total_small = total_small + other_width(total_small)
+    else:
+        total_small = tree_sum(jnp.concatenate([g_g_in, early]))
     rate_table, decay_table = small_table()
     new_small, mom_small, sec_small = adamw_step(
         small_params, moment_small, second_small, total_small, rate_table, decay_table, step_float

time: 633 us -> 631 us (level)
  starting transfers between devices: 60.7 us -> 71.4 us
    ppermute x5 -> x6, waiting for transfers between devices: 19.1 us -> 23.9 us  [other_width(): return lax.ppermute(values, 'width', [(0, 1), (1, 0)])]
    ppermute x7 -> x12, starting transfers between devices: 8.27 us -> 12.8 us  [quad_sum(): lax.ppermute(values, 'dp', [(i, i ^ mask) for i in range(16)])]
  transfers between devices with their start and end apart: 44 -> 50, of which waited for: 25 -> 23; matrix products, arithmetic and copies ran while one was open for 29% -> 27% of each run, Pallas kernels for 22% -> 22%
where the time goes in v6:
time: 631 us; the launch traced here: 622 us
  waiting for transfers between devices  200 us (32%)
  Pallas kernels  138 us (22%)
  matrix products  92.8 us (15%)
  starting transfers between devices  71.4 us (11%)
  other arithmetic  48.2 us (8%)
  local copies, waits for them, and re-layouts  34.2 us (5%)
  blocking collectives  20.7 us (3%)
  between operations  17 us (3%)
    ppermute x16, waiting for transfers between devices, hop(): return lax.ppermute(values, 'dp', pairs)  141 us
    pallas_call x1, Pallas kernels, run_backward(): pl.pallas_call(partial(backward_kernel, heads), grid=(count,), in_specs=[...  50.7 us
    dot_general x16, matrix products, chunk(): jnp.dot(lax.dynamic_slice_in_dim(after(side, deps), start, rows, 0), weig...  43.9 us
    pallas_call x4, Pallas kernels, absorb(): pl.pallas_call(partial(absorb_kernel, count, by_rows), grid_spec=pltpu.Pr...  42 us
    ppermute x16, starting transfers between devices, hop(): return lax.ppermute(values, 'dp', pairs)  35.3 us
    pallas_call x1, Pallas kernels, run_forward(): pl.pallas_call(partial(forward_kernel, heads), grid=(count,), in_specs=[r...  27.6 us
    all_to_all x1, waiting for transfers between devices, per_device(): mine = lax.all_to_all(weight_halves(weight_low, units), 'dp', 0, 0)  24.4 us
    ppermute x6, waiting for transfers between devices, other_width(): return lax.ppermute(values, 'width', [(0, 1), (1, 0)])  23.9 us
  transfers between devices with their start and end apart: 50, of which 23 were waited for; matrix products, arithmetic and copies ran while one was open for 27% of the time, Pallas kernels for 22%

profile of v6, /device:TPU:0, one launch (start us, length us, event | category | flops | bytes accessed | tf_op | source)
XLA Modules:
  0.0 621.7 jit_solution(6907115041857772991)
XLA Ops:
  11.3 7.5 %all-to-all-start = ((bf16[16,416,128]{2,1,0:T(8,128)(2,1)}), bf16[16,416,128]{2,1,0:T(8,128)(2,1)}, u32[]{:S(2)}, u32[]{:S(2)}) async-start(bf16[16,416,128]{2,1,0:T(8,128)(2,1)} %pad_maximum_fusion.1), calls=%async_computation | async-start | bytes 3407872 | tf_op jit(solution)/shard_map/all_to_all | solution.py:947
  25.0 3.9 iota_subtract_fusion
  28.9 24.4 %all-to-all-done = bf16[16,416,128]{2,1,0:T(8,128)(2,1)} async-done(((bf16[16,416,128]{2,1,0:T(8,128)(2,1)}), bf16[16,416,128]{2,1,0:T(8,128)(2,1)}, u32[]{:S(2)}, u32[]{:S(2)}) %all-to-all-start) | async-done | bytes 1703968 | tf_op jit(solution)/shard_map/all_to_all | solution.py:947
  53.3 2.8 copy.59
  56.1 13.8 %collective-permute-done.1.refs_2_ = bf16[256,2048]{1,0:T(8,128)(2,1)} collective-permute-done((bf16[256,2048]{1,0:T(8,128)(2,1)S(1)}, bf16[256,2048]{1,0:T(8,128)(2,1)}, u32[]{:S(2)}, u32[]{:S(2)}) %collective-permute-start.1) | collective-permute-done | bytes 1048608 | tf_op jit(solution)/shard_map/ppermute | solution.py:557
  72.4 3.8 collective-permute-done.3.refs_3_
  76.4 10.7 %collective-permute-start.5 = (bf16[256,2048]{1,0:T(8,128)(2,1)}, bf16[256,2048]{1,0:T(8,128)(2,1)}, u32[]{:S(2)}, u32[]{:S(2)}) collective-permute-start(bf16[256,2048]{1,0:T(8,128)(2,1)} %collective-permute-done.1.refs_2_), channel_id=1, source_target_pairs={{0,4},{1,5},{4,8},{5,9},{8,12},{9,13},{12,14},{13,15},{14,10},{15,... | collective-permute-start | bytes 3145736 | tf_op jit(solution)/shard_map/ppermute | solution.py:557
  90.8 19.3 %collective-permute-done.5.refs_0_ = bf16[256,2048]{1,0:T(8,128)(2,1)} collective-permute-done((bf16[256,2048]{1,0:T(8,128)(2,1)}, bf16[256,2048]{1,0:T(8,128)(2,1)}, u32[]{:S(2)}, u32[]{:S(2)}) %collective-permute-start.5) | collective-permute-done | bytes 1048608 | tf_op jit(solution)/shard_map/ppermute | solution.py:557
  116.8 11.8 %collective-permute-done.11 = bf16[416,2048]{1,0:T(8,128)(2,1)} collective-permute-done((bf16[416,2048]{1,0:T(8,128)(2,1)}, bf16[416,2048]{1,0:T(8,128)(2,1)}, u32[]{:S(2)}, u32[]{:S(2)}) %collective-permute-start.11) | collective-permute-done | bytes 1703968 | tf_op jit(solution)/shard_map/ppermute | solution.py:778
  128.6 3.8 copy.63
  139.6 13.8 %absorb_rows.4 = (bf16[4096,2048]{1,0:T(8,128)(2,1)}, bf16[4096,896]{1,0:T(8,128)(2,1)}) custom-call(s32[6]{0:T(128)} %stack.106.starts_ref, bf16[256,2048]{1,0:T(8,128)(2,1)} %copy-done.10, bf16[256,2048]{1,0:T(8,128)(2,1)} %collective-permute-done.refs_1_, bf16[256,2048]{1,0:T(8,128)(2,1)} %collective-permute-done.1.refs_2_, bf16[256,2048]{1,0:T(8,128)(2,1)} %copy-done.26, ...), custom_call_target="tpu_custom_call" | custom-call | flops 112742891520 | bytes 16252928 | tf_op jit(solution)/shard_map/absorb_rows/pallas_call | solution.py:603
  153.3 10.4 %absorb_rows.5 = (bf16[4096,2048]{1,0:T(8,128)(2,1)}, bf16[4096,896]{1,0:T(8,128)(2,1)}) custom-call(s32[4]{0:T(128)} %get-tuple-element.303.starts_ref, bf16[256,2048]{1,0:T(8,128)(2,1)} %collective-permute-done.5.refs_0_, bf16[256,2048]{1,0:T(8,128)(2,1)} %collective-permute-done.7.refs_1_, ...), custom_call_target="tpu_custom_call", output_to_operand_aliasing={{0}: (6, {}), {1}: (7, {})} | custom-call | flops 75161927680 | bytes 12058624 | tf_op jit(solution)/shard_map/absorb_rows/pallas_call | solution.py:603
  163.8 17.5 %collective-permute-done.10.refs_2_ = bf16[256,2048]{1,0:T(8,128)(2,1)} collective-permute-done((bf16[256,2048]{1,0:T(8,128)(2,1)}, bf16[256,2048]{1,0:T(8,128)(2,1)}, u32[]{:S(2)}, u32[]{:S(2)}) %collective-permute-start.10) | collective-permute-done | bytes 1048608 | tf_op jit(solution)/shard_map/ppermute | solution.py:557
  183.7 3.6 dynamic-slice_bitcast_fusion
  192.1 10.4 %absorb_rows.6 = (bf16[4096,2048]{1,0:T(8,128)(2,1)}, bf16[4096,896]{1,0:T(8,128)(2,1)}) custom-call(s32[4]{0:T(128)} %pad_add_fusion.2.starts_ref, bf16[256,2048]{1,0:T(8,128)(2,1)} %collective-permute-done.9.refs_0_, bf16[256,2048]{1,0:T(8,128)(2,1)} %collective-permute-done.12.refs_1_, ...), custom_call_target="tpu_custom_call", output_to_operand_aliasing={{0}: (6, {}), {1}: (7, {})} | custom-call | flops 75161927680 | bytes 12058624 | tf_op jit(solution)/shard_map/absorb_rows/pallas_call | solution.py:603
  202.5 13.3 %collective-permute-done.14.refs_0_ = bf16[128,2048]{1,0:T(8,128)(2,1)} collective-permute-done((bf16[128,2048]{1,0:T(8,128)(2,1)S(1)}, bf16[128,2048]{1,0:T(8,128)(2,1)}, u32[]{:S(2)}, u32[]{:S(2)}) %collective-permute-start.14) | collective-permute-done | bytes 524320 | tf_op jit(solution)/shard_map/ppermute | solution.py:557
  215.8 14.2 %collective-permute-done.15.refs_2_ = bf16[128,2048]{1,0:T(8,128)(2,1)} collective-permute-done((bf16[128,2048]{1,0:T(8,128)(2,1)S(1)}, bf16[128,2048]{1,0:T(8,128)(2,1)}, u32[]{:S(2)}, u32[]{:S(2)}) %collective-permute-start.15) | collective-permute-done | bytes 524320 | tf_op jit(solution)/shard_map/ppermute | solution.py:557
  233.6 7.5 %absorb_rows.7 = (bf16[4096,2048]{1,0:T(8,128)(2,1)}, bf16[4096,896]{1,0:T(8,128)(2,1)}) custom-call(s32[4]{0:T(128)} %get-tuple-element.302.starts_ref, bf16[128,2048]{1,0:T(8,128)(2,1)} %collective-permute-done.14.refs_0_, bf16[128,2048]{1,0:T(8,128)(2,1)} %copy-done.27, ...), custom_call_target="tpu_custom_call", output_to_operand_aliasing={{0}: (6, {}), {1}: (7, {})} | custom-call | flops 37580963840 | bytes 7864320 | tf_op jit(solution)/shard_map/absorb_rows/pallas_call | solution.py:603
  241.7 27.6 %scan_forward.1 = (bf16[4096,256]{1,0:T(8,128)(2,1)}, f32[4096,256]{1,0:T(8,128)}, f32[8,4096]{1,0:T(8,128)}, f32[16,256,128]{2,1,0:T(8,128)}, f32[256,128]{1,0:T(8,128)}) custom-call(bf16[4096,896]{1,0:T(8,128)(2,1)} %get-tuple-element.193.gate_ref.x_ref.bc_ref.dt_ref.xprev_ref.bcprev_ref, ...), custom_call_target="tpu_custom_call" | custom-call | flops 20971520000 | bytes 20480000 | tf_op jit(solution)/shard_map/scan_forward/pallas_call | solution.py:405
  270.3 9.8 %convolution_convert_fusion = bf16[4096,2048]{1,0:T(8,128)(2,1)} fusion(bf16[4096,256]{1,0:T(8,128)(2,1)} %get-tuple-element.194, f32[256,2048]{1,0:T(8,128)S(1)} %copy-done.2), kind=kOutput, calls=%fused_computation | convolution fusion | flops 4303880192 | bytes 20971520 | tf_op jit(solution)/shard_map/dot_general | solution.py:1006
  280.1 14.2 %multiply_reduce_fusion = (f32[4096]{0:T(1024)S(1)}, f32[4096,256]{1,0:T(8,128)}) fusion(bf16[4096,256]{1,0:T(8,128)(2,1)} %get-tuple-element.194, bf16[4096,2048]{1,0:T(8,128)(2,1)} %all-gather.4.cloned.1.call-done, f32[256,2048]{1,0:T(8,128)S(1)} %copy-done.2), kind=kOutput, calls=%fused_computation.9 | convolution fusion | flops 4298633216 | bytes 25182208 | tf_op jit(solution)/shard_map/dot_general | solution.py:1008
  294.4 20.7 %all-gather.1 = f32[16,2,4096]{2,1,0:T(2,128)S(1)} all-gather(f32[1,2,4096]{2,1,0:T(2,128)S(1)} %maximum_bitcast_fusion), channel_id=2, replica_groups=mesh['width'=2,'dp'=16] {'dp'}, dimensions={0}, use_global_device_ids=true | all-gather | bytes 557056 | tf_op jit(solution)/shard_map/all_gather | solution.py:1012
  317.1 50.7 %scan_backward.1 = (bf16[4096,896]{1,0:T(8,128)(2,1)}, bf16[4096,256]{1,0:T(8,128)(2,1)}, f32[256,128]{1,0:T(8,128)}, f32[16,256]{1,0:T(8,128)}, f32[16,256]{1,0:T(8,128)}, /*index=5*/f32[8,128]{1,0:T(8,128)}) custom-call(bf16[4096,896]{1,0:T(8,128)(2,1)} %get-tuple-element.193.gate_ref.x_ref.bc_ref.dt_ref.xprev_ref.bcprev_ref, ...), custom_call_target="tpu_custom_call" | custom-call | flops 41943040000 | bytes 32768000 | tf_op jit(solution)/shard_map/scan_backward/pallas_call | solution.py:473
  375.4 20.4 %convolution_convert_fusion.1 = bf16[896,2048]{1,0:T(8,128)(2,1)S(1)} fusion(bf16[4096,896]{1,0:T(8,128)(2,1)} %get-tuple-element.237, bf16[4096,2048]{1,0:T(8,128)(2,1)} %get-tuple-element.203), kind=kOutput, calls=%fused_computation.12 | convolution fusion | flops 15034220544 | bytes 27787264 | tf_op jit(solution)/shard_map/dot_general | solution.py:1049
  401.1 3.2 fusion.41
  410.1 4.6 fusion.35
  414.8 4.5 convolution_convert_fusion.2
  419.3 3.2 convolution_add_fusion.5
  422.5 3.1 fusion.38
  432.7 6.3 %collective-permute-done.29 = bf16[416,2048]{1,0:T(8,128)(2,1)S(1)} collective-permute-done((bf16[416,2048]{1,0:T(8,128)(2,1)}, bf16[416,2048]{1,0:T(8,128)(2,1)S(1)}, u32[]{:S(2)}, u32[]{:S(2)}) %collective-permute-start.29) | collective-permute-done | bytes 1703968 | tf_op jit(solution)/shard_map/ppermute | solution.py:778
  440.7 4.4 all-to-all-start.1
  446.7 3.2 fusion.29
  450.0 3.2 fusion.32
  457.0 20.1 %collective-permute-done.22 = bf16[512,1024]{1,0:T(8,128)(2,1)} collective-permute-done((bf16[512,1024]{1,0:T(8,128)(2,1)}, bf16[512,1024]{1,0:T(8,128)(2,1)}, u32[]{:S(2)}, u32[]{:S(2)}) %collective-permute-start.22) | collective-permute-done | bytes 1048608 | tf_op jit(solution)/shard_map/ppermute | solution.py:557
  477.2 9.7 %collective-permute-done.23 = bf16[512,1024]{1,0:T(8,128)(2,1)} collective-permute-done((bf16[512,1024]{1,0:T(8,128)(2,1)}, bf16[512,1024]{1,0:T(8,128)(2,1)}, u32[]{:S(2)}, u32[]{:S(2)}) %collective-permute-start.23) | collective-permute-done | bytes 1048608 | tf_op jit(solution)/shard_map/ppermute | solution.py:557
  490.1 3.0 collective-permute-start.24
  493.4 3.1 fusion.23
  497.7 3.1 fusion.26
  503.8 26.5 %collective-permute-done.24 = bf16[512,1024]{1,0:T(8,128)(2,1)S(1)} collective-permute-done((bf16[512,1024]{1,0:T(8,128)(2,1)S(1)}, bf16[512,1024]{1,0:T(8,128)(2,1)S(1)}, u32[]{:S(2)}, u32[]{:S(2)}) %collective-permute-start.24) | collective-permute-done | bytes 1048608 | tf_op jit(solution)/shard_map/ppermute | solution.py:557
  534.9 10.7 %collective-permute-start.27 = (bf16[512,1024]{1,0:T(8,128)(2,1)}, bf16[512,1024]{1,0:T(8,128)(2,1)}, u32[]{:S(2)}, u32[]{:S(2)}) collective-permute-start(bf16[512,1024]{1,0:T(8,128)(2,1)} %add_convert_fusion.2), channel_id=1, source_target_pairs={{0,4},{1,5},{4,8},{5,9},{8,12},{9,13},{12,14},{13,15},{14,10},{15,... | collective-permute-start | bytes 3145736 | tf_op jit(solution)/shard_map/ppermute | solution.py:557
  545.7 3.1 fusion.20
  557.4 6.4 %fusion.71 = (bf16[256,2048]{1,0:T(8,128)(2,1)}, f32[256,2048]{1,0:T(8,128)}, f32[256,2048]{1,0:T(8,128)}, f32[256,2048]{1,0:T(8,128)}) fusion(f32[256,2048]{1,0:T(8,128)S(1)} %copy-done.2, f32[]{:T(128)} %bitcast.40, f32[256,2048]{1,0:T(8,128)S(1)} %copy-done.4, f32[256,2048]{1,0:T(8,128)} %param.24, f32[256,2048]{1,0:T(8,128)} %param.23), kind=kLoop, calls=%fused_computation.173 | loop fusion | flops 7864320 | bytes 15728644 | tf_op jit(solution)/shard_map/convert_element_type | solution.py:1191
  565.5 7.2 %adamw.3 = (f32[8512,128]{1,0:T(8,128)}, f32[8512,128]{1,0:T(8,128)}, f32[8512,128]{1,0:T(8,128)}, bf16[8512,128]{1,0:T(8,128)(2,1)}) custom-call(s32[1]{0:T(128)} %bitcast.46.first_ref, f32[1,1]{1,0:T(1,128)} %bitcast.47.base_ref, f32[8512,128]{1,0:T(8,128)} %bitcast.100, f32[8512,128]{1,0:T(8,128)} %bitcast.107, f32[8512,128]{1,0:T(8,128)} %bitcast.110, ...), custom_call_target="tpu_custom_call" | custom-call | flops 5242880000 | bytes 15728640 | tf_op jit(solution)/shard_map/adamw/pallas_call | solution.py:854
  575.1 5.8 collective-permute-done.31
  585.6 7.0 %adamw.4 = (f32[8512,128]{1,0:T(8,128)}, f32[8512,128]{1,0:T(8,128)}, f32[8512,128]{1,0:T(8,128)}, bf16[8512,128]{1,0:T(8,128)(2,1)}) custom-call(s32[1]{0:T(128)} %bitcast.50.first_ref, f32[1,1]{1,0:T(1,128)} %bitcast.47.base_ref, f32[8512,128]{1,0:T(8,128)} %bitcast.101, ...), custom_call_target="tpu_custom_call", output_to_operand_aliasing={{0}: (6, {}), {1}: (7, {}), {2}: (8, {}), {3}: (9, {})} | custom-call | flops 5242880000 | bytes 15728640 | tf_op jit(solution)/shard_map/adamw/pallas_call | solution.py:854
  597.1 3.3 adamw.5
  605.4 2.8 collective-permute-done.38
  609.8 3.9 fusion.11
  (277 shorter events, 117.5 us)
Async XLA Ops:
  11.3 42.1 %all-to-all-start = ((bf16[16,416,128]{2,1,0:T(8,128)(2,1)}), bf16[16,416,128]{2,1,0:T(8,128)(2,1)}, u32[]{:S(2)}, u32[]{:S(2)}) async-start(bf16[16,416,128]{2,1,0:T(8,128)(2,1)} %pad_maximum_fusion.1), calls=%async_computation | async-start | bytes 3407872 | tf_op jit(solution)/shard_map/all_to_all | solution.py:947
  18.8 261.3 %all-gather.4.cloned.1.call-start = ((), (), s32[]{:S(2)}) async-start(), calls=%async_computation.4 | async-start | bytes 17825792 | tf_op jit(solution)/shard_map/all_gather | solution.py:999
  19.5 3.5 collective-permute-start
  23.0 46.8 %collective-permute-start.1 = (bf16[256,2048]{1,0:T(8,128)(2,1)S(1)}, bf16[256,2048]{1,0:T(8,128)(2,1)}, u32[]{:S(2)}, u32[]{:S(2)}) collective-permute-start(bf16[256,2048]{1,0:T(8,128)(2,1)S(1)} %fusion.6.refs_0_), channel_id=1, source_target_pairs={{0,4},{1,5},{4,8},{5,9},{8,12},{9,13},{12,14},{13,15},{14,10},{15,... | collective-permute-start | bytes 3145736 | tf_op jit(solution)/shard_map/ppermute | solution.py:557
  24.7 47.2 %collective-permute-start.2 = (bf16[256,2048]{1,0:T(8,128)(2,1)S(1)}, bf16[256,2048]{1,0:T(8,128)(2,1)}, u32[]{:S(2)}, u32[]{:S(2)}) collective-permute-start(bf16[256,2048]{1,0:T(8,128)(2,1)S(1)} %fusion.6.refs_0_), channel_id=1, source_target_pairs={{0,2},{1,3},{4,0},{5,1},{8,4},{9,5},{12,8},{13,9},{14,12},{15,13},... | collective-permute-start | bytes 3145736 | tf_op jit(solution)/shard_map/ppermute | solution.py:557
  71.9 4.3 collective-permute-start.3
  71.9 4.5 collective-permute-start.4
  76.4 33.7 %collective-permute-start.5 = (bf16[256,2048]{1,0:T(8,128)(2,1)}, bf16[256,2048]{1,0:T(8,128)(2,1)}, u32[]{:S(2)}, u32[]{:S(2)}) collective-permute-start(bf16[256,2048]{1,0:T(8,128)(2,1)} %collective-permute-done.1.refs_2_), channel_id=1, source_target_pairs={{0,4},{1,5},{4,8},{5,9},{8,12},{9,13},{12,14},{13,15},{14,10},{15,... | collective-permute-start | bytes 3145736 | tf_op jit(solution)/shard_map/ppermute | solution.py:557
  87.1 25.2 %collective-permute-start.6 = (bf16[256,2048]{1,0:T(8,128)(2,1)}, bf16[256,2048]{1,0:T(8,128)(2,1)}, u32[]{:S(2)}, u32[]{:S(2)}) collective-permute-start(bf16[256,2048]{1,0:T(8,128)(2,1)} %collective-permute-done.2.refs_4_), channel_id=1, source_target_pairs={{0,2},{1,3},{4,0},{5,1},{8,4},{9,5},{12,8},{13,9},{14,12},{15,13},... | collective-permute-start | bytes 3145736 | tf_op jit(solution)/shard_map/ppermute | solution.py:557
  89.3 39.3 %collective-permute-start.11 = (bf16[416,2048]{1,0:T(8,128)(2,1)}, bf16[416,2048]{1,0:T(8,128)(2,1)}, u32[]{:S(2)}, u32[]{:S(2)}) collective-permute-start(bf16[416,2048]{1,0:T(8,128)(2,1)} %copy.62), channel_id=1, source_target_pairs={{0,16},{16,0},{1,17},{17,1},{2,18},{18,2},{3,19},{19,3},{4,20},{20... | collective-permute-start | bytes 5111816 | tf_op jit(solution)/shard_map/ppermute | solution.py:778
  112.3 3.0 collective-permute-start.7
  112.3 4.5 collective-permute-start.8
  114.1 495.7 %reduce-scatter.2.cloned.1.call-start = ((), (), s32[]{:S(2)}) async-start(), calls=%async_computation.3 | async-start | bytes 17825792 | tf_op jit(solution)/shard_map/reduce_scatter | solution.py:1007
  134.6 46.7 %collective-permute-start.10 = (bf16[256,2048]{1,0:T(8,128)(2,1)}, bf16[256,2048]{1,0:T(8,128)(2,1)}, u32[]{:S(2)}, u32[]{:S(2)}) collective-permute-start(bf16[256,2048]{1,0:T(8,128)(2,1)} %collective-permute-done.6.refs_2_), channel_id=1, source_target_pairs={{0,2},{1,3},{4,0},{5,1},{8,4},{9,5},{12,8},{13,9},{14,12},{15,13},... | collective-permute-start | bytes 3145736 | tf_op jit(solution)/shard_map/ppermute | solution.py:557
  136.2 45.1 %collective-permute-start.9 = (bf16[256,2048]{1,0:T(8,128)(2,1)}, bf16[256,2048]{1,0:T(8,128)(2,1)}, u32[]{:S(2)}, u32[]{:S(2)}) collective-permute-start(bf16[256,2048]{1,0:T(8,128)(2,1)} %collective-permute-done.5.refs_0_), channel_id=1, source_target_pairs={{0,4},{1,5},{4,8},{5,9},{8,12},{9,13},{12,14},{13,15},{14,10},{15,... | collective-permute-start | bytes 3145736 | tf_op jit(solution)/shard_map/ppermute | solution.py:557
  181.3 8.5 %collective-permute-start.12 = (bf16[256,2048]{1,0:T(8,128)(2,1)}, bf16[256,2048]{1,0:T(8,128)(2,1)}, u32[]{:S(2)}, u32[]{:S(2)}) collective-permute-start(bf16[256,2048]{1,0:T(8,128)(2,1)} %collective-permute-done.9.refs_0_), channel_id=1, source_target_pairs={{0,1},{1,0},{2,3},{3,2},{4,5},{5,4},{6,7},{7,6},{8,9},{9,8},{10,11... | collective-permute-start | bytes 3145736 | tf_op jit(solution)/shard_map/ppermute | solution.py:561
  181.3 8.5 %collective-permute-start.13 = (bf16[256,2048]{1,0:T(8,128)(2,1)}, bf16[256,2048]{1,0:T(8,128)(2,1)}, u32[]{:S(2)}, u32[]{:S(2)}) collective-permute-start(bf16[256,2048]{1,0:T(8,128)(2,1)} %collective-permute-done.10.refs_2_), channel_id=1, source_target_pairs={{0,1},{1,0},{2,3},{3,2},{4,5},{5,4},{6,7},{7,6},{8,9},{9,8},{10,11... | collective-permute-start | bytes 3145736 | tf_op jit(solution)/shard_map/ppermute | solution.py:561
  187.3 45.1 %collective-permute-start.18 = (bf16[896,1024]{0,1:T(8,128)(2,1)S(1)}, bf16[896,1024]{0,1:T(8,128)(2,1)}, u32[]{:S(2)}, u32[]{:S(2)}) collective-permute-start(bf16[896,1024]{0,1:T(8,128)(2,1)S(1)} %get-tuple-element.279), channel_id=1, source_target_pairs={{0,1},{1,0},{2,3},{3,2},{4,5},{5,4},{6,7},{7,6},{8,9},{9,8},{10,11... | collective-permute-start | bytes 5505032 | tf_op jit(solution)/shard_map/ppermute | solution.py:561
  189.8 26.0 %collective-permute-start.14 = (bf16[128,2048]{1,0:T(8,128)(2,1)S(1)}, bf16[128,2048]{1,0:T(8,128)(2,1)}, u32[]{:S(2)}, u32[]{:S(2)}) collective-permute-start(bf16[128,2048]{1,0:T(8,128)(2,1)S(1)} %slice.132), channel_id=1, source_target_pairs={{0,4},{1,5},{4,8},{5,9},{8,12},{9,13},{12,14},{13,15},{14,10},{15,... | collective-permute-start | bytes 1572872 | tf_op jit(solution)/shard_map/ppermute | solution.py:557
  191.7 38.2 %collective-permute-start.15 = (bf16[128,2048]{1,0:T(8,128)(2,1)S(1)}, bf16[128,2048]{1,0:T(8,128)(2,1)}, u32[]{:S(2)}, u32[]{:S(2)}) collective-permute-start(bf16[128,2048]{1,0:T(8,128)(2,1)S(1)} %slice.133), channel_id=1, source_target_pairs={{0,2},{1,3},{4,0},{5,1},{8,4},{9,5},{12,8},{13,9},{14,12},{15,13},... | collective-permute-start | bytes 1572872 | tf_op jit(solution)/shard_map/ppermute | solution.py:557
  367.8 33.2 %collective-permute-start.19 = (bf16[4096,896]{1,0:T(8,128)(2,1)}, bf16[4096,896]{1,0:T(8,128)(2,1)}, u32[]{:S(2)}, u32[]{:S(2)}) collective-permute-start(bf16[4096,896]{1,0:T(8,128)(2,1)} %get-tuple-element.237), channel_id=1, source_target_pairs={{0,1},{1,0},{2,3},{3,2},{4,5},{5,4},{6,7},{7,6},{8,9},{9,8},{10,11... | collective-permute-start | bytes 22020104 | tf_op jit(solution)/shard_map/ppermute | solution.py:561
  373.5 27.5 %collective-permute-start.39 = (f32[26048]{0:T(1024)S(1)}, f32[26048]{0:T(1024)S(1)}, u32[]{:S(2)}, u32[]{:S(2)}) collective-permute-start(f32[26048]{0:T(1024)S(1)} %concatenate.60), channel_id=1, source_target_pairs={{0,1},{1,0},{2,3},{3,2},{4,5},{5,4},{6,7},{7,6},{8,9},{9,8},{10,11... | collective-permute-start | bytes 312584 | tf_op jit(solution)/shard_map/ppermute | solution.py:882
  373.7 27.3 %collective-permute-start.40 = (f32[26048]{0:T(1024)S(1)}, f32[26048]{0:T(1024)S(1)}, u32[]{:S(2)}, u32[]{:S(2)}) collective-permute-start(f32[26048]{0:T(1024)S(1)} %concatenate.60), channel_id=1, source_target_pairs={{0,2},{1,3},{2,0},{3,1},{4,6},{5,7},{6,4},{7,5},{8,10},{9,11},{10,... | collective-permute-start | bytes 312584 | tf_op jit(solution)/shard_map/ppermute | solution.py:882
  373.9 27.1 %collective-permute-start.41 = (f32[26048]{0:T(1024)S(1)}, f32[26048]{0:T(1024)S(1)}, u32[]{:S(2)}, u32[]{:S(2)}) collective-permute-start(f32[26048]{0:T(1024)S(1)} %concatenate.60), channel_id=1, source_target_pairs={{0,3},{1,2},{2,1},{3,0},{4,7},{5,6},{6,5},{7,4},{8,11},{9,10},{10,... | collective-permute-start | bytes 312584 | tf_op jit(solution)/shard_map/ppermute | solution.py:882
  399.3 39.8 %collective-permute-start.29 = (bf16[416,2048]{1,0:T(8,128)(2,1)}, bf16[416,2048]{1,0:T(8,128)(2,1)S(1)}, u32[]{:S(2)}, u32[]{:S(2)}) collective-permute-start(bf16[416,2048]{1,0:T(8,128)(2,1)} %pad_maximum_fusion.3), channel_id=1, source_target_pairs={{0,16},{16,0},{1,17},{17,1},{2,18},{18,2},{3,19},{19,3},{4,20},{20... | collective-permute-start | bytes 5111816 | tf_op jit(solution)/shard_map/ppermute | solution.py:778
  408.0 20.1 %collective-permute-start.20 = (bf16[256,1024]{1,0:T(8,128)(2,1)}, bf16[256,1024]{1,0:T(8,128)(2,1)S(1)}, u32[]{:S(2)}, u32[]{:S(2)}) collective-permute-start(bf16[256,1024]{1,0:T(8,128)(2,1)} %get-tuple-element.208), channel_id=1, source_target_pairs={{0,4},{1,5},{4,8},{5,9},{8,12},{9,13},{12,14},{13,15},{14,10},{15,... | collective-permute-start | bytes 1572872 | tf_op jit(solution)/shard_map/ppermute | solution.py:557
  408.0 20.1 %collective-permute-start.21 = (bf16[256,1024]{1,0:T(8,128)(2,1)S(1)}, bf16[256,1024]{1,0:T(8,128)(2,1)S(1)}, u32[]{:S(2)}, u32[]{:S(2)}) collective-permute-start(bf16[256,1024]{1,0:T(8,128)(2,1)S(1)} %get-tuple-element.209), channel_id=1, source_target_pairs={{0,2},{1,3},{4,0},{5,1},{8,4},{9,5},{12,8},{13,9},{14,12},{15,13},... | collective-permute-start | bytes 1572872 | tf_op jit(solution)/shard_map/ppermute | solution.py:557
  430.7 46.5 %collective-permute-start.22 = (bf16[512,1024]{1,0:T(8,128)(2,1)}, bf16[512,1024]{1,0:T(8,128)(2,1)}, u32[]{:S(2)}, u32[]{:S(2)}) collective-permute-start(bf16[512,1024]{1,0:T(8,128)(2,1)} %pad_maximum_fusion.4), channel_id=1, source_target_pairs={{0,4},{1,5},{4,8},{5,9},{8,12},{9,13},{12,14},{13,15},{14,10},{15,... | collective-permute-start | bytes 3145736 | tf_op jit(solution)/shard_map/ppermute | solution.py:557
  430.9 56.0 %collective-permute-start.23 = (bf16[512,1024]{1,0:T(8,128)(2,1)}, bf16[512,1024]{1,0:T(8,128)(2,1)}, u32[]{:S(2)}, u32[]{:S(2)}) collective-permute-start(bf16[512,1024]{1,0:T(8,128)(2,1)} %pad_maximum_fusion.5), channel_id=1, source_target_pairs={{0,2},{1,3},{4,0},{5,1},{8,4},{9,5},{12,8},{13,9},{14,12},{15,13},... | collective-permute-start | bytes 3145736 | tf_op jit(solution)/shard_map/ppermute | solution.py:557
  440.7 112.7 %all-to-all-start.1 = ((bf16[16,416,128]{2,1,0:T(8,128)(2,1)}), bf16[16,416,128]{2,1,0:T(8,128)(2,1)}, u32[]{:S(2)}, u32[]{:S(2)}) async-start(bf16[16,416,128]{2,1,0:T(8,128)(2,1)} %bitcast_bitcast_fusion), calls=%async_computation.2 | async-start | bytes 3407872 | tf_op jit(solution)/shard_map/all_to_all | solution.py:1066
  445.1 57.0 %collective-permute-start.26 = (bf16[256,2048]{1,0:T(8,128)(2,1)S(1)}, bf16[256,2048]{1,0:T(8,128)(2,1)S(1)}, u32[]{:S(2)}, u32[]{:S(2)}) collective-permute-start(bf16[256,2048]{1,0:T(8,128)(2,1)S(1)} %convolution_convert_fusion.2), channel_id=1, source_target_pairs={{0,16},{16,0},{1,17},{17,1},{2,18},{18,2},{3,19},{19,3},{4,20},{20... | collective-permute-start | bytes 3145736 | tf_op jit(solution)/shard_map/ppermute | solution.py:778
  490.1 40.2 %collective-permute-start.24 = (bf16[512,1024]{1,0:T(8,128)(2,1)S(1)}, bf16[512,1024]{1,0:T(8,128)(2,1)S(1)}, u32[]{:S(2)}, u32[]{:S(2)}) collective-permute-start(bf16[512,1024]{1,0:T(8,128)(2,1)S(1)} %add_convert_fusion.4), channel_id=1, source_target_pairs={{0,4},{1,5},{4,8},{5,9},{8,12},{9,13},{12,14},{13,15},{14,10},{15,... | collective-permute-start | bytes 3145736 | tf_op jit(solution)/shard_map/ppermute | solution.py:557
  493.1 39.1 %collective-permute-start.25 = (bf16[512,1024]{1,0:T(8,128)(2,1)S(1)}, bf16[512,1024]{1,0:T(8,128)(2,1)S(1)}, u32[]{:S(2)}, u32[]{:S(2)}) collective-permute-start(bf16[512,1024]{1,0:T(8,128)(2,1)S(1)} %add_convert_fusion.3), channel_id=1, source_target_pairs={{0,2},{1,3},{4,0},{5,1},{8,4},{9,5},{12,8},{13,9},{14,12},{15,13},... | collective-permute-start | bytes 3145736 | tf_op jit(solution)/shard_map/ppermute | solution.py:557
  534.9 37.7 %collective-permute-start.27 = (bf16[512,1024]{1,0:T(8,128)(2,1)}, bf16[512,1024]{1,0:T(8,128)(2,1)}, u32[]{:S(2)}, u32[]{:S(2)}) collective-permute-start(bf16[512,1024]{1,0:T(8,128)(2,1)} %add_convert_fusion.2), channel_id=1, source_target_pairs={{0,4},{1,5},{4,8},{5,9},{8,12},{9,13},{12,14},{13,15},{14,10},{15,... | collective-permute-start | bytes 3145736 | tf_op jit(solution)/shard_map/ppermute | solution.py:557
  545.7 27.1 %collective-permute-start.28 = (bf16[512,1024]{1,0:T(8,128)(2,1)}, bf16[512,1024]{1,0:T(8,128)(2,1)}, u32[]{:S(2)}, u32[]{:S(2)}) collective-permute-start(bf16[512,1024]{1,0:T(8,128)(2,1)} %add_convert_fusion.1), channel_id=1, source_target_pairs={{0,2},{1,3},{4,0},{5,1},{8,4},{9,5},{12,8},{13,9},{14,12},{15,13},... | collective-permute-start | bytes 3145736 | tf_op jit(solution)/shard_map/ppermute | solution.py:557
  551.3 33.5 %collective-permute-start.42 = (f32[26048]{0:T(1024)S(1)}, f32[26048]{0:T(1024)S(1)}, u32[]{:S(2)}, u32[]{:S(2)}) collective-permute-start(f32[26048]{0:T(1024)S(1)} %add_add_fusion.1), channel_id=1, source_target_pairs={{0,4},{1,5},{2,6},{3,7},{4,0},{5,1},{6,2},{7,3},{8,12},{9,13},{10,... | collective-permute-start | bytes 312584 | tf_op jit(solution)/shard_map/ppermute | solution.py:882
  555.8 25.1 %collective-permute-start.30 = (bf16[16,256,128]{2,1,0:T(8,128)(2,1)}, bf16[16,256,128]{2,1,0:T(8,128)(2,1)S(1)}, u32[]{:S(2)}, u32[]{:S(2)}) collective-permute-start(bf16[16,256,128]{2,1,0:T(8,128)(2,1)} %slice.155.grad_ref), channel_id=1, source_target_pairs={{0,16},{16,0},{1,17},{17,1},{2,18},{18,2},{3,19},{19,3},{4,20},{20... | collective-permute-start | bytes 3145736 | tf_op jit(solution)/shard_map/ppermute | solution.py:778
  565.0 16.0 %collective-permute-start.31 = (bf16[160,128]{1,0:T(8,128)(2,1)S(1)}, bf16[160,128]{1,0:T(8,128)(2,1)S(1)}, u32[]{:S(2)}, u32[]{:S(2)}) collective-permute-start(bf16[160,128]{1,0:T(8,128)(2,1)S(1)} %slice_reduce_fusion), channel_id=1, source_target_pairs={{0,16},{16,0},{1,17},{17,1},{2,18},{18,2},{3,19},{19,3},{4,20},{20... | collective-permute-start | bytes 122888 | tf_op jit(solution)/shard_map/ppermute | solution.py:778
  572.7 12.2 %collective-permute-start.43 = (f32[26048]{0:T(1024)S(1)}, f32[26048]{0:T(1024)S(1)}, u32[]{:S(2)}, u32[]{:S(2)}) collective-permute-start(f32[26048]{0:T(1024)S(1)} %add_add_fusion.1), channel_id=1, source_target_pairs={{0,8},{1,9},{2,10},{3,11},{4,12},{5,13},{6,14},{7,15},{8,0},{9,1},... | collective-permute-start | bytes 312584 | tf_op jit(solution)/shard_map/ppermute | solution.py:882
  572.8 12.1 %collective-permute-start.44 = (f32[26048]{0:T(1024)S(1)}, f32[26048]{0:T(1024)S(1)}, u32[]{:S(2)}, u32[]{:S(2)}) collective-permute-start(f32[26048]{0:T(1024)S(1)} %add_add_fusion.1), channel_id=1, source_target_pairs={{0,12},{1,13},{2,14},{3,15},{4,8},{5,9},{6,10},{7,11},{8,4},{9,5},... | collective-permute-start | bytes 312584 | tf_op jit(solution)/shard_map/ppermute | solution.py:882
  584.8 7.8 %collective-permute-start.32 = (f32[256,1024]{1,0:T(8,128)S(1)}, f32[256,1024]{1,0:T(8,128)}, u32[]{:S(2)}, u32[]{:S(2)}) collective-permute-start(f32[256,1024]{1,0:T(8,128)S(1)} %constant_dynamic-slice_fusion), channel_id=1, source_target_pairs={{0,1},{1,0},{2,3},{3,2},{4,5},{5,4},{6,7},{7,6},{8,9},{9,8},{10,11... | collective-permute-start | bytes 3145736 | tf_op jit(solution)/shard_map/ppermute | solution.py:561
  595.0 5.4 collective-permute-start.33
  595.6 4.8 collective-permute-start.34
  597.1 3.3 collective-permute-start.35
  600.5 4.5 collective-permute-start.36
  600.8 4.6 collective-permute-start.37
  602.8 5.4 collective-permute-start.38
  608.2 5.4 collective-permute-start.45
  (42 other events, 471.8 us)
Sparse Core Ops, SparseCore 0:
  114.2 155.6 all-gather.3
  280.2 205.4 reduce-scatter.1

commit v7 on v6

--- a/solution.py
+++ b/solution.py
@@ -1140,10 +1140,16 @@
         g_normed = inward.finish(new_out, g_peer, g_apart)
     else:
         g_normed = inward.finish(new_out)
+    ratio = root * g_in
+    lean = jnp.sum(g_in * g_normed * inputs_f, axis=1, keepdims=True)
+    g_inputs = ratio * g_normed - inputs_f * (root * root * root / D * lean)
+    grad_tokens = (cotangent.astype(F32) + g_inputs).astype(BF)
+    g_g_in = jnp.sum(g_normed * inputs_f * root, axis=0)
+
     if paired:
         g_apart = jnp.concatenate(in_order(g_shared, g_apart), axis=0)
     if simple:
-        moved = adamw_rows(base, own, g_peer, (1 - slot) * blocks, size, moved)
+        moved = adamw_rows(base, own, after(g_peer, g_g_in), (1 - slot) * blocks, size, moved)
         moved = adamw_rows(base, own, g_apart, 2 * E // H, H, moved)
         new_in, mom_in, sec_in, low_in = (result.T for result in moved)
     else:
@@ -1162,11 +1168,6 @@
         )
         low_in = new_in.astype(BF)
 
-    ratio = root * g_in
-    lean = jnp.sum(g_in * g_normed * inputs_f, axis=1, keepdims=True)
-    g_inputs = ratio * g_normed - inputs_f * (root * root * root / D * lean)
-    grad_tokens = (cotangent.astype(F32) + g_inputs).astype(BF)
-    g_g_in = jnp.sum(g_normed * inputs_f * root, axis=0)
 
     if stepwise():
         small = quad_sum(quad_sum(g_g_in, 1, 2), 4, 8)

time: 631 us -> 630 us (level)
  transfers between devices with their start and end apart: 50 -> 50, of which waited for: 23 -> 24; matrix products, arithmetic and copies ran while one was open for 27% -> 27% of each run, Pallas kernels for 22% -> 22%
where the time goes in v7:
time: 630 us; the launch traced here: 620 us
  waiting for transfers between devices  201 us (32%)
  Pallas kernels  138 us (22%)
  matrix products  92.8 us (15%)
  starting transfers between devices  70.9 us (11%)
  other arithmetic  46.5 us (7%)
  local copies, waits for them, and re-layouts  33 us (5%)
  blocking collectives  20.7 us (3%)
  between operations  17 us (3%)
    ppermute x16, waiting for transfers between devices, hop(): return lax.ppermute(values, 'dp', pairs)  141 us
    pallas_call x1, Pallas kernels, run_backward(): pl.pallas_call(partial(backward_kernel, heads), grid=(count,), in_specs=[...  50.8 us
    dot_general x16, matrix products, chunk(): jnp.dot(lax.dynamic_slice_in_dim(after(side, deps), start, rows, 0), weig...  44 us
    pallas_call x4, Pallas kernels, absorb(): pl.pallas_call(partial(absorb_kernel, count, by_rows), grid_spec=pltpu.Pr...  42 us
    ppermute x16, starting transfers between devices, hop(): return lax.ppermute(values, 'dp', pairs)  35.2 us
    pallas_call x1, Pallas kernels, run_forward(): pl.pallas_call(partial(forward_kernel, heads), grid=(count,), in_specs=[r...  27.6 us
    all_to_all x1, waiting for transfers between devices, per_device(): mine = lax.all_to_all(weight_halves(weight_low, units), 'dp', 0, 0)  24.4 us
    ppermute x6, waiting for transfers between devices, other_width(): return lax.ppermute(values, 'width', [(0, 1), (1, 0)])  23.9 us
  transfers between devices with their start and end apart: 50, of which 24 were waited for; matrix products, arithmetic and copies ran while one was open for 27% of the time, Pallas kernels for 22%

profile of v7, /device:TPU:0, one launch (start us, length us, event | category | flops | bytes accessed | tf_op | source)
XLA Modules:
  0.0 620.0 jit_solution(6888982369257760138)
XLA Ops:
  11.3 7.5 %all-to-all-start = ((bf16[16,416,128]{2,1,0:T(8,128)(2,1)}), bf16[16,416,128]{2,1,0:T(8,128)(2,1)}, u32[]{:S(2)}, u32[]{:S(2)}) async-start(bf16[16,416,128]{2,1,0:T(8,128)(2,1)} %pad_maximum_fusion.1), calls=%async_computation | async-start | bytes 3407872 | tf_op jit(solution)/shard_map/all_to_all | solution.py:947
  25.0 3.9 iota_subtract_fusion
  28.9 24.4 %all-to-all-done = bf16[16,416,128]{2,1,0:T(8,128)(2,1)} async-done(((bf16[16,416,128]{2,1,0:T(8,128)(2,1)}), bf16[16,416,128]{2,1,0:T(8,128)(2,1)}, u32[]{:S(2)}, u32[]{:S(2)}) %all-to-all-start) | async-done | bytes 1703968 | tf_op jit(solution)/shard_map/all_to_all | solution.py:947
  53.3 2.8 copy.59
  56.1 13.8 %collective-permute-done.1.refs_2_ = bf16[256,2048]{1,0:T(8,128)(2,1)} collective-permute-done((bf16[256,2048]{1,0:T(8,128)(2,1)S(1)}, bf16[256,2048]{1,0:T(8,128)(2,1)}, u32[]{:S(2)}, u32[]{:S(2)}) %collective-permute-start.1) | collective-permute-done | bytes 1048608 | tf_op jit(solution)/shard_map/ppermute | solution.py:557
  72.4 3.8 collective-permute-done.3.refs_3_
  76.4 10.7 %collective-permute-start.5 = (bf16[256,2048]{1,0:T(8,128)(2,1)}, bf16[256,2048]{1,0:T(8,128)(2,1)}, u32[]{:S(2)}, u32[]{:S(2)}) collective-permute-start(bf16[256,2048]{1,0:T(8,128)(2,1)} %collective-permute-done.1.refs_2_), channel_id=1, source_target_pairs={{0,4},{1,5},{4,8},{5,9},{8,12},{9,13},{12,14},{13,15},{14,10},{15,... | collective-permute-start | bytes 3145736 | tf_op jit(solution)/shard_map/ppermute | solution.py:557
  90.8 19.3 %collective-permute-done.5.refs_0_ = bf16[256,2048]{1,0:T(8,128)(2,1)} collective-permute-done((bf16[256,2048]{1,0:T(8,128)(2,1)}, bf16[256,2048]{1,0:T(8,128)(2,1)}, u32[]{:S(2)}, u32[]{:S(2)}) %collective-permute-start.5) | collective-permute-done | bytes 1048608 | tf_op jit(solution)/shard_map/ppermute | solution.py:557
  116.8 11.8 %collective-permute-done.11 = bf16[416,2048]{1,0:T(8,128)(2,1)} collective-permute-done((bf16[416,2048]{1,0:T(8,128)(2,1)}, bf16[416,2048]{1,0:T(8,128)(2,1)}, u32[]{:S(2)}, u32[]{:S(2)}) %collective-permute-start.11) | collective-permute-done | bytes 1703968 | tf_op jit(solution)/shard_map/ppermute | solution.py:778
  128.6 3.8 copy.63
  139.6 13.8 %absorb_rows.4 = (bf16[4096,2048]{1,0:T(8,128)(2,1)}, bf16[4096,896]{1,0:T(8,128)(2,1)}) custom-call(s32[6]{0:T(128)} %stack.106.starts_ref, bf16[256,2048]{1,0:T(8,128)(2,1)} %copy-done.9, bf16[256,2048]{1,0:T(8,128)(2,1)} %collective-permute-done.refs_1_, bf16[256,2048]{1,0:T(8,128)(2,1)} %collective-permute-done.1.refs_2_, bf16[256,2048]{1,0:T(8,128)(2,1)} %copy-done.25, ...), custom_call_target="tpu_custom_call" | custom-call | flops 112742891520 | bytes 16252928 | tf_op jit(solution)/shard_map/absorb_rows/pallas_call | solution.py:603
  153.3 10.4 %absorb_rows.5 = (bf16[4096,2048]{1,0:T(8,128)(2,1)}, bf16[4096,896]{1,0:T(8,128)(2,1)}) custom-call(s32[4]{0:T(128)} %get-tuple-element.305.starts_ref, bf16[256,2048]{1,0:T(8,128)(2,1)} %collective-permute-done.5.refs_0_, bf16[256,2048]{1,0:T(8,128)(2,1)} %collective-permute-done.7.refs_1_, ...), custom_call_target="tpu_custom_call", output_to_operand_aliasing={{0}: (6, {}), {1}: (7, {})} | custom-call | flops 75161927680 | bytes 12058624 | tf_op jit(solution)/shard_map/absorb_rows/pallas_call | solution.py:603
  163.8 17.5 %collective-permute-done.10.refs_2_ = bf16[256,2048]{1,0:T(8,128)(2,1)} collective-permute-done((bf16[256,2048]{1,0:T(8,128)(2,1)}, bf16[256,2048]{1,0:T(8,128)(2,1)}, u32[]{:S(2)}, u32[]{:S(2)}) %collective-permute-start.10) | collective-permute-done | bytes 1048608 | tf_op jit(solution)/shard_map/ppermute | solution.py:557
  183.7 3.6 dynamic-slice_bitcast_fusion
  192.1 10.4 %absorb_rows.6 = (bf16[4096,2048]{1,0:T(8,128)(2,1)}, bf16[4096,896]{1,0:T(8,128)(2,1)}) custom-call(s32[4]{0:T(128)} %pad_add_fusion.2.starts_ref, bf16[256,2048]{1,0:T(8,128)(2,1)} %collective-permute-done.9.refs_0_, bf16[256,2048]{1,0:T(8,128)(2,1)} %collective-permute-done.12.refs_1_, ...), custom_call_target="tpu_custom_call", output_to_operand_aliasing={{0}: (6, {}), {1}: (7, {})} | custom-call | flops 75161927680 | bytes 12058624 | tf_op jit(solution)/shard_map/absorb_rows/pallas_call | solution.py:603
  202.5 13.3 %collective-permute-done.14.refs_0_ = bf16[128,2048]{1,0:T(8,128)(2,1)} collective-permute-done((bf16[128,2048]{1,0:T(8,128)(2,1)S(1)}, bf16[128,2048]{1,0:T(8,128)(2,1)}, u32[]{:S(2)}, u32[]{:S(2)}) %collective-permute-start.14) | collective-permute-done | bytes 524320 | tf_op jit(solution)/shard_map/ppermute | solution.py:557
  215.8 14.2 %collective-permute-done.15.refs_2_ = bf16[128,2048]{1,0:T(8,128)(2,1)} collective-permute-done((bf16[128,2048]{1,0:T(8,128)(2,1)S(1)}, bf16[128,2048]{1,0:T(8,128)(2,1)}, u32[]{:S(2)}, u32[]{:S(2)}) %collective-permute-start.15) | collective-permute-done | bytes 524320 | tf_op jit(solution)/shard_map/ppermute | solution.py:557
  233.6 7.4 %absorb_rows.7 = (bf16[4096,2048]{1,0:T(8,128)(2,1)}, bf16[4096,896]{1,0:T(8,128)(2,1)}) custom-call(s32[4]{0:T(128)} %get-tuple-element.304.starts_ref, bf16[128,2048]{1,0:T(8,128)(2,1)} %collective-permute-done.14.refs_0_, bf16[128,2048]{1,0:T(8,128)(2,1)} %copy-done.26, ...), custom_call_target="tpu_custom_call", output_to_operand_aliasing={{0}: (6, {}), {1}: (7, {})} | custom-call | flops 37580963840 | bytes 7864320 | tf_op jit(solution)/shard_map/absorb_rows/pallas_call | solution.py:603
  241.7 27.6 %scan_forward.1 = (bf16[4096,256]{1,0:T(8,128)(2,1)}, f32[4096,256]{1,0:T(8,128)}, f32[8,4096]{1,0:T(8,128)}, f32[16,256,128]{2,1,0:T(8,128)}, f32[256,128]{1,0:T(8,128)}) custom-call(bf16[4096,896]{1,0:T(8,128)(2,1)} %get-tuple-element.194.gate_ref.x_ref.bc_ref.dt_ref.xprev_ref.bcprev_ref, ...), custom_call_target="tpu_custom_call" | custom-call | flops 20971520000 | bytes 20480000 | tf_op jit(solution)/shard_map/scan_forward/pallas_call | solution.py:405
  270.3 9.7 %convolution_convert_fusion = bf16[4096,2048]{1,0:T(8,128)(2,1)} fusion(bf16[4096,256]{1,0:T(8,128)(2,1)} %get-tuple-element.195, f32[256,2048]{1,0:T(8,128)S(1)} %copy-done.2), kind=kOutput, calls=%fused_computation | convolution fusion | flops 4303880192 | bytes 20971520 | tf_op jit(solution)/shard_map/dot_general | solution.py:1006
  280.1 14.2 %multiply_reduce_fusion = (f32[4096]{0:T(1024)S(1)}, f32[4096,256]{1,0:T(8,128)}) fusion(bf16[4096,256]{1,0:T(8,128)(2,1)} %get-tuple-element.195, bf16[4096,2048]{1,0:T(8,128)(2,1)} %all-gather.4.cloned.1.call-done, f32[256,2048]{1,0:T(8,128)S(1)} %copy-done.2), kind=kOutput, calls=%fused_computation.9 | convolution fusion | flops 4298633216 | bytes 25182208 | tf_op jit(solution)/shard_map/dot_general | solution.py:1008
  294.3 20.7 %all-gather.1 = f32[16,2,4096]{2,1,0:T(2,128)S(1)} all-gather(f32[1,2,4096]{2,1,0:T(2,128)S(1)} %maximum_bitcast_fusion), channel_id=2, replica_groups=mesh['width'=2,'dp'=16] {'dp'}, dimensions={0}, use_global_device_ids=true | all-gather | bytes 557056 | tf_op jit(solution)/shard_map/all_gather | solution.py:1012
  317.1 50.8 %scan_backward.1 = (bf16[4096,896]{1,0:T(8,128)(2,1)}, bf16[4096,256]{1,0:T(8,128)(2,1)}, f32[256,128]{1,0:T(8,128)}, f32[16,256]{1,0:T(8,128)}, f32[16,256]{1,0:T(8,128)}, /*index=5*/f32[8,128]{1,0:T(8,128)}) custom-call(bf16[4096,896]{1,0:T(8,128)(2,1)} %get-tuple-element.194.gate_ref.x_ref.bc_ref.dt_ref.xprev_ref.bcprev_ref, ...), custom_call_target="tpu_custom_call" | custom-call | flops 41943040000 | bytes 32768000 | tf_op jit(solution)/shard_map/scan_backward/pallas_call | solution.py:473
  375.4 20.4 %convolution_convert_fusion.1 = bf16[896,2048]{1,0:T(8,128)(2,1)S(1)} fusion(bf16[4096,896]{1,0:T(8,128)(2,1)} %get-tuple-element.238, bf16[4096,2048]{1,0:T(8,128)(2,1)} %get-tuple-element.204), kind=kOutput, calls=%fused_computation.12 | convolution fusion | flops 15034220544 | bytes 27787264 | tf_op jit(solution)/shard_map/dot_general | solution.py:1049
  401.1 3.2 fusion.41
  404.3 2.7 convolution_add_fusion.7
  410.1 4.6 fusion.35
  414.8 4.5 convolution_convert_fusion.2
  419.3 3.2 convolution_add_fusion.5
  422.4 3.2 fusion.38
  432.7 6.3 %collective-permute-done.29 = bf16[416,2048]{1,0:T(8,128)(2,1)S(1)} collective-permute-done((bf16[416,2048]{1,0:T(8,128)(2,1)}, bf16[416,2048]{1,0:T(8,128)(2,1)S(1)}, u32[]{:S(2)}, u32[]{:S(2)}) %collective-permute-start.29) | collective-permute-done | bytes 1703968 | tf_op jit(solution)/shard_map/ppermute | solution.py:778
  440.7 4.4 all-to-all-start.1
  446.7 3.2 fusion.29
  449.9 3.2 fusion.32
  457.0 20.2 %collective-permute-done.22 = bf16[512,1024]{1,0:T(8,128)(2,1)} collective-permute-done((bf16[512,1024]{1,0:T(8,128)(2,1)}, bf16[512,1024]{1,0:T(8,128)(2,1)}, u32[]{:S(2)}, u32[]{:S(2)}) %collective-permute-start.22) | collective-permute-done | bytes 1048608 | tf_op jit(solution)/shard_map/ppermute | solution.py:557
  477.2 9.6 %collective-permute-done.23 = bf16[512,1024]{1,0:T(8,128)(2,1)} collective-permute-done((bf16[512,1024]{1,0:T(8,128)(2,1)}, bf16[512,1024]{1,0:T(8,128)(2,1)}, u32[]{:S(2)}, u32[]{:S(2)}) %collective-permute-start.23) | collective-permute-done | bytes 1048608 | tf_op jit(solution)/shard_map/ppermute | solution.py:557
  490.0 2.9 collective-permute-start.24
  493.2 3.1 fusion.23
  497.5 3.1 fusion.26
  503.6 26.6 %collective-permute-done.24 = bf16[512,1024]{1,0:T(8,128)(2,1)S(1)} collective-permute-done((bf16[512,1024]{1,0:T(8,128)(2,1)S(1)}, bf16[512,1024]{1,0:T(8,128)(2,1)S(1)}, u32[]{:S(2)}, u32[]{:S(2)}) %collective-permute-start.24) | collective-permute-done | bytes 1048608 | tf_op jit(solution)/shard_map/ppermute | solution.py:557
  534.9 10.7 %collective-permute-start.27 = (bf16[512,1024]{1,0:T(8,128)(2,1)}, bf16[512,1024]{1,0:T(8,128)(2,1)}, u32[]{:S(2)}, u32[]{:S(2)}) collective-permute-start(bf16[512,1024]{1,0:T(8,128)(2,1)} %add_convert_fusion.2), channel_id=1, source_target_pairs={{0,4},{1,5},{4,8},{5,9},{8,12},{9,13},{12,14},{13,15},{14,10},{15,... | collective-permute-start | bytes 3145736 | tf_op jit(solution)/shard_map/ppermute | solution.py:557
  545.6 3.1 fusion.20
  557.3 6.4 %fusion.71 = (bf16[256,2048]{1,0:T(8,128)(2,1)}, f32[256,2048]{1,0:T(8,128)}, f32[256,2048]{1,0:T(8,128)}, f32[256,2048]{1,0:T(8,128)}) fusion(f32[256,2048]{1,0:T(8,128)S(1)} %copy-done.2, f32[]{:T(128)} %bitcast.40, f32[256,2048]{1,0:T(8,128)S(1)} %copy-done.3, f32[256,2048]{1,0:T(8,128)} %param.24, f32[256,2048]{1,0:T(8,128)} %param.23), kind=kLoop, calls=%fused_computation.173 | loop fusion | flops 7864320 | bytes 15728644 | tf_op jit(solution)/shard_map/convert_element_type | solution.py:1192
  565.4 7.2 %adamw.3 = (f32[8512,128]{1,0:T(8,128)}, f32[8512,128]{1,0:T(8,128)}, f32[8512,128]{1,0:T(8,128)}, bf16[8512,128]{1,0:T(8,128)(2,1)}) custom-call(s32[1]{0:T(128)} %bitcast.46.first_ref, f32[1,1]{1,0:T(1,128)} %bitcast.47.base_ref, f32[8512,128]{1,0:T(8,128)} %bitcast.100, f32[8512,128]{1,0:T(8,128)} %bitcast.107, f32[8512,128]{1,0:T(8,128)} %bitcast.110, ...), custom_call_target="tpu_custom_call" | custom-call | flops 5242880000 | bytes 15728640 | tf_op jit(solution)/shard_map/adamw/pallas_call | solution.py:854
  575.0 5.9 collective-permute-done.31
  596.3 3.8 fusion.11
  601.5 7.0 %adamw.4 = (f32[8512,128]{1,0:T(8,128)}, f32[8512,128]{1,0:T(8,128)}, f32[8512,128]{1,0:T(8,128)}, bf16[8512,128]{1,0:T(8,128)(2,1)}) custom-call(s32[1]{0:T(128)} %bitcast.50.first_ref, f32[1,1]{1,0:T(1,128)} %bitcast.47.base_ref, f32[8512,128]{1,0:T(8,128)} %bitcast.101, ...), custom_call_target="tpu_custom_call", output_to_operand_aliasing={{0}: (6, {}), {1}: (7, {}), {2}: (8, {}), {3}: (9, {})} | custom-call | flops 5242880000 | bytes 15728640 | tf_op jit(solution)/shard_map/adamw/pallas_call | solution.py:854
  608.6 3.4 adamw.5
  (275 shorter events, 115.9 us)
Async XLA Ops:
  11.3 42.1 %all-to-all-start = ((bf16[16,416,128]{2,1,0:T(8,128)(2,1)}), bf16[16,416,128]{2,1,0:T(8,128)(2,1)}, u32[]{:S(2)}, u32[]{:S(2)}) async-start(bf16[16,416,128]{2,1,0:T(8,128)(2,1)} %pad_maximum_fusion.1), calls=%async_computation | async-start | bytes 3407872 | tf_op jit(solution)/shard_map/all_to_all | solution.py:947
  18.8 261.3 %all-gather.4.cloned.1.call-start = ((), (), s32[]{:S(2)}) async-start(), calls=%async_computation.4 | async-start | bytes 17825792 | tf_op jit(solution)/shard_map/all_gather | solution.py:999
  19.5 3.5 collective-permute-start
  23.0 46.8 %collective-permute-start.1 = (bf16[256,2048]{1,0:T(8,128)(2,1)S(1)}, bf16[256,2048]{1,0:T(8,128)(2,1)}, u32[]{:S(2)}, u32[]{:S(2)}) collective-permute-start(bf16[256,2048]{1,0:T(8,128)(2,1)S(1)} %fusion.6.refs_0_), channel_id=1, source_target_pairs={{0,4},{1,5},{4,8},{5,9},{8,12},{9,13},{12,14},{13,15},{14,10},{15,... | collective-permute-start | bytes 3145736 | tf_op jit(solution)/shard_map/ppermute | solution.py:557
  24.7 47.2 %collective-permute-start.2 = (bf16[256,2048]{1,0:T(8,128)(2,1)S(1)}, bf16[256,2048]{1,0:T(8,128)(2,1)}, u32[]{:S(2)}, u32[]{:S(2)}) collective-permute-start(bf16[256,2048]{1,0:T(8,128)(2,1)S(1)} %fusion.6.refs_0_), channel_id=1, source_target_pairs={{0,2},{1,3},{4,0},{5,1},{8,4},{9,5},{12,8},{13,9},{14,12},{15,13},... | collective-permute-start | bytes 3145736 | tf_op jit(solution)/shard_map/ppermute | solution.py:557
  71.9 4.3 collective-permute-start.3
  71.9 4.5 collective-permute-start.4
  76.4 33.7 %collective-permute-start.5 = (bf16[256,2048]{1,0:T(8,128)(2,1)}, bf16[256,2048]{1,0:T(8,128)(2,1)}, u32[]{:S(2)}, u32[]{:S(2)}) collective-permute-start(bf16[256,2048]{1,0:T(8,128)(2,1)} %collective-permute-done.1.refs_2_), channel_id=1, source_target_pairs={{0,4},{1,5},{4,8},{5,9},{8,12},{9,13},{12,14},{13,15},{14,10},{15,... | collective-permute-start | bytes 3145736 | tf_op jit(solution)/shard_map/ppermute | solution.py:557
  87.1 25.2 %collective-permute-start.6 = (bf16[256,2048]{1,0:T(8,128)(2,1)}, bf16[256,2048]{1,0:T(8,128)(2,1)}, u32[]{:S(2)}, u32[]{:S(2)}) collective-permute-start(bf16[256,2048]{1,0:T(8,128)(2,1)} %collective-permute-done.2.refs_4_), channel_id=1, source_target_pairs={{0,2},{1,3},{4,0},{5,1},{8,4},{9,5},{12,8},{13,9},{14,12},{15,13},... | collective-permute-start | bytes 3145736 | tf_op jit(solution)/shard_map/ppermute | solution.py:557
  89.3 39.3 %collective-permute-start.11 = (bf16[416,2048]{1,0:T(8,128)(2,1)}, bf16[416,2048]{1,0:T(8,128)(2,1)}, u32[]{:S(2)}, u32[]{:S(2)}) collective-permute-start(bf16[416,2048]{1,0:T(8,128)(2,1)} %copy.62), channel_id=1, source_target_pairs={{0,16},{16,0},{1,17},{17,1},{2,18},{18,2},{3,19},{19,3},{4,20},{20... | collective-permute-start | bytes 5111816 | tf_op jit(solution)/shard_map/ppermute | solution.py:778
  112.3 3.0 collective-permute-start.7
  112.3 4.5 collective-permute-start.8
  114.1 482.2 %reduce-scatter.2.cloned.1.call-start = ((), (), s32[]{:S(2)}) async-start(), calls=%async_computation.3 | async-start | bytes 17825792 | tf_op jit(solution)/shard_map/reduce_scatter | solution.py:1007
  134.6 46.7 %collective-permute-start.10 = (bf16[256,2048]{1,0:T(8,128)(2,1)}, bf16[256,2048]{1,0:T(8,128)(2,1)}, u32[]{:S(2)}, u32[]{:S(2)}) collective-permute-start(bf16[256,2048]{1,0:T(8,128)(2,1)} %collective-permute-done.6.refs_2_), channel_id=1, source_target_pairs={{0,2},{1,3},{4,0},{5,1},{8,4},{9,5},{12,8},{13,9},{14,12},{15,13},... | collective-permute-start | bytes 3145736 | tf_op jit(solution)/shard_map/ppermute | solution.py:557
  136.2 45.1 %collective-permute-start.9 = (bf16[256,2048]{1,0:T(8,128)(2,1)}, bf16[256,2048]{1,0:T(8,128)(2,1)}, u32[]{:S(2)}, u32[]{:S(2)}) collective-permute-start(bf16[256,2048]{1,0:T(8,128)(2,1)} %collective-permute-done.5.refs_0_), channel_id=1, source_target_pairs={{0,4},{1,5},{4,8},{5,9},{8,12},{9,13},{12,14},{13,15},{14,10},{15,... | collective-permute-start | bytes 3145736 | tf_op jit(solution)/shard_map/ppermute | solution.py:557
  181.3 8.5 %collective-permute-start.12 = (bf16[256,2048]{1,0:T(8,128)(2,1)}, bf16[256,2048]{1,0:T(8,128)(2,1)}, u32[]{:S(2)}, u32[]{:S(2)}) collective-permute-start(bf16[256,2048]{1,0:T(8,128)(2,1)} %collective-permute-done.9.refs_0_), channel_id=1, source_target_pairs={{0,1},{1,0},{2,3},{3,2},{4,5},{5,4},{6,7},{7,6},{8,9},{9,8},{10,11... | collective-permute-start | bytes 3145736 | tf_op jit(solution)/shard_map/ppermute | solution.py:561
  181.3 8.5 %collective-permute-start.13 = (bf16[256,2048]{1,0:T(8,128)(2,1)}, bf16[256,2048]{1,0:T(8,128)(2,1)}, u32[]{:S(2)}, u32[]{:S(2)}) collective-permute-start(bf16[256,2048]{1,0:T(8,128)(2,1)} %collective-permute-done.10.refs_2_), channel_id=1, source_target_pairs={{0,1},{1,0},{2,3},{3,2},{4,5},{5,4},{6,7},{7,6},{8,9},{9,8},{10,11... | collective-permute-start | bytes 3145736 | tf_op jit(solution)/shard_map/ppermute | solution.py:561
  187.3 45.1 %collective-permute-start.18 = (bf16[896,1024]{0,1:T(8,128)(2,1)S(1)}, bf16[896,1024]{0,1:T(8,128)(2,1)}, u32[]{:S(2)}, u32[]{:S(2)}) collective-permute-start(bf16[896,1024]{0,1:T(8,128)(2,1)S(1)} %get-tuple-element.281), channel_id=1, source_target_pairs={{0,1},{1,0},{2,3},{3,2},{4,5},{5,4},{6,7},{7,6},{8,9},{9,8},{10,11... | collective-permute-start | bytes 5505032 | tf_op jit(solution)/shard_map/ppermute | solution.py:561
  189.8 26.0 %collective-permute-start.14 = (bf16[128,2048]{1,0:T(8,128)(2,1)S(1)}, bf16[128,2048]{1,0:T(8,128)(2,1)}, u32[]{:S(2)}, u32[]{:S(2)}) collective-permute-start(bf16[128,2048]{1,0:T(8,128)(2,1)S(1)} %slice.132), channel_id=1, source_target_pairs={{0,4},{1,5},{4,8},{5,9},{8,12},{9,13},{12,14},{13,15},{14,10},{15,... | collective-permute-start | bytes 1572872 | tf_op jit(solution)/shard_map/ppermute | solution.py:557
  191.7 38.2 %collective-permute-start.15 = (bf16[128,2048]{1,0:T(8,128)(2,1)S(1)}, bf16[128,2048]{1,0:T(8,128)(2,1)}, u32[]{:S(2)}, u32[]{:S(2)}) collective-permute-start(bf16[128,2048]{1,0:T(8,128)(2,1)S(1)} %slice.133), channel_id=1, source_target_pairs={{0,2},{1,3},{4,0},{5,1},{8,4},{9,5},{12,8},{13,9},{14,12},{15,13},... | collective-permute-start | bytes 1572872 | tf_op jit(solution)/shard_map/ppermute | solution.py:557
  230.0 2.8 collective-permute-start.16
  230.0 3.0 collective-permute-start.17
  367.8 33.2 %collective-permute-start.19 = (bf16[4096,896]{1,0:T(8,128)(2,1)}, bf16[4096,896]{1,0:T(8,128)(2,1)}, u32[]{:S(2)}, u32[]{:S(2)}) collective-permute-start(bf16[4096,896]{1,0:T(8,128)(2,1)} %get-tuple-element.238), channel_id=1, source_target_pairs={{0,1},{1,0},{2,3},{3,2},{4,5},{5,4},{6,7},{7,6},{8,9},{9,8},{10,11... | collective-permute-start | bytes 22020104 | tf_op jit(solution)/shard_map/ppermute | solution.py:561
  373.5 27.5 %collective-permute-start.39 = (f32[26048]{0:T(1024)S(1)}, f32[26048]{0:T(1024)S(1)}, u32[]{:S(2)}, u32[]{:S(2)}) collective-permute-start(f32[26048]{0:T(1024)S(1)} %concatenate.60), channel_id=1, source_target_pairs={{0,1},{1,0},{2,3},{3,2},{4,5},{5,4},{6,7},{7,6},{8,9},{9,8},{10,11... | collective-permute-start | bytes 312584 | tf_op jit(solution)/shard_map/ppermute | solution.py:882
  373.7 27.3 %collective-permute-start.40 = (f32[26048]{0:T(1024)S(1)}, f32[26048]{0:T(1024)S(1)}, u32[]{:S(2)}, u32[]{:S(2)}) collective-permute-start(f32[26048]{0:T(1024)S(1)} %concatenate.60), channel_id=1, source_target_pairs={{0,2},{1,3},{2,0},{3,1},{4,6},{5,7},{6,4},{7,5},{8,10},{9,11},{10,... | collective-permute-start | bytes 312584 | tf_op jit(solution)/shard_map/ppermute | solution.py:882
  373.9 27.1 %collective-permute-start.41 = (f32[26048]{0:T(1024)S(1)}, f32[26048]{0:T(1024)S(1)}, u32[]{:S(2)}, u32[]{:S(2)}) collective-permute-start(f32[26048]{0:T(1024)S(1)} %concatenate.60), channel_id=1, source_target_pairs={{0,3},{1,2},{2,1},{3,0},{4,7},{5,6},{6,5},{7,4},{8,11},{9,10},{10,... | collective-permute-start | bytes 312584 | tf_op jit(solution)/shard_map/ppermute | solution.py:882
  399.3 39.8 %collective-permute-start.29 = (bf16[416,2048]{1,0:T(8,128)(2,1)}, bf16[416,2048]{1,0:T(8,128)(2,1)S(1)}, u32[]{:S(2)}, u32[]{:S(2)}) collective-permute-start(bf16[416,2048]{1,0:T(8,128)(2,1)} %pad_maximum_fusion.3), channel_id=1, source_target_pairs={{0,16},{16,0},{1,17},{17,1},{2,18},{18,2},{3,19},{19,3},{4,20},{20... | collective-permute-start | bytes 5111816 | tf_op jit(solution)/shard_map/ppermute | solution.py:778
  407.9 20.2 %collective-permute-start.20 = (bf16[256,1024]{1,0:T(8,128)(2,1)}, bf16[256,1024]{1,0:T(8,128)(2,1)S(1)}, u32[]{:S(2)}, u32[]{:S(2)}) collective-permute-start(bf16[256,1024]{1,0:T(8,128)(2,1)} %get-tuple-element.209), channel_id=1, source_target_pairs={{0,4},{1,5},{4,8},{5,9},{8,12},{9,13},{12,14},{13,15},{14,10},{15,... | collective-permute-start | bytes 1572872 | tf_op jit(solution)/shard_map/ppermute | solution.py:557
  407.9 20.2 %collective-permute-start.21 = (bf16[256,1024]{1,0:T(8,128)(2,1)S(1)}, bf16[256,1024]{1,0:T(8,128)(2,1)S(1)}, u32[]{:S(2)}, u32[]{:S(2)}) collective-permute-start(bf16[256,1024]{1,0:T(8,128)(2,1)S(1)} %get-tuple-element.210), channel_id=1, source_target_pairs={{0,2},{1,3},{4,0},{5,1},{8,4},{9,5},{12,8},{13,9},{14,12},{15,13},... | collective-permute-start | bytes 1572872 | tf_op jit(solution)/shard_map/ppermute | solution.py:557
  430.7 46.4 %collective-permute-start.22 = (bf16[512,1024]{1,0:T(8,128)(2,1)}, bf16[512,1024]{1,0:T(8,128)(2,1)}, u32[]{:S(2)}, u32[]{:S(2)}) collective-permute-start(bf16[512,1024]{1,0:T(8,128)(2,1)} %pad_maximum_fusion.4), channel_id=1, source_target_pairs={{0,4},{1,5},{4,8},{5,9},{8,12},{9,13},{12,14},{13,15},{14,10},{15,... | collective-permute-start | bytes 3145736 | tf_op jit(solution)/shard_map/ppermute | solution.py:557
  430.9 55.9 %collective-permute-start.23 = (bf16[512,1024]{1,0:T(8,128)(2,1)}, bf16[512,1024]{1,0:T(8,128)(2,1)}, u32[]{:S(2)}, u32[]{:S(2)}) collective-permute-start(bf16[512,1024]{1,0:T(8,128)(2,1)} %pad_maximum_fusion.5), channel_id=1, source_target_pairs={{0,2},{1,3},{4,0},{5,1},{8,4},{9,5},{12,8},{13,9},{14,12},{15,13},... | collective-permute-start | bytes 3145736 | tf_op jit(solution)/shard_map/ppermute | solution.py:557
  440.7 112.6 %all-to-all-start.1 = ((bf16[16,416,128]{2,1,0:T(8,128)(2,1)}), bf16[16,416,128]{2,1,0:T(8,128)(2,1)}, u32[]{:S(2)}, u32[]{:S(2)}) async-start(bf16[16,416,128]{2,1,0:T(8,128)(2,1)} %bitcast_bitcast_fusion), calls=%async_computation.2 | async-start | bytes 3407872 | tf_op jit(solution)/shard_map/all_to_all | solution.py:1066
  445.1 56.8 %collective-permute-start.26 = (bf16[256,2048]{1,0:T(8,128)(2,1)S(1)}, bf16[256,2048]{1,0:T(8,128)(2,1)S(1)}, u32[]{:S(2)}, u32[]{:S(2)}) collective-permute-start(bf16[256,2048]{1,0:T(8,128)(2,1)S(1)} %convolution_convert_fusion.2), channel_id=1, source_target_pairs={{0,16},{16,0},{1,17},{17,1},{2,18},{18,2},{3,19},{19,3},{4,20},{20... | collective-permute-start | bytes 3145736 | tf_op jit(solution)/shard_map/ppermute | solution.py:778
  490.0 40.2 %collective-permute-start.24 = (bf16[512,1024]{1,0:T(8,128)(2,1)S(1)}, bf16[512,1024]{1,0:T(8,128)(2,1)S(1)}, u32[]{:S(2)}, u32[]{:S(2)}) collective-permute-start(bf16[512,1024]{1,0:T(8,128)(2,1)S(1)} %add_convert_fusion.4), channel_id=1, source_target_pairs={{0,4},{1,5},{4,8},{5,9},{8,12},{9,13},{12,14},{13,15},{14,10},{15,... | collective-permute-start | bytes 3145736 | tf_op jit(solution)/shard_map/ppermute | solution.py:557
  492.9 39.3 %collective-permute-start.25 = (bf16[512,1024]{1,0:T(8,128)(2,1)S(1)}, bf16[512,1024]{1,0:T(8,128)(2,1)S(1)}, u32[]{:S(2)}, u32[]{:S(2)}) collective-permute-start(bf16[512,1024]{1,0:T(8,128)(2,1)S(1)} %add_convert_fusion.3), channel_id=1, source_target_pairs={{0,2},{1,3},{4,0},{5,1},{8,4},{9,5},{12,8},{13,9},{14,12},{15,13},... | collective-permute-start | bytes 3145736 | tf_op jit(solution)/shard_map/ppermute | solution.py:557
  534.9 37.7 %collective-permute-start.27 = (bf16[512,1024]{1,0:T(8,128)(2,1)}, bf16[512,1024]{1,0:T(8,128)(2,1)}, u32[]{:S(2)}, u32[]{:S(2)}) collective-permute-start(bf16[512,1024]{1,0:T(8,128)(2,1)} %add_convert_fusion.2), channel_id=1, source_target_pairs={{0,4},{1,5},{4,8},{5,9},{8,12},{9,13},{12,14},{13,15},{14,10},{15,... | collective-permute-start | bytes 3145736 | tf_op jit(solution)/shard_map/ppermute | solution.py:557
  545.6 27.1 %collective-permute-start.28 = (bf16[512,1024]{1,0:T(8,128)(2,1)}, bf16[512,1024]{1,0:T(8,128)(2,1)}, u32[]{:S(2)}, u32[]{:S(2)}) collective-permute-start(bf16[512,1024]{1,0:T(8,128)(2,1)} %add_convert_fusion.1), channel_id=1, source_target_pairs={{0,2},{1,3},{4,0},{5,1},{8,4},{9,5},{12,8},{13,9},{14,12},{15,13},... | collective-permute-start | bytes 3145736 | tf_op jit(solution)/shard_map/ppermute | solution.py:557
  551.2 32.2 %collective-permute-start.42 = (f32[26048]{0:T(1024)S(1)}, f32[26048]{0:T(1024)S(1)}, u32[]{:S(2)}, u32[]{:S(2)}) collective-permute-start(f32[26048]{0:T(1024)S(1)} %add_add_fusion.1), channel_id=1, source_target_pairs={{0,4},{1,5},{2,6},{3,7},{4,0},{5,1},{6,2},{7,3},{8,12},{9,13},{10,... | collective-permute-start | bytes 312584 | tf_op jit(solution)/shard_map/ppermute | solution.py:882
  555.8 25.1 %collective-permute-start.30 = (bf16[16,256,128]{2,1,0:T(8,128)(2,1)}, bf16[16,256,128]{2,1,0:T(8,128)(2,1)S(1)}, u32[]{:S(2)}, u32[]{:S(2)}) collective-permute-start(bf16[16,256,128]{2,1,0:T(8,128)(2,1)} %slice.155.grad_ref), channel_id=1, source_target_pairs={{0,16},{16,0},{1,17},{17,1},{2,18},{18,2},{3,19},{19,3},{4,20},{20... | collective-permute-start | bytes 3145736 | tf_op jit(solution)/shard_map/ppermute | solution.py:778
  564.9 16.0 %collective-permute-start.31 = (bf16[160,128]{1,0:T(8,128)(2,1)S(1)}, bf16[160,128]{1,0:T(8,128)(2,1)S(1)}, u32[]{:S(2)}, u32[]{:S(2)}) collective-permute-start(bf16[160,128]{1,0:T(8,128)(2,1)S(1)} %slice_reduce_fusion), channel_id=1, source_target_pairs={{0,16},{16,0},{1,17},{17,1},{2,18},{18,2},{3,19},{19,3},{4,20},{20... | collective-permute-start | bytes 122888 | tf_op jit(solution)/shard_map/ppermute | solution.py:778
  572.6 10.9 %collective-permute-start.43 = (f32[26048]{0:T(1024)S(1)}, f32[26048]{0:T(1024)S(1)}, u32[]{:S(2)}, u32[]{:S(2)}) collective-permute-start(f32[26048]{0:T(1024)S(1)} %add_add_fusion.1), channel_id=1, source_target_pairs={{0,8},{1,9},{2,10},{3,11},{4,12},{5,13},{6,14},{7,15},{8,0},{9,1},... | collective-permute-start | bytes 312584 | tf_op jit(solution)/shard_map/ppermute | solution.py:882
  572.7 10.8 %collective-permute-start.44 = (f32[26048]{0:T(1024)S(1)}, f32[26048]{0:T(1024)S(1)}, u32[]{:S(2)}, u32[]{:S(2)}) collective-permute-start(f32[26048]{0:T(1024)S(1)} %add_add_fusion.1), channel_id=1, source_target_pairs={{0,12},{1,13},{2,14},{3,15},{4,8},{5,9},{6,10},{7,11},{8,4},{9,5},... | collective-permute-start | bytes 312584 | tf_op jit(solution)/shard_map/ppermute | solution.py:882
  587.2 3.7 collective-permute-start.34
  588.8 3.1 collective-permute-start.35
  591.9 8.2 %collective-permute-start.36 = (f32[2048]{0:T(1024)S(1)}, f32[2048]{0:T(1024)S(1)}, u32[]{:S(2)}, u32[]{:S(2)}) collective-permute-start(f32[2048]{0:T(1024)S(1)} %add_add_fusion.3), channel_id=1, source_target_pairs={{0,4},{1,5},{2,6},{3,7},{4,0},{5,1},{6,2},{7,3},{8,12},{9,13},{10,... | collective-permute-start | bytes 24584 | tf_op jit(solution)/shard_map/ppermute | solution.py:882
  592.2 7.9 %collective-permute-start.37 = (f32[2048]{0:T(1024)S(1)}, f32[2048]{0:T(1024)S(1)}, u32[]{:S(2)}, u32[]{:S(2)}) collective-permute-start(f32[2048]{0:T(1024)S(1)} %add_add_fusion.3), channel_id=1, source_target_pairs={{0,8},{1,9},{2,10},{3,11},{4,12},{5,13},{6,14},{7,15},{8,0},{9,1},... | collective-permute-start | bytes 24584 | tf_op jit(solution)/shard_map/ppermute | solution.py:882
  594.0 6.0 collective-permute-start.38
  600.1 11.9 %collective-permute-start.45 = (f32[28096]{0:T(1024)S(1)}, f32[28096]{0:T(1024)S(1)}, u32[]{:S(2)}, u32[]{:S(2)}) collective-permute-start(f32[28096]{0:T(1024)S(1)} %pad_maximum_fusion.7), channel_id=1, source_target_pairs={{0,16},{16,0},{1,17},{17,1},{2,18},{18,2},{3,19},{19,3},{4,20},{20... | collective-permute-start | bytes 337160 | tf_op jit(solution)/shard_map/ppermute | solution.py:778
  (41 other events, 463.1 us)
Sparse Core Ops, SparseCore 0:
  114.2 155.6 all-gather.3
  280.2 205.2 reduce-scatter.1
